TPU v7x, 32 devices: a whole 2x2x4 slice. The times are simulated.
32 devices in a mesh: seq: 8 (over z, y), head: 4 (over x, core).
Axes of the slice: x: 2, y: 2, z: 4, core: 2. Of those that a mesh axis runs over, the one named last changes fastest.
Arguments:
- hidden_states: bfloat16 [2048, 2048], P('seq', 'head'), may hold values from -0.375 to 0.375
- w_lambda: bfloat16 [2048, 384], P('head'), may hold values from -2 to 2
- queries: bfloat16 [2048, 2048], P('seq', 'head'), may hold values from -6 to 6
- keys: bfloat16 [2048, 2048], P('seq', 'head'), may hold values from -0.046875 to 0.046875
- values: bfloat16 [2048, 4096], P('seq', 'head'), may hold values from -6 to 6
- d_out: bfloat16 [2048, 4096], P('seq', 'head'), may hold values from -0.75 to 0.75
- d_state: float32 [32, 64, 128], P('head'), may hold values from -6 to 6
Outputs:
- out: bfloat16 [2048, 4096], P('seq', 'head')
- d_queries: bfloat16 [2048, 2048], P('seq', 'head')
- d_keys: bfloat16 [2048, 2048], P('seq', 'head')
- d_values: bfloat16 [2048, 4096], P('seq', 'head')
- d_hidden: bfloat16 [2048, 2048], P('seq', 'head')
- d_w_lambda: float32 [2048, 384], P(('head', 'seq'))
All inputs are finite; a program needn't handle non-finite values.
Results may differ from a plain program's by a relative error of at most 0.0049.
Values may be sent and summed in bfloat16 or wider, within the bound.
No kernel may reach another device: no remote copies, remote signals or barrier semaphores. Data moves between devices by JAX's collectives and lax.ppermute only.
A program may use at most 64 MiB of HBM per device.

v0:
```python
import jax
import jax.numpy as jnp
from jax import lax
from jax.sharding import PartitionSpec as P

H = 32
DK = 64
DV = 128


PRECISE = lax.Precision.HIGHEST


def partner_2(value, axis, stride):
    mask = 2**stride
    pairs = [(source, source ^ mask) for source in range(lax.axis_size(axis))]
    return lax.ppermute(value, axis, pairs)


def digit_count(values, width):
    total = jnp.zeros_like(values)
    for shift in range(width):
        total = total + (values >> shift > 0).astype(jnp.int32)
    return total


def level_table(row_count, width, levels):
    later = jnp.arange(row_count, dtype=jnp.int32)[:, None]
    earlier = jnp.arange(row_count, dtype=jnp.int32)[None, :]
    depth = digit_count(jnp.bitwise_xor(later, earlier), width)
    keep = earlier <= later
    grid = jnp.arange(levels, dtype=jnp.int32)[:, None, None]
    return jnp.where((depth[None] == grid) & keep[None], 1.0, 0.0).astype(jnp.float32)


def pick_table(width, seq_bits, levels):
    wanted = width + 1 + jnp.arange(seq_bits, dtype=jnp.int32)
    return jnp.where(
        jnp.arange(levels, dtype=jnp.int32)[None, :] == wanted[:, None], 1.0, 0.0
    ).astype(jnp.float32)


def local_pass(
    query_heads, key_heads, value_heads, level_weights, table, states, picks, grad_heads
):
    query_wide = query_heads.astype(jnp.float32)
    grad_wide = grad_heads.astype(jnp.float32)
    scores = jnp.einsum("thd,shd->hts", query_heads, key_heads, preferred_element_type=jnp.float32)
    spread = jnp.einsum("thl,lts->hts", level_weights, table, precision=PRECISE)
    mixed = (scores * spread).astype(jnp.bfloat16)
    local_out = jnp.einsum("hts,shv->thv", mixed, value_heads, preferred_element_type=jnp.float32)
    chosen = jnp.einsum("thl,kl->thk", level_weights, picks, precision=PRECISE)
    scaled = chosen[:, :, :, None] * query_wide[:, :, None, :]
    carried = jnp.einsum("thkd,khdv->thv", scaled, states, precision=PRECISE)
    result = (local_out + carried).astype(jnp.bfloat16)
    grad_mixed = jnp.einsum(
        "thv,shv->hts", grad_heads, value_heads, preferred_element_type=jnp.float32
    )
    grad_values = jnp.einsum("hts,thv->shv", mixed, grad_heads, preferred_element_type=jnp.float32)
    grad_scores = (grad_mixed * spread).astype(jnp.bfloat16)
    grad_weights = jnp.einsum("hts,lts->thl", grad_mixed * scores, table, precision=PRECISE)
    grad_queries = jnp.einsum(
        "hts,shd->thd", grad_scores, key_heads, preferred_element_type=jnp.float32
    )
    grad_keys = jnp.einsum(
        "hts,thd->shd", grad_scores, query_heads, preferred_element_type=jnp.float32
    )
    grad_scaled = jnp.einsum("thv,khdv->thkd", grad_wide, states, precision=PRECISE)
    grad_queries = grad_queries + jnp.einsum(
        "thk,thkd->thd", chosen, grad_scaled, precision=PRECISE
    )
    grad_chosen = jnp.einsum("thkd,thd->thk", grad_scaled, query_wide, precision=PRECISE)
    grad_weights = grad_weights + jnp.einsum("thk,kl->thl", grad_chosen, picks, precision=PRECISE)
    grad_states = jnp.einsum("thkd,thv->khdv", scaled, grad_wide, precision=PRECISE)
    return (result, grad_queries, grad_keys, grad_values, grad_weights, grad_states)


def body(hidden_states, w_lambda, queries, keys, values, d_out, d_state):
    row_count = hidden_states.shape[0]
    heads = queries.shape[1] // DK
    levels = w_lambda.shape[1] // H
    tok_bits = row_count.bit_length() - 1
    seq_bits = lax.axis_size("seq").bit_length() - 1
    index = lax.axis_index("seq")
    partial_terms = jnp.dot(hidden_states, w_lambda, preferred_element_type=jnp.float32)
    projected = lax.psum_scatter(partial_terms, "head", scatter_dimension=1, tiled=True)
    level_weights = jax.nn.softplus(projected).reshape(row_count, heads, levels)
    query_heads = queries.reshape(row_count, heads, DK)
    key_heads = keys.reshape(row_count, heads, DK)
    value_heads = values.reshape(row_count, heads, DV)
    grad_heads = d_out.reshape(row_count, heads, DV)
    kv_state = jnp.einsum(
        "thd,thv->hdv", key_heads, value_heads, preferred_element_type=jnp.float32
    )
    top_count = 0
    low_count = seq_bits - top_count
    uppers = []
    total = kv_state
    for bit in range(low_count):
        partner = partner_2(total, "seq", bit)
        is_upper = index >> bit & 1 == 1
        uppers.append(jnp.where(is_upper, partner, 0.0))
        total = total + partner
    states = jnp.stack(uppers, 0)
    table = level_table(row_count, tok_bits, levels)
    picks = pick_table(tok_bits, seq_bits, levels)
    result, grad_queries, grad_keys, grad_values, grad_weights, state_grads = local_pass(
        query_heads, key_heads, value_heads, level_weights, table, states, picks, grad_heads
    )
    leader = index % (1 << low_count) == 0
    adjoint = jnp.where(leader, d_state, 0.0)
    for bit in reversed(range(low_count)):
        is_upper = index >> bit & 1 == 1
        pending = adjoint + jnp.where(is_upper, state_grads[bit], 0.0)
        adjoint = adjoint + partner_2(pending, "seq", bit)
    grad_keys = grad_keys + jnp.einsum(
        "thv,hdv->thd", value_heads.astype(jnp.float32), adjoint, precision=PRECISE
    )
    grad_values = grad_values + jnp.einsum(
        "thd,hdv->thv", key_heads.astype(jnp.float32), adjoint, precision=PRECISE
    )
    grad_projected = (
        grad_weights.reshape(row_count, heads * levels) * jax.nn.sigmoid(projected)
    ).astype(jnp.bfloat16)
    gathered = lax.all_gather(grad_projected, "head", axis=1, tiled=True)
    d_hidden = jnp.einsum(
        "tc,dc->td", gathered, w_lambda, preferred_element_type=jnp.float32
    ).astype(jnp.bfloat16)
    d_w_lambda = lax.psum_scatter(
        jnp.einsum("td,tc->dc", hidden_states, gathered, preferred_element_type=jnp.float32),
        "seq",
        scatter_dimension=0,
        tiled=True,
    )
    out = result.reshape(row_count, heads * DV)
    d_queries = grad_queries.reshape(row_count, heads * DK).astype(jnp.bfloat16)
    d_keys = grad_keys.reshape(row_count, heads * DK).astype(jnp.bfloat16)
    d_values = grad_values.reshape(row_count, heads * DV).astype(jnp.bfloat16)
    return (out, d_queries, d_keys, d_values, d_hidden, d_w_lambda)


def solution(mesh):
    in_specs = (
        P("seq", "head"),
        P("head", None),
        P("seq", "head"),
        P("seq", "head"),
        P("seq", "head"),
        P("seq", "head"),
        P("head", None, None),
    )
    out_specs = (
        P("seq", "head"),
        P("seq", "head"),
        P("seq", "head"),
        P("seq", "head"),
        P("seq", "head"),
        P(("head", "seq"), None),
    )
    return jax.shard_map(body, mesh=mesh, in_specs=in_specs, out_specs=out_specs, check_vma=False)
```

profile of v0, /device:TPU:0, one launch (start us, length us, event | category | flops | bytes accessed | tf_op | source)
XLA Modules:
  0.0 149.3 jit_solution(13477709651261025389)
XLA Ops:
  7.2 0.0 reduce-scatter.5.cloned.1.call-start
  7.2 1.1 copy.88
  8.4 0.2 fusion.50
  8.6 3.1 %collective-permute-start = (f32[8,64,128]{2,1,0:T(8,128)S(1)}, f32[8,64,128]{2,1,0:T(8,128)S(1)}, u32[]{:S(2)}, u32[]{:S(2)}) collective-permute-start(f32[8,64,128]{2,1,0:T(8,128)S(1)} %fusion.50), channel_id=1, source_target_pairs={{0,4},{4,0},{8,12},{12,8},{16,20},{20,16},{24,28},{28,24},{1,5},{5... | collective-permute-start | bytes 786440 | tf_op jit(solution)/shard_map/ppermute | solution.py:17
  11.7 2.1 %fusion.92 = f32[256,384]{0,1:T(8,128)} fusion(bf16[256,512]{1,0:T(8,128)(2,1)} %param.7, bf16[512,384]{1,0:T(8,128)(2,1)} %param.8), kind=kOutput, calls=%fused_computation.121 | convolution fusion | flops 100663296 | bytes 1048576 | tf_op jit(solution)/shard_map/dot_general | solution.py:85
  13.8 0.0 reduce-scatter.7.cloned.1.call-start
  13.9 0.1 copy.87
  14.1 0.3 convert_add_fusion
  14.4 3.6 %collective-permute-done = f32[8,64,128]{2,1,0:T(8,128)S(1)} collective-permute-done((f32[8,64,128]{2,1,0:T(8,128)S(1)}, f32[8,64,128]{2,1,0:T(8,128)S(1)}, u32[]{:S(2)}, u32[]{:S(2)}) %collective-permute-start) | collective-permute-done | bytes 262176 | tf_op jit(solution)/shard_map/ppermute | solution.py:17
  18.0 0.7 select_bitcast_fusion.2
  18.7 1.8 %collective-permute-start.1 = (f32[8,64,128]{2,1,0:T(8,128)S(1)}, f32[8,64,128]{2,1,0:T(8,128)S(1)}, u32[]{:S(2)}, u32[]{:S(2)}) collective-permute-start(f32[8,64,128]{2,1,0:T(8,128)S(1)} %get-tuple-element.36), channel_id=1, source_target_pairs={{0,8},{4,12},{8,0},{12,4},{16,24},{20,28},{24,16},{28,20},{1,9},{5... | collective-permute-start | bytes 786440 | tf_op jit(solution)/shard_map/ppermute | solution.py:17
  20.5 1.8 %fusion.91 = f32[8,256,256]{2,1,0:T(8,128)} fusion(bf16[256,8,64]{0,2,1:T(8,128)(2,1)S(1)} %bitcast.161, bf16[256,8,64]{0,2,1:T(8,128)(2,1)S(1)} %bitcast.158), kind=kOutput, calls=%fused_computation.120 | convolution fusion | flops 67108864 | bytes 2621440 | tf_op jit(solution)/shard_map/thd,shd->hts/dot_general | solution.py:48
  22.4 3.8 %collective-permute-done.1 = f32[8,64,128]{2,1,0:T(8,128)S(1)} collective-permute-done((f32[8,64,128]{2,1,0:T(8,128)S(1)}, f32[8,64,128]{2,1,0:T(8,128)S(1)}, u32[]{:S(2)}, u32[]{:S(2)}) %collective-permute-start.1) | collective-permute-done | bytes 262176 | tf_op jit(solution)/shard_map/ppermute | solution.py:17
  26.2 0.7 select_bitcast_fusion.1
  26.9 2.5 %collective-permute-start.2 = (f32[8,64,128]{2,1,0:T(8,128)S(1)}, f32[8,64,128]{2,1,0:T(8,128)S(1)}, u32[]{:S(2)}, u32[]{:S(2)}) collective-permute-start(f32[8,64,128]{2,1,0:T(8,128)S(1)} %get-tuple-element.38), channel_id=1, source_target_pairs={{0,16},{4,20},{8,24},{12,28},{16,0},{20,4},{24,8},{28,12},{1,17},{... | collective-permute-start | bytes 786440 | tf_op jit(solution)/shard_map/ppermute | solution.py:17
  29.5 0.9 copy.132
  30.4 0.8 bitcast_convert_fusion
  31.2 8.8 %collective-permute-done.2 = f32[8,64,128]{2,1,0:T(8,128)S(1)} collective-permute-done((f32[8,64,128]{2,1,0:T(8,128)S(1)}, f32[8,64,128]{2,1,0:T(8,128)S(1)}, u32[]{:S(2)}, u32[]{:S(2)}) %collective-permute-start.2) | collective-permute-done | bytes 262176 | tf_op jit(solution)/shard_map/ppermute | solution.py:17
  40.1 0.7 select_bitcast_fusion
  40.8 1.0 compare_select_fusion
  41.8 0.4 copy.89
  42.2 0.2 fusion.71
  42.5 4.2 %fusion.2 = f32[256,256,8]{1,2,0:T(8,128)S(1)} fusion(f32[256,8,12]{2,1,0:T(8,128)S(1)} %copy.89, s32[256,256]{1,0:T(8,128)S(1)} %convert_add_fusion, pred[256,256]{1,0:T(8,128)(4,1)S(1)} %iota_compare_fusion.1), kind=kOutput, calls=%fused_computation.2 | convolution fusion | flops 77856768 | bytes 2523136 | tf_op jit(solution)/shard_map/thl,lts->hts/dot_general | solution.py:49
  46.8 1.1 fusion.90
  47.9 6.3 %fusion = f32[256,8,12]{2,1,0:T(8,128)} fusion(f32[8,256,256]{2,1,0:T(8,128)S(1)} %get-tuple-element.32, s32[256,256]{1,0:T(8,128)S(1)} %copy-done.22, pred[256,256]{1,0:T(8,128)(4,1)S(1)} %iota_compare_fusion.1), kind=kOutput, calls=%fused_computation | convolution fusion | flops 77856768 | bytes 2523136 | tf_op jit(solution)/shard_map/hts,lts->thl/dot_general | solution.py:61
  54.2 1.6 %copy.103 = f32[256,8,12]{0,1,2:T(8,128)S(1)} copy(f32[256,8,12]{2,1,0:T(8,128)} %fusion) | data formatting | bytes 196608 | tf_op jit(solution)/shard_map/hts,lts->thl/dot_general | solution.py:61
  55.8 0.5 convolution_bitcast_fusion.2
  56.3 0.5 copy-done.3
  56.8 0.1 copy-done.9
  56.8 0.1 copy-done.10
  56.9 0.1 copy-done.11
  57.0 0.2 copy-done.13
  57.2 1.7 %fusion.19 = (f32[256,8,64]{0,2,1:T(8,128)}, f32[256,8,3,64]{0,3,2,1:T(8,128)S(1)}, f32[8,3,64,256]{3,2,1,0:T(8,128)S(1)}) fusion(f32[256,8,3]{0,2,1:T(4,128)S(1)} %fusion.71, f32[256,8,64]{0,2,1:T(8,128)S(1)} %copy-done.3, bf16[256,8,128,1]{2,1,0,3:T(8,128)(2,1)S(1)} %bitcast.165, f32[1,8,64,128]{3,2,1,0:T(8,128)S(1)} %copy-done.9, ...), kind=kOutput, calls=%fused_computation.22 | convolution fusion | flops 605421568 | bytes 5529600 | tf_op jit(solution)/shard_map/thv,khdv->thkd/dot_general | solution.py:68
  58.9 1.8 %fusion.35 = f32[3,8,64,128]{3,2,1,0:T(8,128)} fusion(f32[256,8,3,64]{0,3,2,1:T(8,128)S(1)} %get-tuple-element.40, bf16[256,1024]{1,0:T(8,128)(2,1)S(1)} %copy-done.1), kind=kOutput, calls=%fused_computation.35 | convolution fusion | flops 603979776 | bytes 2883584 | tf_op jit(solution)/shard_map/thkd,thv->khdv/dot_general | solution.py:74
  60.7 2.8 %fusion.31 = bf16[256,8,128]{0,2,1:T(8,128)(2,1)} fusion(f32[256,8,128]{0,2,1:T(8,128)S(1)} %convolution_bitcast_fusion.2, f32[256,8,3,64]{0,3,2,1:T(8,128)S(1)} %get-tuple-element.40, f32[1,8,64,128]{3,2,1,0:T(8,128)S(1)} %copy-done.9, f32[1,8,64,128]{3,2,1,0:T(8,128)S(1)} %copy-done.11, f32[1,8,64,128]{3,2,1,0:T(8,128)S(1)} %copy-done.10), kind=kOutput, calls=%fused_computation.33 | convolution fusion | flops 604897280 | bytes 3932160 | tf_op jit(solution)/shard_map/thkd,khdv->thv/dot_general | solution.py:54
  63.5 0.2 fusion.18
  63.7 0.4 fusion.69
  64.1 0.1 copy_add_fusion
  64.2 0.7 reshape.119
  64.8 1.0 multiply_convert_fusion
  65.8 5.6 %all_gather.3 = bf16[256,384]{0,1:T(8,128)(2,1)S(1)} all-gather(bf16[256,96]{0,1:T(8,128)(2,1)S(1)} %multiply_convert_fusion), channel_id=1, replica_groups=mesh['seq'=8,'head'=4] {'head'}, dimensions={1}, use_global_device_ids=true | all-gather | bytes 245760 | tf_op jit(solution)/shard_map/all_gather | solution.py:125
  71.4 0.7 copy-done.15
  72.1 2.1 %convolution_bitcast_fusion.3 = f32[512,384]{0,1:T(8,128)} fusion(bf16[256,384]{0,1:T(8,128)(2,1)S(1)} %all_gather.3, bf16[256,512]{1,0:T(8,128)(2,1)} %param.7), kind=kOutput, calls=%fused_computation.36 | convolution fusion | flops 100663296 | bytes 1245184 | tf_op jit(solution)/shard_map/td,tc->dc/dot_general | solution.py:130
  74.2 2.3 %copy.126 = f32[512,384]{1,0:T(8,128)} copy(f32[512,384]{0,1:T(8,128)} %convolution_bitcast_fusion.3) | data formatting | bytes 1572864
  76.5 1.1 fusion.65
  77.7 0.1 collective-permute-start.3
  77.7 1.4 convolution_bitcast_fusion.1
  79.1 15.9 %collective-permute-done.3 = f32[8,64,128]{2,1,0:T(8,128)S(1)} collective-permute-done((f32[8,64,128]{2,1,0:T(8,128)S(1)}, f32[8,64,128]{2,1,0:T(8,128)S(1)}, u32[]{:S(2)}, u32[]{:S(2)}) %collective-permute-start.3) | collective-permute-done | bytes 262176 | tf_op jit(solution)/shard_map/ppermute | solution.py:17
  95.0 1.8 %fusion.63 = f32[8,64,128]{2,1,0:T(8,128)} fusion(f32[3,8,64,128]{3,2,1,0:T(8,128)} %fusion.35, pred[]{:T(512)S(6)} %eq.59, f32[8,64,128]{2,1,0:T(8,128)S(1)} %collective-permute-done.3, f32[8,64,128]{2,1,0:T(8,128)S(1)} %copy-done.7, pred[]{:T(512)S(6)} %eq.64), kind=kLoop, calls=%fused_computation.72 | loop fusion | flops 262144 | bytes 1048578 | tf_op jit(solution)/shard_map/add | solution.py:114
  96.9 1.1 fusion.40
  98.0 1.0 copy.106
  99.0 1.8 %copy.107 = bf16[256,512]{1,0:T(8,128)(2,1)} copy(bf16[256,512]{0,1:T(8,128)(2,1)} %bitcast.167) | data formatting | bytes 524288
  100.8 1.0 convolution_convert_fusion
  101.9 5.3 %collective-permute-done.4 = f32[8,64,128]{2,1,0:T(8,128)} collective-permute-done((f32[8,64,128]{2,1,0:T(8,128)}, f32[8,64,128]{2,1,0:T(8,128)}, u32[]{:S(2)}, u32[]{:S(2)}) %collective-permute-start.4) | collective-permute-done | bytes 262176 | tf_op jit(solution)/shard_map/ppermute | solution.py:17
  107.2 1.2 fusion.61
  108.4 1.3 collective-permute-start.5
  109.6 0.3 convolution_bitcast_fusion.4
  109.9 6.4 %collective-permute-done.5 = f32[8,64,128]{2,1,0:T(8,128)S(1)} collective-permute-done((f32[8,64,128]{2,1,0:T(8,128)S(1)}, f32[8,64,128]{2,1,0:T(8,128)S(1)}, u32[]{:S(2)}, u32[]{:S(2)}) %collective-permute-start.5) | collective-permute-done | bytes 262176 | tf_op jit(solution)/shard_map/ppermute | solution.py:17
  116.3 0.7 fusion.41
  117.0 0.0 copy-done.18
  117.0 0.8 copy.108
  117.9 1.6 %fusion.34 = bf16[256,8,128]{0,2,1:T(8,128)(2,1)S(1)} fusion(f32[256,8,128]{0,2,1:T(8,128)S(1)} %copy-done.6, bf16[256,8,64]{0,2,1:T(8,128)(2,1)S(1)} %bitcast.160, f32[8,64,128]{2,1,0:T(8,128)S(1)} %get-tuple-element.31, f32[8,64,128]{2,1,0:T(8,128)} %copy-done.18), kind=kOutput, calls=%fused_computation.34 | convolution fusion | flops 201916416 | bytes 2359296 | tf_op jit(solution)/shard_map/thd,hdv->thv/dot_general | solution.py:119
  119.4 1.0 copy.109
  120.5 22.0 %reduce-scatter.7.cloned.1.call-done = f32[64,384]{1,0:T(8,128)} async-done(((f32[512,384]{1,0:T(8,128)}), f32[64,384]{1,0:T(8,128)}) %reduce-scatter.7.cloned.1.call-update) | async-done | bytes 98320
  (47 shorter events, 0.2 us)
Async XLA Ops:
  7.2 1.2 copy-start
  7.2 6.7 %copy-start.20 = (bf16[256,512]{1,0:T(8,128)(2,1)S(1)}, bf16[256,512]{1,0:T(8,128)(2,1)}, u32[]{:S(2)}) copy-start(bf16[256,512]{1,0:T(8,128)(2,1)} %param.9) | copy-start | bytes 786436
  7.2 33.6 %reduce-scatter.5.cloned.1.call-start = ((), (), s32[]{:S(2)}) async-start(), calls=%async_computation.2 | async-start | bytes 491520 | tf_op jit(solution)/shard_map/reduce_scatter | solution.py:86
  8.6 9.4 %collective-permute-start = (f32[8,64,128]{2,1,0:T(8,128)S(1)}, f32[8,64,128]{2,1,0:T(8,128)S(1)}, u32[]{:S(2)}, u32[]{:S(2)}) collective-permute-start(f32[8,64,128]{2,1,0:T(8,128)S(1)} %fusion.50), channel_id=1, source_target_pairs={{0,4},{4,0},{8,12},{12,8},{16,20},{20,16},{24,28},{28,24},{1,5},{5... | collective-permute-start | bytes 786440 | tf_op jit(solution)/shard_map/ppermute | solution.py:17
  13.8 128.7 %reduce-scatter.7.cloned.1.call-start = ((), (), s32[]{:S(2)}) async-start(), calls=%async_computation.3 | async-start | bytes 884736
  14.0 16.3 %copy-start.4 = (bf16[256,512]{0,1:T(8,128)(2,1)}, bf16[256,512]{0,1:T(8,128)(2,1)S(1)}, u32[]{:S(2)}) copy-start(bf16[256,512]{0,1:T(8,128)(2,1)S(1)} %copy.87) | copy-start | bytes 786436
  14.4 28.1 %copy-start.21 = (s32[256,256]{1,0:T(8,128)}, s32[256,256]{1,0:T(8,128)S(1)}, u32[]{:S(2)}) copy-start(s32[256,256]{1,0:T(8,128)S(1)} %convert_add_fusion) | copy-start | bytes 786436
  18.7 10.8 %copy-start.1 = (bf16[256,1024]{1,0:T(8,128)(2,1)S(1)}, bf16[256,1024]{1,0:T(8,128)(2,1)}, u32[]{:S(2)}) copy-start(bf16[256,1024]{1,0:T(8,128)(2,1)} %param.12) | copy-start | bytes 1572868
  18.7 7.5 %collective-permute-start.1 = (f32[8,64,128]{2,1,0:T(8,128)S(1)}, f32[8,64,128]{2,1,0:T(8,128)S(1)}, u32[]{:S(2)}, u32[]{:S(2)}) collective-permute-start(f32[8,64,128]{2,1,0:T(8,128)S(1)} %get-tuple-element.36), channel_id=1, source_target_pairs={{0,8},{4,12},{8,0},{12,4},{16,24},{20,28},{24,16},{28,20},{1,9},{5... | collective-permute-start | bytes 786440 | tf_op jit(solution)/shard_map/ppermute | solution.py:17
  26.9 13.1 %collective-permute-start.2 = (f32[8,64,128]{2,1,0:T(8,128)S(1)}, f32[8,64,128]{2,1,0:T(8,128)S(1)}, u32[]{:S(2)}, u32[]{:S(2)}) collective-permute-start(f32[8,64,128]{2,1,0:T(8,128)S(1)} %get-tuple-element.38), channel_id=1, source_target_pairs={{0,16},{4,20},{8,24},{12,28},{16,0},{20,4},{24,8},{28,12},{1,17},{... | collective-permute-start | bytes 786440 | tf_op jit(solution)/shard_map/ppermute | solution.py:17
  42.5 4.3 %copy-start.2 = (f32[8,256,256]{2,1,0:T(8,128)S(1)}, f32[8,256,256]{2,1,0:T(8,128)}, u32[]{:S(2)}) copy-start(f32[8,256,256]{2,1,0:T(8,128)} %fusion.91) | copy-start | bytes 6291460
  46.8 1.1 copy-start.22
  55.7 1.0 copy-start.3
  55.7 1.1 copy-start.9
  55.7 1.2 copy-start.10
  55.8 1.2 copy-start.11
  55.8 1.4 copy-start.13
  71.4 0.7 copy-start.15
  76.5 18.5 %copy-start.7 = (f32[8,64,128]{2,1,0:T(8,128)S(1)}, f32[8,64,128]{2,1,0:T(8,128)}, u32[]{:S(2)}) copy-start(f32[8,64,128]{2,1,0:T(8,128)} %param.13) | copy-start | bytes 786436
  76.5 20.3 %copy-start.14 = (f32[256,8,64]{0,2,1:T(8,128)S(1)}, f32[256,8,64]{0,2,1:T(8,128)}, u32[]{:S(2)}) copy-start(f32[256,8,64]{0,2,1:T(8,128)} %get-tuple-element.39) | copy-start | bytes 1572868
  77.7 17.4 %collective-permute-start.3 = (f32[8,64,128]{2,1,0:T(8,128)S(1)}, f32[8,64,128]{2,1,0:T(8,128)S(1)}, u32[]{:S(2)}, u32[]{:S(2)}) collective-permute-start(f32[8,64,128]{2,1,0:T(8,128)S(1)} %fusion.65), channel_id=1, source_target_pairs={{0,16},{4,20},{8,24},{12,28},{16,0},{20,4},{24,8},{28,12},{1,17},{... | collective-permute-start | bytes 786440 | tf_op jit(solution)/shard_map/ppermute | solution.py:17
  79.1 18.9 %copy-start.12 = (bf16[256,8,128]{0,2,1:T(8,128)(2,1)S(1)}, bf16[256,8,128]{0,2,1:T(8,128)(2,1)}, u32[]{:S(2)}) copy-start(bf16[256,8,128]{0,2,1:T(8,128)(2,1)} %fusion.31) | copy-start | bytes 1572868
  95.0 1.8 %copy-start.19 = (f32[8,64,128]{2,1,0:T(8,128)}, f32[8,64,128]{2,1,0:T(8,128)S(1)}, u32[]{:S(2)}) copy-start(f32[8,64,128]{2,1,0:T(8,128)S(1)} %collective-permute-done.3) | copy-start | bytes 786436
  96.8 4.0 %copy-start.16 = (bf16[256,384]{0,1:T(8,128)(2,1)S(1)}, bf16[256,384]{0,1:T(8,128)(2,1)}, u32[]{:S(2)}) copy-start(bf16[256,384]{0,1:T(8,128)(2,1)} %copy-done.15) | copy-start | bytes 589828
  96.8 4.0 %copy-start.17 = (bf16[512,384]{1,0:T(8,128)(2,1)S(1)}, bf16[512,384]{1,0:T(8,128)(2,1)}, u32[]{:S(2)}) copy-start(bf16[512,384]{1,0:T(8,128)(2,1)} %param.8) | copy-start | bytes 1179652
  96.8 10.3 %collective-permute-start.4 = (f32[8,64,128]{2,1,0:T(8,128)}, f32[8,64,128]{2,1,0:T(8,128)}, u32[]{:S(2)}, u32[]{:S(2)}) collective-permute-start(f32[8,64,128]{2,1,0:T(8,128)} %fusion.63), channel_id=1, source_target_pairs={{0,8},{4,12},{8,0},{12,4},{16,24},{20,28},{24,16},{28,20},{1,9},{5... | collective-permute-start | bytes 786440 | tf_op jit(solution)/shard_map/ppermute | solution.py:17
  96.8 10.3 %copy-start.8 = (f32[8,64,128]{2,1,0:T(8,128)S(1)}, f32[8,64,128]{2,1,0:T(8,128)}, u32[]{:S(2)}) copy-start(f32[8,64,128]{2,1,0:T(8,128)} %param.13) | copy-start | bytes 786436
  98.0 11.6 %copy-start.5 = (bf16[256,512]{0,1:T(8,128)(2,1)S(1)}, bf16[256,512]{0,1:T(8,128)(2,1)}, u32[]{:S(2)}) copy-start(bf16[256,512]{0,1:T(8,128)(2,1)} %copy-done.4) | copy-start | bytes 786436
  108.4 9.5 %copy-start.6 = (f32[256,8,128]{0,2,1:T(8,128)S(1)}, f32[256,8,128]{0,2,1:T(8,128)}, u32[]{:S(2)}) copy-start(f32[256,8,128]{0,2,1:T(8,128)} %convolution_bitcast_fusion.1) | copy-start | bytes 3145732
  108.4 7.9 %collective-permute-start.5 = (f32[8,64,128]{2,1,0:T(8,128)S(1)}, f32[8,64,128]{2,1,0:T(8,128)S(1)}, u32[]{:S(2)}, u32[]{:S(2)}) collective-permute-start(f32[8,64,128]{2,1,0:T(8,128)S(1)} %get-tuple-element.30), channel_id=1, source_target_pairs={{0,4},{4,0},{8,12},{12,8},{16,20},{20,16},{24,28},{28,24},{1,5},{5... | collective-permute-start | bytes 786440 | tf_op jit(solution)/shard_map/ppermute | solution.py:17
  116.3 0.7 copy-start.18
Sparse Core Ops, SparseCore 0:
  14.0 21.0 reduce-scatter.4
  76.6 65.8 reduce-scatter.6
where the time goes:
time: 150 us; the launch traced here: 149 us
  waiting for transfers between devices  66 us (44%)
  matrix products  31.4 us (21%)
  between operations  14.4 us (10%)
  local copies, waits for them, and re-layouts  13.5 us (9%)
  other arithmetic  9.67 us (6%)
  starting transfers between devices  8.82 us (6%)
  blocking collectives  5.6 us (4%)
    ppermute x6, waiting for transfers between devices, partner_2(): return lax.ppermute(value, axis, pairs)  43.9 us
    unnamed x3, waiting for transfers between devices  22.1 us
    unnamed x54, local copies, waits for them, and re-layouts  10.8 us
    ppermute x6, starting transfers between devices, partner_2(): return lax.ppermute(value, axis, pairs)  8.74 us
    dot_general x1, matrix products, local_pass(): jnp.einsum('hts,lts->thl', grad_mixed * scores, table, precision=PRECISE)  6.25 us
    all_gather x1, blocking collectives, body(): gathered = lax.all_gather(grad_projected, 'head', axis=1, tiled=True)  5.6 us
    dot_general x1, matrix products, local_pass(): spread = jnp.einsum('thl,lts->hts', level_weights, table, precision=PRECISE)  4.25 us
    add x3, other arithmetic, body(): pending = adjoint + jnp.where(is_upper, state_grads[bit], 0.0)  4.11 us
  transfers between devices with their start and end apart: 8, of which 7 were waited for; matrix products, arithmetic and copies ran while one was open for 16% of the time, Pallas kernels for 0%

commit v1 on v0

v1 whole, which is shorter than its diff:
```python
import functools

import jax
import jax.numpy as jnp
from jax import lax
from jax.experimental import pallas as pl
from jax.experimental.pallas import tpu as pltpu
from jax.sharding import PartitionSpec as P

F32 = jnp.float32
BF16 = jnp.bfloat16
LANES = 128
SUB = 8
VM = pl.BlockSpec(memory_space=pltpu.VMEM)
SM = pl.BlockSpec(memory_space=pltpu.SMEM)


def nn(a, b):
    return lax.dot_general(a, b, (((1,), (0,)), ((), ())), preferred_element_type=F32)


def nt(a, b):
    return lax.dot_general(a, b, (((1,), (1,)), ((), ())), preferred_element_type=F32)


def tn(a, b):
    return lax.dot_general(a, b, (((0,), (0,)), ((), ())), preferred_element_type=F32)


def call(kernel, outs, specs, flops, name, **kwargs):
    size = sum(o.size * o.dtype.itemsize for o in outs)
    return pl.pallas_call(
        kernel,
        out_shape=outs,
        in_specs=specs,
        compiler_params=pltpu.CompilerParams(vmem_limit_bytes=24 << 20),
        cost_estimate=pl.CostEstimate(flops=flops, bytes_accessed=2 * size, transcendentals=0),
        name=name,
        **kwargs,
    )


def swap(value, axis, bit):
    mask = 1 << bit
    pairs = [(source, source ^ mask) for source in range(lax.axis_size(axis))]
    return lax.ppermute(value, axis, pairs)


def state_kernel(dims, k_ref, v_ref, kv_ref, kvb_ref):
    nh, dk, dv = dims
    for pair in range(nh // 2):
        turned = k_ref[:, pair * 2 * dk:(pair + 1) * 2 * dk].T
        for j in range(2):
            h = 2 * pair + j
            kv = nn(turned[j * dk:(j + 1) * dk], v_ref[:, h * dv:(h + 1) * dv])
            kv_ref[h * dk:(h + 1) * dk, :] = kv
            kvb_ref[h * dk:(h + 1) * dk, :] = kv.astype(BF16)


def project_kernel(w_ref, x_ref, p_ref):
    p_ref[...] = lax.dot_general(
        w_ref[...], x_ref[...], (((0,), (1,)), ((), ())), preferred_element_type=F32)


def weight_kernel(dims, levels, first, count, keep_ref, got_ref, q_ref, g_ref,
                  proj_ref, lw_ref, qt_ref, gu_ref):
    nh, dk, dv = dims
    proj = keep_ref[...] + got_ref[...].astype(F32)
    proj_ref[...] = proj
    lw_ref[...] = jnp.maximum(proj, 0.0) + jnp.log1p(jnp.exp(-jnp.abs(proj)))
    for pair in range(nh // 2):
        turned = q_ref[:, pair * 2 * dk:(pair + 1) * 2 * dk].T
        qt_ref[pair * 2 * dk:(pair + 1) * 2 * dk, :] = turned
        wide = turned.astype(F32)
        for j in range(2):
            h = 2 * pair + j
            scaled = jnp.concatenate(
                [wide[j * dk:(j + 1) * dk] * lw_ref[h * levels + first + m:h * levels + first + m + 1, :]
                 for m in range(count)], axis=0)
            grad = nn(scaled.astype(BF16), g_ref[:, h * dv:(h + 1) * dv])
            for m in range(count):
                gu_ref[m, h * dk:(h + 1) * dk, :] = grad[m * dk:(m + 1) * dk]


def spread_half(rows, lane, low, t_low):
    digits = (low ^ t_low)
    near = jnp.where(digits == 0, rows[0], jnp.where(digits < 2, rows[1], jnp.where(digits < 4, rows[2], rows[3])))
    near = jnp.where(low <= t_low, near, 0.0)
    parts = []
    for a in range(LANES // SUB):
        value = None
        for l in reversed(range(4, 8)):
            if (a >> (l - 4)) & 1 == 0:
                end = (((a >> (l - 3)) + 1) << (l - 3)) * SUB
                value = rows[l] if value is None else jnp.where(lane < end, rows[l], value)
        value = near if value is None else jnp.where(lane < (a + 1) * SUB, near, value)
        if a:
            value = jnp.where(lane < a * SUB, 0.0, value)
        parts.append(value)
    return jnp.concatenate(parts, axis=0)


def level_sums(prod, lane, low, t_low):
    count = LANES // SUB
    group = lane // SUB
    cur = [prod[a * SUB:(a + 1) * SUB] for a in range(count)]
    near = jnp.zeros_like(cur[0])
    for a in range(count):
        near = jnp.where(group == a, cur[a], near)
    near = jnp.where(low <= t_low, near, 0.0)
    digits = low ^ t_low
    sums = []
    for l in range(4):
        lo, hi = (0, 1) if l == 0 else (1 << (l - 1), 1 << l)
        sums.append(jnp.where((digits >= lo) & (digits < hi), near, 0.0))
    for l in range(4, 8):
        total = jnp.zeros_like(near)
        for a in range(0, len(cur), 2):
            total = jnp.where((lane >> (l - 1)) == a + 1, cur[a], total)
        sums.append(total)
        cur = [cur[a] + cur[a + 1] for a in range(0, len(cur), 2)]
    return [jnp.sum(s, axis=0, keepdims=True) for s in sums]


def local_kernel(dims, levels, k_ref, q_ref, v_ref, g_ref, lw_ref, out_ref, dq_ref, dk_ref, dv_ref, gl_ref):
    nh, dk, dv = dims
    kp, qp = k_ref[...], q_ref[...]
    kt, qt = kp.T, qp.T
    zero = jnp.zeros_like(qt[:dk])
    lane = lax.broadcasted_iota(jnp.int32, (SUB, LANES), 1)
    low = lax.broadcasted_iota(jnp.int32, (SUB, LANES), 0)
    t_low = lane % SUB
    wide_lane = lax.broadcasted_iota(jnp.int32, qp.shape, 1)
    gl_ref[...] = jnp.zeros_like(gl_ref)
    dk_sum = None
    for j in range(2):
        vj = v_ref[:, j * dv:(j + 1) * dv]
        gj = g_ref[:, j * dv:(j + 1) * dv]
        qz = jnp.concatenate([qt[:dk], zero] if j == 0 else [zero, qt[dk:]], axis=0)
        scores = nn(kp, qz)
        grads = nt(vj, gj)
        base = j * levels
        cross = lw_ref[base + 8:base + 9, LANES:]
        halves = []
        for x in range(2):
            rows = [jnp.broadcast_to(lw_ref[base + l:base + l + 1, x * LANES:(x + 1) * LANES], (SUB, LANES))
                    for l in range(8)]
            halves.append(spread_half(rows, lane, low, t_low))

        def weigh(full):
            top = jnp.concatenate([full[:LANES, :LANES] * halves[0], full[:LANES, LANES:] * cross], axis=1)
            bottom = full[LANES:, LANES:] * halves[1]
            bottom = jnp.concatenate([jnp.zeros_like(bottom), bottom], axis=1)
            return jnp.concatenate([top, bottom], axis=0).astype(BF16)

        mixed = weigh(scores)
        grad_scores = weigh(grads)
        for x in range(2):
            part = slice(x * LANES, (x + 1) * LANES)
            sums = level_sums(scores[part, part] * grads[part, part], lane, low, t_low)
            for l in range(8):
                gl_ref[base + l:base + l + 1, part] = sums[l]
        crossed = scores[:LANES, LANES:] * grads[:LANES, LANES:]
        gl_ref[base + 8:base + 9, LANES:] = jnp.sum(crossed, axis=0, keepdims=True)
        out_ref[j * dv:(j + 1) * dv, :] = tn(vj, mixed)
        dq_ref[j * dk:(j + 1) * dk, :] = nn(kt[j * dk:(j + 1) * dk], grad_scores)
        dv_ref[:, j * dv:(j + 1) * dv] = nn(mixed, gj)
        mine = (wide_lane < dk) if j == 0 else (wide_lane >= dk)
        term = nn(grad_scores, jnp.where(mine, qp, jnp.zeros_like(qp)))
        dk_sum = term if dk_sum is None else dk_sum + term
    dk_ref[...] = dk_sum


def carry_kernel(dims, levels, first, count, idx_ref, *refs):
    nh, dk, dv = dims
    ups = refs[:count]
    g_ref, qt_ref, lw_ref, proj_ref, gl_ref, dql_ref, gp_ref, dq_ref = refs[count:]
    index = idx_ref[0]
    for pair in range(nh // 2):
        halves = []
        for j in range(2):
            h = 2 * pair + j
            rows = slice(h * dk, (h + 1) * dk)
            gj = g_ref[:, h * dv:(h + 1) * dv]
            wide = qt_ref[rows, :].astype(F32)
            total = dql_ref[rows, :]
            for m in range(count):
                r = h * levels + first + m
                up = ((index >> m) & 1).astype(F32)
                x = nt(ups[m][rows, :], gj) * up
                total = total + x * lw_ref[r:r + 1, :]
                gl_ref_row = jnp.sum(x * wide, axis=0, keepdims=True)
                gp_ref[r:r + 1, :] = gl_ref_row
            halves.append(total)
        dq_ref[:, pair * 2 * dk:(pair + 1) * 2 * dk] = jnp.concatenate(halves, axis=0).T.astype(BF16)
        for j in range(2):
            r = (2 * pair + j) * levels
            gp_ref[r:r + first, :] = gl_ref[r:r + first, :]


def out_kernel(dims, levels, first, count, idx_ref, *refs):
    nh, dk, dv = dims
    ups = refs[:count]
    qt_ref, lw_ref, outl_ref, out_ref = refs[count:]
    index = idx_ref[0]
    for h in range(nh):
        rows = slice(h * dk, (h + 1) * dk)
        total = outl_ref[h * dv:(h + 1) * dv, :]
        for m in range(count):
            r = h * levels + first + m
            up = ((index >> m) & 1).astype(F32)
            total = total + tn(ups[m][rows, :], qt_ref[rows, :]) * (lw_ref[r:r + 1, :] * up)
        out_ref[:, h * dv:(h + 1) * dv] = total.T.astype(BF16)


def wgrad_kernel(gp_ref, x_ref, dw_ref):
    dw_ref[...] = lax.dot_general(
        x_ref[...], gp_ref[...], (((0,), (1,)), ((), ())), preferred_element_type=F32)


def hidden_kernel(gp_ref, w_ref, dx_ref):
    dx_ref[...] = lax.dot_general(
        gp_ref[...], w_ref[...], (((0,), (1,)), ((), ())), preferred_element_type=F32).astype(BF16)


def final_kernel(dims, adj_ref, ds_ref, k_ref, v_ref, dkl_ref, dvl_ref, dk_ref, dv_ref):
    nh, dk, dv = dims
    zero = jnp.zeros((dk, dv), BF16)
    for pair in range(nh // 2):
        adj = [(adj_ref[h * dk:(h + 1) * dk, :] + ds_ref[h * dk:(h + 1) * dk, :]).astype(BF16)
               for h in (2 * pair, 2 * pair + 1)]
        kp = k_ref[:, pair * 2 * dk:(pair + 1) * 2 * dk]
        total = dkl_ref[:, pair * 2 * dk:(pair + 1) * 2 * dk]
        for j in range(2):
            h = 2 * pair + j
            padded = jnp.concatenate([adj[j], zero] if j == 0 else [zero, adj[j]], axis=0)
            cols = slice(h * dv, (h + 1) * dv)
            total = total + nt(v_ref[:, cols], padded)
            dv_ref[:, cols] = (dvl_ref[:, cols] + nn(kp, padded)).astype(BF16)
        dk_ref[:, pair * 2 * dk:(pair + 1) * 2 * dk] = total.astype(BF16)


def body(hidden, w, queries, keys, values, d_out, d_state):
    tokens, width = hidden.shape
    dims = d_state.shape
    nh, dk, dv = dims
    n_seq, n_head = lax.axis_size("seq"), lax.axis_size("head")
    seq_bits, head_bits = n_seq.bit_length() - 1, n_head.bit_length() - 1
    cols = w.shape[1]
    levels = cols // (nh * n_head)
    own = nh * levels
    first = tokens.bit_length()
    si, hi = lax.axis_index("seq"), lax.axis_index("head")
    idx = jnp.reshape(si, (1,)).astype(jnp.int32)
    S = jax.ShapeDtypeStruct
    rows = nh * dk

    kv, kvb = call(functools.partial(state_kernel, dims), [S((rows, dv), F32), S((rows, dv), BF16)],
                   [VM, VM], 2 * tokens * rows * dv, "kv_state")(keys, values)
    partial = call(project_kernel, [S((cols, tokens), F32)], [VM, VM], 2 * tokens * width * cols, "project")(w, hidden)[0]

    keep = partial
    got = None
    for bit in reversed(range(head_bits)):
        pair = keep.reshape(2, keep.shape[0] // 2, tokens)
        mine = (hi >> bit) & 1
        send = lax.dynamic_index_in_dim(pair, 1 - mine, 0, keepdims=False).astype(BF16)
        keep = lax.dynamic_index_in_dim(pair, mine, 0, keepdims=False)
        got = swap(send, "head", bit)
        if bit:
            keep = keep + got.astype(F32)
    proj, lw, qt, gu = call(
        functools.partial(weight_kernel, dims, levels, first, seq_bits),
        [S((own, tokens), F32), S((own, tokens), F32), S((rows, tokens), BF16), S((seq_bits, rows, dv), F32)],
        [VM] * 4, 2 * tokens * rows * dv * seq_bits, "level_weights")(keep, got, queries, d_out)

    top = seq_bits - 1
    total, send = kv, kvb
    ups = []
    for bit in range(top):
        partner = swap(send, "seq", bit)
        ups.append(partner)
        total = total + partner.astype(F32)
        send = total.astype(BF16)
    upper_top = ((si >> top) & 1) == 1
    partner = swap(jnp.where(upper_top, gu[top].astype(BF16), send), "seq", top)
    ups.append(partner)
    adjoint = jnp.where(upper_top, 0.0, partner.astype(F32))
    for bit in reversed(range(top)):
        pending = adjoint + jnp.where(((si >> bit) & 1) == 1, gu[bit], 0.0)
        adjoint = adjoint + swap(pending.astype(BF16), "seq", bit).astype(F32)

    pair_spec = lambda n: pl.BlockSpec((tokens, n), lambda p: (0, p))
    row_spec = lambda n: pl.BlockSpec((n, tokens), lambda p: (p, 0))
    out_l, dq_l, dk_l, dv_l, gl = call(
        functools.partial(local_kernel, dims, levels),
        [S((nh * dv, tokens), F32), S((rows, tokens), F32), S((tokens, rows), F32), S((tokens, nh * dv), F32),
         S((own, tokens), F32)],
        [pair_spec(2 * dk), pair_spec(2 * dk), pair_spec(2 * dv), pair_spec(2 * dv), row_spec(2 * levels)],
        2 * tokens * tokens * nh * (3 * dk + 3 * dv), "local", grid=(nh // 2,),
        out_specs=[row_spec(2 * dv), row_spec(2 * dk), pair_spec(2 * dk), pair_spec(2 * dv), row_spec(2 * levels)],
    )(keys, queries, values, d_out, lw)

    grad_level, d_queries = call(
        functools.partial(carry_kernel, dims, levels, first, seq_bits),
        [S((own, tokens), F32), S((tokens, rows), BF16)],
        [SM] + [VM] * (seq_bits + 6), 2 * tokens * rows * dv * seq_bits, "carry")(
            idx, *ups, d_out, qt, lw, proj, gl, dq_l)
    out = call(
        functools.partial(out_kernel, dims, levels, first, seq_bits),
        [S((tokens, nh * dv), BF16)],
        [SM] + [VM] * (seq_bits + 3), 2 * tokens * rows * dv * seq_bits, "out")(idx, *ups, qt, lw, out_l)[0]
    gp = (grad_level * jax.nn.sigmoid(proj)).astype(BF16)

    full = gp[None]
    for bit in reversed(range(head_bits)):
        other = swap(full, "head", bit)
        mine = (hi >> bit) & 1
        full = jnp.where(mine == 0, jnp.stack([full, other]), jnp.stack([other, full]))
        full = full.reshape((-1,) + full.shape[2:]) if bit == head_bits - 1 else full
    full = full.reshape((2,) * head_bits + (own, tokens))
    full = full.transpose(tuple(reversed(range(head_bits))) + (head_bits, head_bits + 1))
    gathered = full.reshape(cols, tokens)
    partial_w = call(wgrad_kernel, [S((width, cols), F32)], [VM, VM], 2 * tokens * width * cols, "wgrad")(gathered, hidden)[0]
    d_hidden = call(hidden_kernel, [S((tokens, width), BF16)], [VM, VM], 2 * tokens * width * cols, "hgrad")(gathered, w)[0]

    keep = partial_w.reshape(n_seq, width // n_seq, cols)
    for bit in range(seq_bits):
        pair = keep.reshape(keep.shape[0] // 2, 2, keep.shape[1], cols)
        mine = (si >> bit) & 1
        send = lax.dynamic_index_in_dim(pair, 1 - mine, 1, keepdims=False).astype(BF16)
        got = swap(send, "seq", bit)
        keep = lax.dynamic_index_in_dim(pair, mine, 1, keepdims=False) + got.astype(F32)
    d_w = keep.reshape(width // n_seq, cols)

    d_keys, d_values = call(
        functools.partial(final_kernel, dims),
        [S((tokens, rows), BF16), S((tokens, nh * dv), BF16)], [VM] * 6, 4 * tokens * rows * dv, "final")(
            adjoint, d_state.reshape(rows, dv), keys, values, dk_l, dv_l)
    return (out, d_queries, d_keys, d_values, d_hidden, d_w)


def solution(mesh):
    two = P("seq", "head")
    return jax.shard_map(
        body, mesh=mesh,
        in_specs=(two, P("head", None), two, two, two, two, P("head", None, None)),
        out_specs=(two, two, two, two, two, P(("head", "seq"), None)),
        check_vma=False)
```

time: 150 us -> 51.5 us (0.34)
  waiting for transfers between devices: 66 us -> 18.7 us
  matrix products: 31.4 us -> 0 us
  between operations: 14.4 us -> 0.86 us
  local copies, waits for them, and re-layouts: 13.5 us -> 3.03 us
  Pallas kernels: 0 us -> 10.2 us
  other arithmetic: 9.67 us -> 1.76 us
  starting transfers between devices: 8.82 us -> 16.6 us
  blocking collectives: 5.6 us -> 0 us
    dot_general x19 -> x0, matrix products: 31.4 us -> none  [the longest x1 6.25 us: local_pass(): jnp.einsum('hts,lts->thl', grad_mixed * scores, table, precision=PRECISE)]
    ppermute x6 -> x12, waiting for transfers between devices: 43.9 us -> 18.7 us  [swap(): return lax.ppermute(value, axis, pairs)]
    unnamed x3 -> x0, waiting for transfers between devices: 22.1 us -> none
    pallas_call x0 -> x9, Pallas kernels: none -> 10.2 us  [the longest x1 3.62 us: body(): call(functools.partial(local_kernel, dims, levels), [S((nh * dv, tokens),...]
    unnamed x54 -> x18, local copies, waits for them, and re-layouts: 10.8 us -> 2.9 us
    ppermute x6 -> x12, starting transfers between devices: 8.74 us -> 16.6 us  [swap(): return lax.ppermute(value, axis, pairs)]
    all_gather x1 -> x0, blocking collectives: 5.6 us -> none  [body(): gathered = lax.all_gather(grad_projected, 'head', axis=1, tiled=True)]
    add x6 -> x4, other arithmetic: 4.45 us -> 0.14 us  [the longest x2 0.06 us: body(): lax.dynamic_index_in_dim(pair, mine, 1, keepdims=False) + got.astype(F32)]
  transfers between devices with their start and end apart: 8 -> 12, of which waited for: 7 -> 10; matrix products, arithmetic and copies ran while one was open for 16% -> 1% of each run, Pallas kernels for 0% -> 16%
where the time goes in v1:
time: 51.5 us; the launch traced here: 51.2 us
  waiting for transfers between devices  18.7 us (36%)
  starting transfers between devices  16.6 us (32%)
  Pallas kernels  10.2 us (20%)
  local copies, waits for them, and re-layouts  3.03 us (6%)
  other arithmetic  1.76 us (3%)
  between operations  0.86 us (2%)
    ppermute x12, waiting for transfers between devices, swap(): return lax.ppermute(value, axis, pairs)  18.7 us
    ppermute x12, starting transfers between devices, swap(): return lax.ppermute(value, axis, pairs)  16.6 us
    pallas_call x1, Pallas kernels, body(): call(functools.partial(local_kernel, dims, levels), [S((nh * dv, tokens),...  3.62 us
    unnamed x18, local copies, waits for them, and re-layouts  2.9 us
    pallas_call x1, Pallas kernels, body(): call(functools.partial(out_kernel, dims, levels, first, seq_bits), [S((to...  1.49 us
    pallas_call x1, Pallas kernels, body(): call(functools.partial(carry_kernel, dims, levels, first, seq_bits), [S((...  1.46 us
    pallas_call x1, Pallas kernels, body(): call(functools.partial(final_kernel, dims), [S((tokens, rows), BF16), S((...  1.31 us
    pallas_call x1, Pallas kernels, body(): call(hidden_kernel, [S((tokens, width), BF16)], [VM, VM], 2 * tokens * wi...  1.04 us
  transfers between devices with their start and end apart: 12, of which 10 were waited for; matrix products, arithmetic and copies ran while one was open for 1% of the time, Pallas kernels for 16%

profile of v1, /device:TPU:0, one launch (start us, length us, event | category | flops | bytes accessed | tf_op | source)
XLA Modules:
  0.0 51.2 jit_solution(1186297716620079188)
XLA Ops:
  0.6 0.0 copy-start.2
  0.7 1.0 %copy-done.2 = bf16[512,384]{1,0:T(8,128)(2,1)S(1)} copy-done((bf16[512,384]{1,0:T(8,128)(2,1)S(1)}, bf16[512,384]{1,0:T(8,128)(2,1)}, u32[]{:S(2)}) %copy-start.2) | copy-done | bytes 393240
  1.6 0.0 copy-start.4
  1.6 0.9 %copy-done.4 = bf16[256,512]{1,0:T(8,128)(2,1)S(1)} copy-done((bf16[256,512]{1,0:T(8,128)(2,1)S(1)}, bf16[256,512]{1,0:T(8,128)(2,1)}, u32[]{:S(2)}) %copy-start.4) | copy-done | bytes 262168
  2.6 0.0 copy-start.1
  2.6 0.0 copy-start.6
  2.6 0.3 project.1
  2.9 3.0 %collective-permute-start.2 = (bf16[192,256]{1,0:T(8,128)(2,1)S(1)}, bf16[192,256]{1,0:T(8,128)(2,1)S(1)}, u32[]{:S(2)}, u32[]{:S(2)}) collective-permute-start(bf16[192,256]{1,0:T(8,128)(2,1)S(1)} %fusion.7), channel_id=1, source_target_pairs={{0,2},{1,3},{2,0},{3,1},{4,6},{5,7},{6,4},{7,5},{8,10},{9,11},{10,... | collective-permute-start | bytes 294920 | tf_op jit(solution)/shard_map/ppermute | solution.py:46
  6.0 0.0 copy-done.1
  6.0 0.0 copy-done.6
  6.0 0.3 kv_state.1
  6.2 1.6 %collective-permute-start = (bf16[512,128]{1,0:T(8,128)(2,1)S(1)}, bf16[512,128]{1,0:T(8,128)(2,1)S(1)}, u32[]{:S(2)}, u32[]{:S(2)}) collective-permute-start(bf16[512,128]{1,0:T(8,128)(2,1)S(1)} %get-tuple-element.21), channel_id=1, source_target_pairs={{0,4},{4,0},{8,12},{12,8},{16,20},{20,16},{24,28},{28,24},{1,5},{5... | collective-permute-start | bytes 393224 | tf_op jit(solution)/shard_map/ppermute | solution.py:46
  7.8 0.9 %collective-permute-done.2 = bf16[192,256]{1,0:T(8,128)(2,1)S(1)} collective-permute-done((bf16[192,256]{1,0:T(8,128)(2,1)S(1)}, bf16[192,256]{1,0:T(8,128)(2,1)S(1)}, u32[]{:S(2)}, u32[]{:S(2)}) %collective-permute-start.2) | collective-permute-done | bytes 98336 | tf_op jit(solution)/shard_map/ppermute | solution.py:46
  8.8 0.0 copy-start
  8.8 2.5 %collective-permute-done.refs_0_ = bf16[512,128]{1,0:T(8,128)(2,1)S(1)} collective-permute-done((bf16[512,128]{1,0:T(8,128)(2,1)S(1)}, bf16[512,128]{1,0:T(8,128)(2,1)S(1)}, u32[]{:S(2)}, u32[]{:S(2)}) %collective-permute-start) | collective-permute-done | bytes 131104 | tf_op jit(solution)/shard_map/ppermute | solution.py:46
  11.3 0.0 copy-start.7
  11.3 1.6 %collective-permute-start.1 = (bf16[512,128]{1,0:T(8,128)(2,1)S(1)}, bf16[512,128]{1,0:T(8,128)(2,1)S(1)}, u32[]{:S(2)}, u32[]{:S(2)}) collective-permute-start(bf16[512,128]{1,0:T(8,128)(2,1)S(1)} %fusion.4), channel_id=1, source_target_pairs={{0,8},{4,12},{8,0},{12,4},{16,24},{20,28},{24,16},{28,20},{1,9},{5... | collective-permute-start | bytes 393224 | tf_op jit(solution)/shard_map/ppermute | solution.py:46
  13.0 0.0 collective-permute-start.3
  13.0 1.2 %collective-permute-done.3.got_ref = bf16[96,256]{1,0:T(8,128)(2,1)S(1)} collective-permute-done((bf16[96,256]{1,0:T(8,128)(2,1)S(1)}, bf16[96,256]{1,0:T(8,128)(2,1)S(1)}, u32[]{:S(2)}, u32[]{:S(2)}) %collective-permute-start.3) | collective-permute-done | bytes 49184 | tf_op jit(solution)/shard_map/ppermute | solution.py:46
  14.2 0.0 copy-done
  14.2 0.0 copy-done.7
  14.2 0.4 level_weights.1
  14.6 1.7 %collective-permute-done.1.refs_1_ = bf16[512,128]{1,0:T(8,128)(2,1)S(1)} collective-permute-done((bf16[512,128]{1,0:T(8,128)(2,1)S(1)}, bf16[512,128]{1,0:T(8,128)(2,1)S(1)}, u32[]{:S(2)}, u32[]{:S(2)}) %collective-permute-start.1) | collective-permute-done | bytes 131104 | tf_op jit(solution)/shard_map/ppermute | solution.py:46
  16.4 0.7 %fusion.5 = bf16[512,128]{1,0:T(8,128)(2,1)} fusion(bf16[512,128]{1,0:T(8,128)(2,1)S(1)} %collective-permute-done.1.refs_1_, f32[512,128]{1,0:T(8,128)S(1)} %get-tuple-element.22, bf16[512,128]{1,0:T(8,128)(2,1)S(1)} %collective-permute-done.refs_0_, f32[3,512,128]{2,1,0:T(8,128)S(1)} %get-tuple-element.23, pred[]{:T(512)S(6)} %eq.15), kind=kLoop, calls=%fused_computation.20 | loop fusion | flops 393216 | bytes 786433 | tf_op jit(solution)/shard_map/jit(_where)/select_n | solution.py:286
  17.1 2.6 %collective-permute-start.4 = (bf16[512,128]{1,0:T(8,128)(2,1)}, bf16[512,128]{1,0:T(8,128)(2,1)S(1)}, u32[]{:S(2)}, u32[]{:S(2)}) collective-permute-start(bf16[512,128]{1,0:T(8,128)(2,1)} %fusion.5), channel_id=1, source_target_pairs={{0,16},{4,20},{8,24},{12,28},{16,0},{20,4},{24,8},{28,12},{1,17},{... | collective-permute-start | bytes 393224 | tf_op jit(solution)/shard_map/ppermute | solution.py:46
  19.7 3.6 %local.1 = (f32[1024,256]{1,0:T(8,128)S(1)}, f32[512,256]{1,0:T(8,128)S(1)}, f32[256,512]{1,0:T(8,128)S(1)}, f32[256,1024]{1,0:T(8,128)S(1)}, f32[96,256]{1,0:T(8,128)S(1)}) custom-call(bf16[256,512]{1,0:T(8,128)(2,1)S(1)} %copy-done.6, bf16[256,512]{1,0:T(8,128)(2,1)S(1)} %copy-done.7, bf16[256,1024]{1,0:T(8,128)(2,1)S(1)} %copy-done.1, ...), custom_call_target="tpu_custom_call" | custom-call | flops 603979776 | bytes 6488064 | tf_op jit(solution)/shard_map/local/pallas_call | solution.py:295
  23.3 1.4 %collective-permute-done.4.refs_2_ = bf16[512,128]{1,0:T(8,128)(2,1)S(1)} collective-permute-done((bf16[512,128]{1,0:T(8,128)(2,1)}, bf16[512,128]{1,0:T(8,128)(2,1)S(1)}, u32[]{:S(2)}, u32[]{:S(2)}) %collective-permute-start.4) | collective-permute-done | bytes 131104 | tf_op jit(solution)/shard_map/ppermute | solution.py:46
  24.7 1.5 %carry.1 = (f32[96,256]{1,0:T(8,128)S(1)}, bf16[256,512]{1,0:T(8,128)(2,1)}) custom-call(s32[1]{0:T(128)} %bitcast.idx_ref, bf16[512,128]{1,0:T(8,128)(2,1)S(1)} %collective-permute-done.refs_0_, bf16[512,128]{1,0:T(8,128)(2,1)S(1)} %collective-permute-done.1.refs_1_, bf16[512,128]{1,0:T(8,128)(2,1)S(1)} %collective-permute-done.4.refs_2_, ...), custom_call_target="tpu_custom_call" | custom-call | flops 100663296 | bytes 720896 | tf_op jit(solution)/shard_map/carry/pallas_call | solution.py:304
  26.2 1.1 %collective-permute-start.7 = (bf16[1,96,256]{2,1,0:T(8,128)(2,1)S(1)}, bf16[1,96,256]{2,1,0:T(8,128)(2,1)S(1)}, u32[]{:S(2)}, u32[]{:S(2)}) collective-permute-start(bf16[1,96,256]{2,1,0:T(8,128)(2,1)S(1)} %fusion.11), channel_id=1, source_target_pairs={{0,2},{1,3},{2,0},{3,1},{4,6},{5,7},{6,4},{7,5},{8,10},{9,11},{10,... | collective-permute-start | bytes 147464 | tf_op jit(solution)/shard_map/ppermute | solution.py:46
  27.4 3.0 %collective-permute-done.7 = bf16[1,96,256]{2,1,0:T(8,128)(2,1)S(1)} collective-permute-done((bf16[1,96,256]{2,1,0:T(8,128)(2,1)S(1)}, bf16[1,96,256]{2,1,0:T(8,128)(2,1)S(1)}, u32[]{:S(2)}, u32[]{:S(2)}) %collective-permute-start.7) | collective-permute-done | bytes 49184 | tf_op jit(solution)/shard_map/ppermute | solution.py:46
  30.4 0.1 collective-permute-start.8
  30.5 1.3 %collective-permute-done.8 = bf16[2,96,256]{2,1,0:T(8,128)(2,1)S(1)} collective-permute-done((bf16[2,96,256]{2,1,0:T(8,128)(2,1)S(1)}, bf16[2,96,256]{2,1,0:T(8,128)(2,1)S(1)}, u32[]{:S(2)}, u32[]{:S(2)}) %collective-permute-start.8) | collective-permute-done | bytes 98336 | tf_op jit(solution)/shard_map/ppermute | solution.py:46
  31.8 0.0 copy-start.5
  31.8 0.9 %copy-done.5 = bf16[256,512]{1,0:T(8,128)(2,1)S(1)} copy-done((bf16[256,512]{1,0:T(8,128)(2,1)S(1)}, bf16[256,512]{1,0:T(8,128)(2,1)}, u32[]{:S(2)}) %copy-start.5) | copy-done | bytes 262168
  32.7 0.3 wgrad.1
  33.1 1.6 %collective-permute-start.9 = (bf16[4,64,384]{2,1,0:T(8,128)(2,1)S(1)}, bf16[4,64,384]{2,1,0:T(8,128)(2,1)S(1)}, u32[]{:S(2)}, u32[]{:S(2)}) collective-permute-start(bf16[4,64,384]{2,1,0:T(8,128)(2,1)S(1)} %fusion.2), channel_id=1, source_target_pairs={{0,4},{4,0},{8,12},{12,8},{16,20},{20,16},{24,28},{28,24},{1,5},{5... | collective-permute-start | bytes 589832 | tf_op jit(solution)/shard_map/ppermute | solution.py:46
  34.7 0.7 %collective-permute-start.5 = (bf16[512,128]{1,0:T(8,128)(2,1)S(1)}, bf16[512,128]{1,0:T(8,128)(2,1)S(1)}, u32[]{:S(2)}, u32[]{:S(2)}) collective-permute-start(bf16[512,128]{1,0:T(8,128)(2,1)S(1)} %fusion.1), channel_id=1, source_target_pairs={{0,8},{4,12},{8,0},{12,4},{16,24},{20,28},{24,16},{28,20},{1,9},{5... | collective-permute-start | bytes 393224 | tf_op jit(solution)/shard_map/ppermute | solution.py:46
  35.4 1.5 %out.1 = bf16[256,1024]{1,0:T(8,128)(2,1)} custom-call(s32[1]{0:T(128)} %bitcast.idx_ref, bf16[512,128]{1,0:T(8,128)(2,1)S(1)} %collective-permute-done.refs_0_, bf16[512,128]{1,0:T(8,128)(2,1)S(1)} %collective-permute-done.1.refs_1_, bf16[512,128]{1,0:T(8,128)(2,1)S(1)} %collective-permute-done.4.refs_2_, ...), custom_call_target="tpu_custom_call" | custom-call | flops 100663296 | bytes 1048576 | tf_op jit(solution)/shard_map/out/pallas_call | solution.py:309
  36.9 3.2 %collective-permute-done.9 = bf16[4,64,384]{2,1,0:T(8,128)(2,1)S(1)} collective-permute-done((bf16[4,64,384]{2,1,0:T(8,128)(2,1)S(1)}, bf16[4,64,384]{2,1,0:T(8,128)(2,1)S(1)}, u32[]{:S(2)}, u32[]{:S(2)}) %collective-permute-start.9) | collective-permute-done | bytes 196640 | tf_op jit(solution)/shard_map/ppermute | solution.py:46
  40.2 0.0 copy-start.3
  40.2 0.7 %collective-permute-start.10 = (bf16[2,64,384]{2,1,0:T(8,128)(2,1)S(1)}, bf16[2,64,384]{2,1,0:T(8,128)(2,1)S(1)}, u32[]{:S(2)}, u32[]{:S(2)}) collective-permute-start(bf16[2,64,384]{2,1,0:T(8,128)(2,1)S(1)} %fusion.8), channel_id=1, source_target_pairs={{0,8},{4,12},{8,0},{12,4},{16,24},{20,28},{24,16},{28,20},{1,9},{5... | collective-permute-start | bytes 294920 | tf_op jit(solution)/shard_map/ppermute | solution.py:46
  40.9 0.0 collective-permute-done.5
  40.9 0.1 fusion
  41.0 1.6 %collective-permute-start.6 = (bf16[512,128]{1,0:T(8,128)(2,1)S(1)}, bf16[512,128]{1,0:T(8,128)(2,1)S(1)}, u32[]{:S(2)}, u32[]{:S(2)}) collective-permute-start(bf16[512,128]{1,0:T(8,128)(2,1)S(1)} %fusion), channel_id=1, source_target_pairs={{0,4},{4,0},{8,12},{12,8},{16,20},{20,16},{24,28},{28,24},{1,5},{5... | collective-permute-start | bytes 393224 | tf_op jit(solution)/shard_map/ppermute | solution.py:46
  42.5 0.0 copy-done.3
  42.5 1.0 %hgrad.1 = bf16[256,512]{1,0:T(8,128)(2,1)} custom-call(bf16[384,256]{1,0:T(8,128)(2,1)S(1)} %bitcast.52, bf16[512,384]{1,0:T(8,128)(2,1)S(1)} %copy-done.3), custom_call_target="tpu_custom_call" | custom-call | flops 100663296 | bytes 524288 | tf_op jit(solution)/shard_map/hgrad/pallas_call | solution.py:325
  43.6 1.3 %collective-permute-done.10 = bf16[2,64,384]{2,1,0:T(8,128)(2,1)S(1)} collective-permute-done((bf16[2,64,384]{2,1,0:T(8,128)(2,1)S(1)}, bf16[2,64,384]{2,1,0:T(8,128)(2,1)S(1)}, u32[]{:S(2)}, u32[]{:S(2)}) %collective-permute-start.10) | collective-permute-done | bytes 98336 | tf_op jit(solution)/shard_map/ppermute | solution.py:46
  44.9 0.0 copy-start.8
  45.0 2.0 %collective-permute-start.11 = (bf16[1,64,384]{2,1,0:T(8,128)(2,1)S(1)}, bf16[1,64,384]{2,1,0:T(8,128)(2,1)S(1)}, u32[]{:S(2)}, u32[]{:S(2)}) collective-permute-start(bf16[1,64,384]{2,1,0:T(8,128)(2,1)S(1)} %dynamic-slice_convert_fusion.2), channel_id=1, source_target_pairs={{0,16},{4,20},{8,24},{12,28},{16,0},{20,4},{24,8},{28,12},{1,17},{... | collective-permute-start | bytes 147464 | tf_op jit(solution)/shard_map/ppermute | solution.py:46
  47.0 0.0 collective-permute-done.6
  47.0 0.1 convert_add_fusion.adj_ref
  47.1 0.0 copy-done.8
  47.1 1.3 %final.1 = (bf16[256,512]{1,0:T(8,128)(2,1)}, bf16[256,1024]{1,0:T(8,128)(2,1)}) custom-call(f32[512,128]{1,0:T(8,128)S(1)} %convert_add_fusion.adj_ref, f32[512,128]{1,0:T(8,128)S(1)} %bitcast.55, bf16[256,512]{1,0:T(8,128)(2,1)S(1)} %copy-done.6, bf16[256,1024]{1,0:T(8,128)(2,1)S(1)} %copy-done.1, f32[256,512]{1,0:T(8,128)S(1)} %get-tuple-element.31.dkl_ref, ...), custom_call_target="tpu_custom_call" | custom-call | flops 67108864 | bytes 1572864 | tf_op jit(solution)/shard_map/final/pallas_call | solution.py:336
  48.4 2.2 %collective-permute-done.11 = bf16[1,64,384]{2,1,0:T(8,128)(2,1)S(1)} collective-permute-done((bf16[1,64,384]{2,1,0:T(8,128)(2,1)S(1)}, bf16[1,64,384]{2,1,0:T(8,128)(2,1)S(1)}, u32[]{:S(2)}, u32[]{:S(2)}) %collective-permute-start.11) | collective-permute-done | bytes 49184 | tf_op jit(solution)/shard_map/ppermute | solution.py:46
  50.5 0.7 %add_bitcast_fusion = f32[64,384]{1,0:T(8,128)} fusion(bf16[1,64,384]{2,1,0:T(8,128)(2,1)S(1)} %collective-permute-done.11, f32[2,64,384]{2,1,0:T(8,128)S(1)} %bitcast_add_fusion.3, s32[]{:T(128)S(6)} %select_n.122), kind=kLoop, calls=%fused_computation.26 | loop fusion | flops 49152 | bytes 245764 | tf_op jit(solution)/shard_map/reshape | solution.py:334
  (17 shorter events, 0.4 us)
Async XLA Ops:
  0.6 1.0 %copy-start.2 = (bf16[512,384]{1,0:T(8,128)(2,1)S(1)}, bf16[512,384]{1,0:T(8,128)(2,1)}, u32[]{:S(2)}) copy-start(bf16[512,384]{1,0:T(8,128)(2,1)} %w_ref.3) | copy-start | bytes 1179652
  1.6 0.9 %copy-start.4 = (bf16[256,512]{1,0:T(8,128)(2,1)S(1)}, bf16[256,512]{1,0:T(8,128)(2,1)}, u32[]{:S(2)}) copy-start(bf16[256,512]{1,0:T(8,128)(2,1)} %x_ref.3) | copy-start | bytes 786436
  2.6 3.4 %copy-start.1 = (bf16[256,1024]{1,0:T(8,128)(2,1)S(1)}, bf16[256,1024]{1,0:T(8,128)(2,1)}, u32[]{:S(2)}) copy-start(bf16[256,1024]{1,0:T(8,128)(2,1)} %v_ref.5) | copy-start | bytes 1572868
  2.6 3.4 %copy-start.6 = (bf16[256,512]{1,0:T(8,128)(2,1)S(1)}, bf16[256,512]{1,0:T(8,128)(2,1)}, u32[]{:S(2)}) copy-start(bf16[256,512]{1,0:T(8,128)(2,1)} %k_ref.5) | copy-start | bytes 786436
  2.9 5.8 %collective-permute-start.2 = (bf16[192,256]{1,0:T(8,128)(2,1)S(1)}, bf16[192,256]{1,0:T(8,128)(2,1)S(1)}, u32[]{:S(2)}, u32[]{:S(2)}) collective-permute-start(bf16[192,256]{1,0:T(8,128)(2,1)S(1)} %fusion.7), channel_id=1, source_target_pairs={{0,2},{1,3},{2,0},{3,1},{4,6},{5,7},{6,4},{7,5},{8,10},{9,11},{10,... | collective-permute-start | bytes 294920 | tf_op jit(solution)/shard_map/ppermute | solution.py:46
  6.2 5.0 %collective-permute-start = (bf16[512,128]{1,0:T(8,128)(2,1)S(1)}, bf16[512,128]{1,0:T(8,128)(2,1)S(1)}, u32[]{:S(2)}, u32[]{:S(2)}) collective-permute-start(bf16[512,128]{1,0:T(8,128)(2,1)S(1)} %get-tuple-element.21), channel_id=1, source_target_pairs={{0,4},{4,0},{8,12},{12,8},{16,20},{20,16},{24,28},{28,24},{1,5},{5... | collective-permute-start | bytes 393224 | tf_op jit(solution)/shard_map/ppermute | solution.py:46
  8.8 5.4 %copy-start = (bf16[256,1024]{1,0:T(8,128)(2,1)S(1)}, bf16[256,1024]{1,0:T(8,128)(2,1)}, u32[]{:S(2)}) copy-start(bf16[256,1024]{1,0:T(8,128)(2,1)} %refs_3_.1) | copy-start | bytes 1572868
  11.3 2.9 %copy-start.7 = (bf16[256,512]{1,0:T(8,128)(2,1)S(1)}, bf16[256,512]{1,0:T(8,128)(2,1)}, u32[]{:S(2)}) copy-start(bf16[256,512]{1,0:T(8,128)(2,1)} %q_ref.3) | copy-start | bytes 786436
  11.3 5.0 %collective-permute-start.1 = (bf16[512,128]{1,0:T(8,128)(2,1)S(1)}, bf16[512,128]{1,0:T(8,128)(2,1)S(1)}, u32[]{:S(2)}, u32[]{:S(2)}) collective-permute-start(bf16[512,128]{1,0:T(8,128)(2,1)S(1)} %fusion.4), channel_id=1, source_target_pairs={{0,8},{4,12},{8,0},{12,4},{16,24},{20,28},{24,16},{28,20},{1,9},{5... | collective-permute-start | bytes 393224 | tf_op jit(solution)/shard_map/ppermute | solution.py:46
  13.0 1.2 %collective-permute-start.3 = (bf16[96,256]{1,0:T(8,128)(2,1)S(1)}, bf16[96,256]{1,0:T(8,128)(2,1)S(1)}, u32[]{:S(2)}, u32[]{:S(2)}) collective-permute-start(bf16[96,256]{1,0:T(8,128)(2,1)S(1)} %fusion.9), channel_id=1, source_target_pairs={{0,1},{1,0},{2,3},{3,2},{4,5},{5,4},{6,7},{7,6},{8,9},{9,8},{10,11... | collective-permute-start | bytes 147464 | tf_op jit(solution)/shard_map/ppermute | solution.py:46
  17.1 7.6 %collective-permute-start.4 = (bf16[512,128]{1,0:T(8,128)(2,1)}, bf16[512,128]{1,0:T(8,128)(2,1)S(1)}, u32[]{:S(2)}, u32[]{:S(2)}) collective-permute-start(bf16[512,128]{1,0:T(8,128)(2,1)} %fusion.5), channel_id=1, source_target_pairs={{0,16},{4,20},{8,24},{12,28},{16,0},{20,4},{24,8},{28,12},{1,17},{... | collective-permute-start | bytes 393224 | tf_op jit(solution)/shard_map/ppermute | solution.py:46
  26.2 4.2 %collective-permute-start.7 = (bf16[1,96,256]{2,1,0:T(8,128)(2,1)S(1)}, bf16[1,96,256]{2,1,0:T(8,128)(2,1)S(1)}, u32[]{:S(2)}, u32[]{:S(2)}) collective-permute-start(bf16[1,96,256]{2,1,0:T(8,128)(2,1)S(1)} %fusion.11), channel_id=1, source_target_pairs={{0,2},{1,3},{2,0},{3,1},{4,6},{5,7},{6,4},{7,5},{8,10},{9,11},{10,... | collective-permute-start | bytes 147464 | tf_op jit(solution)/shard_map/ppermute | solution.py:46
  30.4 1.4 %collective-permute-start.8 = (bf16[2,96,256]{2,1,0:T(8,128)(2,1)S(1)}, bf16[2,96,256]{2,1,0:T(8,128)(2,1)S(1)}, u32[]{:S(2)}, u32[]{:S(2)}) collective-permute-start(bf16[2,96,256]{2,1,0:T(8,128)(2,1)S(1)} %maximum_select_fusion.2), channel_id=1, source_target_pairs={{0,1},{1,0},{2,3},{3,2},{4,5},{5,4},{6,7},{7,6},{8,9},{9,8},{10,11... | collective-permute-start | bytes 294920 | tf_op jit(solution)/shard_map/ppermute | solution.py:46
  31.8 1.0 %copy-start.5 = (bf16[256,512]{1,0:T(8,128)(2,1)S(1)}, bf16[256,512]{1,0:T(8,128)(2,1)}, u32[]{:S(2)}) copy-start(bf16[256,512]{1,0:T(8,128)(2,1)} %x_ref.3) | copy-start | bytes 786436
  33.1 7.0 %collective-permute-start.9 = (bf16[4,64,384]{2,1,0:T(8,128)(2,1)S(1)}, bf16[4,64,384]{2,1,0:T(8,128)(2,1)S(1)}, u32[]{:S(2)}, u32[]{:S(2)}) collective-permute-start(bf16[4,64,384]{2,1,0:T(8,128)(2,1)S(1)} %fusion.2), channel_id=1, source_target_pairs={{0,4},{4,0},{8,12},{12,8},{16,20},{20,16},{24,28},{28,24},{1,5},{5... | collective-permute-start | bytes 589832 | tf_op jit(solution)/shard_map/ppermute | solution.py:46
  34.7 6.2 %collective-permute-start.5 = (bf16[512,128]{1,0:T(8,128)(2,1)S(1)}, bf16[512,128]{1,0:T(8,128)(2,1)S(1)}, u32[]{:S(2)}, u32[]{:S(2)}) collective-permute-start(bf16[512,128]{1,0:T(8,128)(2,1)S(1)} %fusion.1), channel_id=1, source_target_pairs={{0,8},{4,12},{8,0},{12,4},{16,24},{20,28},{24,16},{28,20},{1,9},{5... | collective-permute-start | bytes 393224 | tf_op jit(solution)/shard_map/ppermute | solution.py:46
  40.2 2.4 %copy-start.3 = (bf16[512,384]{1,0:T(8,128)(2,1)S(1)}, bf16[512,384]{1,0:T(8,128)(2,1)}, u32[]{:S(2)}) copy-start(bf16[512,384]{1,0:T(8,128)(2,1)} %w_ref.3) | copy-start | bytes 1179652
  40.2 4.7 %collective-permute-start.10 = (bf16[2,64,384]{2,1,0:T(8,128)(2,1)S(1)}, bf16[2,64,384]{2,1,0:T(8,128)(2,1)S(1)}, u32[]{:S(2)}, u32[]{:S(2)}) collective-permute-start(bf16[2,64,384]{2,1,0:T(8,128)(2,1)S(1)} %fusion.8), channel_id=1, source_target_pairs={{0,8},{4,12},{8,0},{12,4},{16,24},{20,28},{24,16},{28,20},{1,9},{5... | collective-permute-start | bytes 294920 | tf_op jit(solution)/shard_map/ppermute | solution.py:46
  41.0 6.0 %collective-permute-start.6 = (bf16[512,128]{1,0:T(8,128)(2,1)S(1)}, bf16[512,128]{1,0:T(8,128)(2,1)S(1)}, u32[]{:S(2)}, u32[]{:S(2)}) collective-permute-start(bf16[512,128]{1,0:T(8,128)(2,1)S(1)} %fusion), channel_id=1, source_target_pairs={{0,4},{4,0},{8,12},{12,8},{16,20},{20,16},{24,28},{28,24},{1,5},{5... | collective-permute-start | bytes 393224 | tf_op jit(solution)/shard_map/ppermute | solution.py:46
  44.9 2.1 %copy-start.8 = (f32[8,64,128]{2,1,0:T(8,128)S(1)}, f32[8,64,128]{2,1,0:T(8,128)}, u32[]{:S(2)}) copy-start(f32[8,64,128]{2,1,0:T(8,128)} %param.13) | copy-start | bytes 786436
  45.0 5.6 %collective-permute-start.11 = (bf16[1,64,384]{2,1,0:T(8,128)(2,1)S(1)}, bf16[1,64,384]{2,1,0:T(8,128)(2,1)S(1)}, u32[]{:S(2)}, u32[]{:S(2)}) collective-permute-start(bf16[1,64,384]{2,1,0:T(8,128)(2,1)S(1)} %dynamic-slice_convert_fusion.2), channel_id=1, source_target_pairs={{0,16},{4,20},{8,24},{12,28},{16,0},{20,4},{24,8},{28,12},{1,17},{... | collective-permute-start | bytes 147464 | tf_op jit(solution)/shard_map/ppermute | solution.py:46

commit v2 on v1

v2 whole, which is shorter than its diff:
```python
import functools

import jax
import jax.numpy as jnp
from jax import lax
from jax.experimental import pallas as pl
from jax.experimental.pallas import tpu as pltpu
from jax.sharding import PartitionSpec as P

F32 = jnp.float32
BF16 = jnp.bfloat16
LANES = 128
SUB = 8
VM = pl.BlockSpec(memory_space=pltpu.VMEM)
SM = pl.BlockSpec(memory_space=pltpu.SMEM)


def nn(a, b):
    return lax.dot_general(a, b, (((1,), (0,)), ((), ())), preferred_element_type=F32)


def nt(a, b):
    return lax.dot_general(a, b, (((1,), (1,)), ((), ())), preferred_element_type=F32)


def tn(a, b):
    return lax.dot_general(a, b, (((0,), (0,)), ((), ())), preferred_element_type=F32)


def call(kernel, outs, specs, flops, name, **kwargs):
    size = sum(o.size * o.dtype.itemsize for o in outs)
    return pl.pallas_call(
        kernel,
        out_shape=outs,
        in_specs=specs,
        compiler_params=pltpu.CompilerParams(vmem_limit_bytes=16 << 20),
        cost_estimate=pl.CostEstimate(flops=flops, bytes_accessed=2 * size, transcendentals=0),
        name=name,
        **kwargs,
    )


def swap(value, axis, bit, name):
    mask = 1 << bit
    pairs = [(source, source ^ mask) for source in range(lax.axis_size(axis))]
    with jax.named_scope(f"{name}_{axis}{bit}"):
        return lax.ppermute(value, axis, pairs)


def front_kernel(dims, k_hbm, v_hbm, w_hbm, x_hbm, kv_ref, kvb_ref, p_ref, xt_ref,
                 k_ref, v_ref, w_ref, x_ref, sems):
    nh, dk, dv = dims
    copies = [pltpu.make_async_copy(src, dst, sems.at[n]) for n, (src, dst) in enumerate(
        ((k_hbm, k_ref), (v_hbm, v_ref), (x_hbm, x_ref), (w_hbm, w_ref)))]
    for copy in copies:
        copy.start()
    copies[0].wait()
    copies[1].wait()
    for pair in range(nh // 2):
        turned = k_ref[:, pair * 2 * dk:(pair + 1) * 2 * dk].T
        for j in range(2):
            h = 2 * pair + j
            kv = nn(turned[j * dk:(j + 1) * dk], v_ref[:, h * dv:(h + 1) * dv])
            kv_ref[h * dk:(h + 1) * dk, :] = kv
            kvb_ref[h * dk:(h + 1) * dk, :] = kv.astype(BF16)
    copies[2].wait()
    xt = x_ref[...].T
    xt_ref[...] = xt
    copies[3].wait()
    p_ref[...] = tn(w_ref[...], xt)


def weight_kernel(dims, levels, first, count, keep_ref, got_ref, gl_ref, q_ref, g_ref,
                  sig_ref, lw_ref, near_ref, qt_ref, gu_ref):
    nh, dk, dv = dims
    proj = keep_ref[...] + got_ref[...].astype(F32)
    sig = jax.nn.sigmoid(proj)
    sig_ref[...] = sig
    near_ref[...] = (gl_ref[...] * sig).astype(BF16)
    lw_ref[...] = jnp.maximum(proj, 0.0) + jnp.log1p(jnp.exp(-jnp.abs(proj)))
    for pair in range(nh // 2):
        turned = q_ref[:, pair * 2 * dk:(pair + 1) * 2 * dk].T
        qt_ref[pair * 2 * dk:(pair + 1) * 2 * dk, :] = turned
        wide = turned.astype(F32)
        for j in range(2):
            h = 2 * pair + j
            scaled = jnp.concatenate(
                [wide[j * dk:(j + 1) * dk] * lw_ref[h * levels + first + m:h * levels + first + m + 1, :]
                 for m in range(count)], axis=0)
            grad = nn(scaled.astype(BF16), g_ref[:, h * dv:(h + 1) * dv])
            for m in range(count):
                gu_ref[m, h * dk:(h + 1) * dk, :] = grad[m * dk:(m + 1) * dk].astype(BF16)


def spread_half(rows, lane, low, t_low):
    digits = (low ^ t_low)
    near = jnp.where(digits == 0, rows[0], jnp.where(digits < 2, rows[1], jnp.where(digits < 4, rows[2], rows[3])))
    near = jnp.where(low <= t_low, near, 0.0)
    parts = []
    for a in range(LANES // SUB):
        value = None
        for l in reversed(range(4, 8)):
            if (a >> (l - 4)) & 1 == 0:
                end = (((a >> (l - 3)) + 1) << (l - 3)) * SUB
                value = rows[l] if value is None else jnp.where(lane < end, rows[l], value)
        value = near if value is None else jnp.where(lane < (a + 1) * SUB, near, value)
        if a:
            value = jnp.where(lane < a * SUB, 0.0, value)
        parts.append(value)
    return jnp.concatenate(parts, axis=0)


def level_sums(prod, lane, low, t_low):
    count = LANES // SUB
    group = lane // SUB
    cur = [prod[a * SUB:(a + 1) * SUB] for a in range(count)]
    near = jnp.zeros_like(cur[0])
    for a in range(count):
        near = jnp.where(group == a, cur[a], near)
    near = jnp.where(low <= t_low, near, 0.0)
    digits = low ^ t_low
    sums = []
    for l in range(4):
        lo, hi = (0, 1) if l == 0 else (1 << (l - 1), 1 << l)
        sums.append(jnp.where((digits >= lo) & (digits < hi), near, 0.0))
    for l in range(4, 8):
        total = jnp.zeros_like(near)
        for a in range(0, len(cur), 2):
            total = jnp.where((lane >> (l - 1)) == a + 1, cur[a], total)
        sums.append(total)
        cur = [cur[a] + cur[a + 1] for a in range(0, len(cur), 2)]
    return [jnp.sum(s, axis=0, keepdims=True) for s in sums]


def level_kernel(dims, levels, k_ref, q_ref, v_ref, g_ref, gl_ref):
    nh, dk, dv = dims
    kp = k_ref[...]
    qt = q_ref[...].T
    zero = jnp.zeros_like(qt[:dk])
    lane = lax.broadcasted_iota(jnp.int32, (SUB, LANES), 1)
    low = lax.broadcasted_iota(jnp.int32, (SUB, LANES), 0)
    t_low = lane % SUB
    gl_ref[...] = jnp.zeros_like(gl_ref)
    for j in range(2):
        base = j * levels
        qz = jnp.concatenate([qt[:dk], zero] if j == 0 else [zero, qt[dk:]], axis=0)
        prod = nn(kp, qz) * nt(v_ref[:, j * dv:(j + 1) * dv], g_ref[:, j * dv:(j + 1) * dv])
        for x in range(2):
            part = slice(x * LANES, (x + 1) * LANES)
            sums = level_sums(prod[part, part], lane, low, t_low)
            for l in range(8):
                gl_ref[base + l:base + l + 1, part] = sums[l]
        gl_ref[base + 8:base + 9, LANES:] = jnp.sum(prod[:LANES, LANES:], axis=0, keepdims=True)


def local_kernel(dims, levels, k_ref, q_ref, v_ref, g_ref, lw_ref, out_ref, dq_ref, dk_ref, dv_ref):
    nh, dk, dv = dims
    kp, qp = k_ref[...], q_ref[...]
    kt, qt = kp.T, qp.T
    zero = jnp.zeros_like(qt[:dk])
    lane = lax.broadcasted_iota(jnp.int32, (SUB, LANES), 1)
    low = lax.broadcasted_iota(jnp.int32, (SUB, LANES), 0)
    t_low = lane % SUB
    wide_lane = lax.broadcasted_iota(jnp.int32, qp.shape, 1)
    dk_sum = None
    for j in range(2):
        vj = v_ref[:, j * dv:(j + 1) * dv]
        gj = g_ref[:, j * dv:(j + 1) * dv]
        qz = jnp.concatenate([qt[:dk], zero] if j == 0 else [zero, qt[dk:]], axis=0)
        base = j * levels
        cross = lw_ref[base + 8:base + 9, LANES:]
        halves = []
        for x in range(2):
            rows = [jnp.broadcast_to(lw_ref[base + l:base + l + 1, x * LANES:(x + 1) * LANES], (SUB, LANES))
                    for l in range(8)]
            halves.append(spread_half(rows, lane, low, t_low))

        def weigh(full):
            top = jnp.concatenate([full[:LANES, :LANES] * halves[0], full[:LANES, LANES:] * cross], axis=1)
            bottom = full[LANES:, LANES:] * halves[1]
            bottom = jnp.concatenate([jnp.zeros_like(bottom), bottom], axis=1)
            return jnp.concatenate([top, bottom], axis=0).astype(BF16)

        mixed = weigh(nn(kp, qz))
        grad_scores = weigh(nt(vj, gj))
        out_ref[j * dv:(j + 1) * dv, :] = tn(vj, mixed)
        dq_ref[j * dk:(j + 1) * dk, :] = nn(kt[j * dk:(j + 1) * dk], grad_scores)
        dv_ref[:, j * dv:(j + 1) * dv] = nn(mixed, gj)
        mine = (wide_lane < dk) if j == 0 else (wide_lane >= dk)
        term = nn(grad_scores, jnp.where(mine, qp, jnp.zeros_like(qp)))
        dk_sum = term if dk_sum is None else dk_sum + term
    dk_ref[...] = dk_sum


def carry_kernel(dims, levels, first, count, idx_ref, *refs):
    nh, dk, dv = dims
    ups = refs[:count]
    g_ref, qt_ref, sig_ref, far_ref = refs[count:]
    index = idx_ref[0]
    for m in range(count):
        up = ((index >> m) & 1).astype(F32)
        found = []
        for h in range(nh):
            rows = slice(h * dk, (h + 1) * dk)
            r = h * levels + first + m
            x = nt(ups[m][rows, :], g_ref[:, h * dv:(h + 1) * dv])
            row = jnp.sum(x * qt_ref[rows, :].astype(F32), axis=0, keepdims=True)
            found.append(row * (sig_ref[r:r + 1, :] * up))
        far_ref[m * nh:(m + 1) * nh, :] = jnp.concatenate(found, axis=0).astype(BF16)


def query_kernel(dims, levels, first, count, idx_ref, *refs):
    nh, dk, dv = dims
    ups = refs[:count]
    g_ref, lw_ref, low_ref, high_ref, dq_ref = refs[count:]
    index = idx_ref[0]
    for pair in range(nh // 2):
        halves = []
        for j in range(2):
            h = 2 * pair + j
            local_ref, n = (low_ref, h) if h < nh // 2 else (high_ref, h - nh // 2)
            total = local_ref[n * dk:(n + 1) * dk, :]
            for m in range(count):
                r = h * levels + first + m
                up = ((index >> m) & 1).astype(F32)
                x = nt(ups[m][h * dk:(h + 1) * dk, :], g_ref[:, h * dv:(h + 1) * dv])
                total = total + x * (lw_ref[r:r + 1, :] * up)
            halves.append(total)
        dq_ref[:, pair * 2 * dk:(pair + 1) * 2 * dk] = jnp.concatenate(halves, axis=0).T.astype(BF16)


def out_kernel(dims, levels, first, count, idx_ref, *refs):
    nh, dk, dv = dims
    ups = refs[:count]
    qt_ref, lw_ref, low_ref, high_ref, out_ref = refs[count:]
    index = idx_ref[0]
    for h in range(nh):
        rows = slice(h * dk, (h + 1) * dk)
        local_ref, n = (low_ref, h) if h < nh // 2 else (high_ref, h - nh // 2)
        total = local_ref[n * dv:(n + 1) * dv, :]
        for m in range(count):
            r = h * levels + first + m
            up = ((index >> m) & 1).astype(F32)
            total = total + tn(ups[m][rows, :], qt_ref[rows, :]) * (lw_ref[r:r + 1, :] * up)
        out_ref[:, h * dv:(h + 1) * dv] = total.T.astype(BF16)


def wgrad_kernel(xt_ref, gp_ref, dw_ref):
    dw_ref[...] = nt(xt_ref[...], gp_ref[...])


def merge_kernel(half, idx_ref, near_ref, far_ref, place_ref, send_ref, keep_ref):
    total = near_ref[...] + lax.dot_general(
        far_ref[...], place_ref[...], (((1,), (0,)), ((), ())),
        preferred_element_type=F32, precision=lax.Precision.HIGHEST)
    upper = ((idx_ref[0] >> half) & 1) == 1
    n = total.shape[0] // 2
    low, high = total[:n], total[n:]
    keep_ref[...] = jnp.where(upper, high, low)
    send_ref[...] = jnp.where(upper, low, high).astype(BF16)


def hidden_kernel(near_ref, far_ref, place_ref, w_ref, dx_ref):
    gp = near_ref[...].astype(F32) + tn(place_ref[...].astype(BF16), far_ref[...])
    dx_ref[...] = lax.dot_general(
        gp.astype(BF16), w_ref[...], (((0,), (1,)), ((), ())), preferred_element_type=F32).astype(BF16)


def join_kernel(top, count, idx_ref, kv_ref, *refs):
    ups = refs[:count]
    gu_ref, send_ref = refs[count:]
    upper = ((idx_ref[0] >> top) & 1) == 1

    @pl.when(upper)
    def _():
        send_ref[...] = gu_ref[top]

    @pl.when(jnp.logical_not(upper))
    def _():
        total = kv_ref[...]
        for up in ups:
            total = total + up[...].astype(F32)
        send_ref[...] = total.astype(BF16)


def final_kernel(dims, adj_ref, ds_ref, k_ref, v_ref, low_k, high_k, low_v, high_v, dk_ref, dv_ref):
    nh, dk, dv = dims
    zero = jnp.zeros((dk, dv), BF16)
    for pair in range(nh // 2):
        adj = [(adj_ref[h * dk:(h + 1) * dk, :] + ds_ref[h * dk:(h + 1) * dk, :]).astype(BF16)
               for h in (2 * pair, 2 * pair + 1)]
        kp = k_ref[:, pair * 2 * dk:(pair + 1) * 2 * dk]
        dkl_ref, dvl_ref, p = (low_k, low_v, pair) if pair < nh // 4 else (high_k, high_v, pair - nh // 4)
        total = dkl_ref[:, p * 2 * dk:(p + 1) * 2 * dk]
        for j in range(2):
            h = 2 * pair + j
            padded = jnp.concatenate([adj[j], zero] if j == 0 else [zero, adj[j]], axis=0)
            cols = slice(h * dv, (h + 1) * dv)
            total = total + nt(v_ref[:, cols], padded)
            near = dvl_ref[:, (2 * p + j) * dv:(2 * p + j + 1) * dv]
            dv_ref[:, cols] = (near + nn(kp, padded)).astype(BF16)
        dk_ref[:, pair * 2 * dk:(pair + 1) * 2 * dk] = total.astype(BF16)


def gather_heads(value, hi, head_bits, name):
    full = value[None]
    for bit in reversed(range(head_bits)):
        other = swap(full, "head", bit, name)
        mine = (hi >> bit) & 1
        full = jnp.where(mine == 0, jnp.stack([full, other]), jnp.stack([other, full]))
        full = full.reshape((-1,) + full.shape[2:]) if bit == head_bits - 1 else full
    full = full.reshape((2,) * head_bits + value.shape)
    full = full.transpose(tuple(reversed(range(head_bits))) + (head_bits, head_bits + 1))
    return full.reshape((-1,) + value.shape[1:])


def halve(keep, si, bit, name):
    pair = keep.reshape(keep.shape[0] // 2, 2, *keep.shape[1:])
    mine = (si >> bit) & 1
    send = lax.dynamic_index_in_dim(pair, 1 - mine, 1, keepdims=False).astype(BF16)
    got = swap(send, "seq", bit, name)
    return lax.dynamic_index_in_dim(pair, mine, 1, keepdims=False) + got.astype(F32)


def body(hidden, w, queries, keys, values, d_out, d_state):
    tokens, width = hidden.shape
    dims = d_state.shape
    nh, dk, dv = dims
    n_seq, n_head = lax.axis_size("seq"), lax.axis_size("head")
    seq_bits, head_bits = n_seq.bit_length() - 1, n_head.bit_length() - 1
    cols = w.shape[1]
    levels = cols // (nh * n_head)
    own = nh * levels
    far = nh * seq_bits
    first = tokens.bit_length()
    si, hi = lax.axis_index("seq"), lax.axis_index("head")
    idx = jnp.reshape(si, (1,)).astype(jnp.int32)
    S = jax.ShapeDtypeStruct
    rows = nh * dk

    hbm = pl.BlockSpec(memory_space=pltpu.HBM)
    kv, kvb, partial, xt = call(
        functools.partial(front_kernel, dims),
        [S((rows, dv), F32), S((rows, dv), BF16), S((cols, tokens), F32), S((width, tokens), BF16)],
        [hbm] * 4, 2 * tokens * (rows * dv + width * cols), "front",
        scratch_shapes=[pltpu.VMEM((tokens, rows), BF16), pltpu.VMEM((tokens, nh * dv), BF16),
                        pltpu.VMEM((width, cols), BF16), pltpu.VMEM((tokens, width), BF16),
                        pltpu.SemaphoreType.DMA((4,))])(
                            *[pltpu.with_memory_space_constraint(a, pltpu.HBM) for a in (keys, values, w, hidden)])

    top = seq_bits - 1
    total, send = kv, kvb
    ups = []
    for bit in range(top):
        partner = swap(send, "seq", bit, "up")
        ups.append(partner)
        if bit < top - 1:
            total = total + partner.astype(F32)
            send = total.astype(BF16)

    keep = partial
    got = None
    for bit in reversed(range(head_bits)):
        pair = keep.reshape(2, keep.shape[0] // 2, tokens)
        mine = (hi >> bit) & 1
        send = lax.dynamic_index_in_dim(pair, 1 - mine, 0, keepdims=False).astype(BF16)
        keep = lax.dynamic_index_in_dim(pair, mine, 0, keepdims=False)
        got = swap(send, "head", bit, "proj")
        if bit:
            keep = keep + got.astype(F32)

    pair_spec = lambda n: pl.BlockSpec((tokens, n), lambda p: (0, p))
    row_spec = lambda n: pl.BlockSpec((n, tokens), lambda p: (p, 0))
    gl = call(
        functools.partial(level_kernel, dims, levels), [S((own, tokens), F32)],
        [pair_spec(2 * dk), pair_spec(2 * dk), pair_spec(2 * dv), pair_spec(2 * dv)],
        2 * tokens * tokens * nh * (dk + dv), "near_levels", grid=(nh // 2,),
        out_specs=[row_spec(2 * levels)])(keys, queries, values, d_out)[0]
    sig, lw, near, qt, gu = call(
        functools.partial(weight_kernel, dims, levels, first, seq_bits),
        [S((own, tokens), F32), S((own, tokens), F32), S((own, tokens), BF16), S((rows, tokens), BF16),
         S((seq_bits, rows, dv), BF16)],
        [VM] * 5, 2 * tokens * rows * dv * seq_bits, "level_weights")(keep, got, gl, queries, d_out)

    send = call(functools.partial(join_kernel, top, top), [S((rows, dv), BF16)], [SM] + [VM] * (top + 2),
                rows * dv, "join")(idx, kv, *ups, gu)[0]
    partner = swap(send, "seq", top, "up")
    ups.append(partner)
    far_rows = call(
        functools.partial(carry_kernel, dims, levels, first, seq_bits), [S((far, tokens), BF16)],
        [SM] + [VM] * (seq_bits + 3), 2 * tokens * rows * dv * seq_bits, "carry")(idx, *ups, d_out, qt, sig)[0]
    upper_top = ((si >> top) & 1) == 1
    adjoint = jnp.where(upper_top, 0.0, partner.astype(F32))
    for bit in reversed(range(top)):
        pending = adjoint + jnp.where(((si >> bit) & 1) == 1, gu[bit].astype(F32), 0.0)
        adjoint = adjoint + swap(pending.astype(BF16), "seq", bit, "down").astype(F32)

    per = width // n_seq
    near_all = gather_heads(near, hi, head_bits, "near")
    near_w = call(wgrad_kernel, [S((width, cols), F32)], [VM, VM], 2 * tokens * width * cols, "near_wgrad")(
        xt, near_all)[0].reshape(n_seq, per, cols)
    for bit in range(top):
        near_w = halve(near_w, si, bit, "near")

    far_all = gather_heads(far_rows, hi, head_bits, "far")
    far_cols = far * n_head
    far_w = call(wgrad_kernel, [S((width, far_cols), F32)], [VM, VM], 2 * tokens * width * far_cols, "far_wgrad")(
        xt, far_all)[0].reshape(n_seq, per, far_cols)
    for bit in range(top):
        far_w = halve(far_w, si, bit, "far")
    col = jnp.arange(cols, dtype=jnp.int32)[None, :]
    row = jnp.arange(far_cols, dtype=jnp.int32)[:, None]
    at = (row // far * nh + row % nh) * levels + first + row % far // nh
    place = (at == col).astype(F32)
    send, keep = call(
        functools.partial(merge_kernel, top), [S((per, cols), BF16), S((per, cols), F32)], [SM] + [VM] * 3,
        4 * per * far_cols * cols, "merge")(
            idx, near_w.reshape(2 * per, cols), far_w.reshape(2 * per, far_cols), place)
    d_w = keep + swap(send, "seq", top, "last").astype(F32)

    half = nh // 4
    local = []
    for part in range(2):
        shift = part * half
        at_col = lambda n, shift=shift: pl.BlockSpec((tokens, n), lambda p: (0, p + shift))
        local.append(call(
            functools.partial(local_kernel, dims, levels),
            [S((nh * dv // 2, tokens), F32), S((rows // 2, tokens), F32), S((tokens, rows // 2), F32),
             S((tokens, nh * dv // 2), F32)],
            [at_col(2 * dk), at_col(2 * dk), at_col(2 * dv), at_col(2 * dv),
             pl.BlockSpec((2 * levels, tokens), lambda p, shift=shift: (p + shift, 0))],
            tokens * tokens * nh * (3 * dk + 3 * dv), "local", grid=(half,),
            out_specs=[row_spec(2 * dv), row_spec(2 * dk), pair_spec(2 * dk), pair_spec(2 * dv)],
        )(keys, queries, values, d_out, lw))
    out_l, dq_l, dk_l, dv_l = [(local[0][n], local[1][n]) for n in range(4)]
    d_queries = call(
        functools.partial(query_kernel, dims, levels, first, seq_bits), [S((tokens, rows), BF16)],
        [SM] + [VM] * (seq_bits + 4), 2 * tokens * rows * dv * seq_bits, "queries")(idx, *ups, d_out, lw, *dq_l)[0]
    out = call(
        functools.partial(out_kernel, dims, levels, first, seq_bits),
        [S((tokens, nh * dv), BF16)],
        [SM] + [VM] * (seq_bits + 4), 2 * tokens * rows * dv * seq_bits, "out")(idx, *ups, qt, lw, *out_l)[0]
    d_hidden = call(hidden_kernel, [S((tokens, width), BF16)], [VM] * 4, 2 * tokens * width * cols, "hgrad")(
        near_all, far_all, place, w)[0]
    d_keys, d_values = call(
        functools.partial(final_kernel, dims),
        [S((tokens, rows), BF16), S((tokens, nh * dv), BF16)], [VM] * 8, 4 * tokens * rows * dv, "final")(
            adjoint, d_state.reshape(rows, dv), keys, values, *dk_l, *dv_l)
    return (out, d_queries, d_keys, d_values, d_hidden, d_w)


def solution(mesh):
    two = P("seq", "head")
    return jax.shard_map(
        body, mesh=mesh,
        in_specs=(two, P("head", None), two, two, two, two, P("head", None, None)),
        out_specs=(two, two, two, two, two, P(("head", "seq"), None)),
        check_vma=False)
```

time: 51.5 us -> 54.5 us (1.058)
  Pallas kernels: 10.2 us -> 14.8 us
  local copies, waits for them, and re-layouts: 3.03 us -> 0.22 us
  starting transfers between devices: 16.6 us -> 18.4 us
  other arithmetic: 1.76 us -> 1.13 us
    pallas_call x4 -> x9, Pallas kernels: 5.23 us -> 10.6 us  [the longest x2 3.67 us: body(): call(functools.partial(local_kernel, dims, levels), [S((nh * dv // 2, tok...]
    unnamed x18 -> x12, local copies, waits for them, and re-layouts: 2.9 us -> 0.07 us
    ppermute x12 -> x16, starting transfers between devices: 16.6 us -> 18.4 us  [swap(): return lax.ppermute(value, axis, pairs)]
    pallas_call x1, Pallas kernels: 1.46 us -> 0.68 us  [body(): call(functools.partial(carry_kernel, dims, levels, first, seq_bits), [S((...]
    select_n x3 -> x4, other arithmetic: 0.73 us -> 0.04 us  [gather_heads(): jnp.where(mine == 0, jnp.stack([full, other]), jnp.stack([other, full]))]
    add x3 -> x7, other arithmetic: 0.12 us -> 0.81 us  [the longest x1 0.65 us: body(): d_w = keep + swap(send, 'seq', top, 'last').astype(F32)]
    reshape x1 -> x0, other arithmetic: 0.65 us -> none  [body(): d_w = keep.reshape(width // n_seq, cols)]
    ppermute x12 -> x16, waiting for transfers between devices: 18.7 us -> 18.7 us  [swap(): return lax.ppermute(value, axis, pairs)]
  transfers between devices with their start and end apart: 12 -> 16, of which waited for: 10 -> 8; matrix products, arithmetic and copies ran while one was open for 1% -> 2% of each run, Pallas kernels for 16% -> 20%
where the time goes in v2:
time: 54.5 us; the launch traced here: 54.3 us
  waiting for transfers between devices  18.7 us (34%)
  starting transfers between devices  18.4 us (34%)
  Pallas kernels  14.8 us (27%)
  other arithmetic  1.13 us (2%)
  between operations  0.99 us (2%)
    ppermute x16, waiting for transfers between devices, swap(): return lax.ppermute(value, axis, pairs)  18.7 us
    ppermute x16, starting transfers between devices, swap(): return lax.ppermute(value, axis, pairs)  18.4 us
    pallas_call x2, Pallas kernels, body(): call(functools.partial(local_kernel, dims, levels), [S((nh * dv // 2, tok...  3.67 us
    pallas_call x1, Pallas kernels, body(): call(functools.partial(front_kernel, dims), [S((rows, dv), F32), S((rows,...  1.96 us
    pallas_call x1, Pallas kernels, body(): call(functools.partial(level_kernel, dims, levels), [S((own, tokens), F32...  1.73 us
    pallas_call x1, Pallas kernels, body(): call(functools.partial(out_kernel, dims, levels, first, seq_bits), [S((to...  1.47 us
    pallas_call x1, Pallas kernels, body(): call(functools.partial(query_kernel, dims, levels, first, seq_bits), [S((...  1.44 us
    pallas_call x1, Pallas kernels, body(): call(functools.partial(final_kernel, dims), [S((tokens, rows), BF16), S((...  1.33 us
  transfers between devices with their start and end apart: 16, of which 8 were waited for; matrix products, arithmetic and copies ran while one was open for 2% of the time, Pallas kernels for 20%

profile of v2, /device:TPU:0, one launch (start us, length us, event | category | flops | bytes accessed | tf_op | source)
XLA Modules:
  0.0 54.3 jit_solution(8411765128870312737)
XLA Ops:
  0.6 0.0 copy-start
  0.6 0.0 copy-start.1
  0.7 0.0 copy-start.3
  0.7 2.0 %front.1 = (f32[512,128]{1,0:T(8,128)S(1)}, bf16[512,128]{1,0:T(8,128)(2,1)S(1)}, f32[384,256]{1,0:T(8,128)S(1)}, bf16[512,256]{1,0:T(8,128)(2,1)S(1)}) custom-call(bf16[256,512]{1,0:T(8,128)(2,1)} %k_ref.7, bf16[256,1024]{1,0:T(8,128)(2,1)} %v_ref.7, bf16[512,384]{1,0:T(8,128)(2,1)} %w_ref.1, bf16[256,512]{1,0:T(8,128)(2,1)} %x_hbm.1), custom_call_target="tpu_custom_call" | custom-call | flops 134217728 | bytes 2097152 | tf_op jit(solution)/shard_map/front/pallas_call | solution.py:342
  2.6 0.0 copy-start.2
  2.6 3.1 %collective-permute-start = (bf16[512,128]{1,0:T(8,128)(2,1)S(1)}, bf16[512,128]{1,0:T(8,128)(2,1)S(1)}, u32[]{:S(2)}, u32[]{:S(2)}) collective-permute-start(bf16[512,128]{1,0:T(8,128)(2,1)S(1)} %get-tuple-element.27), channel_id=1, source_target_pairs={{0,4},{4,0},{8,12},{12,8},{16,20},{20,16},{24,28},{28,24},{1,5},{5... | collective-permute-start | bytes 393224 | tf_op jit(solution)/shard_map/up_seq0/ppermute | solution.py:47
  5.7 1.6 %collective-permute-start.2 = (bf16[192,256]{1,0:T(8,128)(2,1)S(1)}, bf16[192,256]{1,0:T(8,128)(2,1)S(1)}, u32[]{:S(2)}, u32[]{:S(2)}) collective-permute-start(bf16[192,256]{1,0:T(8,128)(2,1)S(1)} %fusion.5), channel_id=1, source_target_pairs={{0,2},{1,3},{2,0},{3,1},{4,6},{5,7},{6,4},{7,5},{8,10},{9,11},{10,... | collective-permute-start | bytes 294920 | tf_op jit(solution)/shard_map/proj_head1/ppermute | solution.py:47
  7.3 0.1 fusion.4.place_ref
  7.4 0.0 copy-done
  7.4 0.0 copy-done.1
  7.4 0.0 copy-done.3
  7.4 0.0 copy-done.2
  7.4 1.7 %near_levels.1.gl_ref = f32[96,256]{1,0:T(8,128)S(1)} custom-call(bf16[256,512]{1,0:T(8,128)(2,1)S(1)} %copy-done.2, bf16[256,512]{1,0:T(8,128)(2,1)S(1)} %copy-done.3, bf16[256,1024]{1,0:T(8,128)(2,1)S(1)} %copy-done.1, bf16[256,1024]{1,0:T(8,128)(2,1)S(1)} %copy-done), custom_call_target="tpu_custom_call" | custom-call | flops 201326592 | bytes 196608 | tf_op jit(solution)/shard_map/near_levels/pallas_call | solution.py:374
  9.2 1.2 %collective-permute-done.2 = bf16[192,256]{1,0:T(8,128)(2,1)S(1)} collective-permute-done((bf16[192,256]{1,0:T(8,128)(2,1)S(1)}, bf16[192,256]{1,0:T(8,128)(2,1)S(1)}, u32[]{:S(2)}, u32[]{:S(2)}) %collective-permute-start.2) | collective-permute-done | bytes 98336 | tf_op jit(solution)/shard_map/proj_head1/ppermute | solution.py:47
  10.4 0.1 collective-permute-start.3
  10.6 0.0 collective-permute-done.refs_0_
  10.6 1.6 %collective-permute-start.1 = (bf16[512,128]{1,0:T(8,128)(2,1)S(1)}, bf16[512,128]{1,0:T(8,128)(2,1)S(1)}, u32[]{:S(2)}, u32[]{:S(2)}) collective-permute-start(bf16[512,128]{1,0:T(8,128)(2,1)S(1)} %add_convert_fusion), channel_id=1, source_target_pairs={{0,8},{4,12},{8,0},{12,4},{16,24},{20,28},{24,16},{28,20},{1,9},{5... | collective-permute-start | bytes 393224 | tf_op jit(solution)/shard_map/up_seq1/ppermute | solution.py:47
  12.2 0.0 collective-permute-done.3.got_ref
  12.2 0.4 level_weights.1
  12.7 1.6 %collective-permute-start.7 = (bf16[1,96,256]{2,1,0:T(8,128)(2,1)S(1)}, bf16[1,96,256]{2,1,0:T(8,128)(2,1)S(1)}, u32[]{:S(2)}, u32[]{:S(2)}) collective-permute-start(bf16[1,96,256]{2,1,0:T(8,128)(2,1)S(1)} %bitcast.77), channel_id=1, source_target_pairs={{0,2},{1,3},{2,0},{3,1},{4,6},{5,7},{6,4},{7,5},{8,10},{9,11},{10,... | collective-permute-start | bytes 147464 | tf_op jit(solution)/shard_map/near_head1/ppermute | solution.py:47
  14.2 1.8 %local.2 = (f32[512,256]{1,0:T(8,128)S(1)}, f32[256,256]{1,0:T(8,128)S(1)}, f32[256,256]{1,0:T(8,128)S(1)}, f32[256,512]{1,0:T(8,128)S(1)}) custom-call(bf16[256,512]{1,0:T(8,128)(2,1)S(1)} %copy-done.2, bf16[256,512]{1,0:T(8,128)(2,1)S(1)} %copy-done.3, bf16[256,1024]{1,0:T(8,128)(2,1)S(1)} %copy-done.1, bf16[256,1024]{1,0:T(8,128)(2,1)S(1)} %copy-done, ...), custom_call_target="tpu_custom_call" | custom-call | flops 301989888 | bytes 3145728 | tf_op jit(solution)/shard_map/local/pallas_call | solution.py:426
  16.1 1.8 %local.3 = (f32[512,256]{1,0:T(8,128)S(1)}, f32[256,256]{1,0:T(8,128)S(1)}, f32[256,256]{1,0:T(8,128)S(1)}, f32[256,512]{1,0:T(8,128)S(1)}) custom-call(bf16[256,512]{1,0:T(8,128)(2,1)S(1)} %copy-done.2, bf16[256,512]{1,0:T(8,128)(2,1)S(1)} %copy-done.3, bf16[256,1024]{1,0:T(8,128)(2,1)S(1)} %copy-done.1, bf16[256,1024]{1,0:T(8,128)(2,1)S(1)} %copy-done, ...), custom_call_target="tpu_custom_call" | custom-call | flops 301989888 | bytes 3145728 | tf_op jit(solution)/shard_map/local/pallas_call | solution.py:426
  17.9 0.0 collective-permute-done.7
  17.9 0.1 collective-permute-start.8
  18.0 0.0 collective-permute-done.1.refs_1_
  18.0 0.1 join.1
  18.1 2.6 %collective-permute-start.4 = (bf16[512,128]{1,0:T(8,128)(2,1)S(1)}, bf16[512,128]{1,0:T(8,128)(2,1)S(1)}, u32[]{:S(2)}, u32[]{:S(2)}) collective-permute-start(bf16[512,128]{1,0:T(8,128)(2,1)S(1)} %join.1), channel_id=1, source_target_pairs={{0,16},{4,20},{8,24},{12,28},{16,0},{20,4},{24,8},{28,12},{1,17},{... | collective-permute-start | bytes 393224 | tf_op jit(solution)/shard_map/up_seq2/ppermute | solution.py:47
  20.7 0.0 collective-permute-done.8
  20.8 0.3 near_wgrad.1
  21.1 6.6 %collective-permute-done.4.refs_2_ = bf16[512,128]{1,0:T(8,128)(2,1)S(1)} collective-permute-done((bf16[512,128]{1,0:T(8,128)(2,1)S(1)}, bf16[512,128]{1,0:T(8,128)(2,1)S(1)}, u32[]{:S(2)}, u32[]{:S(2)}) %collective-permute-start.4) | collective-permute-done | bytes 131104 | tf_op jit(solution)/shard_map/up_seq2/ppermute | solution.py:47
  27.7 0.7 %carry.1 = bf16[24,256]{1,0:T(8,128)(2,1)S(1)} custom-call(s32[1]{0:T(128)} %bitcast.idx_ref, bf16[512,128]{1,0:T(8,128)(2,1)S(1)} %collective-permute-done.refs_0_, bf16[512,128]{1,0:T(8,128)(2,1)S(1)} %collective-permute-done.1.refs_1_, bf16[512,128]{1,0:T(8,128)(2,1)S(1)} %collective-permute-done.4.refs_2_, bf16[256,1024]{1,0:T(8,128)(2,1)S(1)} %copy-done, ...), custom_call_target="tpu_custom_call" | custom-call | flops 100663296 | bytes 24576 | tf_op jit(solution)/shard_map/carry/pallas_call | solution.py:389
  28.4 0.6 %collective-permute-start.9 = (bf16[1,24,256]{2,1,0:T(8,128)(2,1)S(1)}, bf16[1,24,256]{2,1,0:T(8,128)(2,1)S(1)}, u32[]{:S(2)}, u32[]{:S(2)}) collective-permute-start(bf16[1,24,256]{2,1,0:T(8,128)(2,1)S(1)} %bitcast.80), channel_id=1, source_target_pairs={{0,2},{1,3},{2,0},{3,1},{4,6},{5,7},{6,4},{7,5},{8,10},{9,11},{10,... | collective-permute-start | bytes 36872 | tf_op jit(solution)/shard_map/far_head1/ppermute | solution.py:47
  29.0 0.6 %collective-permute-start.11 = (bf16[4,64,384]{2,1,0:T(8,128)(2,1)S(1)}, bf16[4,64,384]{2,1,0:T(8,128)(2,1)S(1)}, u32[]{:S(2)}, u32[]{:S(2)}) collective-permute-start(bf16[4,64,384]{2,1,0:T(8,128)(2,1)S(1)} %fusion.2), channel_id=1, source_target_pairs={{0,4},{4,0},{8,12},{12,8},{16,20},{20,16},{24,28},{28,24},{1,5},{5... | collective-permute-start | bytes 589832 | tf_op jit(solution)/shard_map/near_seq0/ppermute | solution.py:47
  29.6 2.6 %collective-permute-done.9 = bf16[1,24,256]{2,1,0:T(8,128)(2,1)S(1)} collective-permute-done((bf16[1,24,256]{2,1,0:T(8,128)(2,1)S(1)}, bf16[1,24,256]{2,1,0:T(8,128)(2,1)S(1)}, u32[]{:S(2)}, u32[]{:S(2)}) %collective-permute-start.9) | collective-permute-done | bytes 12320 | tf_op jit(solution)/shard_map/far_head1/ppermute | solution.py:47
  32.2 0.0 collective-permute-start.10
  32.2 1.2 %collective-permute-done.10 = bf16[2,24,256]{2,1,0:T(8,128)(2,1)S(1)} collective-permute-done((bf16[2,24,256]{2,1,0:T(8,128)(2,1)S(1)}, bf16[2,24,256]{2,1,0:T(8,128)(2,1)S(1)}, u32[]{:S(2)}, u32[]{:S(2)}) %collective-permute-start.10) | collective-permute-done | bytes 24608 | tf_op jit(solution)/shard_map/far_head0/ppermute | solution.py:47
  33.4 0.2 far_wgrad.1
  33.7 0.6 %collective-permute-start.13 = (bf16[4,64,96]{2,1,0:T(8,128)(2,1)S(1)}, bf16[4,64,96]{2,1,0:T(8,128)(2,1)S(1)}, u32[]{:S(2)}, u32[]{:S(2)}) collective-permute-start(bf16[4,64,96]{2,1,0:T(8,128)(2,1)S(1)} %fusion.7), channel_id=1, source_target_pairs={{0,4},{4,0},{8,12},{12,8},{16,20},{20,16},{24,28},{28,24},{1,5},{5... | collective-permute-start | bytes 147464 | tf_op jit(solution)/shard_map/far_seq0/ppermute | solution.py:47
  34.2 0.1 fusion.1
  34.3 0.3 collective-permute-start.5
  34.6 1.5 %out.1 = bf16[256,1024]{1,0:T(8,128)(2,1)} custom-call(s32[1]{0:T(128)} %bitcast.idx_ref, bf16[512,128]{1,0:T(8,128)(2,1)S(1)} %collective-permute-done.refs_0_, bf16[512,128]{1,0:T(8,128)(2,1)S(1)} %collective-permute-done.1.refs_1_, bf16[512,128]{1,0:T(8,128)(2,1)S(1)} %collective-permute-done.4.refs_2_, ...), custom_call_target="tpu_custom_call" | custom-call | flops 100663296 | bytes 1048576 | tf_op jit(solution)/shard_map/out/pallas_call | solution.py:439
  36.1 0.0 copy-start.4
  36.1 1.4 %queries.1 = bf16[256,512]{1,0:T(8,128)(2,1)} custom-call(s32[1]{0:T(128)} %bitcast.idx_ref, bf16[512,128]{1,0:T(8,128)(2,1)S(1)} %collective-permute-done.refs_0_, bf16[512,128]{1,0:T(8,128)(2,1)S(1)} %collective-permute-done.1.refs_1_, bf16[512,128]{1,0:T(8,128)(2,1)S(1)} %collective-permute-done.4.refs_2_, bf16[256,1024]{1,0:T(8,128)(2,1)S(1)} %copy-done, ...), custom_call_target="tpu_custom_call" | custom-call | flops 100663296 | bytes 524288 | tf_op jit(solution)/shard_map/queries/pallas_call | solution.py:436
  37.6 0.0 copy-done.4
  37.6 1.3 %hgrad.1 = bf16[256,512]{1,0:T(8,128)(2,1)} custom-call(bf16[384,256]{1,0:T(8,128)(2,1)S(1)} %bitcast.67, bf16[96,256]{1,0:T(8,128)(2,1)S(1)} %bitcast.72, f32[96,384]{1,0:T(8,128)S(1)} %fusion.4.place_ref, bf16[512,384]{1,0:T(8,128)(2,1)S(1)} %copy-done.4), custom_call_target="tpu_custom_call" | custom-call | flops 100663296 | bytes 524288 | tf_op jit(solution)/shard_map/hgrad/pallas_call | solution.py:443
  38.8 0.0 collective-permute-done.13
  38.9 1.8 %collective-permute-start.14 = (bf16[2,64,96]{2,1,0:T(8,128)(2,1)S(1)}, bf16[2,64,96]{2,1,0:T(8,128)(2,1)S(1)}, u32[]{:S(2)}, u32[]{:S(2)}) collective-permute-start(bf16[2,64,96]{2,1,0:T(8,128)(2,1)S(1)} %fusion.10), channel_id=1, source_target_pairs={{0,8},{4,12},{8,0},{12,4},{16,24},{20,28},{24,16},{28,20},{1,9},{5... | collective-permute-start | bytes 73736 | tf_op jit(solution)/shard_map/far_seq1/ppermute | solution.py:47
  40.7 0.0 collective-permute-done.11
  40.7 0.4 collective-permute-start.12
  41.1 1.8 %collective-permute-done.14 = bf16[2,64,96]{2,1,0:T(8,128)(2,1)S(1)} collective-permute-done((bf16[2,64,96]{2,1,0:T(8,128)(2,1)S(1)}, bf16[2,64,96]{2,1,0:T(8,128)(2,1)S(1)}, u32[]{:S(2)}, u32[]{:S(2)}) %collective-permute-start.14) | collective-permute-done | bytes 24608 | tf_op jit(solution)/shard_map/far_seq1/ppermute | solution.py:47
  43.0 2.5 %collective-permute-done.12 = bf16[2,64,384]{2,1,0:T(8,128)(2,1)S(1)} collective-permute-done((bf16[2,64,384]{2,1,0:T(8,128)(2,1)S(1)}, bf16[2,64,384]{2,1,0:T(8,128)(2,1)S(1)}, u32[]{:S(2)}, u32[]{:S(2)}) %collective-permute-start.12) | collective-permute-done | bytes 98336 | tf_op jit(solution)/shard_map/near_seq1/ppermute | solution.py:47
  45.4 0.3 merge.1
  45.8 2.0 %collective-permute-start.15 = (bf16[64,384]{1,0:T(8,128)(2,1)S(1)}, bf16[64,384]{1,0:T(8,128)(2,1)S(1)}, u32[]{:S(2)}, u32[]{:S(2)}) collective-permute-start(bf16[64,384]{1,0:T(8,128)(2,1)S(1)} %get-tuple-element.47), channel_id=1, source_target_pairs={{0,16},{4,20},{8,24},{12,28},{16,0},{20,4},{24,8},{28,12},{1,17},{... | collective-permute-start | bytes 147464 | tf_op jit(solution)/shard_map/last_seq2/ppermute | solution.py:47
  47.7 0.0 collective-permute-done.5
  47.7 0.1 fusion
  47.8 1.6 %collective-permute-start.6 = (bf16[512,128]{1,0:T(8,128)(2,1)S(1)}, bf16[512,128]{1,0:T(8,128)(2,1)S(1)}, u32[]{:S(2)}, u32[]{:S(2)}) collective-permute-start(bf16[512,128]{1,0:T(8,128)(2,1)S(1)} %fusion), channel_id=1, source_target_pairs={{0,4},{4,0},{8,12},{12,8},{16,20},{20,16},{24,28},{28,24},{1,5},{5... | collective-permute-start | bytes 393224 | tf_op jit(solution)/shard_map/down_seq0/ppermute | solution.py:47
  49.4 1.9 %collective-permute-done.15 = bf16[64,384]{1,0:T(8,128)(2,1)S(1)} collective-permute-done((bf16[64,384]{1,0:T(8,128)(2,1)S(1)}, bf16[64,384]{1,0:T(8,128)(2,1)S(1)}, u32[]{:S(2)}, u32[]{:S(2)}) %collective-permute-start.15) | collective-permute-done | bytes 49184 | tf_op jit(solution)/shard_map/last_seq2/ppermute | solution.py:47
  51.3 0.7 %convert_add_fusion.2 = f32[64,384]{1,0:T(8,128)} fusion(f32[64,384]{1,0:T(8,128)S(1)} %get-tuple-element.46, bf16[64,384]{1,0:T(8,128)(2,1)S(1)} %collective-permute-done.15), kind=kLoop, calls=%fused_computation.25 | loop fusion | flops 49152 | bytes 245760 | tf_op jit(solution)/shard_map/add | solution.py:419
  52.0 0.0 copy-start.5
  52.0 0.8 %collective-permute-done.6 = bf16[512,128]{1,0:T(8,128)(2,1)S(1)} collective-permute-done((bf16[512,128]{1,0:T(8,128)(2,1)S(1)}, bf16[512,128]{1,0:T(8,128)(2,1)S(1)}, u32[]{:S(2)}, u32[]{:S(2)}) %collective-permute-start.6) | collective-permute-done | bytes 131104 | tf_op jit(solution)/shard_map/down_seq0/ppermute | solution.py:47
  52.8 0.1 convert_add_fusion.adj_ref
  52.9 0.0 copy-done.5
  53.0 1.3 %final.1 = (bf16[256,512]{1,0:T(8,128)(2,1)}, bf16[256,1024]{1,0:T(8,128)(2,1)}) custom-call(f32[512,128]{1,0:T(8,128)S(1)} %convert_add_fusion.adj_ref, f32[512,128]{1,0:T(8,128)S(1)} %bitcast.74, bf16[256,512]{1,0:T(8,128)(2,1)S(1)} %copy-done.2, bf16[256,1024]{1,0:T(8,128)(2,1)S(1)} %copy-done.1, f32[256,256]{1,0:T(8,128)S(1)} %get-tuple-element.37.low_k, ...), custom_call_target="tpu_custom_call" | custom-call | flops 67108864 | bytes 1572864 | tf_op jit(solution)/shard_map/final/pallas_call | solution.py:445
  (22 shorter events, 0.4 us)
Async XLA Ops:
  0.6 6.8 %copy-start = (bf16[256,1024]{1,0:T(8,128)(2,1)S(1)}, bf16[256,1024]{1,0:T(8,128)(2,1)}, u32[]{:S(2)}) copy-start(bf16[256,1024]{1,0:T(8,128)(2,1)} %refs_3_.3) | copy-start | bytes 1572868
  0.6 6.8 %copy-start.1 = (bf16[256,1024]{1,0:T(8,128)(2,1)S(1)}, bf16[256,1024]{1,0:T(8,128)(2,1)}, u32[]{:S(2)}) copy-start(bf16[256,1024]{1,0:T(8,128)(2,1)} %v_ref.7) | copy-start | bytes 1572868
  0.7 6.8 %copy-start.3 = (bf16[256,512]{1,0:T(8,128)(2,1)S(1)}, bf16[256,512]{1,0:T(8,128)(2,1)}, u32[]{:S(2)}) copy-start(bf16[256,512]{1,0:T(8,128)(2,1)} %q_ref.7) | copy-start | bytes 786436
  2.6 4.8 %copy-start.2 = (bf16[256,512]{1,0:T(8,128)(2,1)S(1)}, bf16[256,512]{1,0:T(8,128)(2,1)}, u32[]{:S(2)}) copy-start(bf16[256,512]{1,0:T(8,128)(2,1)} %k_ref.7) | copy-start | bytes 786436
  2.6 7.9 %collective-permute-start = (bf16[512,128]{1,0:T(8,128)(2,1)S(1)}, bf16[512,128]{1,0:T(8,128)(2,1)S(1)}, u32[]{:S(2)}, u32[]{:S(2)}) collective-permute-start(bf16[512,128]{1,0:T(8,128)(2,1)S(1)} %get-tuple-element.27), channel_id=1, source_target_pairs={{0,4},{4,0},{8,12},{12,8},{16,20},{20,16},{24,28},{28,24},{1,5},{5... | collective-permute-start | bytes 393224 | tf_op jit(solution)/shard_map/up_seq0/ppermute | solution.py:47
  5.7 4.7 %collective-permute-start.2 = (bf16[192,256]{1,0:T(8,128)(2,1)S(1)}, bf16[192,256]{1,0:T(8,128)(2,1)S(1)}, u32[]{:S(2)}, u32[]{:S(2)}) collective-permute-start(bf16[192,256]{1,0:T(8,128)(2,1)S(1)} %fusion.5), channel_id=1, source_target_pairs={{0,2},{1,3},{2,0},{3,1},{4,6},{5,7},{6,4},{7,5},{8,10},{9,11},{10,... | collective-permute-start | bytes 294920 | tf_op jit(solution)/shard_map/proj_head1/ppermute | solution.py:47
  10.4 1.8 %collective-permute-start.3 = (bf16[96,256]{1,0:T(8,128)(2,1)S(1)}, bf16[96,256]{1,0:T(8,128)(2,1)S(1)}, u32[]{:S(2)}, u32[]{:S(2)}) collective-permute-start(bf16[96,256]{1,0:T(8,128)(2,1)S(1)} %fusion.8), channel_id=1, source_target_pairs={{0,1},{1,0},{2,3},{3,2},{4,5},{5,4},{6,7},{7,6},{8,9},{9,8},{10,11... | collective-permute-start | bytes 147464 | tf_op jit(solution)/shard_map/proj_head0/ppermute | solution.py:47
  10.6 7.4 %collective-permute-start.1 = (bf16[512,128]{1,0:T(8,128)(2,1)S(1)}, bf16[512,128]{1,0:T(8,128)(2,1)S(1)}, u32[]{:S(2)}, u32[]{:S(2)}) collective-permute-start(bf16[512,128]{1,0:T(8,128)(2,1)S(1)} %add_convert_fusion), channel_id=1, source_target_pairs={{0,8},{4,12},{8,0},{12,4},{16,24},{20,28},{24,16},{28,20},{1,9},{5... | collective-permute-start | bytes 393224 | tf_op jit(solution)/shard_map/up_seq1/ppermute | solution.py:47
  12.7 5.2 %collective-permute-start.7 = (bf16[1,96,256]{2,1,0:T(8,128)(2,1)S(1)}, bf16[1,96,256]{2,1,0:T(8,128)(2,1)S(1)}, u32[]{:S(2)}, u32[]{:S(2)}) collective-permute-start(bf16[1,96,256]{2,1,0:T(8,128)(2,1)S(1)} %bitcast.77), channel_id=1, source_target_pairs={{0,2},{1,3},{2,0},{3,1},{4,6},{5,7},{6,4},{7,5},{8,10},{9,11},{10,... | collective-permute-start | bytes 147464 | tf_op jit(solution)/shard_map/near_head1/ppermute | solution.py:47
  17.9 2.8 %collective-permute-start.8 = (bf16[2,96,256]{2,1,0:T(8,128)(2,1)S(1)}, bf16[2,96,256]{2,1,0:T(8,128)(2,1)S(1)}, u32[]{:S(2)}, u32[]{:S(2)}) collective-permute-start(bf16[2,96,256]{2,1,0:T(8,128)(2,1)S(1)} %maximum_select_fusion.2), channel_id=1, source_target_pairs={{0,1},{1,0},{2,3},{3,2},{4,5},{5,4},{6,7},{7,6},{8,9},{9,8},{10,11... | collective-permute-start | bytes 294920 | tf_op jit(solution)/shard_map/near_head0/ppermute | solution.py:47
  18.1 9.7 %collective-permute-start.4 = (bf16[512,128]{1,0:T(8,128)(2,1)S(1)}, bf16[512,128]{1,0:T(8,128)(2,1)S(1)}, u32[]{:S(2)}, u32[]{:S(2)}) collective-permute-start(bf16[512,128]{1,0:T(8,128)(2,1)S(1)} %join.1), channel_id=1, source_target_pairs={{0,16},{4,20},{8,24},{12,28},{16,0},{20,4},{24,8},{28,12},{1,17},{... | collective-permute-start | bytes 393224 | tf_op jit(solution)/shard_map/up_seq2/ppermute | solution.py:47
  28.4 3.8 %collective-permute-start.9 = (bf16[1,24,256]{2,1,0:T(8,128)(2,1)S(1)}, bf16[1,24,256]{2,1,0:T(8,128)(2,1)S(1)}, u32[]{:S(2)}, u32[]{:S(2)}) collective-permute-start(bf16[1,24,256]{2,1,0:T(8,128)(2,1)S(1)} %bitcast.80), channel_id=1, source_target_pairs={{0,2},{1,3},{2,0},{3,1},{4,6},{5,7},{6,4},{7,5},{8,10},{9,11},{10,... | collective-permute-start | bytes 36872 | tf_op jit(solution)/shard_map/far_head1/ppermute | solution.py:47
  29.0 11.6 %collective-permute-start.11 = (bf16[4,64,384]{2,1,0:T(8,128)(2,1)S(1)}, bf16[4,64,384]{2,1,0:T(8,128)(2,1)S(1)}, u32[]{:S(2)}, u32[]{:S(2)}) collective-permute-start(bf16[4,64,384]{2,1,0:T(8,128)(2,1)S(1)} %fusion.2), channel_id=1, source_target_pairs={{0,4},{4,0},{8,12},{12,8},{16,20},{20,16},{24,28},{28,24},{1,5},{5... | collective-permute-start | bytes 589832 | tf_op jit(solution)/shard_map/near_seq0/ppermute | solution.py:47
  32.2 1.2 %collective-permute-start.10 = (bf16[2,24,256]{2,1,0:T(8,128)(2,1)S(1)}, bf16[2,24,256]{2,1,0:T(8,128)(2,1)S(1)}, u32[]{:S(2)}, u32[]{:S(2)}) collective-permute-start(bf16[2,24,256]{2,1,0:T(8,128)(2,1)S(1)} %maximum_select_fusion.5), channel_id=1, source_target_pairs={{0,1},{1,0},{2,3},{3,2},{4,5},{5,4},{6,7},{7,6},{8,9},{9,8},{10,11... | collective-permute-start | bytes 73736 | tf_op jit(solution)/shard_map/far_head0/ppermute | solution.py:47
  33.7 5.2 %collective-permute-start.13 = (bf16[4,64,96]{2,1,0:T(8,128)(2,1)S(1)}, bf16[4,64,96]{2,1,0:T(8,128)(2,1)S(1)}, u32[]{:S(2)}, u32[]{:S(2)}) collective-permute-start(bf16[4,64,96]{2,1,0:T(8,128)(2,1)S(1)} %fusion.7), channel_id=1, source_target_pairs={{0,4},{4,0},{8,12},{12,8},{16,20},{20,16},{24,28},{28,24},{1,5},{5... | collective-permute-start | bytes 147464 | tf_op jit(solution)/shard_map/far_seq0/ppermute | solution.py:47
  34.3 13.5 %collective-permute-start.5 = (bf16[512,128]{1,0:T(8,128)(2,1)S(1)}, bf16[512,128]{1,0:T(8,128)(2,1)S(1)}, u32[]{:S(2)}, u32[]{:S(2)}) collective-permute-start(bf16[512,128]{1,0:T(8,128)(2,1)S(1)} %fusion.1), channel_id=1, source_target_pairs={{0,8},{4,12},{8,0},{12,4},{16,24},{20,28},{24,16},{28,20},{1,9},{5... | collective-permute-start | bytes 393224 | tf_op jit(solution)/shard_map/down_seq1/ppermute | solution.py:47
  36.1 1.4 %copy-start.4 = (bf16[512,384]{1,0:T(8,128)(2,1)S(1)}, bf16[512,384]{1,0:T(8,128)(2,1)}, u32[]{:S(2)}) copy-start(bf16[512,384]{1,0:T(8,128)(2,1)} %w_ref.1) | copy-start | bytes 1179652
  38.9 4.1 %collective-permute-start.14 = (bf16[2,64,96]{2,1,0:T(8,128)(2,1)S(1)}, bf16[2,64,96]{2,1,0:T(8,128)(2,1)S(1)}, u32[]{:S(2)}, u32[]{:S(2)}) collective-permute-start(bf16[2,64,96]{2,1,0:T(8,128)(2,1)S(1)} %fusion.10), channel_id=1, source_target_pairs={{0,8},{4,12},{8,0},{12,4},{16,24},{20,28},{24,16},{28,20},{1,9},{5... | collective-permute-start | bytes 73736 | tf_op jit(solution)/shard_map/far_seq1/ppermute | solution.py:47
  40.7 4.7 %collective-permute-start.12 = (bf16[2,64,384]{2,1,0:T(8,128)(2,1)S(1)}, bf16[2,64,384]{2,1,0:T(8,128)(2,1)S(1)}, u32[]{:S(2)}, u32[]{:S(2)}) collective-permute-start(bf16[2,64,384]{2,1,0:T(8,128)(2,1)S(1)} %fusion.6), channel_id=1, source_target_pairs={{0,8},{4,12},{8,0},{12,4},{16,24},{20,28},{24,16},{28,20},{1,9},{5... | collective-permute-start | bytes 294920 | tf_op jit(solution)/shard_map/near_seq1/ppermute | solution.py:47
  45.8 5.6 %collective-permute-start.15 = (bf16[64,384]{1,0:T(8,128)(2,1)S(1)}, bf16[64,384]{1,0:T(8,128)(2,1)S(1)}, u32[]{:S(2)}, u32[]{:S(2)}) collective-permute-start(bf16[64,384]{1,0:T(8,128)(2,1)S(1)} %get-tuple-element.47), channel_id=1, source_target_pairs={{0,16},{4,20},{8,24},{12,28},{16,0},{20,4},{24,8},{28,12},{1,17},{... | collective-permute-start | bytes 147464 | tf_op jit(solution)/shard_map/last_seq2/ppermute | solution.py:47
  47.8 5.0 %collective-permute-start.6 = (bf16[512,128]{1,0:T(8,128)(2,1)S(1)}, bf16[512,128]{1,0:T(8,128)(2,1)S(1)}, u32[]{:S(2)}, u32[]{:S(2)}) collective-permute-start(bf16[512,128]{1,0:T(8,128)(2,1)S(1)} %fusion), channel_id=1, source_target_pairs={{0,4},{4,0},{8,12},{12,8},{16,20},{20,16},{24,28},{28,24},{1,5},{5... | collective-permute-start | bytes 393224 | tf_op jit(solution)/shard_map/down_seq0/ppermute | solution.py:47
  52.0 0.9 %copy-start.5 = (f32[8,64,128]{2,1,0:T(8,128)S(1)}, f32[8,64,128]{2,1,0:T(8,128)}, u32[]{:S(2)}) copy-start(f32[8,64,128]{2,1,0:T(8,128)} %param.13) | copy-start | bytes 786436

commit v3 on v2

--- a/solution.py
+++ b/solution.py
@@ -7,6 +7,7 @@
 from jax.experimental.pallas import tpu as pltpu
 from jax.sharding import PartitionSpec as P
 
+
 F32 = jnp.float32
 BF16 = jnp.bfloat16
 LANES = 128
@@ -27,7 +28,7 @@
     return lax.dot_general(a, b, (((0,), (0,)), ((), ())), preferred_element_type=F32)
 
 
-def call(kernel, outs, specs, flops, name, **kwargs):
+def call(kernel, outs, specs, flops, **kwargs):
     size = sum(o.size * o.dtype.itemsize for o in outs)
     return pl.pallas_call(
         kernel,
@@ -35,23 +36,20 @@
         in_specs=specs,
         compiler_params=pltpu.CompilerParams(vmem_limit_bytes=16 << 20),
         cost_estimate=pl.CostEstimate(flops=flops, bytes_accessed=2 * size, transcendentals=0),
-        name=name,
         **kwargs,
     )
 
 
-def swap(value, axis, bit, name):
+def swap(value, axis, bit):
     mask = 1 << bit
     pairs = [(source, source ^ mask) for source in range(lax.axis_size(axis))]
-    with jax.named_scope(f"{name}_{axis}{bit}"):
-        return lax.ppermute(value, axis, pairs)
-
-
-def front_kernel(dims, k_hbm, v_hbm, w_hbm, x_hbm, kv_ref, kvb_ref, p_ref, xt_ref,
-                 k_ref, v_ref, w_ref, x_ref, sems):
+    return lax.ppermute(value, axis, pairs)
+
+
+def state_kernel(dims, idx_ref, k_hbm, v_hbm, w_hbm, x_hbm, kv_ref, kvb_ref, w_ref, x_ref, k_ref, v_ref, sems):
     nh, dk, dv = dims
     copies = [pltpu.make_async_copy(src, dst, sems.at[n]) for n, (src, dst) in enumerate(
-        ((k_hbm, k_ref), (v_hbm, v_ref), (x_hbm, x_ref), (w_hbm, w_ref)))]
+        ((k_hbm, k_ref), (v_hbm, v_ref), (w_hbm, w_ref), (x_hbm, x_ref)))]
     for copy in copies:
         copy.start()
     copies[0].wait()
@@ -64,10 +62,29 @@
             kv_ref[h * dk:(h + 1) * dk, :] = kv
             kvb_ref[h * dk:(h + 1) * dk, :] = kv.astype(BF16)
     copies[2].wait()
+    copies[3].wait()
+
+
+def part_ways(entries, upper, send_ref, keep_ref, inner):
+    n = entries.shape[0] // inner
+    for e in range(n // 2):
+        low = entries[2 * e * inner:(2 * e + 1) * inner]
+        high = entries[(2 * e + 1) * inner:(2 * e + 2) * inner]
+        out = slice(e * inner, (e + 1) * inner)
+        send_ref[out, :] = jnp.where(upper, low, high).astype(BF16)
+        keep_ref[out, :] = jnp.where(upper, high, low)
+
+
+def project_kernel(bit, idx_ref, w_ref, x_ref, send_ref, keep_ref, xt_ref):
     xt = x_ref[...].T
     xt_ref[...] = xt
-    copies[3].wait()
-    p_ref[...] = tn(w_ref[...], xt)
+    upper = ((idx_ref[1] >> bit) & 1) == 1
+    part_ways(tn(w_ref[...], xt), upper, send_ref, keep_ref, keep_ref.shape[0])
+
+
+def fold_kernel(bit, axis, inner, idx_ref, keep_in, got_ref, send_ref, keep_ref):
+    upper = ((idx_ref[axis] >> bit) & 1) == 1
+    part_ways(keep_in[...] + got_ref[...].astype(F32), upper, send_ref, keep_ref, inner)
 
 
 def weight_kernel(dims, levels, first, count, keep_ref, got_ref, gl_ref, q_ref, g_ref,
@@ -133,7 +150,7 @@
 
 
 def level_kernel(dims, levels, k_ref, q_ref, v_ref, g_ref, gl_ref):
-    nh, dk, dv = dims
+    _, dk, dv = dims
     kp = k_ref[...]
     qt = q_ref[...].T
     zero = jnp.zeros_like(qt[:dk])
@@ -154,7 +171,7 @@
 
 
 def local_kernel(dims, levels, k_ref, q_ref, v_ref, g_ref, lw_ref, out_ref, dq_ref, dk_ref, dv_ref):
-    nh, dk, dv = dims
+    _, dk, dv = dims
     kp, qp = k_ref[...], q_ref[...]
     kt, qt = kp.T, qp.T
     zero = jnp.zeros_like(qt[:dk])
@@ -197,6 +214,7 @@
     ups = refs[:count]
     g_ref, qt_ref, sig_ref, far_ref = refs[count:]
     index = idx_ref[0]
+    far_ref[...] = jnp.zeros_like(far_ref)
     for m in range(count):
         up = ((index >> m) & 1).astype(F32)
         found = []
@@ -245,19 +263,21 @@
         out_ref[:, h * dv:(h + 1) * dv] = total.T.astype(BF16)
 
 
-def wgrad_kernel(xt_ref, gp_ref, dw_ref):
-    dw_ref[...] = nt(xt_ref[...], gp_ref[...])
-
-
-def merge_kernel(half, idx_ref, near_ref, far_ref, place_ref, send_ref, keep_ref):
-    total = near_ref[...] + lax.dot_general(
-        far_ref[...], place_ref[...], (((1,), (0,)), ((), ())),
+def wgrad_kernel(bits, inner, idx_ref, xt_ref, gp_ref, send_ref, keep_ref, sorted_ref):
+    count = 1 << bits
+    own = gp_ref.shape[0] // count
+    for n in range(count):
+        away = sum(((n >> k) & 1) << (bits - 1 - k) for k in range(bits))
+        at = pl.multiple_of((idx_ref[1] ^ away) * own, 16)
+        sorted_ref[pl.ds(at, own), :] = gp_ref[n * own:(n + 1) * own, :]
+    part_ways(nt(xt_ref[...], sorted_ref[...]), (idx_ref[0] & 1) == 1, send_ref, keep_ref, inner)
+
+
+def merge_kernel(bit, idx_ref, near_ref, near_got, far_ref, far_got, place_ref, send_ref, keep_ref):
+    total = near_ref[...] + near_got[...].astype(F32) + lax.dot_general(
+        far_ref[...] + far_got[...].astype(F32), place_ref[...], (((1,), (0,)), ((), ())),
         preferred_element_type=F32, precision=lax.Precision.HIGHEST)
-    upper = ((idx_ref[0] >> half) & 1) == 1
-    n = total.shape[0] // 2
-    low, high = total[:n], total[n:]
-    keep_ref[...] = jnp.where(upper, high, low)
-    send_ref[...] = jnp.where(upper, low, high).astype(BF16)
+    part_ways(total, ((idx_ref[0] >> bit) & 1) == 1, send_ref, keep_ref, keep_ref.shape[0])
 
 
 def hidden_kernel(near_ref, far_ref, place_ref, w_ref, dx_ref):
@@ -283,12 +303,27 @@
         send_ref[...] = total.astype(BF16)
 
 
-def final_kernel(dims, adj_ref, ds_ref, k_ref, v_ref, low_k, high_k, low_v, high_v, dk_ref, dv_ref):
-    nh, dk, dv = dims
+def pend_kernel(bit, top, idx_ref, *refs):
+    gots, (gu_ref, send_ref) = refs[:-2], refs[-2:]
+    index = idx_ref[0]
+    total = jnp.where(((index >> top) & 1) == 1, 0.0, gots[0][...].astype(F32))
+    for got in gots[1:]:
+        total = total + got[...].astype(F32)
+    send_ref[...] = (total + jnp.where(((index >> bit) & 1) == 1, gu_ref[bit].astype(F32), 0.0)).astype(BF16)
+
+
+def final_kernel(dims, top, idx_ref, *refs):
+    nh, dk, dv = dims
+    gots = refs[:top + 1]
+    ds_ref, k_ref, v_ref, low_k, high_k, low_v, high_v, dk_ref, dv_ref = refs[top + 1:]
+    upper = ((idx_ref[0] >> top) & 1) == 1
     zero = jnp.zeros((dk, dv), BF16)
     for pair in range(nh // 2):
-        adj = [(adj_ref[h * dk:(h + 1) * dk, :] + ds_ref[h * dk:(h + 1) * dk, :]).astype(BF16)
-               for h in (2 * pair, 2 * pair + 1)]
+        pair_rows = slice(pair * 2 * dk, (pair + 1) * 2 * dk)
+        total = ds_ref[pair_rows, :] + jnp.where(upper, 0.0, gots[0][pair_rows, :].astype(F32))
+        for got in gots[1:]:
+            total = total + got[pair_rows, :].astype(F32)
+        adj = [total[:dk].astype(BF16), total[dk:].astype(BF16)]
         kp = k_ref[:, pair * 2 * dk:(pair + 1) * 2 * dk]
         dkl_ref, dvl_ref, p = (low_k, low_v, pair) if pair < nh // 4 else (high_k, high_v, pair - nh // 4)
         total = dkl_ref[:, p * 2 * dk:(p + 1) * 2 * dk]
@@ -302,24 +337,11 @@
         dk_ref[:, pair * 2 * dk:(pair + 1) * 2 * dk] = total.astype(BF16)
 
 
-def gather_heads(value, hi, head_bits, name):
-    full = value[None]
+def gather_heads(value, head_bits):
+    full = value
     for bit in reversed(range(head_bits)):
-        other = swap(full, "head", bit, name)
-        mine = (hi >> bit) & 1
-        full = jnp.where(mine == 0, jnp.stack([full, other]), jnp.stack([other, full]))
-        full = full.reshape((-1,) + full.shape[2:]) if bit == head_bits - 1 else full
-    full = full.reshape((2,) * head_bits + value.shape)
-    full = full.transpose(tuple(reversed(range(head_bits))) + (head_bits, head_bits + 1))
-    return full.reshape((-1,) + value.shape[1:])
-
-
-def halve(keep, si, bit, name):
-    pair = keep.reshape(keep.shape[0] // 2, 2, *keep.shape[1:])
-    mine = (si >> bit) & 1
-    send = lax.dynamic_index_in_dim(pair, 1 - mine, 1, keepdims=False).astype(BF16)
-    got = swap(send, "seq", bit, name)
-    return lax.dynamic_index_in_dim(pair, mine, 1, keepdims=False) + got.astype(F32)
+        full = jnp.concatenate([full, swap(full, "head", bit)], axis=0)
+    return full
 
 
 def body(hidden, w, queries, keys, values, d_out, d_state):
@@ -328,95 +350,100 @@
     nh, dk, dv = dims
     n_seq, n_head = lax.axis_size("seq"), lax.axis_size("head")
     seq_bits, head_bits = n_seq.bit_length() - 1, n_head.bit_length() - 1
+    top = seq_bits - 1
     cols = w.shape[1]
     levels = cols // (nh * n_head)
     own = nh * levels
     far = nh * seq_bits
+    far_own = -(-far // 16) * 16
+    far_cols = far_own * n_head
     first = tokens.bit_length()
-    si, hi = lax.axis_index("seq"), lax.axis_index("head")
-    idx = jnp.reshape(si, (1,)).astype(jnp.int32)
+    per = width // n_seq
+    rows = nh * dk
     S = jax.ShapeDtypeStruct
-    rows = nh * dk
+    idx = jnp.stack([lax.axis_index("seq"), lax.axis_index("head")]).astype(jnp.int32)
 
     hbm = pl.BlockSpec(memory_space=pltpu.HBM)
-    kv, kvb, partial, xt = call(
-        functools.partial(front_kernel, dims),
-        [S((rows, dv), F32), S((rows, dv), BF16), S((cols, tokens), F32), S((width, tokens), BF16)],
-        [hbm] * 4, 2 * tokens * (rows * dv + width * cols), "front",
+    kv, kvb, w_near, x_near = call(
+        functools.partial(state_kernel, dims),
+        [S((rows, dv), F32), S((rows, dv), BF16), S(w.shape, BF16), S(hidden.shape, BF16)],
+        [SM] + [hbm] * 4, 2 * tokens * rows * dv,
         scratch_shapes=[pltpu.VMEM((tokens, rows), BF16), pltpu.VMEM((tokens, nh * dv), BF16),
-                        pltpu.VMEM((width, cols), BF16), pltpu.VMEM((tokens, width), BF16),
                         pltpu.SemaphoreType.DMA((4,))])(
-                            *[pltpu.with_memory_space_constraint(a, pltpu.HBM) for a in (keys, values, w, hidden)])
-
-    top = seq_bits - 1
-    total, send = kv, kvb
+                            idx, *[pltpu.with_memory_space_constraint(a, pltpu.HBM) for a in (keys, values, w, hidden)])
+    send, keep, xt = call(
+        functools.partial(project_kernel, head_bits - 1),
+        [S((cols // 2, tokens), BF16), S((cols // 2, tokens), F32), S((width, tokens), BF16)], [SM] + [VM] * 2,
+        2 * tokens * width * cols)(idx, w_near, x_near)
+
+    total, up = kv, kvb
     ups = []
     for bit in range(top):
-        partner = swap(send, "seq", bit, "up")
+        partner = swap(up, "seq", bit)
         ups.append(partner)
         if bit < top - 1:
             total = total + partner.astype(F32)
-            send = total.astype(BF16)
-
-    keep = partial
-    got = None
-    for bit in reversed(range(head_bits)):
-        pair = keep.reshape(2, keep.shape[0] // 2, tokens)
-        mine = (hi >> bit) & 1
-        send = lax.dynamic_index_in_dim(pair, 1 - mine, 0, keepdims=False).astype(BF16)
-        keep = lax.dynamic_index_in_dim(pair, mine, 0, keepdims=False)
-        got = swap(send, "head", bit, "proj")
-        if bit:
-            keep = keep + got.astype(F32)
+            up = total.astype(BF16)
+
+    got = swap(send, "head", head_bits - 1)
+    for bit in reversed(range(head_bits - 1)):
+        n = keep.shape[0] // 2
+        send, keep = call(
+            functools.partial(fold_kernel, bit, 1, n), [S((n, tokens), BF16), S((n, tokens), F32)],
+            [SM] + [VM] * 2, n * tokens)(idx, keep, got)
+        got = swap(send, "head", bit)
 
     pair_spec = lambda n: pl.BlockSpec((tokens, n), lambda p: (0, p))
     row_spec = lambda n: pl.BlockSpec((n, tokens), lambda p: (p, 0))
     gl = call(
         functools.partial(level_kernel, dims, levels), [S((own, tokens), F32)],
         [pair_spec(2 * dk), pair_spec(2 * dk), pair_spec(2 * dv), pair_spec(2 * dv)],
-        2 * tokens * tokens * nh * (dk + dv), "near_levels", grid=(nh // 2,),
+        2 * tokens * tokens * nh * (dk + dv), grid=(nh // 2,),
         out_specs=[row_spec(2 * levels)])(keys, queries, values, d_out)[0]
     sig, lw, near, qt, gu = call(
         functools.partial(weight_kernel, dims, levels, first, seq_bits),
         [S((own, tokens), F32), S((own, tokens), F32), S((own, tokens), BF16), S((rows, tokens), BF16),
          S((seq_bits, rows, dv), BF16)],
-        [VM] * 5, 2 * tokens * rows * dv * seq_bits, "level_weights")(keep, got, gl, queries, d_out)
-
-    send = call(functools.partial(join_kernel, top, top), [S((rows, dv), BF16)], [SM] + [VM] * (top + 2),
-                rows * dv, "join")(idx, kv, *ups, gu)[0]
-    partner = swap(send, "seq", top, "up")
+        [VM] * 5, 2 * tokens * rows * dv * seq_bits)(keep, got, gl, queries, d_out)
+
+    up = call(functools.partial(join_kernel, top, top), [S((rows, dv), BF16)], [SM] + [VM] * (top + 2),
+              rows * dv)(idx, kv, *ups, gu)[0]
+    partner = swap(up, "seq", top)
     ups.append(partner)
     far_rows = call(
-        functools.partial(carry_kernel, dims, levels, first, seq_bits), [S((far, tokens), BF16)],
-        [SM] + [VM] * (seq_bits + 3), 2 * tokens * rows * dv * seq_bits, "carry")(idx, *ups, d_out, qt, sig)[0]
-    upper_top = ((si >> top) & 1) == 1
-    adjoint = jnp.where(upper_top, 0.0, partner.astype(F32))
+        functools.partial(carry_kernel, dims, levels, first, seq_bits), [S((far_own, tokens), BF16)],
+        [SM] + [VM] * (seq_bits + 3), 2 * tokens * rows * dv * seq_bits)(idx, *ups, d_out, qt, sig)[0]
+    gots = [partner]
     for bit in reversed(range(top)):
-        pending = adjoint + jnp.where(((si >> bit) & 1) == 1, gu[bit].astype(F32), 0.0)
-        adjoint = adjoint + swap(pending.astype(BF16), "seq", bit, "down").astype(F32)
-
-    per = width // n_seq
-    near_all = gather_heads(near, hi, head_bits, "near")
-    near_w = call(wgrad_kernel, [S((width, cols), F32)], [VM, VM], 2 * tokens * width * cols, "near_wgrad")(
-        xt, near_all)[0].reshape(n_seq, per, cols)
-    for bit in range(top):
-        near_w = halve(near_w, si, bit, "near")
-
-    far_all = gather_heads(far_rows, hi, head_bits, "far")
-    far_cols = far * n_head
-    far_w = call(wgrad_kernel, [S((width, far_cols), F32)], [VM, VM], 2 * tokens * width * far_cols, "far_wgrad")(
-        xt, far_all)[0].reshape(n_seq, per, far_cols)
-    for bit in range(top):
-        far_w = halve(far_w, si, bit, "far")
+        down = call(functools.partial(pend_kernel, bit, top), [S((rows, dv), BF16)], [SM] + [VM] * (len(gots) + 1),
+                    rows * dv)(idx, *gots, gu)[0]
+        gots.append(swap(down, "seq", bit))
+
+    def reduce(gathered, n_cols):
+        send, keep, ordered = call(
+            functools.partial(wgrad_kernel, head_bits, per),
+            [S((width // 2, n_cols), BF16), S((width // 2, n_cols), F32), S((n_cols, tokens), BF16)],
+            [SM] + [VM] * 2, 2 * tokens * width * n_cols)(idx, xt, gathered)
+        got = swap(send, "seq", 0)
+        for bit in range(1, top):
+            n = keep.shape[0] // 2
+            send, keep = call(
+                functools.partial(fold_kernel, bit, 0, per), [S((n, n_cols), BF16), S((n, n_cols), F32)],
+                [SM] + [VM] * 2, n * n_cols)(idx, keep, got)
+            got = swap(send, "seq", bit)
+        return keep, got, ordered
+
+    near_w, near_got, near_all = reduce(gather_heads(near, head_bits), cols)
+    far_w, far_got, far_all = reduce(gather_heads(far_rows, head_bits), far_cols)
     col = jnp.arange(cols, dtype=jnp.int32)[None, :]
     row = jnp.arange(far_cols, dtype=jnp.int32)[:, None]
-    at = (row // far * nh + row % nh) * levels + first + row % far // nh
-    place = (at == col).astype(F32)
+    within = row % far_own
+    at = (row // far_own * nh + within % nh) * levels + first + within // nh
+    place = ((at == col) & (within < far)).astype(F32)
     send, keep = call(
-        functools.partial(merge_kernel, top), [S((per, cols), BF16), S((per, cols), F32)], [SM] + [VM] * 3,
-        4 * per * far_cols * cols, "merge")(
-            idx, near_w.reshape(2 * per, cols), far_w.reshape(2 * per, far_cols), place)
-    d_w = keep + swap(send, "seq", top, "last").astype(F32)
+        functools.partial(merge_kernel, top), [S((per, cols), BF16), S((per, cols), F32)], [SM] + [VM] * 5,
+        4 * per * far_cols * cols)(idx, near_w, near_got, far_w, far_got, place)
+    d_w = keep + swap(send, "seq", top).astype(F32)
 
     half = nh // 4
     local = []
@@ -429,23 +456,22 @@
              S((tokens, nh * dv // 2), F32)],
             [at_col(2 * dk), at_col(2 * dk), at_col(2 * dv), at_col(2 * dv),
              pl.BlockSpec((2 * levels, tokens), lambda p, shift=shift: (p + shift, 0))],
-            tokens * tokens * nh * (3 * dk + 3 * dv), "local", grid=(half,),
+            tokens * tokens * nh * (3 * dk + 3 * dv), grid=(half,),
             out_specs=[row_spec(2 * dv), row_spec(2 * dk), pair_spec(2 * dk), pair_spec(2 * dv)],
         )(keys, queries, values, d_out, lw))
     out_l, dq_l, dk_l, dv_l = [(local[0][n], local[1][n]) for n in range(4)]
     d_queries = call(
         functools.partial(query_kernel, dims, levels, first, seq_bits), [S((tokens, rows), BF16)],
-        [SM] + [VM] * (seq_bits + 4), 2 * tokens * rows * dv * seq_bits, "queries")(idx, *ups, d_out, lw, *dq_l)[0]
+        [SM] + [VM] * (seq_bits + 4), 2 * tokens * rows * dv * seq_bits)(idx, *ups, d_out, lw, *dq_l)[0]
     out = call(
         functools.partial(out_kernel, dims, levels, first, seq_bits),
         [S((tokens, nh * dv), BF16)],
-        [SM] + [VM] * (seq_bits + 4), 2 * tokens * rows * dv * seq_bits, "out")(idx, *ups, qt, lw, *out_l)[0]
-    d_hidden = call(hidden_kernel, [S((tokens, width), BF16)], [VM] * 4, 2 * tokens * width * cols, "hgrad")(
-        near_all, far_all, place, w)[0]
+        [SM] + [VM] * (seq_bits + 4), 2 * tokens * rows * dv * seq_bits)(idx, *ups, qt, lw, *out_l)[0]
+    d_hidden = call(hidden_kernel, [S((tokens, width), BF16)], [VM] * 4, 2 * tokens * width * cols)(
+        near_all, far_all, place, w_near)[0]
     d_keys, d_values = call(
-        functools.partial(final_kernel, dims),
-        [S((tokens, rows), BF16), S((tokens, nh * dv), BF16)], [VM] * 8, 4 * tokens * rows * dv, "final")(
-            adjoint, d_state.reshape(rows, dv), keys, values, *dk_l, *dv_l)
+        functools.partial(final_kernel, dims, top),
+        [S((tokens, rows), BF16), S((tokens, nh * dv), BF16)], [SM] + [VM] * (top + 8), 4 * tokens * rows * dv)(idx, *gots, d_state.reshape(rows, dv), keys, values, *dk_l, *dv_l)
     return (out, d_queries, d_keys, d_values, d_hidden, d_w)
 
 

time: 54.5 us -> 63.3 us (1.16)
  Pallas kernels: 14.8 us -> 23.1 us
  starting transfers between devices: 18.4 us -> 21.6 us
  waiting for transfers between devices: 18.7 us -> 16.6 us
    pallas_call x4 -> x10, Pallas kernels: 3.81 us -> 9.35 us  [the longest x1 1.97 us: body(): call(functools.partial(state_kernel, dims), [S((rows, dv), F32), S((rows,...]
    ppermute x16, starting transfers between devices: 18.4 us -> 21.6 us  [swap(): return lax.ppermute(value, axis, pairs)]
    ppermute x16, waiting for transfers between devices: 18.7 us -> 16.6 us  [swap(): return lax.ppermute(value, axis, pairs)]
  transfers between devices with their start and end apart: 16 -> 16, of which waited for: 8 -> 8; matrix products, arithmetic and copies ran while one was open for 2% -> 1% of each run, Pallas kernels for 20% -> 30%
where the time goes in v3:
time: 63.3 us; the launch traced here: 63.1 us
  Pallas kernels  23.1 us (36%)
  starting transfers between devices  21.6 us (34%)
  waiting for transfers between devices  16.6 us (26%)
  other arithmetic  0.9 us (1%)
  between operations  0.87 us (1%)
    ppermute x16, starting transfers between devices, swap(): return lax.ppermute(value, axis, pairs)  21.6 us
    ppermute x16, waiting for transfers between devices, swap(): return lax.ppermute(value, axis, pairs)  16.6 us
    pallas_call x2, Pallas kernels, body(): call(functools.partial(local_kernel, dims, levels), [S((nh * dv // 2, tok...  3.67 us
    pallas_call x1, Pallas kernels, body(): call(functools.partial(out_kernel, dims, levels, first, seq_bits), [S((to...  2.03 us
    pallas_call x1, Pallas kernels, body(): call(functools.partial(query_kernel, dims, levels, first, seq_bits), [S((...  1.99 us
    pallas_call x1, Pallas kernels, body(): call(functools.partial(state_kernel, dims), [S((rows, dv), F32), S((rows,...  1.97 us
    pallas_call x1, Pallas kernels, body(): call(functools.partial(final_kernel, dims, top), [S((tokens, rows), BF16)...  1.88 us
    pallas_call x1, Pallas kernels, body(): call(functools.partial(level_kernel, dims, levels), [S((own, tokens), F32...  1.72 us
  transfers between devices with their start and end apart: 16, of which 8 were waited for; matrix products, arithmetic and copies ran while one was open for 1% of the time, Pallas kernels for 30%

profile of v3, /device:TPU:0, one launch (start us, length us, event | category | flops | bytes accessed | tf_op | source)
XLA Modules:
  0.0 63.1 jit_solution(6251116642507176497)
XLA Ops:
  0.6 0.1 pad_add_fusion.idx_ref
  0.7 0.0 copy-start.3
  0.7 2.0 %shard_map.118 = (f32[512,128]{1,0:T(8,128)S(1)}, bf16[512,128]{1,0:T(8,128)(2,1)S(1)}, bf16[512,384]{1,0:T(8,128)(2,1)S(1)}, bf16[256,512]{1,0:T(8,128)(2,1)S(1)}) custom-call(s32[2]{0:T(128)S(1)} %pad_add_fusion.idx_ref, bf16[256,512]{1,0:T(8,128)(2,1)} %refs_4_.1, bf16[256,1024]{1,0:T(8,128)(2,1)} %refs_5_.1, bf16[512,384]{1,0:T(8,128)(2,1)} %w_hbm.1, ...), custom_call_target="tpu_custom_call" | custom-call | flops 33554432 | bytes 2097152 | tf_op jit(solution)/shard_map/pallas_call | solution.py:367
  2.7 3.1 %collective-permute-start = (bf16[512,128]{1,0:T(8,128)(2,1)S(1)}, bf16[512,128]{1,0:T(8,128)(2,1)S(1)}, u32[]{:S(2)}, u32[]{:S(2)}) collective-permute-start(bf16[512,128]{1,0:T(8,128)(2,1)S(1)} %get-tuple-element.42), channel_id=1, source_target_pairs={{0,4},{4,0},{8,12},{12,8},{16,20},{20,16},{24,28},{28,24},{1,5},{5... | collective-permute-start | bytes 393224 | tf_op jit(solution)/shard_map/ppermute | solution.py:46
  5.8 0.0 copy-start.1
  5.8 0.9 %shard_map.119 = (bf16[192,256]{1,0:T(8,128)(2,1)S(1)}, f32[192,256]{1,0:T(8,128)S(1)}, bf16[512,256]{1,0:T(8,128)(2,1)S(1)}) custom-call(s32[2]{0:T(128)S(1)} %pad_add_fusion.idx_ref, bf16[512,384]{1,0:T(8,128)(2,1)S(1)} %get-tuple-element.44.w_ref, bf16[256,512]{1,0:T(8,128)(2,1)S(1)} %get-tuple-element.45.x_ref), custom_call_target="tpu_custom_call" | custom-call | flops 100663296 | bytes 1114112 | tf_op jit(solution)/shard_map/pallas_call | solution.py:374
  6.7 0.0 copy-start
  6.7 1.6 %collective-permute-start.2 = (bf16[192,256]{1,0:T(8,128)(2,1)S(1)}, bf16[192,256]{1,0:T(8,128)(2,1)S(1)}, u32[]{:S(2)}, u32[]{:S(2)}) collective-permute-start(bf16[192,256]{1,0:T(8,128)(2,1)S(1)} %get-tuple-element.47), channel_id=1, source_target_pairs={{0,2},{1,3},{2,0},{3,1},{4,6},{5,7},{6,4},{7,5},{8,10},{9,11},{10,... | collective-permute-start | bytes 294920 | tf_op jit(solution)/shard_map/ppermute | solution.py:46
  8.2 1.0 %collective-permute-done.refs_0_ = bf16[512,128]{1,0:T(8,128)(2,1)S(1)} collective-permute-done((bf16[512,128]{1,0:T(8,128)(2,1)S(1)}, bf16[512,128]{1,0:T(8,128)(2,1)S(1)}, u32[]{:S(2)}, u32[]{:S(2)}) %collective-permute-start) | collective-permute-done | bytes 131104 | tf_op jit(solution)/shard_map/ppermute | solution.py:46
  9.3 0.0 copy-start.2
  9.3 1.9 %collective-permute-start.1 = (bf16[512,128]{1,0:T(8,128)(2,1)S(1)}, bf16[512,128]{1,0:T(8,128)(2,1)S(1)}, u32[]{:S(2)}, u32[]{:S(2)}) collective-permute-start(bf16[512,128]{1,0:T(8,128)(2,1)S(1)} %add_convert_fusion), channel_id=1, source_target_pairs={{0,8},{4,12},{8,0},{12,4},{16,24},{20,28},{24,16},{28,20},{1,9},{5... | collective-permute-start | bytes 393224 | tf_op jit(solution)/shard_map/ppermute | solution.py:46
  11.2 0.2 collective-permute-done.2.got_ref
  11.4 0.6 shard_map.120
  11.9 0.1 collective-permute-start.3
  12.0 0.0 copy-done.3
  12.0 0.0 copy-done.1
  12.0 0.0 copy-done
  12.1 0.0 copy-done.2
  12.1 1.7 %shard_map.121.gl_ref = f32[96,256]{1,0:T(8,128)S(1)} custom-call(bf16[256,512]{1,0:T(8,128)(2,1)S(1)} %copy-done.2, bf16[256,512]{1,0:T(8,128)(2,1)S(1)} %copy-done.3, bf16[256,1024]{1,0:T(8,128)(2,1)S(1)} %copy-done.1, bf16[256,1024]{1,0:T(8,128)(2,1)S(1)} %copy-done), custom_call_target="tpu_custom_call" | custom-call | flops 201326592 | bytes 196608 | tf_op jit(solution)/shard_map/pallas_call | solution.py:398
  13.8 0.0 collective-permute-done.3.got_ref
  13.8 0.4 shard_map.122
  14.2 0.1 collective-permute-done.1.refs_1_
  14.3 0.6 shard_map.123
  14.9 2.8 %collective-permute-start.4 = (bf16[512,128]{1,0:T(8,128)(2,1)S(1)}, bf16[512,128]{1,0:T(8,128)(2,1)S(1)}, u32[]{:S(2)}, u32[]{:S(2)}) collective-permute-start(bf16[512,128]{1,0:T(8,128)(2,1)S(1)} %shard_map.123), channel_id=1, source_target_pairs={{0,16},{4,20},{8,24},{12,28},{16,0},{20,4},{24,8},{28,12},{1,17},{... | collective-permute-start | bytes 393224 | tf_op jit(solution)/shard_map/ppermute | solution.py:46
  17.8 1.5 %collective-permute-start.7 = (bf16[96,256]{1,0:T(8,128)(2,1)S(1)}, bf16[96,256]{1,0:T(8,128)(2,1)S(1)}, u32[]{:S(2)}, u32[]{:S(2)}) collective-permute-start(bf16[96,256]{1,0:T(8,128)(2,1)S(1)} %get-tuple-element.64), channel_id=1, source_target_pairs={{0,2},{1,3},{2,0},{3,1},{4,6},{5,7},{6,4},{7,5},{8,10},{9,11},{10,... | collective-permute-start | bytes 147464 | tf_op jit(solution)/shard_map/ppermute | solution.py:46
  19.3 5.2 %collective-permute-done.4.refs_2_.refs_0_ = bf16[512,128]{1,0:T(8,128)(2,1)S(1)} collective-permute-done((bf16[512,128]{1,0:T(8,128)(2,1)S(1)}, bf16[512,128]{1,0:T(8,128)(2,1)S(1)}, u32[]{:S(2)}, u32[]{:S(2)}) %collective-permute-start.4) | collective-permute-done | bytes 131104 | tf_op jit(solution)/shard_map/ppermute | solution.py:46
  24.5 1.2 %shard_map.132 = bf16[32,256]{1,0:T(8,128)(2,1)S(1)} custom-call(s32[2]{0:T(128)S(1)} %pad_add_fusion.idx_ref, bf16[512,128]{1,0:T(8,128)(2,1)S(1)} %collective-permute-done.refs_0_, bf16[512,128]{1,0:T(8,128)(2,1)S(1)} %collective-permute-done.1.refs_1_, bf16[512,128]{1,0:T(8,128)(2,1)S(1)} %collective-permute-done.4.refs_2_.refs_0_, ...), custom_call_target="tpu_custom_call" | custom-call | flops 100663296 | bytes 32768 | tf_op jit(solution)/shard_map/pallas_call | solution.py:413
  25.7 1.6 %collective-permute-start.9 = (bf16[32,256]{1,0:T(8,128)(2,1)S(1)}, bf16[32,256]{1,0:T(8,128)(2,1)S(1)}, u32[]{:S(2)}, u32[]{:S(2)}) collective-permute-start(bf16[32,256]{1,0:T(8,128)(2,1)S(1)} %shard_map.132), channel_id=1, source_target_pairs={{0,2},{1,3},{2,0},{3,1},{4,6},{5,7},{6,4},{7,5},{8,10},{9,11},{10,... | collective-permute-start | bytes 49160 | tf_op jit(solution)/shard_map/ppermute | solution.py:46
  27.3 0.0 collective-permute-done.7
  27.3 0.1 collective-permute-start.8
  27.4 2.2 %collective-permute-done.9 = bf16[32,256]{1,0:T(8,128)(2,1)S(1)} collective-permute-done((bf16[32,256]{1,0:T(8,128)(2,1)S(1)}, bf16[32,256]{1,0:T(8,128)(2,1)S(1)}, u32[]{:S(2)}, u32[]{:S(2)}) %collective-permute-start.9) | collective-permute-done | bytes 16416 | tf_op jit(solution)/shard_map/ppermute | solution.py:46
  29.5 0.0 collective-permute-start.10
  29.5 0.0 collective-permute-done.8
  29.6 0.9 %shard_map.131 = (bf16[256,384]{1,0:T(8,128)(2,1)S(1)}, f32[256,384]{1,0:T(8,128)S(1)}, bf16[384,256]{1,0:T(8,128)(2,1)S(1)}) custom-call(s32[2]{0:T(128)S(1)} %pad_add_fusion.idx_ref, bf16[512,256]{1,0:T(8,128)(2,1)S(1)} %get-tuple-element.63.xt_ref, bf16[384,256]{1,0:T(8,128)(2,1)S(1)} %pad_maximum_fusion.gp_ref), custom_call_target="tpu_custom_call" | custom-call | flops 100663296 | bytes 1572864 | tf_op jit(solution)/shard_map/pallas_call | solution.py:423
  30.4 1.4 %collective-permute-start.11 = (bf16[256,384]{1,0:T(8,128)(2,1)S(1)}, bf16[256,384]{1,0:T(8,128)(2,1)S(1)}, u32[]{:S(2)}, u32[]{:S(2)}) collective-permute-start(bf16[256,384]{1,0:T(8,128)(2,1)S(1)} %get-tuple-element.69), channel_id=1, source_target_pairs={{0,4},{4,0},{8,12},{12,8},{16,20},{20,16},{24,28},{28,24},{1,5},{5... | collective-permute-start | bytes 589832 | tf_op jit(solution)/shard_map/ppermute | solution.py:46
  31.8 0.0 collective-permute-done.10
  31.8 0.8 %shard_map.133 = (bf16[256,128]{1,0:T(8,128)(2,1)S(1)}, f32[256,128]{1,0:T(8,128)S(1)}, bf16[128,256]{1,0:T(8,128)(2,1)S(1)}) custom-call(s32[2]{0:T(128)S(1)} %pad_add_fusion.idx_ref, bf16[512,256]{1,0:T(8,128)(2,1)S(1)} %get-tuple-element.63.xt_ref, bf16[128,256]{1,0:T(8,128)(2,1)S(1)} %pad_maximum_fusion.2.gp_ref), custom_call_target="tpu_custom_call" | custom-call | flops 33554432 | bytes 524288 | tf_op jit(solution)/shard_map/pallas_call | solution.py:423
  32.6 0.8 %collective-permute-start.13 = (bf16[256,128]{1,0:T(8,128)(2,1)S(1)}, bf16[256,128]{1,0:T(8,128)(2,1)S(1)}, u32[]{:S(2)}, u32[]{:S(2)}) collective-permute-start(bf16[256,128]{1,0:T(8,128)(2,1)S(1)} %get-tuple-element.73), channel_id=1, source_target_pairs={{0,4},{4,0},{8,12},{12,8},{16,20},{20,16},{24,28},{28,24},{1,5},{5... | collective-permute-start | bytes 196616 | tf_op jit(solution)/shard_map/ppermute | solution.py:46
  33.4 0.6 shard_map.128
  34.0 0.7 %collective-permute-start.5 = (bf16[512,128]{1,0:T(8,128)(2,1)S(1)}, bf16[512,128]{1,0:T(8,128)(2,1)S(1)}, u32[]{:S(2)}, u32[]{:S(2)}) collective-permute-start(bf16[512,128]{1,0:T(8,128)(2,1)S(1)} %shard_map.128), channel_id=1, source_target_pairs={{0,8},{4,12},{8,0},{12,4},{16,24},{20,28},{24,16},{28,20},{1,9},{5... | collective-permute-start | bytes 393224 | tf_op jit(solution)/shard_map/ppermute | solution.py:46
  34.7 3.6 %collective-permute-done.11.got_ref = bf16[256,384]{1,0:T(8,128)(2,1)S(1)} collective-permute-done((bf16[256,384]{1,0:T(8,128)(2,1)S(1)}, bf16[256,384]{1,0:T(8,128)(2,1)S(1)}, u32[]{:S(2)}, u32[]{:S(2)}) %collective-permute-start.11) | collective-permute-done | bytes 196640 | tf_op jit(solution)/shard_map/ppermute | solution.py:46
  38.3 0.6 shard_map.135
  38.9 0.7 %collective-permute-start.12 = (bf16[128,384]{1,0:T(8,128)(2,1)S(1)}, bf16[128,384]{1,0:T(8,128)(2,1)S(1)}, u32[]{:S(2)}, u32[]{:S(2)}) collective-permute-start(bf16[128,384]{1,0:T(8,128)(2,1)S(1)} %get-tuple-element.71), channel_id=1, source_target_pairs={{0,8},{4,12},{8,0},{12,4},{16,24},{20,28},{24,16},{28,20},{1,9},{5... | collective-permute-start | bytes 294920 | tf_op jit(solution)/shard_map/ppermute | solution.py:46
  39.6 0.0 collective-permute-done.13.got_ref
  39.6 0.6 shard_map.136
  40.2 1.4 %collective-permute-start.14 = (bf16[128,128]{1,0:T(8,128)(2,1)S(1)}, bf16[128,128]{1,0:T(8,128)(2,1)S(1)}, u32[]{:S(2)}, u32[]{:S(2)}) collective-permute-start(bf16[128,128]{1,0:T(8,128)(2,1)S(1)} %get-tuple-element.75), channel_id=1, source_target_pairs={{0,8},{4,12},{8,0},{12,4},{16,24},{20,28},{24,16},{28,20},{1,9},{5... | collective-permute-start | bytes 98312 | tf_op jit(solution)/shard_map/ppermute | solution.py:46
  41.6 0.1 fusion.1.place_ref
  41.7 1.9 %shard_map.125 = (f32[512,256]{1,0:T(8,128)S(1)}, f32[256,256]{1,0:T(8,128)S(1)}, f32[256,256]{1,0:T(8,128)S(1)}, f32[256,512]{1,0:T(8,128)S(1)}) custom-call(bf16[256,512]{1,0:T(8,128)(2,1)S(1)} %copy-done.2, bf16[256,512]{1,0:T(8,128)(2,1)S(1)} %copy-done.3, bf16[256,1024]{1,0:T(8,128)(2,1)S(1)} %copy-done.1, bf16[256,1024]{1,0:T(8,128)(2,1)S(1)} %copy-done, ...), custom_call_target="tpu_custom_call" | custom-call | flops 301989888 | bytes 3145728 | tf_op jit(solution)/shard_map/pallas_call | solution.py:453
  43.6 0.6 collective-permute-done.14.far_got
  44.2 0.0 collective-permute-done.12.near_got
  44.2 0.9 %shard_map.137 = (bf16[64,384]{1,0:T(8,128)(2,1)S(1)}, f32[64,384]{1,0:T(8,128)S(1)}) custom-call(s32[2]{0:T(128)S(1)} %pad_add_fusion.idx_ref, f32[128,384]{1,0:T(8,128)S(1)} %get-tuple-element.70.near_ref, bf16[128,384]{1,0:T(8,128)(2,1)S(1)} %collective-permute-done.12.near_got, f32[128,128]{1,0:T(8,128)S(1)} %get-tuple-element.74.far_ref, ...), custom_call_target="tpu_custom_call" | custom-call | flops 12582912 | bytes 294912 | tf_op jit(solution)/shard_map/pallas_call | solution.py:443
  45.0 3.4 %collective-permute-start.15 = (bf16[64,384]{1,0:T(8,128)(2,1)S(1)}, bf16[64,384]{1,0:T(8,128)(2,1)S(1)}, u32[]{:S(2)}, u32[]{:S(2)}) collective-permute-start(bf16[64,384]{1,0:T(8,128)(2,1)S(1)} %get-tuple-element.77), channel_id=1, source_target_pairs={{0,16},{4,20},{8,24},{12,28},{16,0},{20,4},{24,8},{28,12},{1,17},{... | collective-permute-start | bytes 147464 | tf_op jit(solution)/shard_map/ppermute | solution.py:46
  48.5 1.8 %shard_map.124 = (f32[512,256]{1,0:T(8,128)S(1)}, f32[256,256]{1,0:T(8,128)S(1)}, f32[256,256]{1,0:T(8,128)S(1)}, f32[256,512]{1,0:T(8,128)S(1)}) custom-call(bf16[256,512]{1,0:T(8,128)(2,1)S(1)} %copy-done.2, bf16[256,512]{1,0:T(8,128)(2,1)S(1)} %copy-done.3, bf16[256,1024]{1,0:T(8,128)(2,1)S(1)} %copy-done.1, bf16[256,1024]{1,0:T(8,128)(2,1)S(1)} %copy-done, ...), custom_call_target="tpu_custom_call" | custom-call | flops 301989888 | bytes 3145728 | tf_op jit(solution)/shard_map/pallas_call | solution.py:453
  50.3 2.0 %shard_map.126 = bf16[256,1024]{1,0:T(8,128)(2,1)} custom-call(s32[2]{0:T(128)S(1)} %pad_add_fusion.idx_ref, bf16[512,128]{1,0:T(8,128)(2,1)S(1)} %collective-permute-done.refs_0_, bf16[512,128]{1,0:T(8,128)(2,1)S(1)} %collective-permute-done.1.refs_1_, bf16[512,128]{1,0:T(8,128)(2,1)S(1)} %collective-permute-done.4.refs_2_.refs_0_, ...), custom_call_target="tpu_custom_call" | custom-call | flops 100663296 | bytes 1048576 | tf_op jit(solution)/shard_map/pallas_call | solution.py:466
  52.3 2.0 %shard_map.127 = bf16[256,512]{1,0:T(8,128)(2,1)} custom-call(s32[2]{0:T(128)S(1)} %pad_add_fusion.idx_ref, bf16[512,128]{1,0:T(8,128)(2,1)S(1)} %collective-permute-done.refs_0_, bf16[512,128]{1,0:T(8,128)(2,1)S(1)} %collective-permute-done.1.refs_1_, bf16[512,128]{1,0:T(8,128)(2,1)S(1)} %collective-permute-done.4.refs_2_.refs_0_, ...), custom_call_target="tpu_custom_call" | custom-call | flops 100663296 | bytes 524288 | tf_op jit(solution)/shard_map/pallas_call | solution.py:463
  54.3 1.3 %shard_map.134 = bf16[256,512]{1,0:T(8,128)(2,1)} custom-call(bf16[384,256]{1,0:T(8,128)(2,1)S(1)} %get-tuple-element.65.near_ref, bf16[128,256]{1,0:T(8,128)(2,1)S(1)} %get-tuple-element.67.far_ref, f32[128,384]{1,0:T(8,128)S(1)} %fusion.1.place_ref, bf16[512,384]{1,0:T(8,128)(2,1)S(1)} %get-tuple-element.44.w_ref), custom_call_target="tpu_custom_call" | custom-call | flops 100663296 | bytes 524288 | tf_op jit(solution)/shard_map/pallas_call | solution.py:470
  55.6 0.0 collective-permute-done.5.refs_1_
  55.6 0.6 shard_map.129
  56.2 0.7 %collective-permute-start.6 = (bf16[512,128]{1,0:T(8,128)(2,1)S(1)}, bf16[512,128]{1,0:T(8,128)(2,1)S(1)}, u32[]{:S(2)}, u32[]{:S(2)}) collective-permute-start(bf16[512,128]{1,0:T(8,128)(2,1)S(1)} %shard_map.129), channel_id=1, source_target_pairs={{0,4},{4,0},{8,12},{12,8},{16,20},{20,16},{24,28},{28,24},{1,5},{5... | collective-permute-start | bytes 393224 | tf_op jit(solution)/shard_map/ppermute | solution.py:46
  56.9 0.0 collective-permute-done.15
  56.9 0.7 %convert_add_fusion = f32[64,384]{1,0:T(8,128)} fusion(f32[64,384]{1,0:T(8,128)S(1)} %get-tuple-element.76, bf16[64,384]{1,0:T(8,128)(2,1)S(1)} %collective-permute-done.15), kind=kLoop, calls=%fused_computation.6 | loop fusion | flops 49152 | bytes 245760 | tf_op jit(solution)/shard_map/add | solution.py:446
  57.5 3.7 %collective-permute-done.6.refs_2_ = bf16[512,128]{1,0:T(8,128)(2,1)S(1)} collective-permute-done((bf16[512,128]{1,0:T(8,128)(2,1)S(1)}, bf16[512,128]{1,0:T(8,128)(2,1)S(1)}, u32[]{:S(2)}, u32[]{:S(2)}) %collective-permute-start.6) | collective-permute-done | bytes 131104 | tf_op jit(solution)/shard_map/ppermute | solution.py:46
  61.2 0.0 copy-done.4
  61.2 1.9 %shard_map.130 = (bf16[256,512]{1,0:T(8,128)(2,1)}, bf16[256,1024]{1,0:T(8,128)(2,1)}) custom-call(s32[2]{0:T(128)S(1)} %pad_add_fusion.idx_ref, bf16[512,128]{1,0:T(8,128)(2,1)S(1)} %collective-permute-done.4.refs_2_.refs_0_, bf16[512,128]{1,0:T(8,128)(2,1)S(1)} %collective-permute-done.5.refs_1_, bf16[512,128]{1,0:T(8,128)(2,1)S(1)} %collective-permute-done.6.refs_2_, ...), custom_call_target="tpu_custom_call" | custom-call | flops 67108864 | bytes 1572864 | tf_op jit(solution)/shard_map/pallas_call | solution.py:472
  (8 shorter events, 0.1 us)
Async XLA Ops:
  0.7 11.3 %copy-start.3 = (bf16[256,512]{1,0:T(8,128)(2,1)S(1)}, bf16[256,512]{1,0:T(8,128)(2,1)}, u32[]{:S(2)}) copy-start(bf16[256,512]{1,0:T(8,128)(2,1)} %q_ref.7) | copy-start | bytes 786436
  2.7 6.6 %collective-permute-start = (bf16[512,128]{1,0:T(8,128)(2,1)S(1)}, bf16[512,128]{1,0:T(8,128)(2,1)S(1)}, u32[]{:S(2)}, u32[]{:S(2)}) collective-permute-start(bf16[512,128]{1,0:T(8,128)(2,1)S(1)} %get-tuple-element.42), channel_id=1, source_target_pairs={{0,4},{4,0},{8,12},{12,8},{16,20},{20,16},{24,28},{28,24},{1,5},{5... | collective-permute-start | bytes 393224 | tf_op jit(solution)/shard_map/ppermute | solution.py:46
  5.8 6.3 %copy-start.1 = (bf16[256,1024]{1,0:T(8,128)(2,1)S(1)}, bf16[256,1024]{1,0:T(8,128)(2,1)}, u32[]{:S(2)}) copy-start(bf16[256,1024]{1,0:T(8,128)(2,1)} %refs_5_.1) | copy-start | bytes 1572868
  6.7 5.4 %copy-start = (bf16[256,1024]{1,0:T(8,128)(2,1)S(1)}, bf16[256,1024]{1,0:T(8,128)(2,1)}, u32[]{:S(2)}) copy-start(bf16[256,1024]{1,0:T(8,128)(2,1)} %refs_3_.3) | copy-start | bytes 1572868
  6.7 4.7 %collective-permute-start.2 = (bf16[192,256]{1,0:T(8,128)(2,1)S(1)}, bf16[192,256]{1,0:T(8,128)(2,1)S(1)}, u32[]{:S(2)}, u32[]{:S(2)}) collective-permute-start(bf16[192,256]{1,0:T(8,128)(2,1)S(1)} %get-tuple-element.47), channel_id=1, source_target_pairs={{0,2},{1,3},{2,0},{3,1},{4,6},{5,7},{6,4},{7,5},{8,10},{9,11},{10,... | collective-permute-start | bytes 294920 | tf_op jit(solution)/shard_map/ppermute | solution.py:46
  9.3 2.8 %copy-start.2 = (bf16[256,512]{1,0:T(8,128)(2,1)S(1)}, bf16[256,512]{1,0:T(8,128)(2,1)}, u32[]{:S(2)}) copy-start(bf16[256,512]{1,0:T(8,128)(2,1)} %refs_4_.1) | copy-start | bytes 786436
  9.3 5.0 %collective-permute-start.1 = (bf16[512,128]{1,0:T(8,128)(2,1)S(1)}, bf16[512,128]{1,0:T(8,128)(2,1)S(1)}, u32[]{:S(2)}, u32[]{:S(2)}) collective-permute-start(bf16[512,128]{1,0:T(8,128)(2,1)S(1)} %add_convert_fusion), channel_id=1, source_target_pairs={{0,8},{4,12},{8,0},{12,4},{16,24},{20,28},{24,16},{28,20},{1,9},{5... | collective-permute-start | bytes 393224 | tf_op jit(solution)/shard_map/ppermute | solution.py:46
  11.9 1.9 %collective-permute-start.3 = (bf16[96,256]{1,0:T(8,128)(2,1)S(1)}, bf16[96,256]{1,0:T(8,128)(2,1)S(1)}, u32[]{:S(2)}, u32[]{:S(2)}) collective-permute-start(bf16[96,256]{1,0:T(8,128)(2,1)S(1)} %get-tuple-element.49), channel_id=1, source_target_pairs={{0,1},{1,0},{2,3},{3,2},{4,5},{5,4},{6,7},{7,6},{8,9},{9,8},{10,11... | collective-permute-start | bytes 147464 | tf_op jit(solution)/shard_map/ppermute | solution.py:46
  14.9 9.6 %collective-permute-start.4 = (bf16[512,128]{1,0:T(8,128)(2,1)S(1)}, bf16[512,128]{1,0:T(8,128)(2,1)S(1)}, u32[]{:S(2)}, u32[]{:S(2)}) collective-permute-start(bf16[512,128]{1,0:T(8,128)(2,1)S(1)} %shard_map.123), channel_id=1, source_target_pairs={{0,16},{4,20},{8,24},{12,28},{16,0},{20,4},{24,8},{28,12},{1,17},{... | collective-permute-start | bytes 393224 | tf_op jit(solution)/shard_map/ppermute | solution.py:46
  17.8 9.5 %collective-permute-start.7 = (bf16[96,256]{1,0:T(8,128)(2,1)S(1)}, bf16[96,256]{1,0:T(8,128)(2,1)S(1)}, u32[]{:S(2)}, u32[]{:S(2)}) collective-permute-start(bf16[96,256]{1,0:T(8,128)(2,1)S(1)} %get-tuple-element.64), channel_id=1, source_target_pairs={{0,2},{1,3},{2,0},{3,1},{4,6},{5,7},{6,4},{7,5},{8,10},{9,11},{10,... | collective-permute-start | bytes 147464 | tf_op jit(solution)/shard_map/ppermute | solution.py:46
  25.7 3.8 %collective-permute-start.9 = (bf16[32,256]{1,0:T(8,128)(2,1)S(1)}, bf16[32,256]{1,0:T(8,128)(2,1)S(1)}, u32[]{:S(2)}, u32[]{:S(2)}) collective-permute-start(bf16[32,256]{1,0:T(8,128)(2,1)S(1)} %shard_map.132), channel_id=1, source_target_pairs={{0,2},{1,3},{2,0},{3,1},{4,6},{5,7},{6,4},{7,5},{8,10},{9,11},{10,... | collective-permute-start | bytes 49160 | tf_op jit(solution)/shard_map/ppermute | solution.py:46
  27.3 2.2 %collective-permute-start.8 = (bf16[192,256]{1,0:T(8,128)(2,1)S(1)}, bf16[192,256]{1,0:T(8,128)(2,1)S(1)}, u32[]{:S(2)}, u32[]{:S(2)}) collective-permute-start(bf16[192,256]{1,0:T(8,128)(2,1)S(1)} %pad_maximum_fusion.1), channel_id=1, source_target_pairs={{0,1},{1,0},{2,3},{3,2},{4,5},{5,4},{6,7},{7,6},{8,9},{9,8},{10,11... | collective-permute-start | bytes 294920 | tf_op jit(solution)/shard_map/ppermute | solution.py:46
  29.5 2.3 %collective-permute-start.10 = (bf16[64,256]{1,0:T(8,128)(2,1)S(1)}, bf16[64,256]{1,0:T(8,128)(2,1)S(1)}, u32[]{:S(2)}, u32[]{:S(2)}) collective-permute-start(bf16[64,256]{1,0:T(8,128)(2,1)S(1)} %pad_maximum_fusion.3), channel_id=1, source_target_pairs={{0,1},{1,0},{2,3},{3,2},{4,5},{5,4},{6,7},{7,6},{8,9},{9,8},{10,11... | collective-permute-start | bytes 98312 | tf_op jit(solution)/shard_map/ppermute | solution.py:46
  30.4 7.8 %collective-permute-start.11 = (bf16[256,384]{1,0:T(8,128)(2,1)S(1)}, bf16[256,384]{1,0:T(8,128)(2,1)S(1)}, u32[]{:S(2)}, u32[]{:S(2)}) collective-permute-start(bf16[256,384]{1,0:T(8,128)(2,1)S(1)} %get-tuple-element.69), channel_id=1, source_target_pairs={{0,4},{4,0},{8,12},{12,8},{16,20},{20,16},{24,28},{28,24},{1,5},{5... | collective-permute-start | bytes 589832 | tf_op jit(solution)/shard_map/ppermute | solution.py:46
  32.6 7.0 %collective-permute-start.13 = (bf16[256,128]{1,0:T(8,128)(2,1)S(1)}, bf16[256,128]{1,0:T(8,128)(2,1)S(1)}, u32[]{:S(2)}, u32[]{:S(2)}) collective-permute-start(bf16[256,128]{1,0:T(8,128)(2,1)S(1)} %get-tuple-element.73), channel_id=1, source_target_pairs={{0,4},{4,0},{8,12},{12,8},{16,20},{20,16},{24,28},{28,24},{1,5},{5... | collective-permute-start | bytes 196616 | tf_op jit(solution)/shard_map/ppermute | solution.py:46
  34.0 21.6 %collective-permute-start.5 = (bf16[512,128]{1,0:T(8,128)(2,1)S(1)}, bf16[512,128]{1,0:T(8,128)(2,1)S(1)}, u32[]{:S(2)}, u32[]{:S(2)}) collective-permute-start(bf16[512,128]{1,0:T(8,128)(2,1)S(1)} %shard_map.128), channel_id=1, source_target_pairs={{0,8},{4,12},{8,0},{12,4},{16,24},{20,28},{24,16},{28,20},{1,9},{5... | collective-permute-start | bytes 393224 | tf_op jit(solution)/shard_map/ppermute | solution.py:46
  38.9 5.3 %collective-permute-start.12 = (bf16[128,384]{1,0:T(8,128)(2,1)S(1)}, bf16[128,384]{1,0:T(8,128)(2,1)S(1)}, u32[]{:S(2)}, u32[]{:S(2)}) collective-permute-start(bf16[128,384]{1,0:T(8,128)(2,1)S(1)} %get-tuple-element.71), channel_id=1, source_target_pairs={{0,8},{4,12},{8,0},{12,4},{16,24},{20,28},{24,16},{28,20},{1,9},{5... | collective-permute-start | bytes 294920 | tf_op jit(solution)/shard_map/ppermute | solution.py:46
  40.2 4.0 %collective-permute-start.14 = (bf16[128,128]{1,0:T(8,128)(2,1)S(1)}, bf16[128,128]{1,0:T(8,128)(2,1)S(1)}, u32[]{:S(2)}, u32[]{:S(2)}) collective-permute-start(bf16[128,128]{1,0:T(8,128)(2,1)S(1)} %get-tuple-element.75), channel_id=1, source_target_pairs={{0,8},{4,12},{8,0},{12,4},{16,24},{20,28},{24,16},{28,20},{1,9},{5... | collective-permute-start | bytes 98312 | tf_op jit(solution)/shard_map/ppermute | solution.py:46
  45.0 11.8 %collective-permute-start.15 = (bf16[64,384]{1,0:T(8,128)(2,1)S(1)}, bf16[64,384]{1,0:T(8,128)(2,1)S(1)}, u32[]{:S(2)}, u32[]{:S(2)}) collective-permute-start(bf16[64,384]{1,0:T(8,128)(2,1)S(1)} %get-tuple-element.77), channel_id=1, source_target_pairs={{0,16},{4,20},{8,24},{12,28},{16,0},{20,4},{24,8},{28,12},{1,17},{... | collective-permute-start | bytes 147464 | tf_op jit(solution)/shard_map/ppermute | solution.py:46
  55.6 5.7 %copy-start.4 = (f32[8,64,128]{2,1,0:T(8,128)S(1)}, f32[8,64,128]{2,1,0:T(8,128)}, u32[]{:S(2)}) copy-start(f32[8,64,128]{2,1,0:T(8,128)} %param.13) | copy-start | bytes 786436
  56.2 5.0 %collective-permute-start.6 = (bf16[512,128]{1,0:T(8,128)(2,1)S(1)}, bf16[512,128]{1,0:T(8,128)(2,1)S(1)}, u32[]{:S(2)}, u32[]{:S(2)}) collective-permute-start(bf16[512,128]{1,0:T(8,128)(2,1)S(1)} %shard_map.129), channel_id=1, source_target_pairs={{0,4},{4,0},{8,12},{12,8},{16,20},{20,16},{24,28},{28,24},{1,5},{5... | collective-permute-start | bytes 393224 | tf_op jit(solution)/shard_map/ppermute | solution.py:46

commit v4 on v3

--- a/solution.py
+++ b/solution.py
@@ -46,7 +46,7 @@
     return lax.ppermute(value, axis, pairs)
 
 
-def state_kernel(dims, idx_ref, k_hbm, v_hbm, w_hbm, x_hbm, kv_ref, kvb_ref, w_ref, x_ref, k_ref, v_ref, sems):
+def state_kernel(dims, idx_ref, head_ref, k_hbm, v_hbm, w_hbm, x_hbm, kv_ref, kvb_ref, w_ref, x_ref, k_ref, v_ref, sems):
     nh, dk, dv = dims
     copies = [pltpu.make_async_copy(src, dst, sems.at[n]) for n, (src, dst) in enumerate(
         ((k_hbm, k_ref), (v_hbm, v_ref), (w_hbm, w_ref), (x_hbm, x_ref)))]
@@ -78,12 +78,12 @@
 def project_kernel(bit, idx_ref, w_ref, x_ref, send_ref, keep_ref, xt_ref):
     xt = x_ref[...].T
     xt_ref[...] = xt
-    upper = ((idx_ref[1] >> bit) & 1) == 1
+    upper = ((idx_ref[0] >> bit) & 1) == 1
     part_ways(tn(w_ref[...], xt), upper, send_ref, keep_ref, keep_ref.shape[0])
 
 
-def fold_kernel(bit, axis, inner, idx_ref, keep_in, got_ref, send_ref, keep_ref):
-    upper = ((idx_ref[axis] >> bit) & 1) == 1
+def fold_kernel(bit, inner, idx_ref, keep_in, got_ref, send_ref, keep_ref):
+    upper = ((idx_ref[0] >> bit) & 1) == 1
     part_ways(keep_in[...] + got_ref[...].astype(F32), upper, send_ref, keep_ref, inner)
 
 
@@ -263,12 +263,12 @@
         out_ref[:, h * dv:(h + 1) * dv] = total.T.astype(BF16)
 
 
-def wgrad_kernel(bits, inner, idx_ref, xt_ref, gp_ref, send_ref, keep_ref, sorted_ref):
+def wgrad_kernel(bits, inner, idx_ref, head_ref, xt_ref, gp_ref, send_ref, keep_ref, sorted_ref):
     count = 1 << bits
     own = gp_ref.shape[0] // count
     for n in range(count):
         away = sum(((n >> k) & 1) << (bits - 1 - k) for k in range(bits))
-        at = pl.multiple_of((idx_ref[1] ^ away) * own, 16)
+        at = pl.multiple_of((head_ref[0] ^ away) * own, 16)
         sorted_ref[pl.ds(at, own), :] = gp_ref[n * own:(n + 1) * own, :]
     part_ways(nt(xt_ref[...], sorted_ref[...]), (idx_ref[0] & 1) == 1, send_ref, keep_ref, inner)
 
@@ -361,20 +361,20 @@
     per = width // n_seq
     rows = nh * dk
     S = jax.ShapeDtypeStruct
-    idx = jnp.stack([lax.axis_index("seq"), lax.axis_index("head")]).astype(jnp.int32)
+    idx, head_idx = [jnp.reshape(lax.axis_index(axis), (1,)) for axis in ("seq", "head")]
 
     hbm = pl.BlockSpec(memory_space=pltpu.HBM)
     kv, kvb, w_near, x_near = call(
         functools.partial(state_kernel, dims),
         [S((rows, dv), F32), S((rows, dv), BF16), S(w.shape, BF16), S(hidden.shape, BF16)],
-        [SM] + [hbm] * 4, 2 * tokens * rows * dv,
+        [SM] * 2 + [hbm] * 4, 2 * tokens * rows * dv,
         scratch_shapes=[pltpu.VMEM((tokens, rows), BF16), pltpu.VMEM((tokens, nh * dv), BF16),
                         pltpu.SemaphoreType.DMA((4,))])(
-                            idx, *[pltpu.with_memory_space_constraint(a, pltpu.HBM) for a in (keys, values, w, hidden)])
+                            idx, head_idx, *[pltpu.with_memory_space_constraint(a, pltpu.HBM) for a in (keys, values, w, hidden)])
     send, keep, xt = call(
         functools.partial(project_kernel, head_bits - 1),
         [S((cols // 2, tokens), BF16), S((cols // 2, tokens), F32), S((width, tokens), BF16)], [SM] + [VM] * 2,
-        2 * tokens * width * cols)(idx, w_near, x_near)
+        2 * tokens * width * cols)(head_idx, w_near, x_near)
 
     total, up = kv, kvb
     ups = []
@@ -389,8 +389,8 @@
     for bit in reversed(range(head_bits - 1)):
         n = keep.shape[0] // 2
         send, keep = call(
-            functools.partial(fold_kernel, bit, 1, n), [S((n, tokens), BF16), S((n, tokens), F32)],
-            [SM] + [VM] * 2, n * tokens)(idx, keep, got)
+            functools.partial(fold_kernel, bit, n), [S((n, tokens), BF16), S((n, tokens), F32)],
+            [SM] + [VM] * 2, n * tokens)(head_idx, keep, got)
         got = swap(send, "head", bit)
 
     pair_spec = lambda n: pl.BlockSpec((tokens, n), lambda p: (0, p))
@@ -423,12 +423,12 @@
         send, keep, ordered = call(
             functools.partial(wgrad_kernel, head_bits, per),
             [S((width // 2, n_cols), BF16), S((width // 2, n_cols), F32), S((n_cols, tokens), BF16)],
-            [SM] + [VM] * 2, 2 * tokens * width * n_cols)(idx, xt, gathered)
+            [SM] * 2 + [VM] * 2, 2 * tokens * width * n_cols)(idx, head_idx, xt, gathered)
         got = swap(send, "seq", 0)
         for bit in range(1, top):
             n = keep.shape[0] // 2
             send, keep = call(
-                functools.partial(fold_kernel, bit, 0, per), [S((n, n_cols), BF16), S((n, n_cols), F32)],
+                functools.partial(fold_kernel, bit, per), [S((n, n_cols), BF16), S((n, n_cols), F32)],
                 [SM] + [VM] * 2, n * n_cols)(idx, keep, got)
             got = swap(send, "seq", bit)
         return keep, got, ordered

time: 63.3 us -> 56.3 us (0.89)
  Pallas kernels: 23.1 us -> 15.1 us
  waiting for transfers between devices: 16.6 us -> 18.8 us
  starting transfers between devices: 21.6 us -> 20.6 us
    ppermute x16, waiting for transfers between devices: 16.6 us -> 18.8 us  [swap(): return lax.ppermute(value, axis, pairs)]
    pallas_call x3, Pallas kernels: 1.73 us -> 0.11 us  [the longest x2 0.08 us: reduce(): call(functools.partial(fold_kernel, bit, per), [S((n, n_cols), BF16), S((...]
    pallas_call x2, Pallas kernels: 1.66 us -> 0.57 us  [reduce(): call(functools.partial(wgrad_kernel, head_bits, per), [S((width // 2, n_c...]
    pallas_call x2, Pallas kernels: 1.2 us -> 0.12 us  [body(): call(functools.partial(pend_kernel, bit, top), [S((rows, dv), BF16)], [SM...]
    ppermute x16, starting transfers between devices: 21.6 us -> 20.6 us  [swap(): return lax.ppermute(value, axis, pairs)]
  transfers between devices with their start and end apart: 16 -> 16, of which waited for: 8 -> 8; matrix products, arithmetic and copies ran while one was open for 1% -> 1% of each run, Pallas kernels for 30% -> 22%
where the time goes in v4:
time: 56.3 us; the launch traced here: 56.2 us
  starting transfers between devices  20.6 us (37%)
  waiting for transfers between devices  18.8 us (33%)
  Pallas kernels  15.1 us (27%)
  between operations  0.86 us (2%)
  other arithmetic  0.83 us (1%)
    ppermute x16, starting transfers between devices, swap(): return lax.ppermute(value, axis, pairs)  20.6 us
    ppermute x16, waiting for transfers between devices, swap(): return lax.ppermute(value, axis, pairs)  18.8 us
    pallas_call x2, Pallas kernels, body(): call(functools.partial(local_kernel, dims, levels), [S((nh * dv // 2, tok...  3.68 us
    pallas_call x1, Pallas kernels, body(): call(functools.partial(level_kernel, dims, levels), [S((own, tokens), F32...  1.73 us
    pallas_call x1, Pallas kernels, body(): call(functools.partial(out_kernel, dims, levels, first, seq_bits), [S((to...  1.49 us
    pallas_call x1, Pallas kernels, body(): call(functools.partial(state_kernel, dims), [S((rows, dv), F32), S((rows,...  1.47 us
    pallas_call x1, Pallas kernels, body(): call(functools.partial(query_kernel, dims, levels, first, seq_bits), [S((...  1.45 us
    pallas_call x1, Pallas kernels, body(): call(functools.partial(final_kernel, dims, top), [S((tokens, rows), BF16)...  1.34 us
  transfers between devices with their start and end apart: 16, of which 8 were waited for; matrix products, arithmetic and copies ran while one was open for 1% of the time, Pallas kernels for 22%

profile of v4, /device:TPU:0, one launch (start us, length us, event | category | flops | bytes accessed | tf_op | source)
XLA Modules:
  0.0 56.2 jit_solution(4399098916567164924)
XLA Ops:
  0.6 0.0 copy-start.3
  0.6 1.5 %shard_map.118 = (f32[512,128]{1,0:T(8,128)S(1)}, bf16[512,128]{1,0:T(8,128)(2,1)S(1)}, bf16[512,384]{1,0:T(8,128)(2,1)S(1)}, bf16[256,512]{1,0:T(8,128)(2,1)S(1)}) custom-call(s32[1]{0:T(128)} %bitcast.idx_ref, s32[1]{0:T(128)} %bitcast.1.head_ref.idx_ref, bf16[256,512]{1,0:T(8,128)(2,1)} %refs_4_.1, bf16[256,1024]{1,0:T(8,128)(2,1)} %refs_5_.1, ...), custom_call_target="tpu_custom_call" | custom-call | flops 33554432 | bytes 2097152 | tf_op jit(solution)/shard_map/pallas_call | solution.py:367
  2.1 3.1 %collective-permute-start = (bf16[512,128]{1,0:T(8,128)(2,1)S(1)}, bf16[512,128]{1,0:T(8,128)(2,1)S(1)}, u32[]{:S(2)}, u32[]{:S(2)}) collective-permute-start(bf16[512,128]{1,0:T(8,128)(2,1)S(1)} %get-tuple-element.42), channel_id=1, source_target_pairs={{0,4},{4,0},{8,12},{12,8},{16,20},{20,16},{24,28},{28,24},{1,5},{5... | collective-permute-start | bytes 393224 | tf_op jit(solution)/shard_map/ppermute | solution.py:46
  5.2 0.0 copy-start.1
  5.2 0.4 shard_map.119
  5.6 0.0 copy-start
  5.6 1.6 %collective-permute-start.2 = (bf16[192,256]{1,0:T(8,128)(2,1)S(1)}, bf16[192,256]{1,0:T(8,128)(2,1)S(1)}, u32[]{:S(2)}, u32[]{:S(2)}) collective-permute-start(bf16[192,256]{1,0:T(8,128)(2,1)S(1)} %get-tuple-element.47), channel_id=1, source_target_pairs={{0,2},{1,3},{2,0},{3,1},{4,6},{5,7},{6,4},{7,5},{8,10},{9,11},{10,... | collective-permute-start | bytes 294920 | tf_op jit(solution)/shard_map/ppermute | solution.py:46
  7.1 1.5 %collective-permute-done.refs_0_ = bf16[512,128]{1,0:T(8,128)(2,1)S(1)} collective-permute-done((bf16[512,128]{1,0:T(8,128)(2,1)S(1)}, bf16[512,128]{1,0:T(8,128)(2,1)S(1)}, u32[]{:S(2)}, u32[]{:S(2)}) %collective-permute-start) | collective-permute-done | bytes 131104 | tf_op jit(solution)/shard_map/ppermute | solution.py:46
  8.7 0.0 copy-start.2
  8.7 1.9 %collective-permute-start.1 = (bf16[512,128]{1,0:T(8,128)(2,1)S(1)}, bf16[512,128]{1,0:T(8,128)(2,1)S(1)}, u32[]{:S(2)}, u32[]{:S(2)}) collective-permute-start(bf16[512,128]{1,0:T(8,128)(2,1)S(1)} %add_convert_fusion), channel_id=1, source_target_pairs={{0,8},{4,12},{8,0},{12,4},{16,24},{20,28},{24,16},{28,20},{1,9},{5... | collective-permute-start | bytes 393224 | tf_op jit(solution)/shard_map/ppermute | solution.py:46
  10.6 0.0 collective-permute-done.2.got_ref
  10.6 0.1 collective-permute-start.3
  10.7 0.0 copy-done.3
  10.7 0.0 copy-done.1
  10.7 0.0 copy-done
  10.7 0.0 copy-done.2
  10.8 1.7 %shard_map.121.gl_ref = f32[96,256]{1,0:T(8,128)S(1)} custom-call(bf16[256,512]{1,0:T(8,128)(2,1)S(1)} %copy-done.2, bf16[256,512]{1,0:T(8,128)(2,1)S(1)} %copy-done.3, bf16[256,1024]{1,0:T(8,128)(2,1)S(1)} %copy-done.1, bf16[256,1024]{1,0:T(8,128)(2,1)S(1)} %copy-done), custom_call_target="tpu_custom_call" | custom-call | flops 201326592 | bytes 196608 | tf_op jit(solution)/shard_map/pallas_call | solution.py:398
  12.5 0.0 collective-permute-done.3.got_ref
  12.5 0.4 shard_map.122
  12.9 0.8 %collective-permute-done.1.refs_1_ = bf16[512,128]{1,0:T(8,128)(2,1)S(1)} collective-permute-done((bf16[512,128]{1,0:T(8,128)(2,1)S(1)}, bf16[512,128]{1,0:T(8,128)(2,1)S(1)}, u32[]{:S(2)}, u32[]{:S(2)}) %collective-permute-start.1) | collective-permute-done | bytes 131104 | tf_op jit(solution)/shard_map/ppermute | solution.py:46
  13.8 2.8 %collective-permute-start.4 = (bf16[512,128]{1,0:T(8,128)(2,1)S(1)}, bf16[512,128]{1,0:T(8,128)(2,1)S(1)}, u32[]{:S(2)}, u32[]{:S(2)}) collective-permute-start(bf16[512,128]{1,0:T(8,128)(2,1)S(1)} %shard_map.123), channel_id=1, source_target_pairs={{0,16},{4,20},{8,24},{12,28},{16,0},{20,4},{24,8},{28,12},{1,17},{... | collective-permute-start | bytes 393224 | tf_op jit(solution)/shard_map/ppermute | solution.py:46
  16.7 1.5 %collective-permute-start.7 = (bf16[96,256]{1,0:T(8,128)(2,1)S(1)}, bf16[96,256]{1,0:T(8,128)(2,1)S(1)}, u32[]{:S(2)}, u32[]{:S(2)}) collective-permute-start(bf16[96,256]{1,0:T(8,128)(2,1)S(1)} %get-tuple-element.64), channel_id=1, source_target_pairs={{0,2},{1,3},{2,0},{3,1},{4,6},{5,7},{6,4},{7,5},{8,10},{9,11},{10,... | collective-permute-start | bytes 147464 | tf_op jit(solution)/shard_map/ppermute | solution.py:46
  18.2 4.5 %collective-permute-done.4.refs_2_.refs_0_ = bf16[512,128]{1,0:T(8,128)(2,1)S(1)} collective-permute-done((bf16[512,128]{1,0:T(8,128)(2,1)S(1)}, bf16[512,128]{1,0:T(8,128)(2,1)S(1)}, u32[]{:S(2)}, u32[]{:S(2)}) %collective-permute-start.4) | collective-permute-done | bytes 131104 | tf_op jit(solution)/shard_map/ppermute | solution.py:46
  22.6 0.7 %shard_map.132 = bf16[32,256]{1,0:T(8,128)(2,1)S(1)} custom-call(s32[1]{0:T(128)} %bitcast.idx_ref, bf16[512,128]{1,0:T(8,128)(2,1)S(1)} %collective-permute-done.refs_0_, bf16[512,128]{1,0:T(8,128)(2,1)S(1)} %collective-permute-done.1.refs_1_, bf16[512,128]{1,0:T(8,128)(2,1)S(1)} %collective-permute-done.4.refs_2_.refs_0_, bf16[256,1024]{1,0:T(8,128)(2,1)S(1)} %copy-done, ...), custom_call_target="tpu_custom_call" | custom-call | flops 100663296 | bytes 32768 | tf_op jit(solution)/shard_map/pallas_call | solution.py:413
  23.3 1.6 %collective-permute-start.9 = (bf16[32,256]{1,0:T(8,128)(2,1)S(1)}, bf16[32,256]{1,0:T(8,128)(2,1)S(1)}, u32[]{:S(2)}, u32[]{:S(2)}) collective-permute-start(bf16[32,256]{1,0:T(8,128)(2,1)S(1)} %shard_map.132), channel_id=1, source_target_pairs={{0,2},{1,3},{2,0},{3,1},{4,6},{5,7},{6,4},{7,5},{8,10},{9,11},{10,... | collective-permute-start | bytes 49160 | tf_op jit(solution)/shard_map/ppermute | solution.py:46
  24.9 0.0 collective-permute-done.7
  24.9 0.1 collective-permute-start.8
  25.0 2.2 %collective-permute-done.9 = bf16[32,256]{1,0:T(8,128)(2,1)S(1)} collective-permute-done((bf16[32,256]{1,0:T(8,128)(2,1)S(1)}, bf16[32,256]{1,0:T(8,128)(2,1)S(1)}, u32[]{:S(2)}, u32[]{:S(2)}) %collective-permute-start.9) | collective-permute-done | bytes 16416 | tf_op jit(solution)/shard_map/ppermute | solution.py:46
  27.1 0.0 collective-permute-start.10
  27.1 0.0 collective-permute-done.8
  27.2 0.3 shard_map.131
  27.5 1.5 %collective-permute-start.11 = (bf16[256,384]{1,0:T(8,128)(2,1)S(1)}, bf16[256,384]{1,0:T(8,128)(2,1)S(1)}, u32[]{:S(2)}, u32[]{:S(2)}) collective-permute-start(bf16[256,384]{1,0:T(8,128)(2,1)S(1)} %get-tuple-element.69), channel_id=1, source_target_pairs={{0,4},{4,0},{8,12},{12,8},{16,20},{20,16},{24,28},{28,24},{1,5},{5... | collective-permute-start | bytes 589832 | tf_op jit(solution)/shard_map/ppermute | solution.py:46
  29.0 0.0 collective-permute-done.10
  29.0 0.2 shard_map.133
  29.2 0.8 %collective-permute-start.13 = (bf16[256,128]{1,0:T(8,128)(2,1)S(1)}, bf16[256,128]{1,0:T(8,128)(2,1)S(1)}, u32[]{:S(2)}, u32[]{:S(2)}) collective-permute-start(bf16[256,128]{1,0:T(8,128)(2,1)S(1)} %get-tuple-element.73), channel_id=1, source_target_pairs={{0,4},{4,0},{8,12},{12,8},{16,20},{20,16},{24,28},{28,24},{1,5},{5... | collective-permute-start | bytes 196616 | tf_op jit(solution)/shard_map/ppermute | solution.py:46
  30.1 0.1 shard_map.128
  30.1 0.3 collective-permute-start.5
  30.5 4.9 %collective-permute-done.11.got_ref = bf16[256,384]{1,0:T(8,128)(2,1)S(1)} collective-permute-done((bf16[256,384]{1,0:T(8,128)(2,1)S(1)}, bf16[256,384]{1,0:T(8,128)(2,1)S(1)}, u32[]{:S(2)}, u32[]{:S(2)}) %collective-permute-start.11) | collective-permute-done | bytes 196640 | tf_op jit(solution)/shard_map/ppermute | solution.py:46
  35.3 0.1 shard_map.135
  35.4 0.5 collective-permute-start.12
  35.9 0.4 collective-permute-done.13.got_ref
  36.3 1.3 %collective-permute-start.14 = (bf16[128,128]{1,0:T(8,128)(2,1)S(1)}, bf16[128,128]{1,0:T(8,128)(2,1)S(1)}, u32[]{:S(2)}, u32[]{:S(2)}) collective-permute-start(bf16[128,128]{1,0:T(8,128)(2,1)S(1)} %get-tuple-element.75), channel_id=1, source_target_pairs={{0,8},{4,12},{8,0},{12,4},{16,24},{20,28},{24,16},{28,20},{1,9},{5... | collective-permute-start | bytes 98312 | tf_op jit(solution)/shard_map/ppermute | solution.py:46
  37.6 0.1 fusion.1.place_ref
  37.7 1.8 %shard_map.125 = (f32[512,256]{1,0:T(8,128)S(1)}, f32[256,256]{1,0:T(8,128)S(1)}, f32[256,256]{1,0:T(8,128)S(1)}, f32[256,512]{1,0:T(8,128)S(1)}) custom-call(bf16[256,512]{1,0:T(8,128)(2,1)S(1)} %copy-done.2, bf16[256,512]{1,0:T(8,128)(2,1)S(1)} %copy-done.3, bf16[256,1024]{1,0:T(8,128)(2,1)S(1)} %copy-done.1, bf16[256,1024]{1,0:T(8,128)(2,1)S(1)} %copy-done, ...), custom_call_target="tpu_custom_call" | custom-call | flops 301989888 | bytes 3145728 | tf_op jit(solution)/shard_map/pallas_call | solution.py:453
  39.6 0.9 %collective-permute-done.14.far_got = bf16[128,128]{1,0:T(8,128)(2,1)S(1)} collective-permute-done((bf16[128,128]{1,0:T(8,128)(2,1)S(1)}, bf16[128,128]{1,0:T(8,128)(2,1)S(1)}, u32[]{:S(2)}, u32[]{:S(2)}) %collective-permute-start.14) | collective-permute-done | bytes 32800 | tf_op jit(solution)/shard_map/ppermute | solution.py:46
  40.4 0.0 collective-permute-done.12.near_got
  40.4 0.3 shard_map.137
  40.8 2.9 %collective-permute-start.15 = (bf16[64,384]{1,0:T(8,128)(2,1)S(1)}, bf16[64,384]{1,0:T(8,128)(2,1)S(1)}, u32[]{:S(2)}, u32[]{:S(2)}) collective-permute-start(bf16[64,384]{1,0:T(8,128)(2,1)S(1)} %get-tuple-element.77), channel_id=1, source_target_pairs={{0,16},{4,20},{8,24},{12,28},{16,0},{20,4},{24,8},{28,12},{1,17},{... | collective-permute-start | bytes 147464 | tf_op jit(solution)/shard_map/ppermute | solution.py:46
  43.7 1.8 %shard_map.124 = (f32[512,256]{1,0:T(8,128)S(1)}, f32[256,256]{1,0:T(8,128)S(1)}, f32[256,256]{1,0:T(8,128)S(1)}, f32[256,512]{1,0:T(8,128)S(1)}) custom-call(bf16[256,512]{1,0:T(8,128)(2,1)S(1)} %copy-done.2, bf16[256,512]{1,0:T(8,128)(2,1)S(1)} %copy-done.3, bf16[256,1024]{1,0:T(8,128)(2,1)S(1)} %copy-done.1, bf16[256,1024]{1,0:T(8,128)(2,1)S(1)} %copy-done, ...), custom_call_target="tpu_custom_call" | custom-call | flops 301989888 | bytes 3145728 | tf_op jit(solution)/shard_map/pallas_call | solution.py:453
  45.5 1.5 %shard_map.126 = bf16[256,1024]{1,0:T(8,128)(2,1)} custom-call(s32[1]{0:T(128)} %bitcast.idx_ref, bf16[512,128]{1,0:T(8,128)(2,1)S(1)} %collective-permute-done.refs_0_, bf16[512,128]{1,0:T(8,128)(2,1)S(1)} %collective-permute-done.1.refs_1_, bf16[512,128]{1,0:T(8,128)(2,1)S(1)} %collective-permute-done.4.refs_2_.refs_0_, ...), custom_call_target="tpu_custom_call" | custom-call | flops 100663296 | bytes 1048576 | tf_op jit(solution)/shard_map/pallas_call | solution.py:466
  47.0 1.4 %shard_map.127 = bf16[256,512]{1,0:T(8,128)(2,1)} custom-call(s32[1]{0:T(128)} %bitcast.idx_ref, bf16[512,128]{1,0:T(8,128)(2,1)S(1)} %collective-permute-done.refs_0_, bf16[512,128]{1,0:T(8,128)(2,1)S(1)} %collective-permute-done.1.refs_1_, bf16[512,128]{1,0:T(8,128)(2,1)S(1)} %collective-permute-done.4.refs_2_.refs_0_, bf16[256,1024]{1,0:T(8,128)(2,1)S(1)} %copy-done, ...), custom_call_target="tpu_custom_call" | custom-call | flops 100663296 | bytes 524288 | tf_op jit(solution)/shard_map/pallas_call | solution.py:463
  48.5 1.3 %shard_map.134 = bf16[256,512]{1,0:T(8,128)(2,1)} custom-call(bf16[384,256]{1,0:T(8,128)(2,1)S(1)} %get-tuple-element.65.near_ref, bf16[128,256]{1,0:T(8,128)(2,1)S(1)} %get-tuple-element.67.far_ref, f32[128,384]{1,0:T(8,128)S(1)} %fusion.1.place_ref, bf16[512,384]{1,0:T(8,128)(2,1)S(1)} %get-tuple-element.44.w_ref), custom_call_target="tpu_custom_call" | custom-call | flops 100663296 | bytes 524288 | tf_op jit(solution)/shard_map/pallas_call | solution.py:470
  49.7 0.0 collective-permute-done.5.refs_1_
  49.7 0.0 copy-start.4
  49.7 0.1 shard_map.129
  49.8 0.8 %collective-permute-start.6 = (bf16[512,128]{1,0:T(8,128)(2,1)S(1)}, bf16[512,128]{1,0:T(8,128)(2,1)S(1)}, u32[]{:S(2)}, u32[]{:S(2)}) collective-permute-start(bf16[512,128]{1,0:T(8,128)(2,1)S(1)} %shard_map.129), channel_id=1, source_target_pairs={{0,4},{4,0},{8,12},{12,8},{16,20},{20,16},{24,28},{28,24},{1,5},{5... | collective-permute-start | bytes 393224 | tf_op jit(solution)/shard_map/ppermute | solution.py:46
  50.6 0.0 collective-permute-done.15
  50.6 0.7 %convert_add_fusion = f32[64,384]{1,0:T(8,128)} fusion(f32[64,384]{1,0:T(8,128)S(1)} %get-tuple-element.76, bf16[64,384]{1,0:T(8,128)(2,1)S(1)} %collective-permute-done.15), kind=kLoop, calls=%fused_computation.6 | loop fusion | flops 49152 | bytes 245760 | tf_op jit(solution)/shard_map/add | solution.py:446
  51.2 3.6 %collective-permute-done.6.refs_2_ = bf16[512,128]{1,0:T(8,128)(2,1)S(1)} collective-permute-done((bf16[512,128]{1,0:T(8,128)(2,1)S(1)}, bf16[512,128]{1,0:T(8,128)(2,1)S(1)}, u32[]{:S(2)}, u32[]{:S(2)}) %collective-permute-start.6) | collective-permute-done | bytes 131104 | tf_op jit(solution)/shard_map/ppermute | solution.py:46
  54.8 0.0 copy-done.4
  54.9 1.3 %shard_map.130 = (bf16[256,512]{1,0:T(8,128)(2,1)}, bf16[256,1024]{1,0:T(8,128)(2,1)}) custom-call(s32[1]{0:T(128)} %bitcast.idx_ref, bf16[512,128]{1,0:T(8,128)(2,1)S(1)} %collective-permute-done.4.refs_2_.refs_0_, bf16[512,128]{1,0:T(8,128)(2,1)S(1)} %collective-permute-done.5.refs_1_, bf16[512,128]{1,0:T(8,128)(2,1)S(1)} %collective-permute-done.6.refs_2_, ...), custom_call_target="tpu_custom_call" | custom-call | flops 67108864 | bytes 1572864 | tf_op jit(solution)/shard_map/pallas_call | solution.py:472
  (10 shorter events, 0.2 us)
Async XLA Ops:
  0.6 10.1 %copy-start.3 = (bf16[256,512]{1,0:T(8,128)(2,1)S(1)}, bf16[256,512]{1,0:T(8,128)(2,1)}, u32[]{:S(2)}) copy-start(bf16[256,512]{1,0:T(8,128)(2,1)} %q_ref.7) | copy-start | bytes 786436
  2.1 6.6 %collective-permute-start = (bf16[512,128]{1,0:T(8,128)(2,1)S(1)}, bf16[512,128]{1,0:T(8,128)(2,1)S(1)}, u32[]{:S(2)}, u32[]{:S(2)}) collective-permute-start(bf16[512,128]{1,0:T(8,128)(2,1)S(1)} %get-tuple-element.42), channel_id=1, source_target_pairs={{0,4},{4,0},{8,12},{12,8},{16,20},{20,16},{24,28},{28,24},{1,5},{5... | collective-permute-start | bytes 393224 | tf_op jit(solution)/shard_map/ppermute | solution.py:46
  5.2 5.5 %copy-start.1 = (bf16[256,1024]{1,0:T(8,128)(2,1)S(1)}, bf16[256,1024]{1,0:T(8,128)(2,1)}, u32[]{:S(2)}) copy-start(bf16[256,1024]{1,0:T(8,128)(2,1)} %refs_5_.1) | copy-start | bytes 1572868
  5.6 5.2 %copy-start = (bf16[256,1024]{1,0:T(8,128)(2,1)S(1)}, bf16[256,1024]{1,0:T(8,128)(2,1)}, u32[]{:S(2)}) copy-start(bf16[256,1024]{1,0:T(8,128)(2,1)} %refs_3_.3) | copy-start | bytes 1572868
  5.6 5.0 %collective-permute-start.2 = (bf16[192,256]{1,0:T(8,128)(2,1)S(1)}, bf16[192,256]{1,0:T(8,128)(2,1)S(1)}, u32[]{:S(2)}, u32[]{:S(2)}) collective-permute-start(bf16[192,256]{1,0:T(8,128)(2,1)S(1)} %get-tuple-element.47), channel_id=1, source_target_pairs={{0,2},{1,3},{2,0},{3,1},{4,6},{5,7},{6,4},{7,5},{8,10},{9,11},{10,... | collective-permute-start | bytes 294920 | tf_op jit(solution)/shard_map/ppermute | solution.py:46
  8.7 2.0 %copy-start.2 = (bf16[256,512]{1,0:T(8,128)(2,1)S(1)}, bf16[256,512]{1,0:T(8,128)(2,1)}, u32[]{:S(2)}) copy-start(bf16[256,512]{1,0:T(8,128)(2,1)} %refs_4_.1) | copy-start | bytes 786436
  8.7 5.0 %collective-permute-start.1 = (bf16[512,128]{1,0:T(8,128)(2,1)S(1)}, bf16[512,128]{1,0:T(8,128)(2,1)S(1)}, u32[]{:S(2)}, u32[]{:S(2)}) collective-permute-start(bf16[512,128]{1,0:T(8,128)(2,1)S(1)} %add_convert_fusion), channel_id=1, source_target_pairs={{0,8},{4,12},{8,0},{12,4},{16,24},{20,28},{24,16},{28,20},{1,9},{5... | collective-permute-start | bytes 393224 | tf_op jit(solution)/shard_map/ppermute | solution.py:46
  10.6 1.9 %collective-permute-start.3 = (bf16[96,256]{1,0:T(8,128)(2,1)S(1)}, bf16[96,256]{1,0:T(8,128)(2,1)S(1)}, u32[]{:S(2)}, u32[]{:S(2)}) collective-permute-start(bf16[96,256]{1,0:T(8,128)(2,1)S(1)} %get-tuple-element.49), channel_id=1, source_target_pairs={{0,1},{1,0},{2,3},{3,2},{4,5},{5,4},{6,7},{7,6},{8,9},{9,8},{10,11... | collective-permute-start | bytes 147464 | tf_op jit(solution)/shard_map/ppermute | solution.py:46
  13.8 8.8 %collective-permute-start.4 = (bf16[512,128]{1,0:T(8,128)(2,1)S(1)}, bf16[512,128]{1,0:T(8,128)(2,1)S(1)}, u32[]{:S(2)}, u32[]{:S(2)}) collective-permute-start(bf16[512,128]{1,0:T(8,128)(2,1)S(1)} %shard_map.123), channel_id=1, source_target_pairs={{0,16},{4,20},{8,24},{12,28},{16,0},{20,4},{24,8},{28,12},{1,17},{... | collective-permute-start | bytes 393224 | tf_op jit(solution)/shard_map/ppermute | solution.py:46
  16.7 8.2 %collective-permute-start.7 = (bf16[96,256]{1,0:T(8,128)(2,1)S(1)}, bf16[96,256]{1,0:T(8,128)(2,1)S(1)}, u32[]{:S(2)}, u32[]{:S(2)}) collective-permute-start(bf16[96,256]{1,0:T(8,128)(2,1)S(1)} %get-tuple-element.64), channel_id=1, source_target_pairs={{0,2},{1,3},{2,0},{3,1},{4,6},{5,7},{6,4},{7,5},{8,10},{9,11},{10,... | collective-permute-start | bytes 147464 | tf_op jit(solution)/shard_map/ppermute | solution.py:46
  23.3 3.8 %collective-permute-start.9 = (bf16[32,256]{1,0:T(8,128)(2,1)S(1)}, bf16[32,256]{1,0:T(8,128)(2,1)S(1)}, u32[]{:S(2)}, u32[]{:S(2)}) collective-permute-start(bf16[32,256]{1,0:T(8,128)(2,1)S(1)} %shard_map.132), channel_id=1, source_target_pairs={{0,2},{1,3},{2,0},{3,1},{4,6},{5,7},{6,4},{7,5},{8,10},{9,11},{10,... | collective-permute-start | bytes 49160 | tf_op jit(solution)/shard_map/ppermute | solution.py:46
  24.9 2.2 %collective-permute-start.8 = (bf16[192,256]{1,0:T(8,128)(2,1)S(1)}, bf16[192,256]{1,0:T(8,128)(2,1)S(1)}, u32[]{:S(2)}, u32[]{:S(2)}) collective-permute-start(bf16[192,256]{1,0:T(8,128)(2,1)S(1)} %pad_maximum_fusion.1), channel_id=1, source_target_pairs={{0,1},{1,0},{2,3},{3,2},{4,5},{5,4},{6,7},{7,6},{8,9},{9,8},{10,11... | collective-permute-start | bytes 294920 | tf_op jit(solution)/shard_map/ppermute | solution.py:46
  27.1 1.9 %collective-permute-start.10 = (bf16[64,256]{1,0:T(8,128)(2,1)S(1)}, bf16[64,256]{1,0:T(8,128)(2,1)S(1)}, u32[]{:S(2)}, u32[]{:S(2)}) collective-permute-start(bf16[64,256]{1,0:T(8,128)(2,1)S(1)} %pad_maximum_fusion.3), channel_id=1, source_target_pairs={{0,1},{1,0},{2,3},{3,2},{4,5},{5,4},{6,7},{7,6},{8,9},{9,8},{10,11... | collective-permute-start | bytes 98312 | tf_op jit(solution)/shard_map/ppermute | solution.py:46
  27.5 7.8 %collective-permute-start.11 = (bf16[256,384]{1,0:T(8,128)(2,1)S(1)}, bf16[256,384]{1,0:T(8,128)(2,1)S(1)}, u32[]{:S(2)}, u32[]{:S(2)}) collective-permute-start(bf16[256,384]{1,0:T(8,128)(2,1)S(1)} %get-tuple-element.69), channel_id=1, source_target_pairs={{0,4},{4,0},{8,12},{12,8},{16,20},{20,16},{24,28},{28,24},{1,5},{5... | collective-permute-start | bytes 589832 | tf_op jit(solution)/shard_map/ppermute | solution.py:46
  29.2 7.0 %collective-permute-start.13 = (bf16[256,128]{1,0:T(8,128)(2,1)S(1)}, bf16[256,128]{1,0:T(8,128)(2,1)S(1)}, u32[]{:S(2)}, u32[]{:S(2)}) collective-permute-start(bf16[256,128]{1,0:T(8,128)(2,1)S(1)} %get-tuple-element.73), channel_id=1, source_target_pairs={{0,4},{4,0},{8,12},{12,8},{16,20},{20,16},{24,28},{28,24},{1,5},{5... | collective-permute-start | bytes 196616 | tf_op jit(solution)/shard_map/ppermute | solution.py:46
  30.1 19.6 %collective-permute-start.5 = (bf16[512,128]{1,0:T(8,128)(2,1)S(1)}, bf16[512,128]{1,0:T(8,128)(2,1)S(1)}, u32[]{:S(2)}, u32[]{:S(2)}) collective-permute-start(bf16[512,128]{1,0:T(8,128)(2,1)S(1)} %shard_map.128), channel_id=1, source_target_pairs={{0,8},{4,12},{8,0},{12,4},{16,24},{20,28},{24,16},{28,20},{1,9},{5... | collective-permute-start | bytes 393224 | tf_op jit(solution)/shard_map/ppermute | solution.py:46
  35.4 5.0 %collective-permute-start.12 = (bf16[128,384]{1,0:T(8,128)(2,1)S(1)}, bf16[128,384]{1,0:T(8,128)(2,1)S(1)}, u32[]{:S(2)}, u32[]{:S(2)}) collective-permute-start(bf16[128,384]{1,0:T(8,128)(2,1)S(1)} %get-tuple-element.71), channel_id=1, source_target_pairs={{0,8},{4,12},{8,0},{12,4},{16,24},{20,28},{24,16},{28,20},{1,9},{5... | collective-permute-start | bytes 294920 | tf_op jit(solution)/shard_map/ppermute | solution.py:46
  36.3 4.1 %collective-permute-start.14 = (bf16[128,128]{1,0:T(8,128)(2,1)S(1)}, bf16[128,128]{1,0:T(8,128)(2,1)S(1)}, u32[]{:S(2)}, u32[]{:S(2)}) collective-permute-start(bf16[128,128]{1,0:T(8,128)(2,1)S(1)} %get-tuple-element.75), channel_id=1, source_target_pairs={{0,8},{4,12},{8,0},{12,4},{16,24},{20,28},{24,16},{28,20},{1,9},{5... | collective-permute-start | bytes 98312 | tf_op jit(solution)/shard_map/ppermute | solution.py:46
  40.8 9.8 %collective-permute-start.15 = (bf16[64,384]{1,0:T(8,128)(2,1)S(1)}, bf16[64,384]{1,0:T(8,128)(2,1)S(1)}, u32[]{:S(2)}, u32[]{:S(2)}) collective-permute-start(bf16[64,384]{1,0:T(8,128)(2,1)S(1)} %get-tuple-element.77), channel_id=1, source_target_pairs={{0,16},{4,20},{8,24},{12,28},{16,0},{20,4},{24,8},{28,12},{1,17},{... | collective-permute-start | bytes 147464 | tf_op jit(solution)/shard_map/ppermute | solution.py:46
  49.7 5.1 %copy-start.4 = (f32[8,64,128]{2,1,0:T(8,128)S(1)}, f32[8,64,128]{2,1,0:T(8,128)}, u32[]{:S(2)}) copy-start(f32[8,64,128]{2,1,0:T(8,128)} %param.13) | copy-start | bytes 786436
  49.8 5.0 %collective-permute-start.6 = (bf16[512,128]{1,0:T(8,128)(2,1)S(1)}, bf16[512,128]{1,0:T(8,128)(2,1)S(1)}, u32[]{:S(2)}, u32[]{:S(2)}) collective-permute-start(bf16[512,128]{1,0:T(8,128)(2,1)S(1)} %shard_map.129), channel_id=1, source_target_pairs={{0,4},{4,0},{8,12},{12,8},{16,20},{20,16},{24,28},{28,24},{1,5},{5... | collective-permute-start | bytes 393224 | tf_op jit(solution)/shard_map/ppermute | solution.py:46

commit v5 on v4

--- a/solution.py
+++ b/solution.py
@@ -38,6 +38,12 @@
         cost_estimate=pl.CostEstimate(flops=flops, bytes_accessed=2 * size, transcendentals=0),
         **kwargs,
     )
+
+
+def leave(buf_ref, hbm_ref, sem, cols):
+    copy = pltpu.make_async_copy(buf_ref.at[:, cols], hbm_ref.at[:, cols], sem)
+    copy.start()
+    return copy
 
 
 def swap(value, axis, bit):
@@ -150,63 +156,68 @@
 
 
 def level_kernel(dims, levels, k_ref, q_ref, v_ref, g_ref, gl_ref):
-    _, dk, dv = dims
-    kp = k_ref[...]
-    qt = q_ref[...].T
-    zero = jnp.zeros_like(qt[:dk])
+    nh, dk, dv = dims
     lane = lax.broadcasted_iota(jnp.int32, (SUB, LANES), 1)
     low = lax.broadcasted_iota(jnp.int32, (SUB, LANES), 0)
     t_low = lane % SUB
     gl_ref[...] = jnp.zeros_like(gl_ref)
-    for j in range(2):
-        base = j * levels
-        qz = jnp.concatenate([qt[:dk], zero] if j == 0 else [zero, qt[dk:]], axis=0)
-        prod = nn(kp, qz) * nt(v_ref[:, j * dv:(j + 1) * dv], g_ref[:, j * dv:(j + 1) * dv])
-        for x in range(2):
-            part = slice(x * LANES, (x + 1) * LANES)
-            sums = level_sums(prod[part, part], lane, low, t_low)
-            for l in range(8):
-                gl_ref[base + l:base + l + 1, part] = sums[l]
-        gl_ref[base + 8:base + 9, LANES:] = jnp.sum(prod[:LANES, LANES:], axis=0, keepdims=True)
-
-
-def local_kernel(dims, levels, k_ref, q_ref, v_ref, g_ref, lw_ref, out_ref, dq_ref, dk_ref, dv_ref):
+    for pair in range(nh // 2):
+        kp = k_ref[:, pair * 2 * dk:(pair + 1) * 2 * dk]
+        qt = q_ref[:, pair * 2 * dk:(pair + 1) * 2 * dk].T
+        zero = jnp.zeros_like(qt[:dk])
+        for j in range(2):
+            h = 2 * pair + j
+            base = h * levels
+            qz = jnp.concatenate([qt[:dk], zero] if j == 0 else [zero, qt[dk:]], axis=0)
+            prod = nn(kp, qz) * nt(v_ref[:, h * dv:(h + 1) * dv], g_ref[:, h * dv:(h + 1) * dv])
+            for x in range(2):
+                part = slice(x * LANES, (x + 1) * LANES)
+                sums = level_sums(prod[part, part], lane, low, t_low)
+                for l in range(8):
+                    gl_ref[base + l:base + l + 1, part] = sums[l]
+            gl_ref[base + 8:base + 9, LANES:] = jnp.sum(prod[:LANES, LANES:], axis=0, keepdims=True)
+
+
+def local_kernel(dims, levels, pairs, k_ref, q_ref, v_ref, g_ref, lw_ref, out_ref, dq_ref, dk_ref, dv_ref):
     _, dk, dv = dims
-    kp, qp = k_ref[...], q_ref[...]
-    kt, qt = kp.T, qp.T
-    zero = jnp.zeros_like(qt[:dk])
     lane = lax.broadcasted_iota(jnp.int32, (SUB, LANES), 1)
     low = lax.broadcasted_iota(jnp.int32, (SUB, LANES), 0)
     t_low = lane % SUB
-    wide_lane = lax.broadcasted_iota(jnp.int32, qp.shape, 1)
-    dk_sum = None
-    for j in range(2):
-        vj = v_ref[:, j * dv:(j + 1) * dv]
-        gj = g_ref[:, j * dv:(j + 1) * dv]
-        qz = jnp.concatenate([qt[:dk], zero] if j == 0 else [zero, qt[dk:]], axis=0)
-        base = j * levels
-        cross = lw_ref[base + 8:base + 9, LANES:]
-        halves = []
-        for x in range(2):
-            rows = [jnp.broadcast_to(lw_ref[base + l:base + l + 1, x * LANES:(x + 1) * LANES], (SUB, LANES))
-                    for l in range(8)]
-            halves.append(spread_half(rows, lane, low, t_low))
-
-        def weigh(full):
-            top = jnp.concatenate([full[:LANES, :LANES] * halves[0], full[:LANES, LANES:] * cross], axis=1)
-            bottom = full[LANES:, LANES:] * halves[1]
-            bottom = jnp.concatenate([jnp.zeros_like(bottom), bottom], axis=1)
-            return jnp.concatenate([top, bottom], axis=0).astype(BF16)
-
-        mixed = weigh(nn(kp, qz))
-        grad_scores = weigh(nt(vj, gj))
-        out_ref[j * dv:(j + 1) * dv, :] = tn(vj, mixed)
-        dq_ref[j * dk:(j + 1) * dk, :] = nn(kt[j * dk:(j + 1) * dk], grad_scores)
-        dv_ref[:, j * dv:(j + 1) * dv] = nn(mixed, gj)
-        mine = (wide_lane < dk) if j == 0 else (wide_lane >= dk)
-        term = nn(grad_scores, jnp.where(mine, qp, jnp.zeros_like(qp)))
-        dk_sum = term if dk_sum is None else dk_sum + term
-    dk_ref[...] = dk_sum
+    for n, pair in enumerate(pairs):
+        kp = k_ref[:, pair * 2 * dk:(pair + 1) * 2 * dk]
+        qp = q_ref[:, pair * 2 * dk:(pair + 1) * 2 * dk]
+        kt, qt = kp.T, qp.T
+        zero = jnp.zeros_like(qt[:dk])
+        wide_lane = lax.broadcasted_iota(jnp.int32, qp.shape, 1)
+        dk_sum = None
+        for j in range(2):
+            h, m = 2 * pair + j, 2 * n + j
+            vj = v_ref[:, h * dv:(h + 1) * dv]
+            gj = g_ref[:, h * dv:(h + 1) * dv]
+            qz = jnp.concatenate([qt[:dk], zero] if j == 0 else [zero, qt[dk:]], axis=0)
+            base = h * levels
+            cross = lw_ref[base + 8:base + 9, LANES:]
+            halves = []
+            for x in range(2):
+                rows = [jnp.broadcast_to(lw_ref[base + l:base + l + 1, x * LANES:(x + 1) * LANES], (SUB, LANES))
+                        for l in range(8)]
+                halves.append(spread_half(rows, lane, low, t_low))
+
+            def weigh(full):
+                top = jnp.concatenate([full[:LANES, :LANES] * halves[0], full[:LANES, LANES:] * cross], axis=1)
+                bottom = full[LANES:, LANES:] * halves[1]
+                bottom = jnp.concatenate([jnp.zeros_like(bottom), bottom], axis=1)
+                return jnp.concatenate([top, bottom], axis=0).astype(BF16)
+
+            mixed = weigh(nn(kp, qz))
+            grad_scores = weigh(nt(vj, gj))
+            out_ref[m * dv:(m + 1) * dv, :] = tn(vj, mixed)
+            dq_ref[m * dk:(m + 1) * dk, :] = nn(kt[j * dk:(j + 1) * dk], grad_scores)
+            dv_ref[:, m * dv:(m + 1) * dv] = nn(mixed, gj)
+            mine = (wide_lane < dk) if j == 0 else (wide_lane >= dk)
+            term = nn(grad_scores, jnp.where(mine, qp, jnp.zeros_like(qp)))
+            dk_sum = term if dk_sum is None else dk_sum + term
+        dk_ref[:, n * 2 * dk:(n + 1) * 2 * dk] = dk_sum
 
 
 def carry_kernel(dims, levels, first, count, idx_ref, *refs):
@@ -230,8 +241,9 @@
 def query_kernel(dims, levels, first, count, idx_ref, *refs):
     nh, dk, dv = dims
     ups = refs[:count]
-    g_ref, lw_ref, low_ref, high_ref, dq_ref = refs[count:]
+    g_ref, lw_ref, low_ref, high_ref, dq_hbm, dq_ref, sems = refs[count:]
     index = idx_ref[0]
+    copies = []
     for pair in range(nh // 2):
         halves = []
         for j in range(2):
@@ -244,14 +256,19 @@
                 x = nt(ups[m][h * dk:(h + 1) * dk, :], g_ref[:, h * dv:(h + 1) * dv])
                 total = total + x * (lw_ref[r:r + 1, :] * up)
             halves.append(total)
-        dq_ref[:, pair * 2 * dk:(pair + 1) * 2 * dk] = jnp.concatenate(halves, axis=0).T.astype(BF16)
+        cols = slice(pair * 2 * dk, (pair + 1) * 2 * dk)
+        dq_ref[:, cols] = jnp.concatenate(halves, axis=0).T.astype(BF16)
+        copies.append(leave(dq_ref, dq_hbm, sems.at[pair], cols))
+    for copy in copies:
+        copy.wait()
 
 
 def out_kernel(dims, levels, first, count, idx_ref, *refs):
     nh, dk, dv = dims
     ups = refs[:count]
-    qt_ref, lw_ref, low_ref, high_ref, out_ref = refs[count:]
+    qt_ref, lw_ref, low_ref, high_ref, out_hbm, out_ref, sems = refs[count:]
     index = idx_ref[0]
+    copies = []
     for h in range(nh):
         rows = slice(h * dk, (h + 1) * dk)
         local_ref, n = (low_ref, h) if h < nh // 2 else (high_ref, h - nh // 2)
@@ -261,6 +278,10 @@
             up = ((index >> m) & 1).astype(F32)
             total = total + tn(ups[m][rows, :], qt_ref[rows, :]) * (lw_ref[r:r + 1, :] * up)
         out_ref[:, h * dv:(h + 1) * dv] = total.T.astype(BF16)
+        if h % 2:
+            copies.append(leave(out_ref, out_hbm, sems.at[h // 2], slice((h - 1) * dv, (h + 1) * dv)))
+    for copy in copies:
+        copy.wait()
 
 
 def wgrad_kernel(bits, inner, idx_ref, head_ref, xt_ref, gp_ref, send_ref, keep_ref, sorted_ref):
@@ -280,10 +301,16 @@
     part_ways(total, ((idx_ref[0] >> bit) & 1) == 1, send_ref, keep_ref, keep_ref.shape[0])
 
 
-def hidden_kernel(near_ref, far_ref, place_ref, w_ref, dx_ref):
-    gp = near_ref[...].astype(F32) + tn(place_ref[...].astype(BF16), far_ref[...])
-    dx_ref[...] = lax.dot_general(
-        gp.astype(BF16), w_ref[...], (((0,), (1,)), ((), ())), preferred_element_type=F32).astype(BF16)
+def hidden_kernel(near_ref, far_ref, place_ref, w_ref, dx_hbm, dx_ref, sems):
+    gp = (near_ref[...].astype(F32) + tn(place_ref[...].astype(BF16), far_ref[...])).astype(BF16).T
+    half = dx_ref.shape[1] // 2
+    copies = []
+    for n in range(2):
+        cols = slice(n * half, (n + 1) * half)
+        dx_ref[:, cols] = nt(gp, w_ref[cols, :]).astype(BF16)
+        copies.append(leave(dx_ref, dx_hbm, sems.at[n], cols))
+    for copy in copies:
+        copy.wait()
 
 
 def join_kernel(top, count, idx_ref, kv_ref, *refs):
@@ -315,7 +342,8 @@
 def final_kernel(dims, top, idx_ref, *refs):
     nh, dk, dv = dims
     gots = refs[:top + 1]
-    ds_ref, k_ref, v_ref, low_k, high_k, low_v, high_v, dk_ref, dv_ref = refs[top + 1:]
+    ds_ref, k_ref, v_ref, low_k, high_k, low_v, high_v, dk_hbm, dv_hbm, dk_ref, dv_ref, sems = refs[top + 1:]
+    copies = []
     upper = ((idx_ref[0] >> top) & 1) == 1
     zero = jnp.zeros((dk, dv), BF16)
     for pair in range(nh // 2):
@@ -335,6 +363,10 @@
             near = dvl_ref[:, (2 * p + j) * dv:(2 * p + j + 1) * dv]
             dv_ref[:, cols] = (near + nn(kp, padded)).astype(BF16)
         dk_ref[:, pair * 2 * dk:(pair + 1) * 2 * dk] = total.astype(BF16)
+        copies.append(leave(dv_ref, dv_hbm, sems.at[2 * pair], slice(2 * pair * dv, (2 * pair + 2) * dv)))
+        copies.append(leave(dk_ref, dk_hbm, sems.at[2 * pair + 1], slice(pair * 2 * dk, (pair + 1) * 2 * dk)))
+    for copy in copies:
+        copy.wait()
 
 
 def gather_heads(value, head_bits):
@@ -393,13 +425,9 @@
             [SM] + [VM] * 2, n * tokens)(head_idx, keep, got)
         got = swap(send, "head", bit)
 
-    pair_spec = lambda n: pl.BlockSpec((tokens, n), lambda p: (0, p))
-    row_spec = lambda n: pl.BlockSpec((n, tokens), lambda p: (p, 0))
     gl = call(
-        functools.partial(level_kernel, dims, levels), [S((own, tokens), F32)],
-        [pair_spec(2 * dk), pair_spec(2 * dk), pair_spec(2 * dv), pair_spec(2 * dv)],
-        2 * tokens * tokens * nh * (dk + dv), grid=(nh // 2,),
-        out_specs=[row_spec(2 * levels)])(keys, queries, values, d_out)[0]
+        functools.partial(level_kernel, dims, levels), [S((own, tokens), F32)], [VM] * 4,
+        2 * tokens * tokens * nh * (dk + dv))(keys, queries, values, d_out)[0]
     sig, lw, near, qt, gu = call(
         functools.partial(weight_kernel, dims, levels, first, seq_bits),
         [S((own, tokens), F32), S((own, tokens), F32), S((own, tokens), BF16), S((rows, tokens), BF16),
@@ -448,30 +476,37 @@
     half = nh // 4
     local = []
     for part in range(2):
-        shift = part * half
-        at_col = lambda n, shift=shift: pl.BlockSpec((tokens, n), lambda p: (0, p + shift))
         local.append(call(
-            functools.partial(local_kernel, dims, levels),
+            functools.partial(local_kernel, dims, levels, tuple(range(part * half, (part + 1) * half))),
             [S((nh * dv // 2, tokens), F32), S((rows // 2, tokens), F32), S((tokens, rows // 2), F32),
              S((tokens, nh * dv // 2), F32)],
-            [at_col(2 * dk), at_col(2 * dk), at_col(2 * dv), at_col(2 * dv),
-             pl.BlockSpec((2 * levels, tokens), lambda p, shift=shift: (p + shift, 0))],
-            tokens * tokens * nh * (3 * dk + 3 * dv), grid=(half,),
-            out_specs=[row_spec(2 * dv), row_spec(2 * dk), pair_spec(2 * dk), pair_spec(2 * dv)],
+            [VM] * 5, tokens * tokens * nh * (3 * dk + 3 * dv),
         )(keys, queries, values, d_out, lw))
     out_l, dq_l, dk_l, dv_l = [(local[0][n], local[1][n]) for n in range(4)]
+
+    def leaving(shapes, copies):
+        return dict(out_specs=[hbm] * len(shapes),
+                    scratch_shapes=[pltpu.VMEM(shape, BF16) for shape in shapes] + [pltpu.SemaphoreType.DMA((copies,))])
+
+    def results(*shapes):
+        return [S(shape, BF16) for shape in shapes]
+
+    narrow, broad = (tokens, rows), (tokens, nh * dv)
     d_queries = call(
-        functools.partial(query_kernel, dims, levels, first, seq_bits), [S((tokens, rows), BF16)],
-        [SM] + [VM] * (seq_bits + 4), 2 * tokens * rows * dv * seq_bits)(idx, *ups, d_out, lw, *dq_l)[0]
+        functools.partial(query_kernel, dims, levels, first, seq_bits), results(narrow),
+        [SM] + [VM] * (seq_bits + 4), 2 * tokens * rows * dv * seq_bits, **leaving([narrow], nh // 2))(
+            idx, *ups, d_out, lw, *dq_l)[0]
     out = call(
-        functools.partial(out_kernel, dims, levels, first, seq_bits),
-        [S((tokens, nh * dv), BF16)],
-        [SM] + [VM] * (seq_bits + 4), 2 * tokens * rows * dv * seq_bits)(idx, *ups, qt, lw, *out_l)[0]
-    d_hidden = call(hidden_kernel, [S((tokens, width), BF16)], [VM] * 4, 2 * tokens * width * cols)(
-        near_all, far_all, place, w_near)[0]
+        functools.partial(out_kernel, dims, levels, first, seq_bits), results(broad),
+        [SM] + [VM] * (seq_bits + 4), 2 * tokens * rows * dv * seq_bits, **leaving([broad], nh // 2))(
+            idx, *ups, qt, lw, *out_l)[0]
+    d_hidden = call(
+        hidden_kernel, results((tokens, width)), [VM] * 4, 2 * tokens * width * cols,
+        **leaving([(tokens, width)], 2))(near_all, far_all, place, w_near)[0]
     d_keys, d_values = call(
-        functools.partial(final_kernel, dims, top),
-        [S((tokens, rows), BF16), S((tokens, nh * dv), BF16)], [SM] + [VM] * (top + 8), 4 * tokens * rows * dv)(idx, *gots, d_state.reshape(rows, dv), keys, values, *dk_l, *dv_l)
+        functools.partial(final_kernel, dims, top), results(narrow, broad), [SM] + [VM] * (top + 8),
+        4 * tokens * rows * dv, **leaving([narrow, broad], nh))(
+            idx, *gots, d_state.reshape(rows, dv), keys, values, *dk_l, *dv_l)
     return (out, d_queries, d_keys, d_values, d_hidden, d_w)
 
 

time: 56.3 us -> 54.8 us (0.973)
  Pallas kernels: 15.1 us -> 13 us
  starting transfers between devices: 20.6 us -> 21.3 us
    pallas_call x6, Pallas kernels: 9.22 us -> 8.09 us  [the longest x2 2.8 us: body(): call(functools.partial(local_kernel, dims, levels, tuple(range(part * hal...]
    pallas_call x1, Pallas kernels: 1.73 us -> 0.76 us  [body(): call(functools.partial(level_kernel, dims, levels), [S((own, tokens), F32...]
    ppermute x16, starting transfers between devices: 20.6 us -> 21.3 us  [swap(): return lax.ppermute(value, axis, pairs)]
  transfers between devices with their start and end apart: 16 -> 16, of which waited for: 8 -> 9; matrix products, arithmetic and copies ran while one was open for 1% -> 2% of each run, Pallas kernels for 22% -> 19%
where the time goes in v5:
time: 54.8 us; the launch traced here: 54.7 us
  starting transfers between devices  21.3 us (39%)
  waiting for transfers between devices  18.6 us (34%)
  Pallas kernels  13 us (24%)
  between operations  0.89 us (2%)
  other arithmetic  0.83 us (2%)
    ppermute x16, starting transfers between devices, swap(): return lax.ppermute(value, axis, pairs)  21.3 us
    ppermute x16, waiting for transfers between devices, swap(): return lax.ppermute(value, axis, pairs)  18.6 us
    pallas_call x2, Pallas kernels, body(): call(functools.partial(local_kernel, dims, levels, tuple(range(part * hal...  2.8 us
    pallas_call x1, Pallas kernels, body(): call(functools.partial(state_kernel, dims), [S((rows, dv), F32), S((rows,...  1.47 us
    pallas_call x1, Pallas kernels, body(): call(functools.partial(query_kernel, dims, levels, first, seq_bits), resu...  1.42 us
    pallas_call x1, Pallas kernels, body(): call(functools.partial(out_kernel, dims, levels, first, seq_bits), result...  1.39 us
    pallas_call x1, Pallas kernels, body(): call(hidden_kernel, results((tokens, width)), [VM] * 4, 2 * tokens * widt...  1.27 us
    pallas_call x1, Pallas kernels, body(): call(functools.partial(final_kernel, dims, top), results(narrow, broad),...  1.22 us
  transfers between devices with their start and end apart: 16, of which 9 were waited for; matrix products, arithmetic and copies ran while one was open for 2% of the time, Pallas kernels for 19%

profile of v5, /device:TPU:0, one launch (start us, length us, event | category | flops | bytes accessed | tf_op | source)
XLA Modules:
  0.0 54.7 jit_solution(13104426170702405815)
XLA Ops:
  0.6 0.0 copy-start.3
  0.6 1.5 %shard_map.118 = (f32[512,128]{1,0:T(8,128)S(1)}, bf16[512,128]{1,0:T(8,128)(2,1)S(1)}, bf16[512,384]{1,0:T(8,128)(2,1)S(1)}, bf16[256,512]{1,0:T(8,128)(2,1)S(1)}) custom-call(s32[1]{0:T(128)} %bitcast.idx_ref, s32[1]{0:T(128)} %bitcast.1.head_ref.idx_ref, bf16[256,512]{1,0:T(8,128)(2,1)} %refs_4_.1, bf16[256,1024]{1,0:T(8,128)(2,1)} %refs_5_.1, ...), custom_call_target="tpu_custom_call" | custom-call | flops 33554432 | bytes 2097152 | tf_op jit(solution)/shard_map/pallas_call | solution.py:399
  2.1 3.1 %collective-permute-start = (bf16[512,128]{1,0:T(8,128)(2,1)S(1)}, bf16[512,128]{1,0:T(8,128)(2,1)S(1)}, u32[]{:S(2)}, u32[]{:S(2)}) collective-permute-start(bf16[512,128]{1,0:T(8,128)(2,1)S(1)} %get-tuple-element.42), channel_id=1, source_target_pairs={{0,4},{4,0},{8,12},{12,8},{16,20},{20,16},{24,28},{28,24},{1,5},{5... | collective-permute-start | bytes 393224 | tf_op jit(solution)/shard_map/ppermute | solution.py:52
  5.2 0.0 copy-start.1
  5.2 0.4 shard_map.119
  5.6 0.0 copy-start
  5.6 1.6 %collective-permute-start.2 = (bf16[192,256]{1,0:T(8,128)(2,1)S(1)}, bf16[192,256]{1,0:T(8,128)(2,1)S(1)}, u32[]{:S(2)}, u32[]{:S(2)}) collective-permute-start(bf16[192,256]{1,0:T(8,128)(2,1)S(1)} %get-tuple-element.47), channel_id=1, source_target_pairs={{0,2},{1,3},{2,0},{3,1},{4,6},{5,7},{6,4},{7,5},{8,10},{9,11},{10,... | collective-permute-start | bytes 294920 | tf_op jit(solution)/shard_map/ppermute | solution.py:52
  7.1 1.5 %collective-permute-done.refs_0_ = bf16[512,128]{1,0:T(8,128)(2,1)S(1)} collective-permute-done((bf16[512,128]{1,0:T(8,128)(2,1)S(1)}, bf16[512,128]{1,0:T(8,128)(2,1)S(1)}, u32[]{:S(2)}, u32[]{:S(2)}) %collective-permute-start) | collective-permute-done | bytes 131104 | tf_op jit(solution)/shard_map/ppermute | solution.py:52
  8.7 0.0 copy-start.2
  8.7 1.9 %collective-permute-start.1 = (bf16[512,128]{1,0:T(8,128)(2,1)S(1)}, bf16[512,128]{1,0:T(8,128)(2,1)S(1)}, u32[]{:S(2)}, u32[]{:S(2)}) collective-permute-start(bf16[512,128]{1,0:T(8,128)(2,1)S(1)} %add_convert_fusion), channel_id=1, source_target_pairs={{0,8},{4,12},{8,0},{12,4},{16,24},{20,28},{24,16},{28,20},{1,9},{5... | collective-permute-start | bytes 393224 | tf_op jit(solution)/shard_map/ppermute | solution.py:52
  10.6 0.0 collective-permute-done.2.got_ref
  10.6 0.1 collective-permute-start.3
  10.7 0.0 copy-done.3
  10.7 0.0 copy-done.1
  10.7 0.0 copy-done
  10.7 0.0 copy-done.2
  10.8 0.8 %shard_map.121.gl_ref = f32[96,256]{1,0:T(8,128)S(1)} custom-call(bf16[256,512]{1,0:T(8,128)(2,1)S(1)} %copy-done.2, bf16[256,512]{1,0:T(8,128)(2,1)S(1)} %copy-done.3, bf16[256,1024]{1,0:T(8,128)(2,1)S(1)} %copy-done.1, bf16[256,1024]{1,0:T(8,128)(2,1)S(1)} %copy-done), custom_call_target="tpu_custom_call" | custom-call | flops 201326592 | bytes 196608 | tf_op jit(solution)/shard_map/pallas_call | solution.py:428
  11.5 0.4 collective-permute-done.3.got_ref
  11.9 0.4 shard_map.122
  12.4 1.4 %collective-permute-done.1.refs_1_ = bf16[512,128]{1,0:T(8,128)(2,1)S(1)} collective-permute-done((bf16[512,128]{1,0:T(8,128)(2,1)S(1)}, bf16[512,128]{1,0:T(8,128)(2,1)S(1)}, u32[]{:S(2)}, u32[]{:S(2)}) %collective-permute-start.1) | collective-permute-done | bytes 131104 | tf_op jit(solution)/shard_map/ppermute | solution.py:52
  13.8 2.8 %collective-permute-start.4 = (bf16[512,128]{1,0:T(8,128)(2,1)S(1)}, bf16[512,128]{1,0:T(8,128)(2,1)S(1)}, u32[]{:S(2)}, u32[]{:S(2)}) collective-permute-start(bf16[512,128]{1,0:T(8,128)(2,1)S(1)} %shard_map.123), channel_id=1, source_target_pairs={{0,16},{4,20},{8,24},{12,28},{16,0},{20,4},{24,8},{28,12},{1,17},{... | collective-permute-start | bytes 393224 | tf_op jit(solution)/shard_map/ppermute | solution.py:52
  16.7 1.5 %collective-permute-start.7 = (bf16[96,256]{1,0:T(8,128)(2,1)S(1)}, bf16[96,256]{1,0:T(8,128)(2,1)S(1)}, u32[]{:S(2)}, u32[]{:S(2)}) collective-permute-start(bf16[96,256]{1,0:T(8,128)(2,1)S(1)} %get-tuple-element.64), channel_id=1, source_target_pairs={{0,2},{1,3},{2,0},{3,1},{4,6},{5,7},{6,4},{7,5},{8,10},{9,11},{10,... | collective-permute-start | bytes 147464 | tf_op jit(solution)/shard_map/ppermute | solution.py:52
  18.2 3.6 %collective-permute-done.4.refs_2_.refs_0_ = bf16[512,128]{1,0:T(8,128)(2,1)S(1)} collective-permute-done((bf16[512,128]{1,0:T(8,128)(2,1)S(1)}, bf16[512,128]{1,0:T(8,128)(2,1)S(1)}, u32[]{:S(2)}, u32[]{:S(2)}) %collective-permute-start.4) | collective-permute-done | bytes 131104 | tf_op jit(solution)/shard_map/ppermute | solution.py:52
  21.8 0.7 %shard_map.132 = bf16[32,256]{1,0:T(8,128)(2,1)S(1)} custom-call(s32[1]{0:T(128)} %bitcast.idx_ref, bf16[512,128]{1,0:T(8,128)(2,1)S(1)} %collective-permute-done.refs_0_, bf16[512,128]{1,0:T(8,128)(2,1)S(1)} %collective-permute-done.1.refs_1_, bf16[512,128]{1,0:T(8,128)(2,1)S(1)} %collective-permute-done.4.refs_2_.refs_0_, bf16[256,1024]{1,0:T(8,128)(2,1)S(1)} %copy-done, ...), custom_call_target="tpu_custom_call" | custom-call | flops 100663296 | bytes 32768 | tf_op jit(solution)/shard_map/pallas_call | solution.py:441
  22.4 1.6 %collective-permute-start.9 = (bf16[32,256]{1,0:T(8,128)(2,1)S(1)}, bf16[32,256]{1,0:T(8,128)(2,1)S(1)}, u32[]{:S(2)}, u32[]{:S(2)}) collective-permute-start(bf16[32,256]{1,0:T(8,128)(2,1)S(1)} %shard_map.132), channel_id=1, source_target_pairs={{0,2},{1,3},{2,0},{3,1},{4,6},{5,7},{6,4},{7,5},{8,10},{9,11},{10,... | collective-permute-start | bytes 49160 | tf_op jit(solution)/shard_map/ppermute | solution.py:52
  24.0 0.0 collective-permute-done.7
  24.0 0.1 collective-permute-start.8
  24.1 2.2 %collective-permute-done.9 = bf16[32,256]{1,0:T(8,128)(2,1)S(1)} collective-permute-done((bf16[32,256]{1,0:T(8,128)(2,1)S(1)}, bf16[32,256]{1,0:T(8,128)(2,1)S(1)}, u32[]{:S(2)}, u32[]{:S(2)}) %collective-permute-start.9) | collective-permute-done | bytes 16416 | tf_op jit(solution)/shard_map/ppermute | solution.py:52
  26.3 0.0 collective-permute-start.10
  26.3 0.0 collective-permute-done.8
  26.3 0.3 shard_map.131
  26.6 1.6 %collective-permute-start.11 = (bf16[256,384]{1,0:T(8,128)(2,1)S(1)}, bf16[256,384]{1,0:T(8,128)(2,1)S(1)}, u32[]{:S(2)}, u32[]{:S(2)}) collective-permute-start(bf16[256,384]{1,0:T(8,128)(2,1)S(1)} %get-tuple-element.69), channel_id=1, source_target_pairs={{0,4},{4,0},{8,12},{12,8},{16,20},{20,16},{24,28},{28,24},{1,5},{5... | collective-permute-start | bytes 589832 | tf_op jit(solution)/shard_map/ppermute | solution.py:52
  28.2 0.0 collective-permute-done.10
  28.2 0.2 shard_map.133
  28.5 0.8 %collective-permute-start.13 = (bf16[256,128]{1,0:T(8,128)(2,1)S(1)}, bf16[256,128]{1,0:T(8,128)(2,1)S(1)}, u32[]{:S(2)}, u32[]{:S(2)}) collective-permute-start(bf16[256,128]{1,0:T(8,128)(2,1)S(1)} %get-tuple-element.73), channel_id=1, source_target_pairs={{0,4},{4,0},{8,12},{12,8},{16,20},{20,16},{24,28},{28,24},{1,5},{5... | collective-permute-start | bytes 196616 | tf_op jit(solution)/shard_map/ppermute | solution.py:52
  29.3 0.1 shard_map.128
  29.4 0.3 collective-permute-start.5
  29.7 4.8 %collective-permute-done.11.got_ref = bf16[256,384]{1,0:T(8,128)(2,1)S(1)} collective-permute-done((bf16[256,384]{1,0:T(8,128)(2,1)S(1)}, bf16[256,384]{1,0:T(8,128)(2,1)S(1)}, u32[]{:S(2)}, u32[]{:S(2)}) %collective-permute-start.11) | collective-permute-done | bytes 196640 | tf_op jit(solution)/shard_map/ppermute | solution.py:52
  34.5 0.1 shard_map.135
  34.5 0.5 collective-permute-start.12
  35.0 0.4 collective-permute-done.13.got_ref
  35.4 1.3 %collective-permute-start.14 = (bf16[128,128]{1,0:T(8,128)(2,1)S(1)}, bf16[128,128]{1,0:T(8,128)(2,1)S(1)}, u32[]{:S(2)}, u32[]{:S(2)}) collective-permute-start(bf16[128,128]{1,0:T(8,128)(2,1)S(1)} %get-tuple-element.75), channel_id=1, source_target_pairs={{0,8},{4,12},{8,0},{12,4},{16,24},{20,28},{24,16},{28,20},{1,9},{5... | collective-permute-start | bytes 98312 | tf_op jit(solution)/shard_map/ppermute | solution.py:52
  36.7 0.1 fusion.1.place_ref
  36.8 1.4 %shard_map.125 = (f32[512,256]{1,0:T(8,128)S(1)}, f32[256,256]{1,0:T(8,128)S(1)}, f32[256,256]{1,0:T(8,128)S(1)}, f32[256,512]{1,0:T(8,128)S(1)}) custom-call(bf16[256,512]{1,0:T(8,128)(2,1)S(1)} %copy-done.2, bf16[256,512]{1,0:T(8,128)(2,1)S(1)} %copy-done.3, bf16[256,1024]{1,0:T(8,128)(2,1)S(1)} %copy-done.1, bf16[256,1024]{1,0:T(8,128)(2,1)S(1)} %copy-done, ...), custom_call_target="tpu_custom_call" | custom-call | flops 301989888 | bytes 3145728 | tf_op jit(solution)/shard_map/pallas_call | solution.py:479
  38.2 1.3 %collective-permute-done.14.far_got = bf16[128,128]{1,0:T(8,128)(2,1)S(1)} collective-permute-done((bf16[128,128]{1,0:T(8,128)(2,1)S(1)}, bf16[128,128]{1,0:T(8,128)(2,1)S(1)}, u32[]{:S(2)}, u32[]{:S(2)}) %collective-permute-start.14) | collective-permute-done | bytes 32800 | tf_op jit(solution)/shard_map/ppermute | solution.py:52
  39.6 0.0 collective-permute-done.12.near_got
  39.6 0.3 shard_map.137
  39.9 2.9 %collective-permute-start.15 = (bf16[64,384]{1,0:T(8,128)(2,1)S(1)}, bf16[64,384]{1,0:T(8,128)(2,1)S(1)}, u32[]{:S(2)}, u32[]{:S(2)}) collective-permute-start(bf16[64,384]{1,0:T(8,128)(2,1)S(1)} %get-tuple-element.77), channel_id=1, source_target_pairs={{0,16},{4,20},{8,24},{12,28},{16,0},{20,4},{24,8},{28,12},{1,17},{... | collective-permute-start | bytes 147464 | tf_op jit(solution)/shard_map/ppermute | solution.py:52
  42.8 1.4 %shard_map.124 = (f32[512,256]{1,0:T(8,128)S(1)}, f32[256,256]{1,0:T(8,128)S(1)}, f32[256,256]{1,0:T(8,128)S(1)}, f32[256,512]{1,0:T(8,128)S(1)}) custom-call(bf16[256,512]{1,0:T(8,128)(2,1)S(1)} %copy-done.2, bf16[256,512]{1,0:T(8,128)(2,1)S(1)} %copy-done.3, bf16[256,1024]{1,0:T(8,128)(2,1)S(1)} %copy-done.1, bf16[256,1024]{1,0:T(8,128)(2,1)S(1)} %copy-done, ...), custom_call_target="tpu_custom_call" | custom-call | flops 301989888 | bytes 3145728 | tf_op jit(solution)/shard_map/pallas_call | solution.py:479
  44.2 1.4 %shard_map.126 = bf16[256,1024]{1,0:T(8,128)(2,1)} custom-call(s32[1]{0:T(128)} %bitcast.idx_ref, bf16[512,128]{1,0:T(8,128)(2,1)S(1)} %collective-permute-done.refs_0_, bf16[512,128]{1,0:T(8,128)(2,1)S(1)} %collective-permute-done.1.refs_1_, bf16[512,128]{1,0:T(8,128)(2,1)S(1)} %collective-permute-done.4.refs_2_.refs_0_, ...), custom_call_target="tpu_custom_call" | custom-call | flops 100663296 | bytes 1048576 | tf_op jit(solution)/shard_map/pallas_call | solution.py:499
  45.6 1.4 %shard_map.127 = bf16[256,512]{1,0:T(8,128)(2,1)} custom-call(s32[1]{0:T(128)} %bitcast.idx_ref, bf16[512,128]{1,0:T(8,128)(2,1)S(1)} %collective-permute-done.refs_0_, bf16[512,128]{1,0:T(8,128)(2,1)S(1)} %collective-permute-done.1.refs_1_, bf16[512,128]{1,0:T(8,128)(2,1)S(1)} %collective-permute-done.4.refs_2_.refs_0_, bf16[256,1024]{1,0:T(8,128)(2,1)S(1)} %copy-done, ...), custom_call_target="tpu_custom_call" | custom-call | flops 100663296 | bytes 524288 | tf_op jit(solution)/shard_map/pallas_call | solution.py:495
  47.0 1.3 %shard_map.134 = bf16[256,512]{1,0:T(8,128)(2,1)} custom-call(bf16[384,256]{1,0:T(8,128)(2,1)S(1)} %get-tuple-element.65.near_ref, bf16[128,256]{1,0:T(8,128)(2,1)S(1)} %get-tuple-element.67.far_ref, f32[128,384]{1,0:T(8,128)S(1)} %fusion.1.place_ref, bf16[512,384]{1,0:T(8,128)(2,1)S(1)} %get-tuple-element.44.w_ref), custom_call_target="tpu_custom_call" | custom-call | flops 100663296 | bytes 524288 | tf_op jit(solution)/shard_map/pallas_call | solution.py:503
  48.3 0.0 collective-permute-done.5.refs_1_
  48.3 0.0 copy-start.4
  48.3 0.1 shard_map.129
  48.4 1.4 %collective-permute-start.6 = (bf16[512,128]{1,0:T(8,128)(2,1)S(1)}, bf16[512,128]{1,0:T(8,128)(2,1)S(1)}, u32[]{:S(2)}, u32[]{:S(2)}) collective-permute-start(bf16[512,128]{1,0:T(8,128)(2,1)S(1)} %shard_map.129), channel_id=1, source_target_pairs={{0,4},{4,0},{8,12},{12,8},{16,20},{20,16},{24,28},{28,24},{1,5},{5... | collective-permute-start | bytes 393224 | tf_op jit(solution)/shard_map/ppermute | solution.py:52
  49.8 0.0 collective-permute-done.15
  49.8 0.7 %convert_add_fusion = f32[64,384]{1,0:T(8,128)} fusion(f32[64,384]{1,0:T(8,128)S(1)} %get-tuple-element.76, bf16[64,384]{1,0:T(8,128)(2,1)S(1)} %collective-permute-done.15), kind=kLoop, calls=%fused_computation.6 | loop fusion | flops 49152 | bytes 245760 | tf_op jit(solution)/shard_map/add | solution.py:474
  50.5 3.0 %collective-permute-done.6.refs_2_ = bf16[512,128]{1,0:T(8,128)(2,1)S(1)} collective-permute-done((bf16[512,128]{1,0:T(8,128)(2,1)S(1)}, bf16[512,128]{1,0:T(8,128)(2,1)S(1)}, u32[]{:S(2)}, u32[]{:S(2)}) %collective-permute-start.6) | collective-permute-done | bytes 131104 | tf_op jit(solution)/shard_map/ppermute | solution.py:52
  53.5 0.0 copy-done.4
  53.5 1.2 %shard_map.130 = (bf16[256,512]{1,0:T(8,128)(2,1)}, bf16[256,1024]{1,0:T(8,128)(2,1)}) custom-call(s32[1]{0:T(128)} %bitcast.idx_ref, bf16[512,128]{1,0:T(8,128)(2,1)S(1)} %collective-permute-done.4.refs_2_.refs_0_, bf16[512,128]{1,0:T(8,128)(2,1)S(1)} %collective-permute-done.5.refs_1_, bf16[512,128]{1,0:T(8,128)(2,1)S(1)} %collective-permute-done.6.refs_2_, ...), custom_call_target="tpu_custom_call" | custom-call | flops 67108864 | bytes 1572864 | tf_op jit(solution)/shard_map/pallas_call | solution.py:506
  (10 shorter events, 0.2 us)
Async XLA Ops:
  0.6 10.1 %copy-start.3 = (bf16[256,512]{1,0:T(8,128)(2,1)S(1)}, bf16[256,512]{1,0:T(8,128)(2,1)}, u32[]{:S(2)}) copy-start(bf16[256,512]{1,0:T(8,128)(2,1)} %q_ref.7) | copy-start | bytes 786436
  2.1 6.6 %collective-permute-start = (bf16[512,128]{1,0:T(8,128)(2,1)S(1)}, bf16[512,128]{1,0:T(8,128)(2,1)S(1)}, u32[]{:S(2)}, u32[]{:S(2)}) collective-permute-start(bf16[512,128]{1,0:T(8,128)(2,1)S(1)} %get-tuple-element.42), channel_id=1, source_target_pairs={{0,4},{4,0},{8,12},{12,8},{16,20},{20,16},{24,28},{28,24},{1,5},{5... | collective-permute-start | bytes 393224 | tf_op jit(solution)/shard_map/ppermute | solution.py:52
  5.2 5.5 %copy-start.1 = (bf16[256,1024]{1,0:T(8,128)(2,1)S(1)}, bf16[256,1024]{1,0:T(8,128)(2,1)}, u32[]{:S(2)}) copy-start(bf16[256,1024]{1,0:T(8,128)(2,1)} %refs_5_.1) | copy-start | bytes 1572868
  5.6 5.2 %copy-start = (bf16[256,1024]{1,0:T(8,128)(2,1)S(1)}, bf16[256,1024]{1,0:T(8,128)(2,1)}, u32[]{:S(2)}) copy-start(bf16[256,1024]{1,0:T(8,128)(2,1)} %refs_3_.3) | copy-start | bytes 1572868
  5.6 5.0 %collective-permute-start.2 = (bf16[192,256]{1,0:T(8,128)(2,1)S(1)}, bf16[192,256]{1,0:T(8,128)(2,1)S(1)}, u32[]{:S(2)}, u32[]{:S(2)}) collective-permute-start(bf16[192,256]{1,0:T(8,128)(2,1)S(1)} %get-tuple-element.47), channel_id=1, source_target_pairs={{0,2},{1,3},{2,0},{3,1},{4,6},{5,7},{6,4},{7,5},{8,10},{9,11},{10,... | collective-permute-start | bytes 294920 | tf_op jit(solution)/shard_map/ppermute | solution.py:52
  8.7 2.0 %copy-start.2 = (bf16[256,512]{1,0:T(8,128)(2,1)S(1)}, bf16[256,512]{1,0:T(8,128)(2,1)}, u32[]{:S(2)}) copy-start(bf16[256,512]{1,0:T(8,128)(2,1)} %refs_4_.1) | copy-start | bytes 786436
  8.7 5.0 %collective-permute-start.1 = (bf16[512,128]{1,0:T(8,128)(2,1)S(1)}, bf16[512,128]{1,0:T(8,128)(2,1)S(1)}, u32[]{:S(2)}, u32[]{:S(2)}) collective-permute-start(bf16[512,128]{1,0:T(8,128)(2,1)S(1)} %add_convert_fusion), channel_id=1, source_target_pairs={{0,8},{4,12},{8,0},{12,4},{16,24},{20,28},{24,16},{28,20},{1,9},{5... | collective-permute-start | bytes 393224 | tf_op jit(solution)/shard_map/ppermute | solution.py:52
  10.6 1.3 %collective-permute-start.3 = (bf16[96,256]{1,0:T(8,128)(2,1)S(1)}, bf16[96,256]{1,0:T(8,128)(2,1)S(1)}, u32[]{:S(2)}, u32[]{:S(2)}) collective-permute-start(bf16[96,256]{1,0:T(8,128)(2,1)S(1)} %get-tuple-element.49), channel_id=1, source_target_pairs={{0,1},{1,0},{2,3},{3,2},{4,5},{5,4},{6,7},{7,6},{8,9},{9,8},{10,11... | collective-permute-start | bytes 147464 | tf_op jit(solution)/shard_map/ppermute | solution.py:52
  13.8 8.0 %collective-permute-start.4 = (bf16[512,128]{1,0:T(8,128)(2,1)S(1)}, bf16[512,128]{1,0:T(8,128)(2,1)S(1)}, u32[]{:S(2)}, u32[]{:S(2)}) collective-permute-start(bf16[512,128]{1,0:T(8,128)(2,1)S(1)} %shard_map.123), channel_id=1, source_target_pairs={{0,16},{4,20},{8,24},{12,28},{16,0},{20,4},{24,8},{28,12},{1,17},{... | collective-permute-start | bytes 393224 | tf_op jit(solution)/shard_map/ppermute | solution.py:52
  16.7 7.3 %collective-permute-start.7 = (bf16[96,256]{1,0:T(8,128)(2,1)S(1)}, bf16[96,256]{1,0:T(8,128)(2,1)S(1)}, u32[]{:S(2)}, u32[]{:S(2)}) collective-permute-start(bf16[96,256]{1,0:T(8,128)(2,1)S(1)} %get-tuple-element.64), channel_id=1, source_target_pairs={{0,2},{1,3},{2,0},{3,1},{4,6},{5,7},{6,4},{7,5},{8,10},{9,11},{10,... | collective-permute-start | bytes 147464 | tf_op jit(solution)/shard_map/ppermute | solution.py:52
  22.4 3.8 %collective-permute-start.9 = (bf16[32,256]{1,0:T(8,128)(2,1)S(1)}, bf16[32,256]{1,0:T(8,128)(2,1)S(1)}, u32[]{:S(2)}, u32[]{:S(2)}) collective-permute-start(bf16[32,256]{1,0:T(8,128)(2,1)S(1)} %shard_map.132), channel_id=1, source_target_pairs={{0,2},{1,3},{2,0},{3,1},{4,6},{5,7},{6,4},{7,5},{8,10},{9,11},{10,... | collective-permute-start | bytes 49160 | tf_op jit(solution)/shard_map/ppermute | solution.py:52
  24.0 2.2 %collective-permute-start.8 = (bf16[192,256]{1,0:T(8,128)(2,1)S(1)}, bf16[192,256]{1,0:T(8,128)(2,1)S(1)}, u32[]{:S(2)}, u32[]{:S(2)}) collective-permute-start(bf16[192,256]{1,0:T(8,128)(2,1)S(1)} %pad_maximum_fusion.1), channel_id=1, source_target_pairs={{0,1},{1,0},{2,3},{3,2},{4,5},{5,4},{6,7},{7,6},{8,9},{9,8},{10,11... | collective-permute-start | bytes 294920 | tf_op jit(solution)/shard_map/ppermute | solution.py:52
  26.3 2.0 %collective-permute-start.10 = (bf16[64,256]{1,0:T(8,128)(2,1)S(1)}, bf16[64,256]{1,0:T(8,128)(2,1)S(1)}, u32[]{:S(2)}, u32[]{:S(2)}) collective-permute-start(bf16[64,256]{1,0:T(8,128)(2,1)S(1)} %pad_maximum_fusion.3), channel_id=1, source_target_pairs={{0,1},{1,0},{2,3},{3,2},{4,5},{5,4},{6,7},{7,6},{8,9},{9,8},{10,11... | collective-permute-start | bytes 98312 | tf_op jit(solution)/shard_map/ppermute | solution.py:52
  26.6 7.8 %collective-permute-start.11 = (bf16[256,384]{1,0:T(8,128)(2,1)S(1)}, bf16[256,384]{1,0:T(8,128)(2,1)S(1)}, u32[]{:S(2)}, u32[]{:S(2)}) collective-permute-start(bf16[256,384]{1,0:T(8,128)(2,1)S(1)} %get-tuple-element.69), channel_id=1, source_target_pairs={{0,4},{4,0},{8,12},{12,8},{16,20},{20,16},{24,28},{28,24},{1,5},{5... | collective-permute-start | bytes 589832 | tf_op jit(solution)/shard_map/ppermute | solution.py:52
  28.5 6.9 %collective-permute-start.13 = (bf16[256,128]{1,0:T(8,128)(2,1)S(1)}, bf16[256,128]{1,0:T(8,128)(2,1)S(1)}, u32[]{:S(2)}, u32[]{:S(2)}) collective-permute-start(bf16[256,128]{1,0:T(8,128)(2,1)S(1)} %get-tuple-element.73), channel_id=1, source_target_pairs={{0,4},{4,0},{8,12},{12,8},{16,20},{20,16},{24,28},{28,24},{1,5},{5... | collective-permute-start | bytes 196616 | tf_op jit(solution)/shard_map/ppermute | solution.py:52
  29.4 19.0 %collective-permute-start.5 = (bf16[512,128]{1,0:T(8,128)(2,1)S(1)}, bf16[512,128]{1,0:T(8,128)(2,1)S(1)}, u32[]{:S(2)}, u32[]{:S(2)}) collective-permute-start(bf16[512,128]{1,0:T(8,128)(2,1)S(1)} %shard_map.128), channel_id=1, source_target_pairs={{0,8},{4,12},{8,0},{12,4},{16,24},{20,28},{24,16},{28,20},{1,9},{5... | collective-permute-start | bytes 393224 | tf_op jit(solution)/shard_map/ppermute | solution.py:52
  34.5 5.0 %collective-permute-start.12 = (bf16[128,384]{1,0:T(8,128)(2,1)S(1)}, bf16[128,384]{1,0:T(8,128)(2,1)S(1)}, u32[]{:S(2)}, u32[]{:S(2)}) collective-permute-start(bf16[128,384]{1,0:T(8,128)(2,1)S(1)} %get-tuple-element.71), channel_id=1, source_target_pairs={{0,8},{4,12},{8,0},{12,4},{16,24},{20,28},{24,16},{28,20},{1,9},{5... | collective-permute-start | bytes 294920 | tf_op jit(solution)/shard_map/ppermute | solution.py:52
  35.4 4.1 %collective-permute-start.14 = (bf16[128,128]{1,0:T(8,128)(2,1)S(1)}, bf16[128,128]{1,0:T(8,128)(2,1)S(1)}, u32[]{:S(2)}, u32[]{:S(2)}) collective-permute-start(bf16[128,128]{1,0:T(8,128)(2,1)S(1)} %get-tuple-element.75), channel_id=1, source_target_pairs={{0,8},{4,12},{8,0},{12,4},{16,24},{20,28},{24,16},{28,20},{1,9},{5... | collective-permute-start | bytes 98312 | tf_op jit(solution)/shard_map/ppermute | solution.py:52
  39.9 9.9 %collective-permute-start.15 = (bf16[64,384]{1,0:T(8,128)(2,1)S(1)}, bf16[64,384]{1,0:T(8,128)(2,1)S(1)}, u32[]{:S(2)}, u32[]{:S(2)}) collective-permute-start(bf16[64,384]{1,0:T(8,128)(2,1)S(1)} %get-tuple-element.77), channel_id=1, source_target_pairs={{0,16},{4,20},{8,24},{12,28},{16,0},{20,4},{24,8},{28,12},{1,17},{... | collective-permute-start | bytes 147464 | tf_op jit(solution)/shard_map/ppermute | solution.py:52
  48.3 5.1 %copy-start.4 = (f32[8,64,128]{2,1,0:T(8,128)S(1)}, f32[8,64,128]{2,1,0:T(8,128)}, u32[]{:S(2)}) copy-start(f32[8,64,128]{2,1,0:T(8,128)} %param.13) | copy-start | bytes 786436
  48.4 5.0 %collective-permute-start.6 = (bf16[512,128]{1,0:T(8,128)(2,1)S(1)}, bf16[512,128]{1,0:T(8,128)(2,1)S(1)}, u32[]{:S(2)}, u32[]{:S(2)}) collective-permute-start(bf16[512,128]{1,0:T(8,128)(2,1)S(1)} %shard_map.129), channel_id=1, source_target_pairs={{0,4},{4,0},{8,12},{12,8},{16,20},{20,16},{24,28},{28,24},{1,5},{5... | collective-permute-start | bytes 393224 | tf_op jit(solution)/shard_map/ppermute | solution.py:52

commit v6 on v5

--- a/solution.py
+++ b/solution.py
@@ -257,7 +257,7 @@
                 total = total + x * (lw_ref[r:r + 1, :] * up)
             halves.append(total)
         cols = slice(pair * 2 * dk, (pair + 1) * 2 * dk)
-        dq_ref[:, cols] = jnp.concatenate(halves, axis=0).T.astype(BF16)
+        dq_ref[:, cols] = jnp.concatenate(halves, axis=0).astype(BF16).T
         copies.append(leave(dq_ref, dq_hbm, sems.at[pair], cols))
     for copy in copies:
         copy.wait()
@@ -277,7 +277,7 @@
             r = h * levels + first + m
             up = ((index >> m) & 1).astype(F32)
             total = total + tn(ups[m][rows, :], qt_ref[rows, :]) * (lw_ref[r:r + 1, :] * up)
-        out_ref[:, h * dv:(h + 1) * dv] = total.T.astype(BF16)
+        out_ref[:, h * dv:(h + 1) * dv] = total.astype(BF16).T
         if h % 2:
             copies.append(leave(out_ref, out_hbm, sems.at[h // 2], slice((h - 1) * dv, (h + 1) * dv)))
     for copy in copies:
@@ -294,23 +294,11 @@
     part_ways(nt(xt_ref[...], sorted_ref[...]), (idx_ref[0] & 1) == 1, send_ref, keep_ref, inner)
 
 
-def merge_kernel(bit, idx_ref, near_ref, near_got, far_ref, far_got, place_ref, send_ref, keep_ref):
+def merge_kernel(bit, inner, idx_ref, near_ref, near_got, far_ref, far_got, place_ref, send_ref, keep_ref):
     total = near_ref[...] + near_got[...].astype(F32) + lax.dot_general(
         far_ref[...] + far_got[...].astype(F32), place_ref[...], (((1,), (0,)), ((), ())),
         preferred_element_type=F32, precision=lax.Precision.HIGHEST)
-    part_ways(total, ((idx_ref[0] >> bit) & 1) == 1, send_ref, keep_ref, keep_ref.shape[0])
-
-
-def hidden_kernel(near_ref, far_ref, place_ref, w_ref, dx_hbm, dx_ref, sems):
-    gp = (near_ref[...].astype(F32) + tn(place_ref[...].astype(BF16), far_ref[...])).astype(BF16).T
-    half = dx_ref.shape[1] // 2
-    copies = []
-    for n in range(2):
-        cols = slice(n * half, (n + 1) * half)
-        dx_ref[:, cols] = nt(gp, w_ref[cols, :]).astype(BF16)
-        copies.append(leave(dx_ref, dx_hbm, sems.at[n], cols))
-    for copy in copies:
-        copy.wait()
+    part_ways(total, ((idx_ref[0] >> bit) & 1) == 1, send_ref, keep_ref, inner)
 
 
 def join_kernel(top, count, idx_ref, kv_ref, *refs):
@@ -342,8 +330,12 @@
 def final_kernel(dims, top, idx_ref, *refs):
     nh, dk, dv = dims
     gots = refs[:top + 1]
-    ds_ref, k_ref, v_ref, low_k, high_k, low_v, high_v, dk_hbm, dv_hbm, dk_ref, dv_ref, sems = refs[top + 1:]
-    copies = []
+    (ds_ref, k_ref, v_ref, low_k, high_k, low_v, high_v, near_ref, far_ref, place_ref, w_ref,
+     dx_hbm, dk_hbm, dv_hbm, dx_ref, dk_ref, dv_ref, sems) = refs[top + 1:]
+    gp = (near_ref[...].astype(F32) + tn(place_ref[...].astype(BF16), far_ref[...])).astype(BF16)
+    dx_ref[...] = lax.dot_general(
+        gp, w_ref[...], (((0,), (1,)), ((), ())), preferred_element_type=F32).astype(BF16)
+    copies = [leave(dx_ref, dx_hbm, sems.at[nh], slice(0, dx_ref.shape[1]))]
     upper = ((idx_ref[0] >> top) & 1) == 1
     zero = jnp.zeros((dk, dv), BF16)
     for pair in range(nh // 2):
@@ -447,31 +439,32 @@
                     rows * dv)(idx, *gots, gu)[0]
         gots.append(swap(down, "seq", bit))
 
-    def reduce(gathered, n_cols):
+    def begin(gathered, n_cols):
         send, keep, ordered = call(
             functools.partial(wgrad_kernel, head_bits, per),
             [S((width // 2, n_cols), BF16), S((width // 2, n_cols), F32), S((n_cols, tokens), BF16)],
             [SM] * 2 + [VM] * 2, 2 * tokens * width * n_cols)(idx, head_idx, xt, gathered)
-        got = swap(send, "seq", 0)
-        for bit in range(1, top):
-            n = keep.shape[0] // 2
-            send, keep = call(
-                functools.partial(fold_kernel, bit, per), [S((n, n_cols), BF16), S((n, n_cols), F32)],
-                [SM] + [VM] * 2, n * n_cols)(idx, keep, got)
-            got = swap(send, "seq", bit)
-        return keep, got, ordered
-
-    near_w, near_got, near_all = reduce(gather_heads(near, head_bits), cols)
-    far_w, far_got, far_all = reduce(gather_heads(far_rows, head_bits), far_cols)
+        return keep, swap(send, "seq", 0), ordered
+
+    near_w, near_got, near_all = begin(gather_heads(near, head_bits), cols)
+    far_w, far_got, far_all = begin(gather_heads(far_rows, head_bits), far_cols)
     col = jnp.arange(cols, dtype=jnp.int32)[None, :]
     row = jnp.arange(far_cols, dtype=jnp.int32)[:, None]
     within = row % far_own
     at = (row // far_own * nh + within % nh) * levels + first + within // nh
     place = ((at == col) & (within < far)).astype(F32)
+    n = width // 4
     send, keep = call(
-        functools.partial(merge_kernel, top), [S((per, cols), BF16), S((per, cols), F32)], [SM] + [VM] * 5,
-        4 * per * far_cols * cols)(idx, near_w, near_got, far_w, far_got, place)
-    d_w = keep + swap(send, "seq", top).astype(F32)
+        functools.partial(merge_kernel, 1, per), [S((n, cols), BF16), S((n, cols), F32)], [SM] + [VM] * 5,
+        4 * n * far_cols * cols)(idx, near_w, near_got, far_w, far_got, place)
+    got = swap(send, "seq", 1)
+    for bit in range(2, seq_bits):
+        n = n // 2
+        send, keep = call(
+            functools.partial(fold_kernel, bit, per), [S((n, cols), BF16), S((n, cols), F32)],
+            [SM] + [VM] * 2, n * cols)(idx, keep, got)
+        got = swap(send, "seq", bit)
+    d_w = keep + got.astype(F32)
 
     half = nh // 4
     local = []
@@ -500,13 +493,10 @@
         functools.partial(out_kernel, dims, levels, first, seq_bits), results(broad),
         [SM] + [VM] * (seq_bits + 4), 2 * tokens * rows * dv * seq_bits, **leaving([broad], nh // 2))(
             idx, *ups, qt, lw, *out_l)[0]
-    d_hidden = call(
-        hidden_kernel, results((tokens, width)), [VM] * 4, 2 * tokens * width * cols,
-        **leaving([(tokens, width)], 2))(near_all, far_all, place, w_near)[0]
-    d_keys, d_values = call(
-        functools.partial(final_kernel, dims, top), results(narrow, broad), [SM] + [VM] * (top + 8),
-        4 * tokens * rows * dv, **leaving([narrow, broad], nh))(
-            idx, *gots, d_state.reshape(rows, dv), keys, values, *dk_l, *dv_l)
+    d_hidden, d_keys, d_values = call(
+        functools.partial(final_kernel, dims, top), results((tokens, width), narrow, broad), [SM] + [VM] * (top + 12),
+        4 * tokens * rows * dv, **leaving([(tokens, width), narrow, broad], nh + 1))(
+            idx, *gots, d_state.reshape(rows, dv), keys, values, *dk_l, *dv_l, near_all, far_all, place, w_near)
     return (out, d_queries, d_keys, d_values, d_hidden, d_w)
 
 

time: 54.8 us -> 55.6 us (1.015)
  waiting for transfers between devices: 18.6 us -> 21.6 us
  starting transfers between devices: 21.3 us -> 19.9 us
  Pallas kernels: 13 us -> 12.2 us
    ppermute x16 -> x15, waiting for transfers between devices: 18.6 us -> 21.6 us  [swap(): return lax.ppermute(value, axis, pairs)]
    ppermute x16 -> x15, starting transfers between devices: 21.3 us -> 19.9 us  [swap(): return lax.ppermute(value, axis, pairs)]
    pallas_call x7 -> x5, Pallas kernels: 3.46 us -> 2.71 us  [the longest x1 1.62 us: body(): call(functools.partial(final_kernel, dims, top), results((tokens, width),...]
  transfers between devices with their start and end apart: 16 -> 15, of which waited for: 9 -> 9; matrix products, arithmetic and copies ran while one was open for 2% -> 1% of each run, Pallas kernels for 19% -> 16%
where the time goes in v6:
time: 55.6 us; the launch traced here: 55.4 us
  waiting for transfers between devices  21.6 us (39%)
  starting transfers between devices  19.9 us (36%)
  Pallas kernels  12.2 us (22%)
  between operations  0.87 us (2%)
  other arithmetic  0.83 us (1%)
    ppermute x15, waiting for transfers between devices, swap(): return lax.ppermute(value, axis, pairs)  21.6 us
    ppermute x15, starting transfers between devices, swap(): return lax.ppermute(value, axis, pairs)  19.9 us
    pallas_call x2, Pallas kernels, body(): call(functools.partial(local_kernel, dims, levels, tuple(range(part * hal...  2.81 us
    pallas_call x1, Pallas kernels, body(): call(functools.partial(final_kernel, dims, top), results((tokens, width),...  1.62 us
    pallas_call x1, Pallas kernels, body(): call(functools.partial(state_kernel, dims), [S((rows, dv), F32), S((rows,...  1.47 us
    pallas_call x1, Pallas kernels, body(): call(functools.partial(query_kernel, dims, levels, first, seq_bits), resu...  1.39 us
    pallas_call x1, Pallas kernels, body(): call(functools.partial(out_kernel, dims, levels, first, seq_bits), result...  1.38 us
  transfers between devices with their start and end apart: 15, of which 9 were waited for; matrix products, arithmetic and copies ran while one was open for 1% of the time, Pallas kernels for 16%

profile of v6, /device:TPU:0, one launch (start us, length us, event | category | flops | bytes accessed | tf_op | source)
XLA Modules:
  0.0 55.4 jit_solution(8915960620481023551)
XLA Ops:
  0.6 0.0 copy-start.3
  0.6 1.5 %shard_map.118 = (f32[512,128]{1,0:T(8,128)S(1)}, bf16[512,128]{1,0:T(8,128)(2,1)S(1)}, bf16[512,384]{1,0:T(8,128)(2,1)S(1)}, bf16[256,512]{1,0:T(8,128)(2,1)S(1)}) custom-call(s32[1]{0:T(128)} %bitcast.idx_ref, s32[1]{0:T(128)} %bitcast.1.head_ref.idx_ref, bf16[256,512]{1,0:T(8,128)(2,1)} %refs_4_.1, bf16[256,1024]{1,0:T(8,128)(2,1)} %refs_5_.1, ...), custom_call_target="tpu_custom_call" | custom-call | flops 33554432 | bytes 2097152 | tf_op jit(solution)/shard_map/pallas_call | solution.py:391
  2.1 3.1 %collective-permute-start = (bf16[512,128]{1,0:T(8,128)(2,1)S(1)}, bf16[512,128]{1,0:T(8,128)(2,1)S(1)}, u32[]{:S(2)}, u32[]{:S(2)}) collective-permute-start(bf16[512,128]{1,0:T(8,128)(2,1)S(1)} %get-tuple-element.41), channel_id=1, source_target_pairs={{0,4},{4,0},{8,12},{12,8},{16,20},{20,16},{24,28},{28,24},{1,5},{5... | collective-permute-start | bytes 393224 | tf_op jit(solution)/shard_map/ppermute | solution.py:52
  5.2 0.0 copy-start.1
  5.2 0.4 shard_map.119
  5.6 0.0 copy-start
  5.6 1.6 %collective-permute-start.2 = (bf16[192,256]{1,0:T(8,128)(2,1)S(1)}, bf16[192,256]{1,0:T(8,128)(2,1)S(1)}, u32[]{:S(2)}, u32[]{:S(2)}) collective-permute-start(bf16[192,256]{1,0:T(8,128)(2,1)S(1)} %get-tuple-element.46), channel_id=1, source_target_pairs={{0,2},{1,3},{2,0},{3,1},{4,6},{5,7},{6,4},{7,5},{8,10},{9,11},{10,... | collective-permute-start | bytes 294920 | tf_op jit(solution)/shard_map/ppermute | solution.py:52
  7.1 1.5 %collective-permute-done.refs_0_ = bf16[512,128]{1,0:T(8,128)(2,1)S(1)} collective-permute-done((bf16[512,128]{1,0:T(8,128)(2,1)S(1)}, bf16[512,128]{1,0:T(8,128)(2,1)S(1)}, u32[]{:S(2)}, u32[]{:S(2)}) %collective-permute-start) | collective-permute-done | bytes 131104 | tf_op jit(solution)/shard_map/ppermute | solution.py:52
  8.7 0.0 copy-start.2
  8.7 1.9 %collective-permute-start.1 = (bf16[512,128]{1,0:T(8,128)(2,1)S(1)}, bf16[512,128]{1,0:T(8,128)(2,1)S(1)}, u32[]{:S(2)}, u32[]{:S(2)}) collective-permute-start(bf16[512,128]{1,0:T(8,128)(2,1)S(1)} %add_convert_fusion), channel_id=1, source_target_pairs={{0,8},{4,12},{8,0},{12,4},{16,24},{20,28},{24,16},{28,20},{1,9},{5... | collective-permute-start | bytes 393224 | tf_op jit(solution)/shard_map/ppermute | solution.py:52
  10.6 0.0 collective-permute-done.2.got_ref
  10.6 0.1 collective-permute-start.3
  10.7 0.0 copy-done.3
  10.7 0.0 copy-done.1
  10.7 0.0 copy-done
  10.7 0.0 copy-done.2
  10.8 0.8 %shard_map.121.gl_ref = f32[96,256]{1,0:T(8,128)S(1)} custom-call(bf16[256,512]{1,0:T(8,128)(2,1)S(1)} %copy-done.2, bf16[256,512]{1,0:T(8,128)(2,1)S(1)} %copy-done.3, bf16[256,1024]{1,0:T(8,128)(2,1)S(1)} %copy-done.1, bf16[256,1024]{1,0:T(8,128)(2,1)S(1)} %copy-done), custom_call_target="tpu_custom_call" | custom-call | flops 201326592 | bytes 196608 | tf_op jit(solution)/shard_map/pallas_call | solution.py:420
  11.5 0.4 collective-permute-done.3.got_ref
  11.9 0.4 shard_map.122
  12.4 1.4 %collective-permute-done.1.refs_1_ = bf16[512,128]{1,0:T(8,128)(2,1)S(1)} collective-permute-done((bf16[512,128]{1,0:T(8,128)(2,1)S(1)}, bf16[512,128]{1,0:T(8,128)(2,1)S(1)}, u32[]{:S(2)}, u32[]{:S(2)}) %collective-permute-start.1) | collective-permute-done | bytes 131104 | tf_op jit(solution)/shard_map/ppermute | solution.py:52
  13.8 2.8 %collective-permute-start.4 = (bf16[512,128]{1,0:T(8,128)(2,1)S(1)}, bf16[512,128]{1,0:T(8,128)(2,1)S(1)}, u32[]{:S(2)}, u32[]{:S(2)}) collective-permute-start(bf16[512,128]{1,0:T(8,128)(2,1)S(1)} %shard_map.123), channel_id=1, source_target_pairs={{0,16},{4,20},{8,24},{12,28},{16,0},{20,4},{24,8},{28,12},{1,17},{... | collective-permute-start | bytes 393224 | tf_op jit(solution)/shard_map/ppermute | solution.py:52
  16.7 1.5 %collective-permute-start.7 = (bf16[96,256]{1,0:T(8,128)(2,1)S(1)}, bf16[96,256]{1,0:T(8,128)(2,1)S(1)}, u32[]{:S(2)}, u32[]{:S(2)}) collective-permute-start(bf16[96,256]{1,0:T(8,128)(2,1)S(1)} %get-tuple-element.61), channel_id=1, source_target_pairs={{0,2},{1,3},{2,0},{3,1},{4,6},{5,7},{6,4},{7,5},{8,10},{9,11},{10,... | collective-permute-start | bytes 147464 | tf_op jit(solution)/shard_map/ppermute | solution.py:52
  18.2 3.6 %collective-permute-done.4.refs_2_.refs_0_ = bf16[512,128]{1,0:T(8,128)(2,1)S(1)} collective-permute-done((bf16[512,128]{1,0:T(8,128)(2,1)S(1)}, bf16[512,128]{1,0:T(8,128)(2,1)S(1)}, u32[]{:S(2)}, u32[]{:S(2)}) %collective-permute-start.4) | collective-permute-done | bytes 131104 | tf_op jit(solution)/shard_map/ppermute | solution.py:52
  21.8 0.7 %shard_map.131 = bf16[32,256]{1,0:T(8,128)(2,1)S(1)} custom-call(s32[1]{0:T(128)} %bitcast.idx_ref, bf16[512,128]{1,0:T(8,128)(2,1)S(1)} %collective-permute-done.refs_0_, bf16[512,128]{1,0:T(8,128)(2,1)S(1)} %collective-permute-done.1.refs_1_, bf16[512,128]{1,0:T(8,128)(2,1)S(1)} %collective-permute-done.4.refs_2_.refs_0_, bf16[256,1024]{1,0:T(8,128)(2,1)S(1)} %copy-done, ...), custom_call_target="tpu_custom_call" | custom-call | flops 100663296 | bytes 32768 | tf_op jit(solution)/shard_map/pallas_call | solution.py:433
  22.5 1.6 %collective-permute-start.9 = (bf16[32,256]{1,0:T(8,128)(2,1)S(1)}, bf16[32,256]{1,0:T(8,128)(2,1)S(1)}, u32[]{:S(2)}, u32[]{:S(2)}) collective-permute-start(bf16[32,256]{1,0:T(8,128)(2,1)S(1)} %shard_map.131), channel_id=1, source_target_pairs={{0,2},{1,3},{2,0},{3,1},{4,6},{5,7},{6,4},{7,5},{8,10},{9,11},{10,... | collective-permute-start | bytes 49160 | tf_op jit(solution)/shard_map/ppermute | solution.py:52
  24.0 0.0 collective-permute-done.7
  24.0 0.1 collective-permute-start.8
  24.1 2.2 %collective-permute-done.9 = bf16[32,256]{1,0:T(8,128)(2,1)S(1)} collective-permute-done((bf16[32,256]{1,0:T(8,128)(2,1)S(1)}, bf16[32,256]{1,0:T(8,128)(2,1)S(1)}, u32[]{:S(2)}, u32[]{:S(2)}) %collective-permute-start.9) | collective-permute-done | bytes 16416 | tf_op jit(solution)/shard_map/ppermute | solution.py:52
  26.3 0.0 collective-permute-start.10
  26.3 0.0 collective-permute-done.8
  26.3 0.3 shard_map.130
  26.7 1.6 %collective-permute-start.11 = (bf16[256,384]{1,0:T(8,128)(2,1)S(1)}, bf16[256,384]{1,0:T(8,128)(2,1)S(1)}, u32[]{:S(2)}, u32[]{:S(2)}) collective-permute-start(bf16[256,384]{1,0:T(8,128)(2,1)S(1)} %get-tuple-element.69), channel_id=1, source_target_pairs={{0,4},{4,0},{8,12},{12,8},{16,20},{20,16},{24,28},{28,24},{1,5},{5... | collective-permute-start | bytes 589832 | tf_op jit(solution)/shard_map/ppermute | solution.py:52
  28.2 0.0 collective-permute-done.10
  28.3 0.2 shard_map.132
  28.5 0.8 %collective-permute-start.12 = (bf16[256,128]{1,0:T(8,128)(2,1)S(1)}, bf16[256,128]{1,0:T(8,128)(2,1)S(1)}, u32[]{:S(2)}, u32[]{:S(2)}) collective-permute-start(bf16[256,128]{1,0:T(8,128)(2,1)S(1)} %get-tuple-element.71), channel_id=1, source_target_pairs={{0,4},{4,0},{8,12},{12,8},{16,20},{20,16},{24,28},{28,24},{1,5},{5... | collective-permute-start | bytes 196616 | tf_op jit(solution)/shard_map/ppermute | solution.py:52
  29.3 0.1 fusion.1.refs_12_.place_ref
  29.4 5.1 %collective-permute-done.11.near_got = bf16[256,384]{1,0:T(8,128)(2,1)S(1)} collective-permute-done((bf16[256,384]{1,0:T(8,128)(2,1)S(1)}, bf16[256,384]{1,0:T(8,128)(2,1)S(1)}, u32[]{:S(2)}, u32[]{:S(2)}) %collective-permute-start.11) | collective-permute-done | bytes 196640 | tf_op jit(solution)/shard_map/ppermute | solution.py:52
  34.5 0.9 %collective-permute-done.12.far_got = bf16[256,128]{1,0:T(8,128)(2,1)S(1)} collective-permute-done((bf16[256,128]{1,0:T(8,128)(2,1)S(1)}, bf16[256,128]{1,0:T(8,128)(2,1)S(1)}, u32[]{:S(2)}, u32[]{:S(2)}) %collective-permute-start.12) | collective-permute-done | bytes 65568 | tf_op jit(solution)/shard_map/ppermute | solution.py:52
  35.4 0.5 shard_map.134
  35.9 0.5 collective-permute-start.13
  36.4 0.1 shard_map.128
  36.5 1.7 %collective-permute-start.5 = (bf16[512,128]{1,0:T(8,128)(2,1)S(1)}, bf16[512,128]{1,0:T(8,128)(2,1)S(1)}, u32[]{:S(2)}, u32[]{:S(2)}) collective-permute-start(bf16[512,128]{1,0:T(8,128)(2,1)S(1)} %shard_map.128), channel_id=1, source_target_pairs={{0,8},{4,12},{8,0},{12,4},{16,24},{20,28},{24,16},{28,20},{1,9},{5... | collective-permute-start | bytes 393224 | tf_op jit(solution)/shard_map/ppermute | solution.py:52
  38.1 3.5 %collective-permute-done.13.got_ref = bf16[128,384]{1,0:T(8,128)(2,1)S(1)} collective-permute-done((bf16[128,384]{1,0:T(8,128)(2,1)S(1)}, bf16[128,384]{1,0:T(8,128)(2,1)S(1)}, u32[]{:S(2)}, u32[]{:S(2)}) %collective-permute-start.13) | collective-permute-done | bytes 98336 | tf_op jit(solution)/shard_map/ppermute | solution.py:52
  41.7 1.4 %collective-permute-start.14 = (bf16[64,384]{1,0:T(8,128)(2,1)S(1)}, bf16[64,384]{1,0:T(8,128)(2,1)S(1)}, u32[]{:S(2)}, u32[]{:S(2)}) collective-permute-start(bf16[64,384]{1,0:T(8,128)(2,1)S(1)} %get-tuple-element.75), channel_id=1, source_target_pairs={{0,16},{4,20},{8,24},{12,28},{16,0},{20,4},{24,8},{28,12},{1,17},{... | collective-permute-start | bytes 147464 | tf_op jit(solution)/shard_map/ppermute | solution.py:52
  43.1 1.4 %shard_map.124 = (f32[512,256]{1,0:T(8,128)S(1)}, f32[256,256]{1,0:T(8,128)S(1)}, f32[256,256]{1,0:T(8,128)S(1)}, f32[256,512]{1,0:T(8,128)S(1)}) custom-call(bf16[256,512]{1,0:T(8,128)(2,1)S(1)} %copy-done.2, bf16[256,512]{1,0:T(8,128)(2,1)S(1)} %copy-done.3, bf16[256,1024]{1,0:T(8,128)(2,1)S(1)} %copy-done.1, bf16[256,1024]{1,0:T(8,128)(2,1)S(1)} %copy-done, ...), custom_call_target="tpu_custom_call" | custom-call | flops 301989888 | bytes 3145728 | tf_op jit(solution)/shard_map/pallas_call | solution.py:472
  44.5 1.4 %shard_map.125 = (f32[512,256]{1,0:T(8,128)S(1)}, f32[256,256]{1,0:T(8,128)S(1)}, f32[256,256]{1,0:T(8,128)S(1)}, f32[256,512]{1,0:T(8,128)S(1)}) custom-call(bf16[256,512]{1,0:T(8,128)(2,1)S(1)} %copy-done.2, bf16[256,512]{1,0:T(8,128)(2,1)S(1)} %copy-done.3, bf16[256,1024]{1,0:T(8,128)(2,1)S(1)} %copy-done.1, bf16[256,1024]{1,0:T(8,128)(2,1)S(1)} %copy-done, ...), custom_call_target="tpu_custom_call" | custom-call | flops 301989888 | bytes 3145728 | tf_op jit(solution)/shard_map/pallas_call | solution.py:472
  45.9 1.4 %shard_map.126 = bf16[256,1024]{1,0:T(8,128)(2,1)} custom-call(s32[1]{0:T(128)} %bitcast.idx_ref, bf16[512,128]{1,0:T(8,128)(2,1)S(1)} %collective-permute-done.refs_0_, bf16[512,128]{1,0:T(8,128)(2,1)S(1)} %collective-permute-done.1.refs_1_, bf16[512,128]{1,0:T(8,128)(2,1)S(1)} %collective-permute-done.4.refs_2_.refs_0_, ...), custom_call_target="tpu_custom_call" | custom-call | flops 100663296 | bytes 1048576 | tf_op jit(solution)/shard_map/pallas_call | solution.py:492
  47.3 1.4 %shard_map.127 = bf16[256,512]{1,0:T(8,128)(2,1)} custom-call(s32[1]{0:T(128)} %bitcast.idx_ref, bf16[512,128]{1,0:T(8,128)(2,1)S(1)} %collective-permute-done.refs_0_, bf16[512,128]{1,0:T(8,128)(2,1)S(1)} %collective-permute-done.1.refs_1_, bf16[512,128]{1,0:T(8,128)(2,1)S(1)} %collective-permute-done.4.refs_2_.refs_0_, bf16[256,1024]{1,0:T(8,128)(2,1)S(1)} %copy-done, ...), custom_call_target="tpu_custom_call" | custom-call | flops 100663296 | bytes 524288 | tf_op jit(solution)/shard_map/pallas_call | solution.py:488
  48.7 0.0 collective-permute-done.5.refs_1_
  48.7 0.0 copy-start.4
  48.7 0.1 shard_map.129
  48.8 1.4 %collective-permute-start.6 = (bf16[512,128]{1,0:T(8,128)(2,1)S(1)}, bf16[512,128]{1,0:T(8,128)(2,1)S(1)}, u32[]{:S(2)}, u32[]{:S(2)}) collective-permute-start(bf16[512,128]{1,0:T(8,128)(2,1)S(1)} %shard_map.129), channel_id=1, source_target_pairs={{0,4},{4,0},{8,12},{12,8},{16,20},{20,16},{24,28},{28,24},{1,5},{5... | collective-permute-start | bytes 393224 | tf_op jit(solution)/shard_map/ppermute | solution.py:52
  50.2 0.0 collective-permute-done.14
  50.2 0.7 %convert_add_fusion = f32[64,384]{1,0:T(8,128)} fusion(f32[64,384]{1,0:T(8,128)S(1)} %get-tuple-element.74, bf16[64,384]{1,0:T(8,128)(2,1)S(1)} %collective-permute-done.14), kind=kLoop, calls=%fused_computation.6 | loop fusion | flops 49152 | bytes 245760 | tf_op jit(solution)/shard_map/add | solution.py:467
  50.8 3.0 %collective-permute-done.6.refs_2_ = bf16[512,128]{1,0:T(8,128)(2,1)S(1)} collective-permute-done((bf16[512,128]{1,0:T(8,128)(2,1)S(1)}, bf16[512,128]{1,0:T(8,128)(2,1)S(1)}, u32[]{:S(2)}, u32[]{:S(2)}) %collective-permute-start.6) | collective-permute-done | bytes 131104 | tf_op jit(solution)/shard_map/ppermute | solution.py:52
  53.8 0.0 copy-done.4
  53.8 1.6 %shard_map.133 = (bf16[256,512]{1,0:T(8,128)(2,1)}, bf16[256,512]{1,0:T(8,128)(2,1)}, bf16[256,1024]{1,0:T(8,128)(2,1)}) custom-call(s32[1]{0:T(128)} %bitcast.idx_ref, bf16[512,128]{1,0:T(8,128)(2,1)S(1)} %collective-permute-done.4.refs_2_.refs_0_, bf16[512,128]{1,0:T(8,128)(2,1)S(1)} %collective-permute-done.5.refs_1_, ...), custom_call_target="tpu_custom_call" | custom-call | flops 67108864 | bytes 2097152 | tf_op jit(solution)/shard_map/pallas_call | solution.py:496
  (10 shorter events, 0.2 us)
Async XLA Ops:
  0.6 10.1 %copy-start.3 = (bf16[256,512]{1,0:T(8,128)(2,1)S(1)}, bf16[256,512]{1,0:T(8,128)(2,1)}, u32[]{:S(2)}) copy-start(bf16[256,512]{1,0:T(8,128)(2,1)} %q_ref.7) | copy-start | bytes 786436
  2.1 6.6 %collective-permute-start = (bf16[512,128]{1,0:T(8,128)(2,1)S(1)}, bf16[512,128]{1,0:T(8,128)(2,1)S(1)}, u32[]{:S(2)}, u32[]{:S(2)}) collective-permute-start(bf16[512,128]{1,0:T(8,128)(2,1)S(1)} %get-tuple-element.41), channel_id=1, source_target_pairs={{0,4},{4,0},{8,12},{12,8},{16,20},{20,16},{24,28},{28,24},{1,5},{5... | collective-permute-start | bytes 393224 | tf_op jit(solution)/shard_map/ppermute | solution.py:52
  5.2 5.5 %copy-start.1 = (bf16[256,1024]{1,0:T(8,128)(2,1)S(1)}, bf16[256,1024]{1,0:T(8,128)(2,1)}, u32[]{:S(2)}) copy-start(bf16[256,1024]{1,0:T(8,128)(2,1)} %refs_5_.1) | copy-start | bytes 1572868
  5.6 5.2 %copy-start = (bf16[256,1024]{1,0:T(8,128)(2,1)S(1)}, bf16[256,1024]{1,0:T(8,128)(2,1)}, u32[]{:S(2)}) copy-start(bf16[256,1024]{1,0:T(8,128)(2,1)} %refs_3_.3) | copy-start | bytes 1572868
  5.6 5.0 %collective-permute-start.2 = (bf16[192,256]{1,0:T(8,128)(2,1)S(1)}, bf16[192,256]{1,0:T(8,128)(2,1)S(1)}, u32[]{:S(2)}, u32[]{:S(2)}) collective-permute-start(bf16[192,256]{1,0:T(8,128)(2,1)S(1)} %get-tuple-element.46), channel_id=1, source_target_pairs={{0,2},{1,3},{2,0},{3,1},{4,6},{5,7},{6,4},{7,5},{8,10},{9,11},{10,... | collective-permute-start | bytes 294920 | tf_op jit(solution)/shard_map/ppermute | solution.py:52
  8.7 2.0 %copy-start.2 = (bf16[256,512]{1,0:T(8,128)(2,1)S(1)}, bf16[256,512]{1,0:T(8,128)(2,1)}, u32[]{:S(2)}) copy-start(bf16[256,512]{1,0:T(8,128)(2,1)} %refs_4_.1) | copy-start | bytes 786436
  8.7 5.0 %collective-permute-start.1 = (bf16[512,128]{1,0:T(8,128)(2,1)S(1)}, bf16[512,128]{1,0:T(8,128)(2,1)S(1)}, u32[]{:S(2)}, u32[]{:S(2)}) collective-permute-start(bf16[512,128]{1,0:T(8,128)(2,1)S(1)} %add_convert_fusion), channel_id=1, source_target_pairs={{0,8},{4,12},{8,0},{12,4},{16,24},{20,28},{24,16},{28,20},{1,9},{5... | collective-permute-start | bytes 393224 | tf_op jit(solution)/shard_map/ppermute | solution.py:52
  10.6 1.3 %collective-permute-start.3 = (bf16[96,256]{1,0:T(8,128)(2,1)S(1)}, bf16[96,256]{1,0:T(8,128)(2,1)S(1)}, u32[]{:S(2)}, u32[]{:S(2)}) collective-permute-start(bf16[96,256]{1,0:T(8,128)(2,1)S(1)} %get-tuple-element.48), channel_id=1, source_target_pairs={{0,1},{1,0},{2,3},{3,2},{4,5},{5,4},{6,7},{7,6},{8,9},{9,8},{10,11... | collective-permute-start | bytes 147464 | tf_op jit(solution)/shard_map/ppermute | solution.py:52
  13.8 8.0 %collective-permute-start.4 = (bf16[512,128]{1,0:T(8,128)(2,1)S(1)}, bf16[512,128]{1,0:T(8,128)(2,1)S(1)}, u32[]{:S(2)}, u32[]{:S(2)}) collective-permute-start(bf16[512,128]{1,0:T(8,128)(2,1)S(1)} %shard_map.123), channel_id=1, source_target_pairs={{0,16},{4,20},{8,24},{12,28},{16,0},{20,4},{24,8},{28,12},{1,17},{... | collective-permute-start | bytes 393224 | tf_op jit(solution)/shard_map/ppermute | solution.py:52
  16.7 7.4 %collective-permute-start.7 = (bf16[96,256]{1,0:T(8,128)(2,1)S(1)}, bf16[96,256]{1,0:T(8,128)(2,1)S(1)}, u32[]{:S(2)}, u32[]{:S(2)}) collective-permute-start(bf16[96,256]{1,0:T(8,128)(2,1)S(1)} %get-tuple-element.61), channel_id=1, source_target_pairs={{0,2},{1,3},{2,0},{3,1},{4,6},{5,7},{6,4},{7,5},{8,10},{9,11},{10,... | collective-permute-start | bytes 147464 | tf_op jit(solution)/shard_map/ppermute | solution.py:52
  22.5 3.8 %collective-permute-start.9 = (bf16[32,256]{1,0:T(8,128)(2,1)S(1)}, bf16[32,256]{1,0:T(8,128)(2,1)S(1)}, u32[]{:S(2)}, u32[]{:S(2)}) collective-permute-start(bf16[32,256]{1,0:T(8,128)(2,1)S(1)} %shard_map.131), channel_id=1, source_target_pairs={{0,2},{1,3},{2,0},{3,1},{4,6},{5,7},{6,4},{7,5},{8,10},{9,11},{10,... | collective-permute-start | bytes 49160 | tf_op jit(solution)/shard_map/ppermute | solution.py:52
  24.0 2.2 %collective-permute-start.8 = (bf16[192,256]{1,0:T(8,128)(2,1)S(1)}, bf16[192,256]{1,0:T(8,128)(2,1)S(1)}, u32[]{:S(2)}, u32[]{:S(2)}) collective-permute-start(bf16[192,256]{1,0:T(8,128)(2,1)S(1)} %pad_maximum_fusion.1), channel_id=1, source_target_pairs={{0,1},{1,0},{2,3},{3,2},{4,5},{5,4},{6,7},{7,6},{8,9},{9,8},{10,11... | collective-permute-start | bytes 294920 | tf_op jit(solution)/shard_map/ppermute | solution.py:52
  26.3 2.0 %collective-permute-start.10 = (bf16[64,256]{1,0:T(8,128)(2,1)S(1)}, bf16[64,256]{1,0:T(8,128)(2,1)S(1)}, u32[]{:S(2)}, u32[]{:S(2)}) collective-permute-start(bf16[64,256]{1,0:T(8,128)(2,1)S(1)} %pad_maximum_fusion.3), channel_id=1, source_target_pairs={{0,1},{1,0},{2,3},{3,2},{4,5},{5,4},{6,7},{7,6},{8,9},{9,8},{10,11... | collective-permute-start | bytes 98312 | tf_op jit(solution)/shard_map/ppermute | solution.py:52
  26.7 7.8 %collective-permute-start.11 = (bf16[256,384]{1,0:T(8,128)(2,1)S(1)}, bf16[256,384]{1,0:T(8,128)(2,1)S(1)}, u32[]{:S(2)}, u32[]{:S(2)}) collective-permute-start(bf16[256,384]{1,0:T(8,128)(2,1)S(1)} %get-tuple-element.69), channel_id=1, source_target_pairs={{0,4},{4,0},{8,12},{12,8},{16,20},{20,16},{24,28},{28,24},{1,5},{5... | collective-permute-start | bytes 589832 | tf_op jit(solution)/shard_map/ppermute | solution.py:52
  28.5 6.9 %collective-permute-start.12 = (bf16[256,128]{1,0:T(8,128)(2,1)S(1)}, bf16[256,128]{1,0:T(8,128)(2,1)S(1)}, u32[]{:S(2)}, u32[]{:S(2)}) collective-permute-start(bf16[256,128]{1,0:T(8,128)(2,1)S(1)} %get-tuple-element.71), channel_id=1, source_target_pairs={{0,4},{4,0},{8,12},{12,8},{16,20},{20,16},{24,28},{28,24},{1,5},{5... | collective-permute-start | bytes 196616 | tf_op jit(solution)/shard_map/ppermute | solution.py:52
  35.9 5.7 %collective-permute-start.13 = (bf16[128,384]{1,0:T(8,128)(2,1)S(1)}, bf16[128,384]{1,0:T(8,128)(2,1)S(1)}, u32[]{:S(2)}, u32[]{:S(2)}) collective-permute-start(bf16[128,384]{1,0:T(8,128)(2,1)S(1)} %get-tuple-element.73), channel_id=1, source_target_pairs={{0,8},{4,12},{8,0},{12,4},{16,24},{20,28},{24,16},{28,20},{1,9},{5... | collective-permute-start | bytes 294920 | tf_op jit(solution)/shard_map/ppermute | solution.py:52
  36.5 12.2 %collective-permute-start.5 = (bf16[512,128]{1,0:T(8,128)(2,1)S(1)}, bf16[512,128]{1,0:T(8,128)(2,1)S(1)}, u32[]{:S(2)}, u32[]{:S(2)}) collective-permute-start(bf16[512,128]{1,0:T(8,128)(2,1)S(1)} %shard_map.128), channel_id=1, source_target_pairs={{0,8},{4,12},{8,0},{12,4},{16,24},{20,28},{24,16},{28,20},{1,9},{5... | collective-permute-start | bytes 393224 | tf_op jit(solution)/shard_map/ppermute | solution.py:52
  41.7 8.5 %collective-permute-start.14 = (bf16[64,384]{1,0:T(8,128)(2,1)S(1)}, bf16[64,384]{1,0:T(8,128)(2,1)S(1)}, u32[]{:S(2)}, u32[]{:S(2)}) collective-permute-start(bf16[64,384]{1,0:T(8,128)(2,1)S(1)} %get-tuple-element.75), channel_id=1, source_target_pairs={{0,16},{4,20},{8,24},{12,28},{16,0},{20,4},{24,8},{28,12},{1,17},{... | collective-permute-start | bytes 147464 | tf_op jit(solution)/shard_map/ppermute | solution.py:52
  48.7 5.1 %copy-start.4 = (f32[8,64,128]{2,1,0:T(8,128)S(1)}, f32[8,64,128]{2,1,0:T(8,128)}, u32[]{:S(2)}) copy-start(f32[8,64,128]{2,1,0:T(8,128)} %param.13) | copy-start | bytes 786436
  48.8 5.0 %collective-permute-start.6 = (bf16[512,128]{1,0:T(8,128)(2,1)S(1)}, bf16[512,128]{1,0:T(8,128)(2,1)S(1)}, u32[]{:S(2)}, u32[]{:S(2)}) collective-permute-start(bf16[512,128]{1,0:T(8,128)(2,1)S(1)} %shard_map.129), channel_id=1, source_target_pairs={{0,4},{4,0},{8,12},{12,8},{16,20},{20,16},{24,28},{28,24},{1,5},{5... | collective-permute-start | bytes 393224 | tf_op jit(solution)/shard_map/ppermute | solution.py:52

commit v7 on v6

--- a/solution.py
+++ b/solution.py
@@ -46,10 +46,13 @@
     return copy
 
 
-def swap(value, axis, bit):
-    mask = 1 << bit
+def exchange(value, axis, mask):
     pairs = [(source, source ^ mask) for source in range(lax.axis_size(axis))]
     return lax.ppermute(value, axis, pairs)
+
+
+def swap(value, axis, bit):
+    return exchange(value, axis, 1 << bit)
 
 
 def state_kernel(dims, idx_ref, head_ref, k_hbm, v_hbm, w_hbm, x_hbm, kv_ref, kvb_ref, w_ref, x_ref, k_ref, v_ref, sems):
@@ -238,66 +241,40 @@
         far_ref[m * nh:(m + 1) * nh, :] = jnp.concatenate(found, axis=0).astype(BF16)
 
 
-def query_kernel(dims, levels, first, count, idx_ref, *refs):
-    nh, dk, dv = dims
-    ups = refs[:count]
-    g_ref, lw_ref, low_ref, high_ref, dq_hbm, dq_ref, sems = refs[count:]
-    index = idx_ref[0]
-    copies = []
-    for pair in range(nh // 2):
-        halves = []
-        for j in range(2):
-            h = 2 * pair + j
-            local_ref, n = (low_ref, h) if h < nh // 2 else (high_ref, h - nh // 2)
-            total = local_ref[n * dk:(n + 1) * dk, :]
-            for m in range(count):
-                r = h * levels + first + m
-                up = ((index >> m) & 1).astype(F32)
-                x = nt(ups[m][h * dk:(h + 1) * dk, :], g_ref[:, h * dv:(h + 1) * dv])
-                total = total + x * (lw_ref[r:r + 1, :] * up)
-            halves.append(total)
-        cols = slice(pair * 2 * dk, (pair + 1) * 2 * dk)
-        dq_ref[:, cols] = jnp.concatenate(halves, axis=0).astype(BF16).T
-        copies.append(leave(dq_ref, dq_hbm, sems.at[pair], cols))
-    for copy in copies:
-        copy.wait()
-
-
-def out_kernel(dims, levels, first, count, idx_ref, *refs):
-    nh, dk, dv = dims
-    ups = refs[:count]
-    qt_ref, lw_ref, low_ref, high_ref, out_hbm, out_ref, sems = refs[count:]
-    index = idx_ref[0]
-    copies = []
-    for h in range(nh):
-        rows = slice(h * dk, (h + 1) * dk)
-        local_ref, n = (low_ref, h) if h < nh // 2 else (high_ref, h - nh // 2)
-        total = local_ref[n * dv:(n + 1) * dv, :]
-        for m in range(count):
-            r = h * levels + first + m
-            up = ((index >> m) & 1).astype(F32)
-            total = total + tn(ups[m][rows, :], qt_ref[rows, :]) * (lw_ref[r:r + 1, :] * up)
-        out_ref[:, h * dv:(h + 1) * dv] = total.astype(BF16).T
-        if h % 2:
-            copies.append(leave(out_ref, out_hbm, sems.at[h // 2], slice((h - 1) * dv, (h + 1) * dv)))
-    for copy in copies:
-        copy.wait()
-
-
-def wgrad_kernel(bits, inner, idx_ref, head_ref, xt_ref, gp_ref, send_ref, keep_ref, sorted_ref):
+def put_in_order(bits, head_ref, gp_ref, sorted_ref):
     count = 1 << bits
     own = gp_ref.shape[0] // count
     for n in range(count):
         away = sum(((n >> k) & 1) << (bits - 1 - k) for k in range(bits))
         at = pl.multiple_of((head_ref[0] ^ away) * own, 16)
         sorted_ref[pl.ds(at, own), :] = gp_ref[n * own:(n + 1) * own, :]
+
+
+def near_wgrad_kernel(bits, inner, idx_ref, head_ref, xt_ref, gp_ref, send_ref, keep_ref, sorted_ref):
+    put_in_order(bits, head_ref, gp_ref, sorted_ref)
     part_ways(nt(xt_ref[...], sorted_ref[...]), (idx_ref[0] & 1) == 1, send_ref, keep_ref, inner)
 
 
-def merge_kernel(bit, inner, idx_ref, near_ref, near_got, far_ref, far_got, place_ref, send_ref, keep_ref):
+def far_wgrad_kernel(bits, inner, idx_ref, head_ref, xt_ref, gp_ref, keep_ref, one_ref, two_ref, both_ref, sorted_ref):
+    put_in_order(bits, head_ref, gp_ref, sorted_ref)
+    total = nt(xt_ref[...], sorted_ref[...])
+    right, upper = (idx_ref[0] & 1) == 1, ((idx_ref[0] >> 1) & 1) == 1
+    for e in range(total.shape[0] // (4 * inner)):
+        parts = [total[(4 * e + n) * inner:(4 * e + n + 1) * inner] for n in range(4)]
+        kept, sent = jnp.where(right, parts[1], parts[0]), jnp.where(right, parts[0], parts[1])
+        kept_up, sent_up = jnp.where(right, parts[3], parts[2]), jnp.where(right, parts[2], parts[3])
+        at = slice(e * inner, (e + 1) * inner)
+        keep_ref[at, :] = jnp.where(upper, kept_up, kept)
+        one_ref[at, :] = jnp.where(upper, sent_up, sent).astype(BF16)
+        two_ref[at, :] = jnp.where(upper, kept, kept_up).astype(BF16)
+        both_ref[at, :] = jnp.where(upper, sent, sent_up).astype(BF16)
+
+
+def merge_kernel(bit, inner, idx_ref, near_ref, near_got, far_ref, one_ref, two_ref, both_ref, place_ref,
+                 send_ref, keep_ref):
+    far = far_ref[...] + one_ref[...].astype(F32) + two_ref[...].astype(F32) + both_ref[...].astype(F32)
     total = near_ref[...] + near_got[...].astype(F32) + lax.dot_general(
-        far_ref[...] + far_got[...].astype(F32), place_ref[...], (((1,), (0,)), ((), ())),
-        preferred_element_type=F32, precision=lax.Precision.HIGHEST)
+        far, place_ref[...], (((1,), (0,)), ((), ())), preferred_element_type=F32, precision=lax.Precision.HIGHEST)
     part_ways(total, ((idx_ref[0] >> bit) & 1) == 1, send_ref, keep_ref, inner)
 
 
@@ -327,16 +304,49 @@
     send_ref[...] = (total + jnp.where(((index >> bit) & 1) == 1, gu_ref[bit].astype(F32), 0.0)).astype(BF16)
 
 
-def final_kernel(dims, top, idx_ref, *refs):
+def final_kernel(dims, levels, first, count, idx_ref, *refs):
     nh, dk, dv = dims
-    gots = refs[:top + 1]
-    (ds_ref, k_ref, v_ref, low_k, high_k, low_v, high_v, near_ref, far_ref, place_ref, w_ref,
-     dx_hbm, dk_hbm, dv_hbm, dx_ref, dk_ref, dv_ref, sems) = refs[top + 1:]
+    top = count - 1
+    ups, gots = refs[:count], refs[count:2 * count]
+    (qt_ref, lw_ref, g_ref, ds_ref, k_ref, v_ref, low_o, low_q, low_k, low_v, high_o, high_q, high_k, high_v,
+     near_ref, far_ref, place_ref, w_ref, out_hbm, dq_hbm, dx_hbm, dk_hbm, dv_hbm,
+     out_ref, dq_ref, dx_ref, dk_ref, dv_ref, sems) = refs[2 * count:]
+    index = idx_ref[0]
+    copies = []
+
+    def send(buf_ref, hbm_ref, cols):
+        copies.append(leave(buf_ref, hbm_ref, sems.at[len(copies)], cols))
+
+    def weights(h, m):
+        r = h * levels + first + m
+        return lw_ref[r:r + 1, :] * ((index >> m) & 1).astype(F32)
+
+    for h in range(nh):
+        rows = slice(h * dk, (h + 1) * dk)
+        local_ref, n = (low_o, h) if h < nh // 2 else (high_o, h - nh // 2)
+        total = local_ref[n * dv:(n + 1) * dv, :]
+        for m in range(count):
+            total = total + tn(ups[m][rows, :], qt_ref[rows, :]) * weights(h, m)
+        out_ref[:, h * dv:(h + 1) * dv] = total.astype(BF16).T
+        if h % 2:
+            send(out_ref, out_hbm, slice((h - 1) * dv, (h + 1) * dv))
+    for pair in range(nh // 2):
+        halves = []
+        for j in range(2):
+            h = 2 * pair + j
+            local_ref, n = (low_q, h) if h < nh // 2 else (high_q, h - nh // 2)
+            total = local_ref[n * dk:(n + 1) * dk, :]
+            for m in range(count):
+                total = total + nt(ups[m][h * dk:(h + 1) * dk, :], g_ref[:, h * dv:(h + 1) * dv]) * weights(h, m)
+            halves.append(total)
+        cols = slice(pair * 2 * dk, (pair + 1) * 2 * dk)
+        dq_ref[:, cols] = jnp.concatenate(halves, axis=0).astype(BF16).T
+        send(dq_ref, dq_hbm, cols)
     gp = (near_ref[...].astype(F32) + tn(place_ref[...].astype(BF16), far_ref[...])).astype(BF16)
     dx_ref[...] = lax.dot_general(
         gp, w_ref[...], (((0,), (1,)), ((), ())), preferred_element_type=F32).astype(BF16)
-    copies = [leave(dx_ref, dx_hbm, sems.at[nh], slice(0, dx_ref.shape[1]))]
-    upper = ((idx_ref[0] >> top) & 1) == 1
+    send(dx_ref, dx_hbm, slice(0, dx_ref.shape[1]))
+    upper = ((index >> top) & 1) == 1
     zero = jnp.zeros((dk, dv), BF16)
     for pair in range(nh // 2):
         pair_rows = slice(pair * 2 * dk, (pair + 1) * 2 * dk)
@@ -355,8 +365,8 @@
             near = dvl_ref[:, (2 * p + j) * dv:(2 * p + j + 1) * dv]
             dv_ref[:, cols] = (near + nn(kp, padded)).astype(BF16)
         dk_ref[:, pair * 2 * dk:(pair + 1) * 2 * dk] = total.astype(BF16)
-        copies.append(leave(dv_ref, dv_hbm, sems.at[2 * pair], slice(2 * pair * dv, (2 * pair + 2) * dv)))
-        copies.append(leave(dk_ref, dk_hbm, sems.at[2 * pair + 1], slice(pair * 2 * dk, (pair + 1) * 2 * dk)))
+        send(dv_ref, dv_hbm, slice(2 * pair * dv, (2 * pair + 2) * dv))
+        send(dk_ref, dk_hbm, slice(pair * 2 * dk, (pair + 1) * 2 * dk))
     for copy in copies:
         copy.wait()
 
@@ -439,26 +449,38 @@
                     rows * dv)(idx, *gots, gu)[0]
         gots.append(swap(down, "seq", bit))
 
-    def begin(gathered, n_cols):
-        send, keep, ordered = call(
-            functools.partial(wgrad_kernel, head_bits, per),
-            [S((width // 2, n_cols), BF16), S((width // 2, n_cols), F32), S((n_cols, tokens), BF16)],
-            [SM] * 2 + [VM] * 2, 2 * tokens * width * n_cols)(idx, head_idx, xt, gathered)
-        return keep, swap(send, "seq", 0), ordered
-
-    near_w, near_got, near_all = begin(gather_heads(near, head_bits), cols)
-    far_w, far_got, far_all = begin(gather_heads(far_rows, head_bits), far_cols)
+    near_all = gather_heads(near, head_bits)
+    n = width // 2
+    send, near_w, near_all = call(
+        functools.partial(near_wgrad_kernel, head_bits, per),
+        [S((n, cols), BF16), S((n, cols), F32), S((cols, tokens), BF16)],
+        [SM] * 2 + [VM] * 2, 2 * tokens * width * cols)(idx, head_idx, xt, near_all)
+    got = swap(send, "seq", 0)
+    n = n // 2
+    send, near_w = call(
+        functools.partial(fold_kernel, 1, per), [S((n, cols), BF16), S((n, cols), F32)],
+        [SM] + [VM] * 2, n * cols)(idx, near_w, got)
+    near_got = swap(send, "seq", 1)
+
+    far_all = gather_heads(far_rows, head_bits)
+    far_w, one, two, both, far_all = call(
+        functools.partial(far_wgrad_kernel, head_bits, per),
+        [S((n, far_cols), F32)] + [S((n, far_cols), BF16)] * 3 + [S((far_cols, tokens), BF16)],
+        [SM] * 2 + [VM] * 2, 2 * tokens * width * far_cols)(idx, head_idx, xt, far_all)
+    far_gots = [exchange(one, "seq", 1), exchange(two, "seq", 2),
+                exchange(both, "seq", 3)]
+
     col = jnp.arange(cols, dtype=jnp.int32)[None, :]
     row = jnp.arange(far_cols, dtype=jnp.int32)[:, None]
     within = row % far_own
     at = (row // far_own * nh + within % nh) * levels + first + within // nh
     place = ((at == col) & (within < far)).astype(F32)
-    n = width // 4
+    n = n // 2
     send, keep = call(
-        functools.partial(merge_kernel, 1, per), [S((n, cols), BF16), S((n, cols), F32)], [SM] + [VM] * 5,
-        4 * n * far_cols * cols)(idx, near_w, near_got, far_w, far_got, place)
-    got = swap(send, "seq", 1)
-    for bit in range(2, seq_bits):
+        functools.partial(merge_kernel, 2, per), [S((n, cols), BF16), S((n, cols), F32)], [SM] + [VM] * 7,
+        4 * n * far_cols * cols)(idx, near_w, near_got, far_w, *far_gots, place)
+    got = swap(send, "seq", 2)
+    for bit in range(3, seq_bits):
         n = n // 2
         send, keep = call(
             functools.partial(fold_kernel, bit, per), [S((n, cols), BF16), S((n, cols), F32)],
@@ -475,28 +497,13 @@
              S((tokens, nh * dv // 2), F32)],
             [VM] * 5, tokens * tokens * nh * (3 * dk + 3 * dv),
         )(keys, queries, values, d_out, lw))
-    out_l, dq_l, dk_l, dv_l = [(local[0][n], local[1][n]) for n in range(4)]
-
-    def leaving(shapes, copies):
-        return dict(out_specs=[hbm] * len(shapes),
-                    scratch_shapes=[pltpu.VMEM(shape, BF16) for shape in shapes] + [pltpu.SemaphoreType.DMA((copies,))])
-
-    def results(*shapes):
-        return [S(shape, BF16) for shape in shapes]
-
-    narrow, broad = (tokens, rows), (tokens, nh * dv)
-    d_queries = call(
-        functools.partial(query_kernel, dims, levels, first, seq_bits), results(narrow),
-        [SM] + [VM] * (seq_bits + 4), 2 * tokens * rows * dv * seq_bits, **leaving([narrow], nh // 2))(
-            idx, *ups, d_out, lw, *dq_l)[0]
-    out = call(
-        functools.partial(out_kernel, dims, levels, first, seq_bits), results(broad),
-        [SM] + [VM] * (seq_bits + 4), 2 * tokens * rows * dv * seq_bits, **leaving([broad], nh // 2))(
-            idx, *ups, qt, lw, *out_l)[0]
-    d_hidden, d_keys, d_values = call(
-        functools.partial(final_kernel, dims, top), results((tokens, width), narrow, broad), [SM] + [VM] * (top + 12),
-        4 * tokens * rows * dv, **leaving([(tokens, width), narrow, broad], nh + 1))(
-            idx, *gots, d_state.reshape(rows, dv), keys, values, *dk_l, *dv_l, near_all, far_all, place, w_near)
+    shapes = [(tokens, nh * dv), (tokens, rows), (tokens, width), (tokens, rows), (tokens, nh * dv)]
+    out, d_queries, d_hidden, d_keys, d_values = call(
+        functools.partial(final_kernel, dims, levels, first, seq_bits), [S(shape, BF16) for shape in shapes],
+        [SM] + [VM] * (2 * seq_bits + 18), 8 * tokens * rows * dv * seq_bits, out_specs=[hbm] * len(shapes),
+        scratch_shapes=[pltpu.VMEM(shape, BF16) for shape in shapes] + [pltpu.SemaphoreType.DMA((2 * nh + 1,))])(
+            idx, *ups, *gots, qt, lw, d_out, d_state.reshape(rows, dv), keys, values, *local[0], *local[1],
+            near_all, far_all, place, w_near)
     return (out, d_queries, d_keys, d_values, d_hidden, d_w)
 
 

time: 55.6 us -> 51.4 us (0.924)
  waiting for transfers between devices: 21.6 us -> 17.3 us
  starting transfers between devices: 19.9 us -> 21.7 us
  Pallas kernels: 12.2 us -> 10.6 us
    ppermute x15 -> x17, waiting for transfers between devices: 21.6 us -> 17.3 us  [exchange(): return lax.ppermute(value, axis, pairs)]
    ppermute x15 -> x17, starting transfers between devices: 19.9 us -> 21.7 us  [exchange(): return lax.ppermute(value, axis, pairs)]
    pallas_call x7 -> x5, Pallas kernels: 5.48 us -> 3.83 us  [the longest x1 2.88 us: body(): call(functools.partial(final_kernel, dims, levels, first, seq_bits), [S(s...]
  transfers between devices with their start and end apart: 15 -> 17, of which waited for: 9 -> 9; matrix products, arithmetic and copies ran while one was open for 1% -> 2% of each run, Pallas kernels for 16% -> 12%
where the time goes in v7:
time: 51.4 us; the launch traced here: 51.3 us
  starting transfers between devices  21.7 us (42%)
  waiting for transfers between devices  17.3 us (34%)
  Pallas kernels  10.6 us (21%)
  between operations  0.87 us (2%)
  other arithmetic  0.83 us (2%)
    ppermute x17, starting transfers between devices, exchange(): return lax.ppermute(value, axis, pairs)  21.7 us
    ppermute x17, waiting for transfers between devices, exchange(): return lax.ppermute(value, axis, pairs)  17.3 us
    pallas_call x1, Pallas kernels, body(): call(functools.partial(final_kernel, dims, levels, first, seq_bits), [S(s...  2.88 us
    pallas_call x2, Pallas kernels, body(): call(functools.partial(local_kernel, dims, levels, tuple(range(part * hal...  2.81 us
    pallas_call x1, Pallas kernels, body(): call(functools.partial(state_kernel, dims), [S((rows, dv), F32), S((rows,...  1.47 us
  transfers between devices with their start and end apart: 17, of which 9 were waited for; matrix products, arithmetic and copies ran while one was open for 2% of the time, Pallas kernels for 12%

profile of v7, /device:TPU:0, one launch (start us, length us, event | category | flops | bytes accessed | tf_op | source)
XLA Modules:
  0.0 51.3 jit_solution(1447680888868586138)
XLA Ops:
  0.6 0.0 copy-start.3
  0.6 1.5 %shard_map.118 = (f32[512,128]{1,0:T(8,128)S(1)}, bf16[512,128]{1,0:T(8,128)(2,1)S(1)}, bf16[512,384]{1,0:T(8,128)(2,1)S(1)}, bf16[256,512]{1,0:T(8,128)(2,1)S(1)}) custom-call(s32[1]{0:T(128)} %bitcast.idx_ref, s32[1]{0:T(128)} %bitcast.1.head_ref.idx_ref, bf16[256,512]{1,0:T(8,128)(2,1)} %refs_10_.1, bf16[256,1024]{1,0:T(8,128)(2,1)} %refs_11_.1, ...), custom_call_target="tpu_custom_call" | custom-call | flops 33554432 | bytes 2097152 | tf_op jit(solution)/shard_map/pallas_call | solution.py:401
  2.1 3.1 %collective-permute-start = (bf16[512,128]{1,0:T(8,128)(2,1)S(1)}, bf16[512,128]{1,0:T(8,128)(2,1)S(1)}, u32[]{:S(2)}, u32[]{:S(2)}) collective-permute-start(bf16[512,128]{1,0:T(8,128)(2,1)S(1)} %get-tuple-element.45), channel_id=1, source_target_pairs={{0,4},{4,0},{8,12},{12,8},{16,20},{20,16},{24,28},{28,24},{1,5},{5... | collective-permute-start | bytes 393224 | tf_op jit(solution)/shard_map/ppermute | solution.py:51
  5.2 0.0 copy-start.1
  5.2 0.4 shard_map.119
  5.6 0.0 copy-start
  5.6 1.6 %collective-permute-start.2 = (bf16[192,256]{1,0:T(8,128)(2,1)S(1)}, bf16[192,256]{1,0:T(8,128)(2,1)S(1)}, u32[]{:S(2)}, u32[]{:S(2)}) collective-permute-start(bf16[192,256]{1,0:T(8,128)(2,1)S(1)} %get-tuple-element.50), channel_id=1, source_target_pairs={{0,2},{1,3},{2,0},{3,1},{4,6},{5,7},{6,4},{7,5},{8,10},{9,11},{10,... | collective-permute-start | bytes 294920 | tf_op jit(solution)/shard_map/ppermute | solution.py:51
  7.1 1.5 %collective-permute-done.refs_0_ = bf16[512,128]{1,0:T(8,128)(2,1)S(1)} collective-permute-done((bf16[512,128]{1,0:T(8,128)(2,1)S(1)}, bf16[512,128]{1,0:T(8,128)(2,1)S(1)}, u32[]{:S(2)}, u32[]{:S(2)}) %collective-permute-start) | collective-permute-done | bytes 131104 | tf_op jit(solution)/shard_map/ppermute | solution.py:51
  8.7 0.0 copy-start.2
  8.7 1.9 %collective-permute-start.1 = (bf16[512,128]{1,0:T(8,128)(2,1)S(1)}, bf16[512,128]{1,0:T(8,128)(2,1)S(1)}, u32[]{:S(2)}, u32[]{:S(2)}) collective-permute-start(bf16[512,128]{1,0:T(8,128)(2,1)S(1)} %add_convert_fusion), channel_id=1, source_target_pairs={{0,8},{4,12},{8,0},{12,4},{16,24},{20,28},{24,16},{28,20},{1,9},{5... | collective-permute-start | bytes 393224 | tf_op jit(solution)/shard_map/ppermute | solution.py:51
  10.6 0.0 collective-permute-done.2.got_ref
  10.6 0.1 collective-permute-start.3
  10.7 0.0 copy-done.3
  10.7 0.0 copy-done.1
  10.7 0.0 copy-done
  10.7 0.0 copy-done.2
  10.8 0.8 %shard_map.121.gl_ref = f32[96,256]{1,0:T(8,128)S(1)} custom-call(bf16[256,512]{1,0:T(8,128)(2,1)S(1)} %copy-done.2, bf16[256,512]{1,0:T(8,128)(2,1)S(1)} %copy-done.3, bf16[256,1024]{1,0:T(8,128)(2,1)S(1)} %copy-done.1, bf16[256,1024]{1,0:T(8,128)(2,1)S(1)} %copy-done), custom_call_target="tpu_custom_call" | custom-call | flops 201326592 | bytes 196608 | tf_op jit(solution)/shard_map/pallas_call | solution.py:430
  11.5 0.4 collective-permute-done.3.got_ref
  11.9 0.4 shard_map.122
  12.4 1.6 %collective-permute-start.7 = (bf16[96,256]{1,0:T(8,128)(2,1)S(1)}, bf16[96,256]{1,0:T(8,128)(2,1)S(1)}, u32[]{:S(2)}, u32[]{:S(2)}) collective-permute-start(bf16[96,256]{1,0:T(8,128)(2,1)S(1)} %get-tuple-element.65), channel_id=1, source_target_pairs={{0,2},{1,3},{2,0},{3,1},{4,6},{5,7},{6,4},{7,5},{8,10},{9,11},{10,... | collective-permute-start | bytes 147464 | tf_op jit(solution)/shard_map/ppermute | solution.py:51
  13.9 0.0 collective-permute-done.1.refs_1_
  14.0 2.7 %collective-permute-start.4 = (bf16[512,128]{1,0:T(8,128)(2,1)S(1)}, bf16[512,128]{1,0:T(8,128)(2,1)S(1)}, u32[]{:S(2)}, u32[]{:S(2)}) collective-permute-start(bf16[512,128]{1,0:T(8,128)(2,1)S(1)} %shard_map.123), channel_id=1, source_target_pairs={{0,16},{4,20},{8,24},{12,28},{16,0},{20,4},{24,8},{28,12},{1,17},{... | collective-permute-start | bytes 393224 | tf_op jit(solution)/shard_map/ppermute | solution.py:51
  16.7 0.0 collective-permute-done.7
  16.7 0.1 collective-permute-start.8
  16.8 6.3 %collective-permute-done.4.refs_0_.refs_2_.refs_3_ = bf16[512,128]{1,0:T(8,128)(2,1)S(1)} collective-permute-done((bf16[512,128]{1,0:T(8,128)(2,1)S(1)}, bf16[512,128]{1,0:T(8,128)(2,1)S(1)}, u32[]{:S(2)}, u32[]{:S(2)}) %collective-permute-start.4) | collective-permute-done | bytes 131104 | tf_op jit(solution)/shard_map/ppermute | solution.py:51
  23.0 0.7 %shard_map.129 = bf16[32,256]{1,0:T(8,128)(2,1)S(1)} custom-call(s32[1]{0:T(128)} %bitcast.idx_ref, bf16[512,128]{1,0:T(8,128)(2,1)S(1)} %collective-permute-done.refs_0_, bf16[512,128]{1,0:T(8,128)(2,1)S(1)} %collective-permute-done.1.refs_1_, bf16[512,128]{1,0:T(8,128)(2,1)S(1)} %collective-permute-done.4.refs_0_.refs_2_.refs_3_, ...), custom_call_target="tpu_custom_call" | custom-call | flops 100663296 | bytes 32768 | tf_op jit(solution)/shard_map/pallas_call | solution.py:443
  23.7 0.6 %collective-permute-start.9 = (bf16[32,256]{1,0:T(8,128)(2,1)S(1)}, bf16[32,256]{1,0:T(8,128)(2,1)S(1)}, u32[]{:S(2)}, u32[]{:S(2)}) collective-permute-start(bf16[32,256]{1,0:T(8,128)(2,1)S(1)} %shard_map.129), channel_id=1, source_target_pairs={{0,2},{1,3},{2,0},{3,1},{4,6},{5,7},{6,4},{7,5},{8,10},{9,11},{10,... | collective-permute-start | bytes 49160 | tf_op jit(solution)/shard_map/ppermute | solution.py:51
  24.3 0.0 collective-permute-done.8
  24.3 0.3 shard_map.128
  24.7 1.6 %collective-permute-start.11 = (bf16[256,384]{1,0:T(8,128)(2,1)S(1)}, bf16[256,384]{1,0:T(8,128)(2,1)S(1)}, u32[]{:S(2)}, u32[]{:S(2)}) collective-permute-start(bf16[256,384]{1,0:T(8,128)(2,1)S(1)} %get-tuple-element.75), channel_id=1, source_target_pairs={{0,4},{4,0},{8,12},{12,8},{16,20},{20,16},{24,28},{28,24},{1,5},{5... | collective-permute-start | bytes 589832 | tf_op jit(solution)/shard_map/ppermute | solution.py:51
  26.2 1.3 %collective-permute-done.9 = bf16[32,256]{1,0:T(8,128)(2,1)S(1)} collective-permute-done((bf16[32,256]{1,0:T(8,128)(2,1)S(1)}, bf16[32,256]{1,0:T(8,128)(2,1)S(1)}, u32[]{:S(2)}, u32[]{:S(2)}) %collective-permute-start.9) | collective-permute-done | bytes 16416 | tf_op jit(solution)/shard_map/ppermute | solution.py:51
  27.5 0.0 collective-permute-start.10
  27.5 0.1 shard_map.124
  27.6 0.5 collective-permute-start.5
  28.1 0.7 %collective-permute-done.10 = bf16[64,256]{1,0:T(8,128)(2,1)S(1)} collective-permute-done((bf16[64,256]{1,0:T(8,128)(2,1)S(1)}, bf16[64,256]{1,0:T(8,128)(2,1)S(1)}, u32[]{:S(2)}, u32[]{:S(2)}) %collective-permute-start.10) | collective-permute-done | bytes 32800 | tf_op jit(solution)/shard_map/ppermute | solution.py:51
  28.7 0.2 shard_map.130
  29.0 1.5 %collective-permute-start.13 = (bf16[128,128]{1,0:T(8,128)(2,1)S(1)}, bf16[128,128]{1,0:T(8,128)(2,1)S(1)}, u32[]{:S(2)}, u32[]{:S(2)}) collective-permute-start(bf16[128,128]{1,0:T(8,128)(2,1)S(1)} %get-tuple-element.79), channel_id=1, source_target_pairs={{0,4},{4,0},{8,12},{12,8},{16,20},{20,16},{24,28},{28,24},{1,5},{5... | collective-permute-start | bytes 98312 | tf_op jit(solution)/shard_map/ppermute | solution.py:51
  30.5 1.0 %collective-permute-start.14 = (bf16[128,128]{1,0:T(8,128)(2,1)S(1)}, bf16[128,128]{1,0:T(8,128)(2,1)S(1)}, u32[]{:S(2)}, u32[]{:S(2)}) collective-permute-start(bf16[128,128]{1,0:T(8,128)(2,1)S(1)} %get-tuple-element.80), channel_id=1, source_target_pairs={{0,8},{4,12},{8,0},{12,4},{16,24},{20,28},{24,16},{28,20},{1,9},{5... | collective-permute-start | bytes 98312 | tf_op jit(solution)/shard_map/ppermute | solution.py:51
  31.4 1.1 %collective-permute-start.15 = (bf16[128,128]{1,0:T(8,128)(2,1)S(1)}, bf16[128,128]{1,0:T(8,128)(2,1)S(1)}, u32[]{:S(2)}, u32[]{:S(2)}) collective-permute-start(bf16[128,128]{1,0:T(8,128)(2,1)S(1)} %get-tuple-element.81), channel_id=1, source_target_pairs={{0,12},{4,8},{8,4},{12,0},{16,28},{20,24},{24,20},{28,16},{1,13},{... | collective-permute-start | bytes 98312 | tf_op jit(solution)/shard_map/ppermute | solution.py:51
  32.6 0.0 collective-permute-done.11.got_ref
  32.6 0.1 shard_map.132
  32.6 1.0 %collective-permute-start.12 = (bf16[128,384]{1,0:T(8,128)(2,1)S(1)}, bf16[128,384]{1,0:T(8,128)(2,1)S(1)}, u32[]{:S(2)}, u32[]{:S(2)}) collective-permute-start(bf16[128,384]{1,0:T(8,128)(2,1)S(1)} %get-tuple-element.77), channel_id=1, source_target_pairs={{0,8},{4,12},{8,0},{12,4},{16,24},{20,28},{24,16},{28,20},{1,9},{5... | collective-permute-start | bytes 294920 | tf_op jit(solution)/shard_map/ppermute | solution.py:51
  33.6 0.1 fusion.1.refs_22_.place_ref
  33.8 0.0 collective-permute-done.13.one_ref
  33.8 0.9 %collective-permute-done.14.two_ref = bf16[128,128]{1,0:T(8,128)(2,1)S(1)} collective-permute-done((bf16[128,128]{1,0:T(8,128)(2,1)S(1)}, bf16[128,128]{1,0:T(8,128)(2,1)S(1)}, u32[]{:S(2)}, u32[]{:S(2)}) %collective-permute-start.14) | collective-permute-done | bytes 32800 | tf_op jit(solution)/shard_map/ppermute | solution.py:51
  34.7 1.9 %collective-permute-done.15.both_ref = bf16[128,128]{1,0:T(8,128)(2,1)S(1)} collective-permute-done((bf16[128,128]{1,0:T(8,128)(2,1)S(1)}, bf16[128,128]{1,0:T(8,128)(2,1)S(1)}, u32[]{:S(2)}, u32[]{:S(2)}) %collective-permute-start.15) | collective-permute-done | bytes 32800 | tf_op jit(solution)/shard_map/ppermute | solution.py:51
  36.6 0.7 %collective-permute-done.12.near_got = bf16[128,384]{1,0:T(8,128)(2,1)S(1)} collective-permute-done((bf16[128,384]{1,0:T(8,128)(2,1)S(1)}, bf16[128,384]{1,0:T(8,128)(2,1)S(1)}, u32[]{:S(2)}, u32[]{:S(2)}) %collective-permute-start.12) | collective-permute-done | bytes 98336 | tf_op jit(solution)/shard_map/ppermute | solution.py:51
  37.3 0.3 shard_map.133
  37.6 2.8 %collective-permute-start.16 = (bf16[64,384]{1,0:T(8,128)(2,1)S(1)}, bf16[64,384]{1,0:T(8,128)(2,1)S(1)}, u32[]{:S(2)}, u32[]{:S(2)}) collective-permute-start(bf16[64,384]{1,0:T(8,128)(2,1)S(1)} %get-tuple-element.83), channel_id=1, source_target_pairs={{0,16},{4,20},{8,24},{12,28},{16,0},{20,4},{24,8},{28,12},{1,17},{... | collective-permute-start | bytes 147464 | tf_op jit(solution)/shard_map/ppermute | solution.py:51
  40.4 1.4 %shard_map.127 = (f32[512,256]{1,0:T(8,128)S(1)}, f32[256,256]{1,0:T(8,128)S(1)}, f32[256,256]{1,0:T(8,128)S(1)}, f32[256,512]{1,0:T(8,128)S(1)}) custom-call(bf16[256,512]{1,0:T(8,128)(2,1)S(1)} %copy-done.2, bf16[256,512]{1,0:T(8,128)(2,1)S(1)} %copy-done.3, bf16[256,1024]{1,0:T(8,128)(2,1)S(1)} %copy-done.1, bf16[256,1024]{1,0:T(8,128)(2,1)S(1)} %copy-done, ...), custom_call_target="tpu_custom_call" | custom-call | flops 301989888 | bytes 3145728 | tf_op jit(solution)/shard_map/pallas_call | solution.py:494
  41.8 1.4 %shard_map.126 = (f32[512,256]{1,0:T(8,128)S(1)}, f32[256,256]{1,0:T(8,128)S(1)}, f32[256,256]{1,0:T(8,128)S(1)}, f32[256,512]{1,0:T(8,128)S(1)}) custom-call(bf16[256,512]{1,0:T(8,128)(2,1)S(1)} %copy-done.2, bf16[256,512]{1,0:T(8,128)(2,1)S(1)} %copy-done.3, bf16[256,1024]{1,0:T(8,128)(2,1)S(1)} %copy-done.1, bf16[256,1024]{1,0:T(8,128)(2,1)S(1)} %copy-done, ...), custom_call_target="tpu_custom_call" | custom-call | flops 301989888 | bytes 3145728 | tf_op jit(solution)/shard_map/pallas_call | solution.py:494
  43.2 0.0 collective-permute-done.5.refs_1_.refs_4_
  43.3 0.1 shard_map.125
  43.3 0.0 copy-start.4
  43.3 0.8 %collective-permute-start.6 = (bf16[512,128]{1,0:T(8,128)(2,1)S(1)}, bf16[512,128]{1,0:T(8,128)(2,1)S(1)}, u32[]{:S(2)}, u32[]{:S(2)}) collective-permute-start(bf16[512,128]{1,0:T(8,128)(2,1)S(1)} %shard_map.125), channel_id=1, source_target_pairs={{0,4},{4,0},{8,12},{12,8},{16,20},{20,16},{24,28},{28,24},{1,5},{5... | collective-permute-start | bytes 393224 | tf_op jit(solution)/shard_map/ppermute | solution.py:51
  44.1 0.0 collective-permute-done.16
  44.1 0.7 %convert_add_fusion = f32[64,384]{1,0:T(8,128)} fusion(f32[64,384]{1,0:T(8,128)S(1)} %get-tuple-element.82, bf16[64,384]{1,0:T(8,128)(2,1)S(1)} %collective-permute-done.16), kind=kLoop, calls=%fused_computation.6 | loop fusion | flops 49152 | bytes 245760 | tf_op jit(solution)/shard_map/add | solution.py:489
  44.8 3.6 %collective-permute-done.6.refs_5_ = bf16[512,128]{1,0:T(8,128)(2,1)S(1)} collective-permute-done((bf16[512,128]{1,0:T(8,128)(2,1)S(1)}, bf16[512,128]{1,0:T(8,128)(2,1)S(1)}, u32[]{:S(2)}, u32[]{:S(2)}) %collective-permute-start.6) | collective-permute-done | bytes 131104 | tf_op jit(solution)/shard_map/ppermute | solution.py:51
  48.4 0.0 copy-done.4
  48.4 2.9 %shard_map.131 = (bf16[256,1024]{1,0:T(8,128)(2,1)}, bf16[256,512]{1,0:T(8,128)(2,1)}, bf16[256,512]{1,0:T(8,128)(2,1)}, bf16[256,512]{1,0:T(8,128)(2,1)}, bf16[256,1024]{1,0:T(8,128)(2,1)}) custom-call(s32[1]{0:T(128)} %bitcast.idx_ref, bf16[512,128]{1,0:T(8,128)(2,1)S(1)} %collective-permute-done.refs_0_, ...), custom_call_target="tpu_custom_call" | custom-call | flops 402653184 | bytes 3670016 | tf_op jit(solution)/shard_map/pallas_call | solution.py:501
  (9 shorter events, 0.2 us)
Async XLA Ops:
  0.6 10.1 %copy-start.3 = (bf16[256,512]{1,0:T(8,128)(2,1)S(1)}, bf16[256,512]{1,0:T(8,128)(2,1)}, u32[]{:S(2)}) copy-start(bf16[256,512]{1,0:T(8,128)(2,1)} %q_ref.7) | copy-start | bytes 786436
  2.1 6.6 %collective-permute-start = (bf16[512,128]{1,0:T(8,128)(2,1)S(1)}, bf16[512,128]{1,0:T(8,128)(2,1)S(1)}, u32[]{:S(2)}, u32[]{:S(2)}) collective-permute-start(bf16[512,128]{1,0:T(8,128)(2,1)S(1)} %get-tuple-element.45), channel_id=1, source_target_pairs={{0,4},{4,0},{8,12},{12,8},{16,20},{20,16},{24,28},{28,24},{1,5},{5... | collective-permute-start | bytes 393224 | tf_op jit(solution)/shard_map/ppermute | solution.py:51
  5.2 5.5 %copy-start.1 = (bf16[256,1024]{1,0:T(8,128)(2,1)S(1)}, bf16[256,1024]{1,0:T(8,128)(2,1)}, u32[]{:S(2)}) copy-start(bf16[256,1024]{1,0:T(8,128)(2,1)} %refs_11_.1) | copy-start | bytes 1572868
  5.6 5.2 %copy-start = (bf16[256,1024]{1,0:T(8,128)(2,1)S(1)}, bf16[256,1024]{1,0:T(8,128)(2,1)}, u32[]{:S(2)}) copy-start(bf16[256,1024]{1,0:T(8,128)(2,1)} %refs_8_.1) | copy-start | bytes 1572868
  5.6 5.0 %collective-permute-start.2 = (bf16[192,256]{1,0:T(8,128)(2,1)S(1)}, bf16[192,256]{1,0:T(8,128)(2,1)S(1)}, u32[]{:S(2)}, u32[]{:S(2)}) collective-permute-start(bf16[192,256]{1,0:T(8,128)(2,1)S(1)} %get-tuple-element.50), channel_id=1, source_target_pairs={{0,2},{1,3},{2,0},{3,1},{4,6},{5,7},{6,4},{7,5},{8,10},{9,11},{10,... | collective-permute-start | bytes 294920 | tf_op jit(solution)/shard_map/ppermute | solution.py:51
  8.7 2.0 %copy-start.2 = (bf16[256,512]{1,0:T(8,128)(2,1)S(1)}, bf16[256,512]{1,0:T(8,128)(2,1)}, u32[]{:S(2)}) copy-start(bf16[256,512]{1,0:T(8,128)(2,1)} %refs_10_.1) | copy-start | bytes 786436
  8.7 5.2 %collective-permute-start.1 = (bf16[512,128]{1,0:T(8,128)(2,1)S(1)}, bf16[512,128]{1,0:T(8,128)(2,1)S(1)}, u32[]{:S(2)}, u32[]{:S(2)}) collective-permute-start(bf16[512,128]{1,0:T(8,128)(2,1)S(1)} %add_convert_fusion), channel_id=1, source_target_pairs={{0,8},{4,12},{8,0},{12,4},{16,24},{20,28},{24,16},{28,20},{1,9},{5... | collective-permute-start | bytes 393224 | tf_op jit(solution)/shard_map/ppermute | solution.py:51
  10.6 1.3 %collective-permute-start.3 = (bf16[96,256]{1,0:T(8,128)(2,1)S(1)}, bf16[96,256]{1,0:T(8,128)(2,1)S(1)}, u32[]{:S(2)}, u32[]{:S(2)}) collective-permute-start(bf16[96,256]{1,0:T(8,128)(2,1)S(1)} %get-tuple-element.52), channel_id=1, source_target_pairs={{0,1},{1,0},{2,3},{3,2},{4,5},{5,4},{6,7},{7,6},{8,9},{9,8},{10,11... | collective-permute-start | bytes 147464 | tf_op jit(solution)/shard_map/ppermute | solution.py:51
  12.4 4.3 %collective-permute-start.7 = (bf16[96,256]{1,0:T(8,128)(2,1)S(1)}, bf16[96,256]{1,0:T(8,128)(2,1)S(1)}, u32[]{:S(2)}, u32[]{:S(2)}) collective-permute-start(bf16[96,256]{1,0:T(8,128)(2,1)S(1)} %get-tuple-element.65), channel_id=1, source_target_pairs={{0,2},{1,3},{2,0},{3,1},{4,6},{5,7},{6,4},{7,5},{8,10},{9,11},{10,... | collective-permute-start | bytes 147464 | tf_op jit(solution)/shard_map/ppermute | solution.py:51
  14.0 9.1 %collective-permute-start.4 = (bf16[512,128]{1,0:T(8,128)(2,1)S(1)}, bf16[512,128]{1,0:T(8,128)(2,1)S(1)}, u32[]{:S(2)}, u32[]{:S(2)}) collective-permute-start(bf16[512,128]{1,0:T(8,128)(2,1)S(1)} %shard_map.123), channel_id=1, source_target_pairs={{0,16},{4,20},{8,24},{12,28},{16,0},{20,4},{24,8},{28,12},{1,17},{... | collective-permute-start | bytes 393224 | tf_op jit(solution)/shard_map/ppermute | solution.py:51
  16.7 7.6 %collective-permute-start.8 = (bf16[192,256]{1,0:T(8,128)(2,1)S(1)}, bf16[192,256]{1,0:T(8,128)(2,1)S(1)}, u32[]{:S(2)}, u32[]{:S(2)}) collective-permute-start(bf16[192,256]{1,0:T(8,128)(2,1)S(1)} %pad_maximum_fusion.1), channel_id=1, source_target_pairs={{0,1},{1,0},{2,3},{3,2},{4,5},{5,4},{6,7},{7,6},{8,9},{9,8},{10,11... | collective-permute-start | bytes 294920 | tf_op jit(solution)/shard_map/ppermute | solution.py:51
  23.7 3.8 %collective-permute-start.9 = (bf16[32,256]{1,0:T(8,128)(2,1)S(1)}, bf16[32,256]{1,0:T(8,128)(2,1)S(1)}, u32[]{:S(2)}, u32[]{:S(2)}) collective-permute-start(bf16[32,256]{1,0:T(8,128)(2,1)S(1)} %shard_map.129), channel_id=1, source_target_pairs={{0,2},{1,3},{2,0},{3,1},{4,6},{5,7},{6,4},{7,5},{8,10},{9,11},{10,... | collective-permute-start | bytes 49160 | tf_op jit(solution)/shard_map/ppermute | solution.py:51
  24.7 7.9 %collective-permute-start.11 = (bf16[256,384]{1,0:T(8,128)(2,1)S(1)}, bf16[256,384]{1,0:T(8,128)(2,1)S(1)}, u32[]{:S(2)}, u32[]{:S(2)}) collective-permute-start(bf16[256,384]{1,0:T(8,128)(2,1)S(1)} %get-tuple-element.75), channel_id=1, source_target_pairs={{0,4},{4,0},{8,12},{12,8},{16,20},{20,16},{24,28},{28,24},{1,5},{5... | collective-permute-start | bytes 589832 | tf_op jit(solution)/shard_map/ppermute | solution.py:51
  27.5 1.2 %collective-permute-start.10 = (bf16[64,256]{1,0:T(8,128)(2,1)S(1)}, bf16[64,256]{1,0:T(8,128)(2,1)S(1)}, u32[]{:S(2)}, u32[]{:S(2)}) collective-permute-start(bf16[64,256]{1,0:T(8,128)(2,1)S(1)} %pad_maximum_fusion.3), channel_id=1, source_target_pairs={{0,1},{1,0},{2,3},{3,2},{4,5},{5,4},{6,7},{7,6},{8,9},{9,8},{10,11... | collective-permute-start | bytes 98312 | tf_op jit(solution)/shard_map/ppermute | solution.py:51
  27.6 15.6 %collective-permute-start.5 = (bf16[512,128]{1,0:T(8,128)(2,1)S(1)}, bf16[512,128]{1,0:T(8,128)(2,1)S(1)}, u32[]{:S(2)}, u32[]{:S(2)}) collective-permute-start(bf16[512,128]{1,0:T(8,128)(2,1)S(1)} %shard_map.124), channel_id=1, source_target_pairs={{0,8},{4,12},{8,0},{12,4},{16,24},{20,28},{24,16},{28,20},{1,9},{5... | collective-permute-start | bytes 393224 | tf_op jit(solution)/shard_map/ppermute | solution.py:51
  29.0 4.8 %collective-permute-start.13 = (bf16[128,128]{1,0:T(8,128)(2,1)S(1)}, bf16[128,128]{1,0:T(8,128)(2,1)S(1)}, u32[]{:S(2)}, u32[]{:S(2)}) collective-permute-start(bf16[128,128]{1,0:T(8,128)(2,1)S(1)} %get-tuple-element.79), channel_id=1, source_target_pairs={{0,4},{4,0},{8,12},{12,8},{16,20},{20,16},{24,28},{28,24},{1,5},{5... | collective-permute-start | bytes 98312 | tf_op jit(solution)/shard_map/ppermute | solution.py:51
  30.5 4.2 %collective-permute-start.14 = (bf16[128,128]{1,0:T(8,128)(2,1)S(1)}, bf16[128,128]{1,0:T(8,128)(2,1)S(1)}, u32[]{:S(2)}, u32[]{:S(2)}) collective-permute-start(bf16[128,128]{1,0:T(8,128)(2,1)S(1)} %get-tuple-element.80), channel_id=1, source_target_pairs={{0,8},{4,12},{8,0},{12,4},{16,24},{20,28},{24,16},{28,20},{1,9},{5... | collective-permute-start | bytes 98312 | tf_op jit(solution)/shard_map/ppermute | solution.py:51
  31.4 5.2 %collective-permute-start.15 = (bf16[128,128]{1,0:T(8,128)(2,1)S(1)}, bf16[128,128]{1,0:T(8,128)(2,1)S(1)}, u32[]{:S(2)}, u32[]{:S(2)}) collective-permute-start(bf16[128,128]{1,0:T(8,128)(2,1)S(1)} %get-tuple-element.81), channel_id=1, source_target_pairs={{0,12},{4,8},{8,4},{12,0},{16,28},{20,24},{24,20},{28,16},{1,13},{... | collective-permute-start | bytes 98312 | tf_op jit(solution)/shard_map/ppermute | solution.py:51
  32.6 4.7 %collective-permute-start.12 = (bf16[128,384]{1,0:T(8,128)(2,1)S(1)}, bf16[128,384]{1,0:T(8,128)(2,1)S(1)}, u32[]{:S(2)}, u32[]{:S(2)}) collective-permute-start(bf16[128,384]{1,0:T(8,128)(2,1)S(1)} %get-tuple-element.77), channel_id=1, source_target_pairs={{0,8},{4,12},{8,0},{12,4},{16,24},{20,28},{24,16},{28,20},{1,9},{5... | collective-permute-start | bytes 294920 | tf_op jit(solution)/shard_map/ppermute | solution.py:51
  37.6 6.5 %collective-permute-start.16 = (bf16[64,384]{1,0:T(8,128)(2,1)S(1)}, bf16[64,384]{1,0:T(8,128)(2,1)S(1)}, u32[]{:S(2)}, u32[]{:S(2)}) collective-permute-start(bf16[64,384]{1,0:T(8,128)(2,1)S(1)} %get-tuple-element.83), channel_id=1, source_target_pairs={{0,16},{4,20},{8,24},{12,28},{16,0},{20,4},{24,8},{28,12},{1,17},{... | collective-permute-start | bytes 147464 | tf_op jit(solution)/shard_map/ppermute | solution.py:51
  43.3 5.0 %copy-start.4 = (f32[8,64,128]{2,1,0:T(8,128)S(1)}, f32[8,64,128]{2,1,0:T(8,128)}, u32[]{:S(2)}) copy-start(f32[8,64,128]{2,1,0:T(8,128)} %param.13) | copy-start | bytes 786436
  43.3 5.0 %collective-permute-start.6 = (bf16[512,128]{1,0:T(8,128)(2,1)S(1)}, bf16[512,128]{1,0:T(8,128)(2,1)S(1)}, u32[]{:S(2)}, u32[]{:S(2)}) collective-permute-start(bf16[512,128]{1,0:T(8,128)(2,1)S(1)} %shard_map.125), channel_id=1, source_target_pairs={{0,4},{4,0},{8,12},{12,8},{16,20},{20,16},{24,28},{28,24},{1,5},{5... | collective-permute-start | bytes 393224 | tf_op jit(solution)/shard_map/ppermute | solution.py:51

commit v8 on v7

--- a/solution.py
+++ b/solution.py
@@ -57,21 +57,26 @@
 
 def state_kernel(dims, idx_ref, head_ref, k_hbm, v_hbm, w_hbm, x_hbm, kv_ref, kvb_ref, w_ref, x_ref, k_ref, v_ref, sems):
     nh, dk, dv = dims
-    copies = [pltpu.make_async_copy(src, dst, sems.at[n]) for n, (src, dst) in enumerate(
-        ((k_hbm, k_ref), (v_hbm, v_ref), (w_hbm, w_ref), (x_hbm, x_ref)))]
+    copies = []
+    for pair in range(nh // 2):
+        for src, dst, n in ((k_hbm, k_ref, 2 * dk), (v_hbm, v_ref, 2 * dv)):
+            cols = slice(pair * n, (pair + 1) * n)
+            copies.append(pltpu.make_async_copy(src.at[:, cols], dst.at[:, cols], sems.at[len(copies)]))
+    copies.append(pltpu.make_async_copy(w_hbm, w_ref, sems.at[nh]))
+    copies.append(pltpu.make_async_copy(x_hbm, x_ref, sems.at[nh + 1]))
     for copy in copies:
         copy.start()
-    copies[0].wait()
-    copies[1].wait()
     for pair in range(nh // 2):
+        copies[2 * pair].wait()
+        copies[2 * pair + 1].wait()
         turned = k_ref[:, pair * 2 * dk:(pair + 1) * 2 * dk].T
         for j in range(2):
             h = 2 * pair + j
             kv = nn(turned[j * dk:(j + 1) * dk], v_ref[:, h * dv:(h + 1) * dv])
             kv_ref[h * dk:(h + 1) * dk, :] = kv
             kvb_ref[h * dk:(h + 1) * dk, :] = kv.astype(BF16)
-    copies[2].wait()
-    copies[3].wait()
+    copies[nh].wait()
+    copies[nh + 1].wait()
 
 
 def part_ways(entries, upper, send_ref, keep_ref, inner):
@@ -255,8 +260,11 @@
     part_ways(nt(xt_ref[...], sorted_ref[...]), (idx_ref[0] & 1) == 1, send_ref, keep_ref, inner)
 
 
-def far_wgrad_kernel(bits, inner, idx_ref, head_ref, xt_ref, gp_ref, keep_ref, one_ref, two_ref, both_ref, sorted_ref):
-    put_in_order(bits, head_ref, gp_ref, sorted_ref)
+def far_wgrad_kernel(inner, idx_ref, head_ref, xt_ref, *refs):
+    gathered, (keep_ref, one_ref, two_ref, both_ref, sorted_ref) = refs[:-5], refs[-5:]
+    for away, gp_ref in enumerate(gathered):
+        own = gp_ref.shape[0]
+        sorted_ref[pl.ds(pl.multiple_of((head_ref[0] ^ away) * own, 16), own), :] = gp_ref[...]
     total = nt(xt_ref[...], sorted_ref[...])
     right, upper = (idx_ref[0] & 1) == 1, ((idx_ref[0] >> 1) & 1) == 1
     for e in range(total.shape[0] // (4 * inner)):
@@ -273,7 +281,10 @@
 def merge_kernel(bit, inner, idx_ref, near_ref, near_got, far_ref, one_ref, two_ref, both_ref, place_ref,
                  send_ref, keep_ref):
     far = far_ref[...] + one_ref[...].astype(F32) + two_ref[...].astype(F32) + both_ref[...].astype(F32)
-    total = near_ref[...] + near_got[...].astype(F32) + lax.dot_general(
+    n, width = near_ref.shape
+    below = near_got.shape[0] - n * (width // LANES)
+    got = jnp.concatenate([near_got[below + c * n:below + (c + 1) * n, :] for c in range(width // LANES)], axis=1)
+    total = near_ref[...] + got.astype(F32) + lax.dot_general(
         far, place_ref[...], (((1,), (0,)), ((), ())), preferred_element_type=F32, precision=lax.Precision.HIGHEST)
     part_ways(total, ((idx_ref[0] >> bit) & 1) == 1, send_ref, keep_ref, inner)
 
@@ -295,13 +306,28 @@
         send_ref[...] = total.astype(BF16)
 
 
+def pending(bit, top, index, gots, gu_ref):
+    rows = gu_ref.shape[1]
+    total = jnp.where(((index >> top) & 1) == 1, 0.0, gots[0][...].astype(F32))
+    for got in gots[1:]:
+        total = total + got[:rows, :].astype(F32)
+    return (total + jnp.where(((index >> bit) & 1) == 1, gu_ref[bit].astype(F32), 0.0)).astype(BF16)
+
+
 def pend_kernel(bit, top, idx_ref, *refs):
     gots, (gu_ref, send_ref) = refs[:-2], refs[-2:]
-    index = idx_ref[0]
-    total = jnp.where(((index >> top) & 1) == 1, 0.0, gots[0][...].astype(F32))
-    for got in gots[1:]:
-        total = total + got[...].astype(F32)
-    send_ref[...] = (total + jnp.where(((index >> bit) & 1) == 1, gu_ref[bit].astype(F32), 0.0)).astype(BF16)
+    send_ref[...] = pending(bit, top, idx_ref[0], gots, gu_ref)
+
+
+def pack_kernel(bit, top, inner, idx_ref, *refs):
+    gots, (gu_ref, keep_in, got_ref, send_ref, keep_ref, part_ref) = refs[:-6], refs[-6:]
+    rows = gu_ref.shape[1]
+    send_ref[:rows, :] = pending(bit, top, idx_ref[0], gots, gu_ref)
+    upper = ((idx_ref[0] >> bit) & 1) == 1
+    part_ways(keep_in[...] + got_ref[...].astype(F32), upper, part_ref, keep_ref, inner)
+    n = part_ref.shape[0]
+    for c in range(part_ref.shape[1] // LANES):
+        send_ref[rows + c * n:rows + (c + 1) * n, :] = part_ref[:, c * LANES:(c + 1) * LANES]
 
 
 def final_kernel(dims, levels, first, count, idx_ref, *refs):
@@ -403,7 +429,7 @@
         [S((rows, dv), F32), S((rows, dv), BF16), S(w.shape, BF16), S(hidden.shape, BF16)],
         [SM] * 2 + [hbm] * 4, 2 * tokens * rows * dv,
         scratch_shapes=[pltpu.VMEM((tokens, rows), BF16), pltpu.VMEM((tokens, nh * dv), BF16),
-                        pltpu.SemaphoreType.DMA((4,))])(
+                        pltpu.SemaphoreType.DMA((nh + 2,))])(
                             idx, head_idx, *[pltpu.with_memory_space_constraint(a, pltpu.HBM) for a in (keys, values, w, hidden)])
     send, keep, xt = call(
         functools.partial(project_kernel, head_bits - 1),
@@ -443,30 +469,34 @@
     far_rows = call(
         functools.partial(carry_kernel, dims, levels, first, seq_bits), [S((far_own, tokens), BF16)],
         [SM] + [VM] * (seq_bits + 3), 2 * tokens * rows * dv * seq_bits)(idx, *ups, d_out, qt, sig)[0]
-    gots = [partner]
-    for bit in reversed(range(top)):
-        down = call(functools.partial(pend_kernel, bit, top), [S((rows, dv), BF16)], [SM] + [VM] * (len(gots) + 1),
-                    rows * dv)(idx, *gots, gu)[0]
-        gots.append(swap(down, "seq", bit))
-
     near_all = gather_heads(near, head_bits)
     n = width // 2
     send, near_w, near_all = call(
         functools.partial(near_wgrad_kernel, head_bits, per),
         [S((n, cols), BF16), S((n, cols), F32), S((cols, tokens), BF16)],
         [SM] * 2 + [VM] * 2, 2 * tokens * width * cols)(idx, head_idx, xt, near_all)
-    got = swap(send, "seq", 0)
+    near_first = swap(send, "seq", 0)
     n = n // 2
-    send, near_w = call(
-        functools.partial(fold_kernel, 1, per), [S((n, cols), BF16), S((n, cols), F32)],
-        [SM] + [VM] * 2, n * cols)(idx, near_w, got)
-    near_got = swap(send, "seq", 1)
-
-    far_all = gather_heads(far_rows, head_bits)
+
+    gots = [partner]
+    for bit in reversed(range(top)):
+        if bit == 1:
+            down, near_w = call(
+                functools.partial(pack_kernel, bit, top, per),
+                [S((rows + n * (cols // LANES), dv), BF16), S((n, cols), F32)], [SM] + [VM] * (len(gots) + 3),
+                rows * dv + n * cols, scratch_shapes=[pltpu.VMEM((n, cols), BF16)])(
+                    idx, *gots, gu, near_w, near_first)
+        else:
+            down = call(functools.partial(pend_kernel, bit, top), [S((rows, dv), BF16)], [SM] + [VM] * (len(gots) + 1),
+                        rows * dv)(idx, *gots, gu)[0]
+        gots.append(swap(down, "seq", bit))
+    near_got = gots[top - 1]
+
+    far_all = [far_rows] + [exchange(far_rows, "head", away) for away in range(1, n_head)]
     far_w, one, two, both, far_all = call(
-        functools.partial(far_wgrad_kernel, head_bits, per),
+        functools.partial(far_wgrad_kernel, per),
         [S((n, far_cols), F32)] + [S((n, far_cols), BF16)] * 3 + [S((far_cols, tokens), BF16)],
-        [SM] * 2 + [VM] * 2, 2 * tokens * width * far_cols)(idx, head_idx, xt, far_all)
+        [SM] * 2 + [VM] * (n_head + 1), 2 * tokens * width * far_cols)(idx, head_idx, xt, *far_all)
     far_gots = [exchange(one, "seq", 1), exchange(two, "seq", 2),
                 exchange(both, "seq", 3)]
 

time: 51.4 us -> 54.4 us (1.058)
  waiting for transfers between devices: 17.3 us -> 19 us
  starting transfers between devices: 21.7 us -> 22.5 us
    ppermute x17, waiting for transfers between devices: 17.3 us -> 19 us  [exchange(): return lax.ppermute(value, axis, pairs)]
    ppermute x17, starting transfers between devices: 21.7 us -> 22.5 us  [exchange(): return lax.ppermute(value, axis, pairs)]
  transfers between devices with their start and end apart: 17 -> 17, of which waited for: 9 -> 10; matrix products, arithmetic and copies ran while one was open for 2% -> 2% of each run, Pallas kernels for 12% -> 10%
where the time goes in v8:
time: 54.4 us; the launch traced here: 54.3 us
  starting transfers between devices  22.5 us (41%)
  waiting for transfers between devices  19 us (35%)
  Pallas kernels  11.1 us (20%)
  between operations  0.86 us (2%)
  other arithmetic  0.82 us (2%)
    ppermute x17, starting transfers between devices, exchange(): return lax.ppermute(value, axis, pairs)  22.5 us
    ppermute x17, waiting for transfers between devices, exchange(): return lax.ppermute(value, axis, pairs)  19 us
    pallas_call x1, Pallas kernels, body(): call(functools.partial(final_kernel, dims, levels, first, seq_bits), [S(s...  2.88 us
    pallas_call x2, Pallas kernels, body(): call(functools.partial(local_kernel, dims, levels, tuple(range(part * hal...  2.81 us
    pallas_call x1, Pallas kernels, body(): call(functools.partial(state_kernel, dims), [S((rows, dv), F32), S((rows,...  1.92 us
  transfers between devices with their start and end apart: 17, of which 10 were waited for; matrix products, arithmetic and copies ran while one was open for 2% of the time, Pallas kernels for 10%

profile of v8, /device:TPU:0, one launch (start us, length us, event | category | flops | bytes accessed | tf_op | source)
XLA Modules:
  0.0 54.3 jit_solution(11397290469973838739)
XLA Ops:
  0.6 0.0 copy-start.1
  0.6 0.0 copy-start.3
  0.7 1.9 %shard_map.118 = (f32[512,128]{1,0:T(8,128)S(1)}, bf16[512,128]{1,0:T(8,128)(2,1)S(1)}, bf16[512,384]{1,0:T(8,128)(2,1)S(1)}, bf16[256,512]{1,0:T(8,128)(2,1)S(1)}) custom-call(s32[1]{0:T(128)} %bitcast.idx_ref, s32[1]{0:T(128)} %bitcast.1.head_ref.idx_ref, bf16[256,512]{1,0:T(8,128)(2,1)} %refs_10_.1, bf16[256,1024]{1,0:T(8,128)(2,1)} %refs_11_.1, ...), custom_call_target="tpu_custom_call" | custom-call | flops 33554432 | bytes 2097152 | tf_op jit(solution)/shard_map/pallas_call | solution.py:427
  2.6 0.0 copy-start
  2.6 0.4 shard_map.119
  3.0 0.0 copy-start.2
  3.0 3.0 %collective-permute-start.2 = (bf16[192,256]{1,0:T(8,128)(2,1)S(1)}, bf16[192,256]{1,0:T(8,128)(2,1)S(1)}, u32[]{:S(2)}, u32[]{:S(2)}) collective-permute-start(bf16[192,256]{1,0:T(8,128)(2,1)S(1)} %get-tuple-element.50), channel_id=1, source_target_pairs={{0,2},{1,3},{2,0},{3,1},{4,6},{5,7},{6,4},{7,5},{8,10},{9,11},{10,... | collective-permute-start | bytes 294920 | tf_op jit(solution)/shard_map/ppermute | solution.py:51
  6.0 1.5 %collective-permute-start = (bf16[512,128]{1,0:T(8,128)(2,1)S(1)}, bf16[512,128]{1,0:T(8,128)(2,1)S(1)}, u32[]{:S(2)}, u32[]{:S(2)}) collective-permute-start(bf16[512,128]{1,0:T(8,128)(2,1)S(1)} %get-tuple-element.45), channel_id=1, source_target_pairs={{0,4},{4,0},{8,12},{12,8},{16,20},{20,16},{24,28},{28,24},{1,5},{5... | collective-permute-start | bytes 393224 | tf_op jit(solution)/shard_map/ppermute | solution.py:51
  7.5 1.3 %collective-permute-done.2.got_ref = bf16[192,256]{1,0:T(8,128)(2,1)S(1)} collective-permute-done((bf16[192,256]{1,0:T(8,128)(2,1)S(1)}, bf16[192,256]{1,0:T(8,128)(2,1)S(1)}, u32[]{:S(2)}, u32[]{:S(2)}) %collective-permute-start.2) | collective-permute-done | bytes 98336 | tf_op jit(solution)/shard_map/ppermute | solution.py:51
  8.9 0.1 collective-permute-start.3
  8.9 0.0 copy-done.1
  8.9 0.0 copy-done.3
  9.0 0.0 copy-done
  9.0 0.0 copy-done.2
  9.0 0.8 %shard_map.121.gl_ref = f32[96,256]{1,0:T(8,128)S(1)} custom-call(bf16[256,512]{1,0:T(8,128)(2,1)S(1)} %copy-done.2, bf16[256,512]{1,0:T(8,128)(2,1)S(1)} %copy-done.3, bf16[256,1024]{1,0:T(8,128)(2,1)S(1)} %copy-done.1, bf16[256,1024]{1,0:T(8,128)(2,1)S(1)} %copy-done), custom_call_target="tpu_custom_call" | custom-call | flops 201326592 | bytes 196608 | tf_op jit(solution)/shard_map/pallas_call | solution.py:456
  9.7 0.4 collective-permute-done.3.got_ref
  10.1 0.4 shard_map.122
  10.6 1.9 %collective-permute-start.5 = (bf16[96,256]{1,0:T(8,128)(2,1)S(1)}, bf16[96,256]{1,0:T(8,128)(2,1)S(1)}, u32[]{:S(2)}, u32[]{:S(2)}) collective-permute-start(bf16[96,256]{1,0:T(8,128)(2,1)S(1)} %get-tuple-element.55), channel_id=1, source_target_pairs={{0,2},{1,3},{2,0},{3,1},{4,6},{5,7},{6,4},{7,5},{8,10},{9,11},{10,... | collective-permute-start | bytes 147464 | tf_op jit(solution)/shard_map/ppermute | solution.py:51
  12.5 0.0 collective-permute-done.refs_0_
  12.5 1.6 %collective-permute-start.1 = (bf16[512,128]{1,0:T(8,128)(2,1)S(1)}, bf16[512,128]{1,0:T(8,128)(2,1)S(1)}, u32[]{:S(2)}, u32[]{:S(2)}) collective-permute-start(bf16[512,128]{1,0:T(8,128)(2,1)S(1)} %add_convert_fusion), channel_id=1, source_target_pairs={{0,8},{4,12},{8,0},{12,4},{16,24},{20,28},{24,16},{28,20},{1,9},{5... | collective-permute-start | bytes 393224 | tf_op jit(solution)/shard_map/ppermute | solution.py:51
  14.2 0.6 %collective-permute-done.5 = bf16[96,256]{1,0:T(8,128)(2,1)S(1)} collective-permute-done((bf16[96,256]{1,0:T(8,128)(2,1)S(1)}, bf16[96,256]{1,0:T(8,128)(2,1)S(1)}, u32[]{:S(2)}, u32[]{:S(2)}) %collective-permute-start.5) | collective-permute-done | bytes 49184 | tf_op jit(solution)/shard_map/ppermute | solution.py:51
  14.8 0.1 collective-permute-start.6
  14.8 3.0 %collective-permute-done.1.refs_1_ = bf16[512,128]{1,0:T(8,128)(2,1)S(1)} collective-permute-done((bf16[512,128]{1,0:T(8,128)(2,1)S(1)}, bf16[512,128]{1,0:T(8,128)(2,1)S(1)}, u32[]{:S(2)}, u32[]{:S(2)}) %collective-permute-start.1) | collective-permute-done | bytes 131104 | tf_op jit(solution)/shard_map/ppermute | solution.py:51
  17.9 2.6 %collective-permute-start.4 = (bf16[512,128]{1,0:T(8,128)(2,1)S(1)}, bf16[512,128]{1,0:T(8,128)(2,1)S(1)}, u32[]{:S(2)}, u32[]{:S(2)}) collective-permute-start(bf16[512,128]{1,0:T(8,128)(2,1)S(1)} %shard_map.123), channel_id=1, source_target_pairs={{0,16},{4,20},{8,24},{12,28},{16,0},{20,4},{24,8},{28,12},{1,17},{... | collective-permute-start | bytes 393224 | tf_op jit(solution)/shard_map/ppermute | solution.py:51
  20.5 0.0 collective-permute-done.6
  20.6 0.3 shard_map.124
  20.9 1.6 %collective-permute-start.7 = (bf16[256,384]{1,0:T(8,128)(2,1)S(1)}, bf16[256,384]{1,0:T(8,128)(2,1)S(1)}, u32[]{:S(2)}, u32[]{:S(2)}) collective-permute-start(bf16[256,384]{1,0:T(8,128)(2,1)S(1)} %get-tuple-element.57), channel_id=1, source_target_pairs={{0,4},{4,0},{8,12},{12,8},{16,20},{20,16},{24,28},{28,24},{1,5},{5... | collective-permute-start | bytes 589832 | tf_op jit(solution)/shard_map/ppermute | solution.py:51
  22.5 3.6 %collective-permute-done.4.refs_0_.refs_2_.refs_3_ = bf16[512,128]{1,0:T(8,128)(2,1)S(1)} collective-permute-done((bf16[512,128]{1,0:T(8,128)(2,1)S(1)}, bf16[512,128]{1,0:T(8,128)(2,1)S(1)}, u32[]{:S(2)}, u32[]{:S(2)}) %collective-permute-start.4) | collective-permute-done | bytes 131104 | tf_op jit(solution)/shard_map/ppermute | solution.py:51
  26.1 0.7 %shard_map.129.refs_0_ = bf16[32,256]{1,0:T(8,128)(2,1)S(1)} custom-call(s32[1]{0:T(128)} %bitcast.idx_ref, bf16[512,128]{1,0:T(8,128)(2,1)S(1)} %collective-permute-done.refs_0_, bf16[512,128]{1,0:T(8,128)(2,1)S(1)} %collective-permute-done.1.refs_1_, bf16[512,128]{1,0:T(8,128)(2,1)S(1)} %collective-permute-done.4.refs_0_.refs_2_.refs_3_, ...), custom_call_target="tpu_custom_call" | custom-call | flops 100663296 | bytes 32768 | tf_op jit(solution)/shard_map/pallas_call | solution.py:469
  26.8 0.1 collective-permute-start.12
  26.9 0.6 %collective-permute-start.11 = (bf16[32,256]{1,0:T(8,128)(2,1)S(1)}, bf16[32,256]{1,0:T(8,128)(2,1)S(1)}, u32[]{:S(2)}, u32[]{:S(2)}) collective-permute-start(bf16[32,256]{1,0:T(8,128)(2,1)S(1)} %shard_map.129.refs_0_), channel_id=1, source_target_pairs={{0,2},{1,3},{2,0},{3,1},{4,6},{5,7},{6,4},{7,5},{8,10},{9,11},{10,... | collective-permute-start | bytes 49160 | tf_op jit(solution)/shard_map/ppermute | solution.py:51
  27.5 1.2 %collective-permute-start.10 = (bf16[32,256]{1,0:T(8,128)(2,1)S(1)}, bf16[32,256]{1,0:T(8,128)(2,1)S(1)}, u32[]{:S(2)}, u32[]{:S(2)}) collective-permute-start(bf16[32,256]{1,0:T(8,128)(2,1)S(1)} %shard_map.129.refs_0_), channel_id=1, source_target_pairs={{0,1},{1,0},{2,3},{3,2},{4,5},{5,4},{6,7},{7,6},{8,9},{9,8},{10,11... | collective-permute-start | bytes 49160 | tf_op jit(solution)/shard_map/ppermute | solution.py:51
  28.7 1.3 %collective-permute-done.12.refs_3_ = bf16[32,256]{1,0:T(8,128)(2,1)S(1)} collective-permute-done((bf16[32,256]{1,0:T(8,128)(2,1)S(1)}, bf16[32,256]{1,0:T(8,128)(2,1)S(1)}, u32[]{:S(2)}, u32[]{:S(2)}) %collective-permute-start.12) | collective-permute-done | bytes 16416 | tf_op jit(solution)/shard_map/ppermute | solution.py:51
  30.0 0.7 %collective-permute-done.11.refs_2_ = bf16[32,256]{1,0:T(8,128)(2,1)S(1)} collective-permute-done((bf16[32,256]{1,0:T(8,128)(2,1)S(1)}, bf16[32,256]{1,0:T(8,128)(2,1)S(1)}, u32[]{:S(2)}, u32[]{:S(2)}) %collective-permute-start.11) | collective-permute-done | bytes 16416 | tf_op jit(solution)/shard_map/ppermute | solution.py:51
  30.7 0.0 collective-permute-done.10.refs_1_
  30.7 0.2 shard_map.130
  30.9 1.6 %collective-permute-start.13 = (bf16[128,128]{1,0:T(8,128)(2,1)S(1)}, bf16[128,128]{1,0:T(8,128)(2,1)S(1)}, u32[]{:S(2)}, u32[]{:S(2)}) collective-permute-start(bf16[128,128]{1,0:T(8,128)(2,1)S(1)} %get-tuple-element.79), channel_id=1, source_target_pairs={{0,4},{4,0},{8,12},{12,8},{16,20},{20,16},{24,28},{28,24},{1,5},{5... | collective-permute-start | bytes 98312 | tf_op jit(solution)/shard_map/ppermute | solution.py:51
  32.5 0.0 collective-permute-done.7.refs_3_
  32.5 0.1 shard_map.125
  32.7 0.7 %collective-permute-start.8 = (bf16[896,128]{1,0:T(8,128)(2,1)S(1)}, bf16[896,128]{1,0:T(8,128)(2,1)S(1)}, u32[]{:S(2)}, u32[]{:S(2)}) collective-permute-start(bf16[896,128]{1,0:T(8,128)(2,1)S(1)} %get-tuple-element.58), channel_id=1, source_target_pairs={{0,8},{4,12},{8,0},{12,4},{16,24},{20,28},{24,16},{28,20},{1,9},{5... | collective-permute-start | bytes 688136 | tf_op jit(solution)/shard_map/ppermute | solution.py:51
  33.4 1.4 %collective-permute-start.14 = (bf16[128,128]{1,0:T(8,128)(2,1)S(1)}, bf16[128,128]{1,0:T(8,128)(2,1)S(1)}, u32[]{:S(2)}, u32[]{:S(2)}) collective-permute-start(bf16[128,128]{1,0:T(8,128)(2,1)S(1)} %get-tuple-element.80), channel_id=1, source_target_pairs={{0,8},{4,12},{8,0},{12,4},{16,24},{20,28},{24,16},{28,20},{1,9},{5... | collective-permute-start | bytes 98312 | tf_op jit(solution)/shard_map/ppermute | solution.py:51
  34.8 0.6 %collective-permute-start.15 = (bf16[128,128]{1,0:T(8,128)(2,1)S(1)}, bf16[128,128]{1,0:T(8,128)(2,1)S(1)}, u32[]{:S(2)}, u32[]{:S(2)}) collective-permute-start(bf16[128,128]{1,0:T(8,128)(2,1)S(1)} %get-tuple-element.81), channel_id=1, source_target_pairs={{0,12},{4,8},{8,4},{12,0},{16,28},{20,24},{24,20},{28,16},{1,13},{... | collective-permute-start | bytes 98312 | tf_op jit(solution)/shard_map/ppermute | solution.py:51
  35.3 0.1 fusion.1.refs_22_.place_ref
  35.4 0.0 collective-permute-done.13.one_ref
  35.5 5.0 %collective-permute-done.14.two_ref = bf16[128,128]{1,0:T(8,128)(2,1)S(1)} collective-permute-done((bf16[128,128]{1,0:T(8,128)(2,1)S(1)}, bf16[128,128]{1,0:T(8,128)(2,1)S(1)}, u32[]{:S(2)}, u32[]{:S(2)}) %collective-permute-start.14) | collective-permute-done | bytes 32800 | tf_op jit(solution)/shard_map/ppermute | solution.py:51
  40.5 0.3 collective-permute-done.15.both_ref
  40.8 0.0 collective-permute-done.8.refs_1_.refs_4_.near_got
  40.8 0.3 shard_map.132
  41.1 2.3 %collective-permute-start.16 = (bf16[64,384]{1,0:T(8,128)(2,1)S(1)}, bf16[64,384]{1,0:T(8,128)(2,1)S(1)}, u32[]{:S(2)}, u32[]{:S(2)}) collective-permute-start(bf16[64,384]{1,0:T(8,128)(2,1)S(1)} %get-tuple-element.83), channel_id=1, source_target_pairs={{0,16},{4,20},{8,24},{12,28},{16,0},{20,4},{24,8},{28,12},{1,17},{... | collective-permute-start | bytes 147464 | tf_op jit(solution)/shard_map/ppermute | solution.py:51
  43.4 1.4 %shard_map.128 = (f32[512,256]{1,0:T(8,128)S(1)}, f32[256,256]{1,0:T(8,128)S(1)}, f32[256,256]{1,0:T(8,128)S(1)}, f32[256,512]{1,0:T(8,128)S(1)}) custom-call(bf16[256,512]{1,0:T(8,128)(2,1)S(1)} %copy-done.2, bf16[256,512]{1,0:T(8,128)(2,1)S(1)} %copy-done.3, bf16[256,1024]{1,0:T(8,128)(2,1)S(1)} %copy-done.1, bf16[256,1024]{1,0:T(8,128)(2,1)S(1)} %copy-done, ...), custom_call_target="tpu_custom_call" | custom-call | flops 301989888 | bytes 3145728 | tf_op jit(solution)/shard_map/pallas_call | solution.py:524
  44.9 1.4 %shard_map.127 = (f32[512,256]{1,0:T(8,128)S(1)}, f32[256,256]{1,0:T(8,128)S(1)}, f32[256,256]{1,0:T(8,128)S(1)}, f32[256,512]{1,0:T(8,128)S(1)}) custom-call(bf16[256,512]{1,0:T(8,128)(2,1)S(1)} %copy-done.2, bf16[256,512]{1,0:T(8,128)(2,1)S(1)} %copy-done.3, bf16[256,1024]{1,0:T(8,128)(2,1)S(1)} %copy-done.1, bf16[256,1024]{1,0:T(8,128)(2,1)S(1)} %copy-done, ...), custom_call_target="tpu_custom_call" | custom-call | flops 301989888 | bytes 3145728 | tf_op jit(solution)/shard_map/pallas_call | solution.py:524
  46.3 0.1 shard_map.126
  46.3 0.0 copy-start.4
  46.4 1.6 %collective-permute-start.9 = (bf16[512,128]{1,0:T(8,128)(2,1)S(1)}, bf16[512,128]{1,0:T(8,128)(2,1)S(1)}, u32[]{:S(2)}, u32[]{:S(2)}) collective-permute-start(bf16[512,128]{1,0:T(8,128)(2,1)S(1)} %shard_map.126), channel_id=1, source_target_pairs={{0,4},{4,0},{8,12},{12,8},{16,20},{20,16},{24,28},{28,24},{1,5},{5... | collective-permute-start | bytes 393224 | tf_op jit(solution)/shard_map/ppermute | solution.py:51
  47.9 0.0 collective-permute-done.16
  48.0 0.7 %convert_add_fusion = f32[64,384]{1,0:T(8,128)} fusion(f32[64,384]{1,0:T(8,128)S(1)} %get-tuple-element.82, bf16[64,384]{1,0:T(8,128)(2,1)S(1)} %collective-permute-done.16), kind=kLoop, calls=%fused_computation.6 | loop fusion | flops 49152 | bytes 245760 | tf_op jit(solution)/shard_map/add | solution.py:519
  48.6 2.8 %collective-permute-done.9.refs_5_ = bf16[512,128]{1,0:T(8,128)(2,1)S(1)} collective-permute-done((bf16[512,128]{1,0:T(8,128)(2,1)S(1)}, bf16[512,128]{1,0:T(8,128)(2,1)S(1)}, u32[]{:S(2)}, u32[]{:S(2)}) %collective-permute-start.9) | collective-permute-done | bytes 131104 | tf_op jit(solution)/shard_map/ppermute | solution.py:51
  51.4 0.0 copy-done.4
  51.4 2.9 %shard_map.131 = (bf16[256,1024]{1,0:T(8,128)(2,1)}, bf16[256,512]{1,0:T(8,128)(2,1)}, bf16[256,512]{1,0:T(8,128)(2,1)}, bf16[256,512]{1,0:T(8,128)(2,1)}, bf16[256,1024]{1,0:T(8,128)(2,1)}) custom-call(s32[1]{0:T(128)} %bitcast.idx_ref, bf16[512,128]{1,0:T(8,128)(2,1)S(1)} %collective-permute-done.refs_0_, ...), custom_call_target="tpu_custom_call" | custom-call | flops 402653184 | bytes 3670016 | tf_op jit(solution)/shard_map/pallas_call | solution.py:531
  (7 shorter events, 0.1 us)
Async XLA Ops:
  0.6 8.3 %copy-start.1 = (bf16[256,1024]{1,0:T(8,128)(2,1)S(1)}, bf16[256,1024]{1,0:T(8,128)(2,1)}, u32[]{:S(2)}) copy-start(bf16[256,1024]{1,0:T(8,128)(2,1)} %refs_11_.1) | copy-start | bytes 1572868
  0.6 8.3 %copy-start.3 = (bf16[256,512]{1,0:T(8,128)(2,1)S(1)}, bf16[256,512]{1,0:T(8,128)(2,1)}, u32[]{:S(2)}) copy-start(bf16[256,512]{1,0:T(8,128)(2,1)} %q_ref.7) | copy-start | bytes 786436
  2.6 6.4 %copy-start = (bf16[256,1024]{1,0:T(8,128)(2,1)S(1)}, bf16[256,1024]{1,0:T(8,128)(2,1)}, u32[]{:S(2)}) copy-start(bf16[256,1024]{1,0:T(8,128)(2,1)} %refs_8_.1) | copy-start | bytes 1572868
  3.0 6.0 %copy-start.2 = (bf16[256,512]{1,0:T(8,128)(2,1)S(1)}, bf16[256,512]{1,0:T(8,128)(2,1)}, u32[]{:S(2)}) copy-start(bf16[256,512]{1,0:T(8,128)(2,1)} %refs_10_.1) | copy-start | bytes 786436
  3.0 5.8 %collective-permute-start.2 = (bf16[192,256]{1,0:T(8,128)(2,1)S(1)}, bf16[192,256]{1,0:T(8,128)(2,1)S(1)}, u32[]{:S(2)}, u32[]{:S(2)}) collective-permute-start(bf16[192,256]{1,0:T(8,128)(2,1)S(1)} %get-tuple-element.50), channel_id=1, source_target_pairs={{0,2},{1,3},{2,0},{3,1},{4,6},{5,7},{6,4},{7,5},{8,10},{9,11},{10,... | collective-permute-start | bytes 294920 | tf_op jit(solution)/shard_map/ppermute | solution.py:51
  6.0 6.5 %collective-permute-start = (bf16[512,128]{1,0:T(8,128)(2,1)S(1)}, bf16[512,128]{1,0:T(8,128)(2,1)S(1)}, u32[]{:S(2)}, u32[]{:S(2)}) collective-permute-start(bf16[512,128]{1,0:T(8,128)(2,1)S(1)} %get-tuple-element.45), channel_id=1, source_target_pairs={{0,4},{4,0},{8,12},{12,8},{16,20},{20,16},{24,28},{28,24},{1,5},{5... | collective-permute-start | bytes 393224 | tf_op jit(solution)/shard_map/ppermute | solution.py:51
  8.9 1.3 %collective-permute-start.3 = (bf16[96,256]{1,0:T(8,128)(2,1)S(1)}, bf16[96,256]{1,0:T(8,128)(2,1)S(1)}, u32[]{:S(2)}, u32[]{:S(2)}) collective-permute-start(bf16[96,256]{1,0:T(8,128)(2,1)S(1)} %get-tuple-element.52), channel_id=1, source_target_pairs={{0,1},{1,0},{2,3},{3,2},{4,5},{5,4},{6,7},{7,6},{8,9},{9,8},{10,11... | collective-permute-start | bytes 147464 | tf_op jit(solution)/shard_map/ppermute | solution.py:51
  10.6 4.2 %collective-permute-start.5 = (bf16[96,256]{1,0:T(8,128)(2,1)S(1)}, bf16[96,256]{1,0:T(8,128)(2,1)S(1)}, u32[]{:S(2)}, u32[]{:S(2)}) collective-permute-start(bf16[96,256]{1,0:T(8,128)(2,1)S(1)} %get-tuple-element.55), channel_id=1, source_target_pairs={{0,2},{1,3},{2,0},{3,1},{4,6},{5,7},{6,4},{7,5},{8,10},{9,11},{10,... | collective-permute-start | bytes 147464 | tf_op jit(solution)/shard_map/ppermute | solution.py:51
  12.5 5.3 %collective-permute-start.1 = (bf16[512,128]{1,0:T(8,128)(2,1)S(1)}, bf16[512,128]{1,0:T(8,128)(2,1)S(1)}, u32[]{:S(2)}, u32[]{:S(2)}) collective-permute-start(bf16[512,128]{1,0:T(8,128)(2,1)S(1)} %add_convert_fusion), channel_id=1, source_target_pairs={{0,8},{4,12},{8,0},{12,4},{16,24},{20,28},{24,16},{28,20},{1,9},{5... | collective-permute-start | bytes 393224 | tf_op jit(solution)/shard_map/ppermute | solution.py:51
  14.8 5.8 %collective-permute-start.6 = (bf16[192,256]{1,0:T(8,128)(2,1)S(1)}, bf16[192,256]{1,0:T(8,128)(2,1)S(1)}, u32[]{:S(2)}, u32[]{:S(2)}) collective-permute-start(bf16[192,256]{1,0:T(8,128)(2,1)S(1)} %pad_maximum_fusion.1), channel_id=1, source_target_pairs={{0,1},{1,0},{2,3},{3,2},{4,5},{5,4},{6,7},{7,6},{8,9},{9,8},{10,11... | collective-permute-start | bytes 294920 | tf_op jit(solution)/shard_map/ppermute | solution.py:51
  17.9 8.2 %collective-permute-start.4 = (bf16[512,128]{1,0:T(8,128)(2,1)S(1)}, bf16[512,128]{1,0:T(8,128)(2,1)S(1)}, u32[]{:S(2)}, u32[]{:S(2)}) collective-permute-start(bf16[512,128]{1,0:T(8,128)(2,1)S(1)} %shard_map.123), channel_id=1, source_target_pairs={{0,16},{4,20},{8,24},{12,28},{16,0},{20,4},{24,8},{28,12},{1,17},{... | collective-permute-start | bytes 393224 | tf_op jit(solution)/shard_map/ppermute | solution.py:51
  20.9 11.6 %collective-permute-start.7 = (bf16[256,384]{1,0:T(8,128)(2,1)S(1)}, bf16[256,384]{1,0:T(8,128)(2,1)S(1)}, u32[]{:S(2)}, u32[]{:S(2)}) collective-permute-start(bf16[256,384]{1,0:T(8,128)(2,1)S(1)} %get-tuple-element.57), channel_id=1, source_target_pairs={{0,4},{4,0},{8,12},{12,8},{16,20},{20,16},{24,28},{28,24},{1,5},{5... | collective-permute-start | bytes 589832 | tf_op jit(solution)/shard_map/ppermute | solution.py:51
  26.8 3.2 %collective-permute-start.12 = (bf16[32,256]{1,0:T(8,128)(2,1)S(1)}, bf16[32,256]{1,0:T(8,128)(2,1)S(1)}, u32[]{:S(2)}, u32[]{:S(2)}) collective-permute-start(bf16[32,256]{1,0:T(8,128)(2,1)S(1)} %shard_map.129.refs_0_), channel_id=1, source_target_pairs={{0,3},{1,2},{2,1},{3,0},{4,7},{5,6},{6,5},{7,4},{8,11},{9,10},{10,... | collective-permute-start | bytes 49160 | tf_op jit(solution)/shard_map/ppermute | solution.py:51
  26.9 3.8 %collective-permute-start.11 = (bf16[32,256]{1,0:T(8,128)(2,1)S(1)}, bf16[32,256]{1,0:T(8,128)(2,1)S(1)}, u32[]{:S(2)}, u32[]{:S(2)}) collective-permute-start(bf16[32,256]{1,0:T(8,128)(2,1)S(1)} %shard_map.129.refs_0_), channel_id=1, source_target_pairs={{0,2},{1,3},{2,0},{3,1},{4,6},{5,7},{6,4},{7,5},{8,10},{9,11},{10,... | collective-permute-start | bytes 49160 | tf_op jit(solution)/shard_map/ppermute | solution.py:51
  27.5 3.2 %collective-permute-start.10 = (bf16[32,256]{1,0:T(8,128)(2,1)S(1)}, bf16[32,256]{1,0:T(8,128)(2,1)S(1)}, u32[]{:S(2)}, u32[]{:S(2)}) collective-permute-start(bf16[32,256]{1,0:T(8,128)(2,1)S(1)} %shard_map.129.refs_0_), channel_id=1, source_target_pairs={{0,1},{1,0},{2,3},{3,2},{4,5},{5,4},{6,7},{7,6},{8,9},{9,8},{10,11... | collective-permute-start | bytes 49160 | tf_op jit(solution)/shard_map/ppermute | solution.py:51
  30.9 4.5 %collective-permute-start.13 = (bf16[128,128]{1,0:T(8,128)(2,1)S(1)}, bf16[128,128]{1,0:T(8,128)(2,1)S(1)}, u32[]{:S(2)}, u32[]{:S(2)}) collective-permute-start(bf16[128,128]{1,0:T(8,128)(2,1)S(1)} %get-tuple-element.79), channel_id=1, source_target_pairs={{0,4},{4,0},{8,12},{12,8},{16,20},{20,16},{24,28},{28,24},{1,5},{5... | collective-permute-start | bytes 98312 | tf_op jit(solution)/shard_map/ppermute | solution.py:51
  32.7 8.1 %collective-permute-start.8 = (bf16[896,128]{1,0:T(8,128)(2,1)S(1)}, bf16[896,128]{1,0:T(8,128)(2,1)S(1)}, u32[]{:S(2)}, u32[]{:S(2)}) collective-permute-start(bf16[896,128]{1,0:T(8,128)(2,1)S(1)} %get-tuple-element.58), channel_id=1, source_target_pairs={{0,8},{4,12},{8,0},{12,4},{16,24},{20,28},{24,16},{28,20},{1,9},{5... | collective-permute-start | bytes 688136 | tf_op jit(solution)/shard_map/ppermute | solution.py:51
  33.4 7.1 %collective-permute-start.14 = (bf16[128,128]{1,0:T(8,128)(2,1)S(1)}, bf16[128,128]{1,0:T(8,128)(2,1)S(1)}, u32[]{:S(2)}, u32[]{:S(2)}) collective-permute-start(bf16[128,128]{1,0:T(8,128)(2,1)S(1)} %get-tuple-element.80), channel_id=1, source_target_pairs={{0,8},{4,12},{8,0},{12,4},{16,24},{20,28},{24,16},{28,20},{1,9},{5... | collective-permute-start | bytes 98312 | tf_op jit(solution)/shard_map/ppermute | solution.py:51
  34.8 6.0 %collective-permute-start.15 = (bf16[128,128]{1,0:T(8,128)(2,1)S(1)}, bf16[128,128]{1,0:T(8,128)(2,1)S(1)}, u32[]{:S(2)}, u32[]{:S(2)}) collective-permute-start(bf16[128,128]{1,0:T(8,128)(2,1)S(1)} %get-tuple-element.81), channel_id=1, source_target_pairs={{0,12},{4,8},{8,4},{12,0},{16,28},{20,24},{24,20},{28,16},{1,13},{... | collective-permute-start | bytes 98312 | tf_op jit(solution)/shard_map/ppermute | solution.py:51
  41.1 6.8 %collective-permute-start.16 = (bf16[64,384]{1,0:T(8,128)(2,1)S(1)}, bf16[64,384]{1,0:T(8,128)(2,1)S(1)}, u32[]{:S(2)}, u32[]{:S(2)}) collective-permute-start(bf16[64,384]{1,0:T(8,128)(2,1)S(1)} %get-tuple-element.83), channel_id=1, source_target_pairs={{0,16},{4,20},{8,24},{12,28},{16,0},{20,4},{24,8},{28,12},{1,17},{... | collective-permute-start | bytes 147464 | tf_op jit(solution)/shard_map/ppermute | solution.py:51
  46.3 5.0 %copy-start.4 = (f32[8,64,128]{2,1,0:T(8,128)S(1)}, f32[8,64,128]{2,1,0:T(8,128)}, u32[]{:S(2)}) copy-start(f32[8,64,128]{2,1,0:T(8,128)} %param.13) | copy-start | bytes 786436
  46.4 5.0 %collective-permute-start.9 = (bf16[512,128]{1,0:T(8,128)(2,1)S(1)}, bf16[512,128]{1,0:T(8,128)(2,1)S(1)}, u32[]{:S(2)}, u32[]{:S(2)}) collective-permute-start(bf16[512,128]{1,0:T(8,128)(2,1)S(1)} %shard_map.126), channel_id=1, source_target_pairs={{0,4},{4,0},{8,12},{12,8},{16,20},{20,16},{24,28},{28,24},{1,5},{5... | collective-permute-start | bytes 393224 | tf_op jit(solution)/shard_map/ppermute | solution.py:51

commit v9 on v7

--- a/solution.py
+++ b/solution.py
@@ -255,10 +255,15 @@
     part_ways(nt(xt_ref[...], sorted_ref[...]), (idx_ref[0] & 1) == 1, send_ref, keep_ref, inner)
 
 
-def far_wgrad_kernel(bits, inner, idx_ref, head_ref, xt_ref, gp_ref, keep_ref, one_ref, two_ref, both_ref, sorted_ref):
-    put_in_order(bits, head_ref, gp_ref, sorted_ref)
+def far_wgrad_kernel(inner, idx_ref, head_ref, xt_ref, near_in, near_got, *refs):
+    gathered, (keep_ref, one_ref, two_ref, both_ref, near_ref, sorted_ref) = refs[:-6], refs[-6:]
+    for away, gp_ref in enumerate(gathered):
+        own = gp_ref.shape[0]
+        sorted_ref[pl.ds(pl.multiple_of((head_ref[0] ^ away) * own, 16), own), :] = gp_ref[...]
     total = nt(xt_ref[...], sorted_ref[...])
     right, upper = (idx_ref[0] & 1) == 1, ((idx_ref[0] >> 1) & 1) == 1
+    cols = near_ref.shape[1]
+    part_ways(near_in[...] + near_got[...].astype(F32), upper, two_ref.at[:, :cols], near_ref, inner)
     for e in range(total.shape[0] // (4 * inner)):
         parts = [total[(4 * e + n) * inner:(4 * e + n + 1) * inner] for n in range(4)]
         kept, sent = jnp.where(right, parts[1], parts[0]), jnp.where(right, parts[0], parts[1])
@@ -266,14 +271,14 @@
         at = slice(e * inner, (e + 1) * inner)
         keep_ref[at, :] = jnp.where(upper, kept_up, kept)
         one_ref[at, :] = jnp.where(upper, sent_up, sent).astype(BF16)
-        two_ref[at, :] = jnp.where(upper, kept, kept_up).astype(BF16)
+        two_ref[at, cols:] = jnp.where(upper, kept, kept_up).astype(BF16)
         both_ref[at, :] = jnp.where(upper, sent, sent_up).astype(BF16)
 
 
-def merge_kernel(bit, inner, idx_ref, near_ref, near_got, far_ref, one_ref, two_ref, both_ref, place_ref,
-                 send_ref, keep_ref):
-    far = far_ref[...] + one_ref[...].astype(F32) + two_ref[...].astype(F32) + both_ref[...].astype(F32)
-    total = near_ref[...] + near_got[...].astype(F32) + lax.dot_general(
+def merge_kernel(bit, inner, idx_ref, near_ref, far_ref, one_ref, two_ref, both_ref, place_ref, send_ref, keep_ref):
+    cols = near_ref.shape[1]
+    far = far_ref[...] + one_ref[...].astype(F32) + two_ref[:, cols:].astype(F32) + both_ref[...].astype(F32)
+    total = near_ref[...] + two_ref[:, :cols].astype(F32) + lax.dot_general(
         far, place_ref[...], (((1,), (0,)), ((), ())), preferred_element_type=F32, precision=lax.Precision.HIGHEST)
     part_ways(total, ((idx_ref[0] >> bit) & 1) == 1, send_ref, keep_ref, inner)
 
@@ -455,18 +460,16 @@
         functools.partial(near_wgrad_kernel, head_bits, per),
         [S((n, cols), BF16), S((n, cols), F32), S((cols, tokens), BF16)],
         [SM] * 2 + [VM] * 2, 2 * tokens * width * cols)(idx, head_idx, xt, near_all)
-    got = swap(send, "seq", 0)
+    near_got = swap(send, "seq", 0)
+
+    far_all = [far_rows] + [exchange(far_rows, "head", away) for away in range(1, n_head)]
     n = n // 2
-    send, near_w = call(
-        functools.partial(fold_kernel, 1, per), [S((n, cols), BF16), S((n, cols), F32)],
-        [SM] + [VM] * 2, n * cols)(idx, near_w, got)
-    near_got = swap(send, "seq", 1)
-
-    far_all = gather_heads(far_rows, head_bits)
-    far_w, one, two, both, far_all = call(
-        functools.partial(far_wgrad_kernel, head_bits, per),
-        [S((n, far_cols), F32)] + [S((n, far_cols), BF16)] * 3 + [S((far_cols, tokens), BF16)],
-        [SM] * 2 + [VM] * 2, 2 * tokens * width * far_cols)(idx, head_idx, xt, far_all)
+    part, joined = S((n, far_cols), BF16), S((n, cols + far_cols), BF16)
+    far_w, one, two, both, near_w, far_all = call(
+        functools.partial(far_wgrad_kernel, per),
+        [S((n, far_cols), F32), part, joined, part, S((n, cols), F32), S((far_cols, tokens), BF16)],
+        [SM] * 2 + [VM] * (n_head + 3), 2 * tokens * width * far_cols)(
+            idx, head_idx, xt, near_w, near_got, *far_all)
     far_gots = [exchange(one, "seq", 1), exchange(two, "seq", 2),
                 exchange(both, "seq", 3)]
 
@@ -477,8 +480,8 @@
     place = ((at == col) & (within < far)).astype(F32)
     n = n // 2
     send, keep = call(
-        functools.partial(merge_kernel, 2, per), [S((n, cols), BF16), S((n, cols), F32)], [SM] + [VM] * 7,
-        4 * n * far_cols * cols)(idx, near_w, near_got, far_w, *far_gots, place)
+        functools.partial(merge_kernel, 2, per), [S((n, cols), BF16), S((n, cols), F32)], [SM] + [VM] * 6,
+        4 * n * far_cols * cols)(idx, near_w, far_w, *far_gots, place)
     got = swap(send, "seq", 2)
     for bit in range(3, seq_bits):
         n = n // 2

time: 51.4 us -> 47.1 us (0.916)
  waiting for transfers between devices: 17.3 us -> 12 us
  starting transfers between devices: 21.7 us -> 22.6 us
    ppermute x17, waiting for transfers between devices: 17.3 us -> 12 us  [exchange(): return lax.ppermute(value, axis, pairs)]
    ppermute x17, starting transfers between devices: 21.7 us -> 22.6 us  [exchange(): return lax.ppermute(value, axis, pairs)]
  transfers between devices with their start and end apart: 17 -> 17, of which waited for: 9 -> 8; matrix products, arithmetic and copies ran while one was open for 2% -> 0% of each run, Pallas kernels for 12% -> 19%
where the time goes in v9:
time: 47.1 us; the launch traced here: 46.9 us
  starting transfers between devices  22.6 us (48%)
  waiting for transfers between devices  12 us (25%)
  Pallas kernels  10.6 us (23%)
  between operations  0.89 us (2%)
  other arithmetic  0.82 us (2%)
    ppermute x17, starting transfers between devices, exchange(): return lax.ppermute(value, axis, pairs)  22.6 us
    ppermute x17, waiting for transfers between devices, exchange(): return lax.ppermute(value, axis, pairs)  12 us
    pallas_call x1, Pallas kernels, body(): call(functools.partial(final_kernel, dims, levels, first, seq_bits), [S(s...  2.89 us
    pallas_call x2, Pallas kernels, body(): call(functools.partial(local_kernel, dims, levels, tuple(range(part * hal...  2.81 us
    pallas_call x1, Pallas kernels, body(): call(functools.partial(state_kernel, dims), [S((rows, dv), F32), S((rows,...  1.5 us
  transfers between devices with their start and end apart: 17, of which 8 were waited for; matrix products, arithmetic and copies ran while one was open for 0% of the time, Pallas kernels for 19%

profile of v9, /device:TPU:0, one launch (start us, length us, event | category | flops | bytes accessed | tf_op | source)
XLA Modules:
  0.0 46.9 jit_solution(5405923661509616187)
XLA Ops:
  0.6 0.0 copy-start.1
  0.6 0.0 copy-start.3
  0.7 1.5 %shard_map.118 = (f32[512,128]{1,0:T(8,128)S(1)}, bf16[512,128]{1,0:T(8,128)(2,1)S(1)}, bf16[512,384]{1,0:T(8,128)(2,1)S(1)}, bf16[256,512]{1,0:T(8,128)(2,1)S(1)}) custom-call(s32[1]{0:T(128)} %bitcast.idx_ref, s32[1]{0:T(128)} %bitcast.1.head_ref.idx_ref, bf16[256,512]{1,0:T(8,128)(2,1)} %refs_10_.1, bf16[256,1024]{1,0:T(8,128)(2,1)} %refs_11_.1, ...), custom_call_target="tpu_custom_call" | custom-call | flops 33554432 | bytes 2097152 | tf_op jit(solution)/shard_map/pallas_call | solution.py:406
  2.2 0.0 copy-start
  2.2 0.4 shard_map.119
  2.6 0.0 copy-start.2
  2.6 3.0 %collective-permute-start.2 = (bf16[192,256]{1,0:T(8,128)(2,1)S(1)}, bf16[192,256]{1,0:T(8,128)(2,1)S(1)}, u32[]{:S(2)}, u32[]{:S(2)}) collective-permute-start(bf16[192,256]{1,0:T(8,128)(2,1)S(1)} %get-tuple-element.49), channel_id=1, source_target_pairs={{0,2},{1,3},{2,0},{3,1},{4,6},{5,7},{6,4},{7,5},{8,10},{9,11},{10,... | collective-permute-start | bytes 294920 | tf_op jit(solution)/shard_map/ppermute | solution.py:51
  5.6 1.5 %collective-permute-start = (bf16[512,128]{1,0:T(8,128)(2,1)S(1)}, bf16[512,128]{1,0:T(8,128)(2,1)S(1)}, u32[]{:S(2)}, u32[]{:S(2)}) collective-permute-start(bf16[512,128]{1,0:T(8,128)(2,1)S(1)} %get-tuple-element.44), channel_id=1, source_target_pairs={{0,4},{4,0},{8,12},{12,8},{16,20},{20,16},{24,28},{28,24},{1,5},{5... | collective-permute-start | bytes 393224 | tf_op jit(solution)/shard_map/ppermute | solution.py:51
  7.1 1.3 %collective-permute-done.2.got_ref = bf16[192,256]{1,0:T(8,128)(2,1)S(1)} collective-permute-done((bf16[192,256]{1,0:T(8,128)(2,1)S(1)}, bf16[192,256]{1,0:T(8,128)(2,1)S(1)}, u32[]{:S(2)}, u32[]{:S(2)}) %collective-permute-start.2) | collective-permute-done | bytes 98336 | tf_op jit(solution)/shard_map/ppermute | solution.py:51
  8.4 0.1 collective-permute-start.3
  8.5 0.0 copy-done.1
  8.5 0.0 copy-done.3
  8.5 0.0 copy-done
  8.5 0.0 copy-done.2
  8.6 0.8 %shard_map.121.gl_ref = f32[96,256]{1,0:T(8,128)S(1)} custom-call(bf16[256,512]{1,0:T(8,128)(2,1)S(1)} %copy-done.2, bf16[256,512]{1,0:T(8,128)(2,1)S(1)} %copy-done.3, bf16[256,1024]{1,0:T(8,128)(2,1)S(1)} %copy-done.1, bf16[256,1024]{1,0:T(8,128)(2,1)S(1)} %copy-done), custom_call_target="tpu_custom_call" | custom-call | flops 201326592 | bytes 196608 | tf_op jit(solution)/shard_map/pallas_call | solution.py:435
  9.3 0.4 collective-permute-done.3.got_ref
  9.7 0.4 shard_map.122
  10.2 1.9 %collective-permute-start.7 = (bf16[96,256]{1,0:T(8,128)(2,1)S(1)}, bf16[96,256]{1,0:T(8,128)(2,1)S(1)}, u32[]{:S(2)}, u32[]{:S(2)}) collective-permute-start(bf16[96,256]{1,0:T(8,128)(2,1)S(1)} %get-tuple-element.64), channel_id=1, source_target_pairs={{0,2},{1,3},{2,0},{3,1},{4,6},{5,7},{6,4},{7,5},{8,10},{9,11},{10,... | collective-permute-start | bytes 147464 | tf_op jit(solution)/shard_map/ppermute | solution.py:51
  12.1 0.0 collective-permute-done.refs_0_
  12.1 1.6 %collective-permute-start.1 = (bf16[512,128]{1,0:T(8,128)(2,1)S(1)}, bf16[512,128]{1,0:T(8,128)(2,1)S(1)}, u32[]{:S(2)}, u32[]{:S(2)}) collective-permute-start(bf16[512,128]{1,0:T(8,128)(2,1)S(1)} %add_convert_fusion), channel_id=1, source_target_pairs={{0,8},{4,12},{8,0},{12,4},{16,24},{20,28},{24,16},{28,20},{1,9},{5... | collective-permute-start | bytes 393224 | tf_op jit(solution)/shard_map/ppermute | solution.py:51
  13.7 0.6 %collective-permute-done.7 = bf16[96,256]{1,0:T(8,128)(2,1)S(1)} collective-permute-done((bf16[96,256]{1,0:T(8,128)(2,1)S(1)}, bf16[96,256]{1,0:T(8,128)(2,1)S(1)}, u32[]{:S(2)}, u32[]{:S(2)}) %collective-permute-start.7) | collective-permute-done | bytes 49184 | tf_op jit(solution)/shard_map/ppermute | solution.py:51
  14.3 0.1 collective-permute-start.8
  14.4 3.0 %collective-permute-done.1.refs_1_ = bf16[512,128]{1,0:T(8,128)(2,1)S(1)} collective-permute-done((bf16[512,128]{1,0:T(8,128)(2,1)S(1)}, bf16[512,128]{1,0:T(8,128)(2,1)S(1)}, u32[]{:S(2)}, u32[]{:S(2)}) %collective-permute-start.1) | collective-permute-done | bytes 131104 | tf_op jit(solution)/shard_map/ppermute | solution.py:51
  17.5 2.6 %collective-permute-start.4 = (bf16[512,128]{1,0:T(8,128)(2,1)S(1)}, bf16[512,128]{1,0:T(8,128)(2,1)S(1)}, u32[]{:S(2)}, u32[]{:S(2)}) collective-permute-start(bf16[512,128]{1,0:T(8,128)(2,1)S(1)} %shard_map.123), channel_id=1, source_target_pairs={{0,16},{4,20},{8,24},{12,28},{16,0},{20,4},{24,8},{28,12},{1,17},{... | collective-permute-start | bytes 393224 | tf_op jit(solution)/shard_map/ppermute | solution.py:51
  20.1 0.0 collective-permute-done.8
  20.1 0.3 shard_map.128
  20.5 1.6 %collective-permute-start.9 = (bf16[256,384]{1,0:T(8,128)(2,1)S(1)}, bf16[256,384]{1,0:T(8,128)(2,1)S(1)}, u32[]{:S(2)}, u32[]{:S(2)}) collective-permute-start(bf16[256,384]{1,0:T(8,128)(2,1)S(1)} %get-tuple-element.67), channel_id=1, source_target_pairs={{0,4},{4,0},{8,12},{12,8},{16,20},{20,16},{24,28},{28,24},{1,5},{5... | collective-permute-start | bytes 589832 | tf_op jit(solution)/shard_map/ppermute | solution.py:51
  22.1 3.6 %collective-permute-done.4.refs_0_.refs_2_.refs_3_ = bf16[512,128]{1,0:T(8,128)(2,1)S(1)} collective-permute-done((bf16[512,128]{1,0:T(8,128)(2,1)S(1)}, bf16[512,128]{1,0:T(8,128)(2,1)S(1)}, u32[]{:S(2)}, u32[]{:S(2)}) %collective-permute-start.4) | collective-permute-done | bytes 131104 | tf_op jit(solution)/shard_map/ppermute | solution.py:51
  25.7 0.1 shard_map.124
  25.7 0.7 %collective-permute-start.5 = (bf16[512,128]{1,0:T(8,128)(2,1)S(1)}, bf16[512,128]{1,0:T(8,128)(2,1)S(1)}, u32[]{:S(2)}, u32[]{:S(2)}) collective-permute-start(bf16[512,128]{1,0:T(8,128)(2,1)S(1)} %shard_map.124), channel_id=1, source_target_pairs={{0,8},{4,12},{8,0},{12,4},{16,24},{20,28},{24,16},{28,20},{1,9},{5... | collective-permute-start | bytes 393224 | tf_op jit(solution)/shard_map/ppermute | solution.py:51
  26.5 0.7 %shard_map.129.refs_0_ = bf16[32,256]{1,0:T(8,128)(2,1)S(1)} custom-call(s32[1]{0:T(128)} %bitcast.idx_ref, bf16[512,128]{1,0:T(8,128)(2,1)S(1)} %collective-permute-done.refs_0_, bf16[512,128]{1,0:T(8,128)(2,1)S(1)} %collective-permute-done.1.refs_1_, bf16[512,128]{1,0:T(8,128)(2,1)S(1)} %collective-permute-done.4.refs_0_.refs_2_.refs_3_, ...), custom_call_target="tpu_custom_call" | custom-call | flops 100663296 | bytes 32768 | tf_op jit(solution)/shard_map/pallas_call | solution.py:448
  27.2 0.1 collective-permute-start.12
  27.2 0.9 %collective-permute-start.11 = (bf16[32,256]{1,0:T(8,128)(2,1)S(1)}, bf16[32,256]{1,0:T(8,128)(2,1)S(1)}, u32[]{:S(2)}, u32[]{:S(2)}) collective-permute-start(bf16[32,256]{1,0:T(8,128)(2,1)S(1)} %shard_map.129.refs_0_), channel_id=1, source_target_pairs={{0,2},{1,3},{2,0},{3,1},{4,6},{5,7},{6,4},{7,5},{8,10},{9,11},{10,... | collective-permute-start | bytes 49160 | tf_op jit(solution)/shard_map/ppermute | solution.py:51
  28.1 0.9 %collective-permute-start.10 = (bf16[32,256]{1,0:T(8,128)(2,1)S(1)}, bf16[32,256]{1,0:T(8,128)(2,1)S(1)}, u32[]{:S(2)}, u32[]{:S(2)}) collective-permute-start(bf16[32,256]{1,0:T(8,128)(2,1)S(1)} %shard_map.129.refs_0_), channel_id=1, source_target_pairs={{0,1},{1,0},{2,3},{3,2},{4,5},{5,4},{6,7},{7,6},{8,9},{9,8},{10,11... | collective-permute-start | bytes 49160 | tf_op jit(solution)/shard_map/ppermute | solution.py:51
  29.1 1.3 %collective-permute-done.12.refs_3_ = bf16[32,256]{1,0:T(8,128)(2,1)S(1)} collective-permute-done((bf16[32,256]{1,0:T(8,128)(2,1)S(1)}, bf16[32,256]{1,0:T(8,128)(2,1)S(1)}, u32[]{:S(2)}, u32[]{:S(2)}) %collective-permute-start.12) | collective-permute-done | bytes 16416 | tf_op jit(solution)/shard_map/ppermute | solution.py:51
  30.4 0.7 %collective-permute-done.11.refs_2_ = bf16[32,256]{1,0:T(8,128)(2,1)S(1)} collective-permute-done((bf16[32,256]{1,0:T(8,128)(2,1)S(1)}, bf16[32,256]{1,0:T(8,128)(2,1)S(1)}, u32[]{:S(2)}, u32[]{:S(2)}) %collective-permute-start.11) | collective-permute-done | bytes 16416 | tf_op jit(solution)/shard_map/ppermute | solution.py:51
  31.0 0.0 collective-permute-done.10.refs_1_
  31.0 0.0 collective-permute-done.9.near_got
  31.0 0.3 shard_map.130
  31.3 1.6 %collective-permute-start.13 = (bf16[128,128]{1,0:T(8,128)(2,1)S(1)}, bf16[128,128]{1,0:T(8,128)(2,1)S(1)}, u32[]{:S(2)}, u32[]{:S(2)}) collective-permute-start(bf16[128,128]{1,0:T(8,128)(2,1)S(1)} %get-tuple-element.77), channel_id=1, source_target_pairs={{0,4},{4,0},{8,12},{12,8},{16,20},{20,16},{24,28},{28,24},{1,5},{5... | collective-permute-start | bytes 98312 | tf_op jit(solution)/shard_map/ppermute | solution.py:51
  32.9 1.3 %collective-permute-start.15 = (bf16[128,128]{1,0:T(8,128)(2,1)S(1)}, bf16[128,128]{1,0:T(8,128)(2,1)S(1)}, u32[]{:S(2)}, u32[]{:S(2)}) collective-permute-start(bf16[128,128]{1,0:T(8,128)(2,1)S(1)} %get-tuple-element.79), channel_id=1, source_target_pairs={{0,12},{4,8},{8,4},{12,0},{16,28},{20,24},{24,20},{28,16},{1,13},{... | collective-permute-start | bytes 98312 | tf_op jit(solution)/shard_map/ppermute | solution.py:51
  34.2 0.7 %collective-permute-start.14 = (bf16[128,512]{1,0:T(8,128)(2,1)S(1)}, bf16[128,512]{1,0:T(8,128)(2,1)S(1)}, u32[]{:S(2)}, u32[]{:S(2)}) collective-permute-start(bf16[128,512]{1,0:T(8,128)(2,1)S(1)} %get-tuple-element.78), channel_id=1, source_target_pairs={{0,8},{4,12},{8,0},{12,4},{16,24},{20,28},{24,16},{28,20},{1,9},{5... | collective-permute-start | bytes 393224 | tf_op jit(solution)/shard_map/ppermute | solution.py:51
  34.9 0.0 collective-permute-done.5.refs_1_.refs_4_
  34.9 0.1 shard_map.125
  34.9 1.6 %collective-permute-start.6 = (bf16[512,128]{1,0:T(8,128)(2,1)S(1)}, bf16[512,128]{1,0:T(8,128)(2,1)S(1)}, u32[]{:S(2)}, u32[]{:S(2)}) collective-permute-start(bf16[512,128]{1,0:T(8,128)(2,1)S(1)} %shard_map.125), channel_id=1, source_target_pairs={{0,4},{4,0},{8,12},{12,8},{16,20},{20,16},{24,28},{28,24},{1,5},{5... | collective-permute-start | bytes 393224 | tf_op jit(solution)/shard_map/ppermute | solution.py:51
  36.5 0.1 fusion.1.refs_22_.place_ref
  36.6 1.4 %shard_map.127 = (f32[512,256]{1,0:T(8,128)S(1)}, f32[256,256]{1,0:T(8,128)S(1)}, f32[256,256]{1,0:T(8,128)S(1)}, f32[256,512]{1,0:T(8,128)S(1)}) custom-call(bf16[256,512]{1,0:T(8,128)(2,1)S(1)} %copy-done.2, bf16[256,512]{1,0:T(8,128)(2,1)S(1)} %copy-done.3, bf16[256,1024]{1,0:T(8,128)(2,1)S(1)} %copy-done.1, bf16[256,1024]{1,0:T(8,128)(2,1)S(1)} %copy-done, ...), custom_call_target="tpu_custom_call" | custom-call | flops 301989888 | bytes 3145728 | tf_op jit(solution)/shard_map/pallas_call | solution.py:497
  38.0 0.0 collective-permute-done.13.one_ref
  38.0 0.0 collective-permute-done.15.both_ref
  38.1 1.1 %collective-permute-done.14.two_ref = bf16[128,512]{1,0:T(8,128)(2,1)S(1)} collective-permute-done((bf16[128,512]{1,0:T(8,128)(2,1)S(1)}, bf16[128,512]{1,0:T(8,128)(2,1)S(1)}, u32[]{:S(2)}, u32[]{:S(2)}) %collective-permute-start.14) | collective-permute-done | bytes 131104 | tf_op jit(solution)/shard_map/ppermute | solution.py:51
  39.2 0.3 shard_map.132
  39.5 0.0 copy-start.4
  39.5 2.4 %collective-permute-start.16 = (bf16[64,384]{1,0:T(8,128)(2,1)S(1)}, bf16[64,384]{1,0:T(8,128)(2,1)S(1)}, u32[]{:S(2)}, u32[]{:S(2)}) collective-permute-start(bf16[64,384]{1,0:T(8,128)(2,1)S(1)} %get-tuple-element.81), channel_id=1, source_target_pairs={{0,16},{4,20},{8,24},{12,28},{16,0},{20,4},{24,8},{28,12},{1,17},{... | collective-permute-start | bytes 147464 | tf_op jit(solution)/shard_map/ppermute | solution.py:51
  41.9 1.4 %shard_map.126 = (f32[512,256]{1,0:T(8,128)S(1)}, f32[256,256]{1,0:T(8,128)S(1)}, f32[256,256]{1,0:T(8,128)S(1)}, f32[256,512]{1,0:T(8,128)S(1)}) custom-call(bf16[256,512]{1,0:T(8,128)(2,1)S(1)} %copy-done.2, bf16[256,512]{1,0:T(8,128)(2,1)S(1)} %copy-done.3, bf16[256,1024]{1,0:T(8,128)(2,1)S(1)} %copy-done.1, bf16[256,1024]{1,0:T(8,128)(2,1)S(1)} %copy-done, ...), custom_call_target="tpu_custom_call" | custom-call | flops 301989888 | bytes 3145728 | tf_op jit(solution)/shard_map/pallas_call | solution.py:497
  43.4 0.0 collective-permute-done.6.refs_5_
  43.4 0.0 copy-done.4
  43.4 2.9 %shard_map.131 = (bf16[256,1024]{1,0:T(8,128)(2,1)}, bf16[256,512]{1,0:T(8,128)(2,1)}, bf16[256,512]{1,0:T(8,128)(2,1)}, bf16[256,512]{1,0:T(8,128)(2,1)}, bf16[256,1024]{1,0:T(8,128)(2,1)}) custom-call(s32[1]{0:T(128)} %bitcast.idx_ref, bf16[512,128]{1,0:T(8,128)(2,1)S(1)} %collective-permute-done.refs_0_, ...), custom_call_target="tpu_custom_call" | custom-call | flops 402653184 | bytes 3670016 | tf_op jit(solution)/shard_map/pallas_call | solution.py:504
  46.3 0.0 collective-permute-done.16
  46.3 0.7 %convert_add_fusion = f32[64,384]{1,0:T(8,128)} fusion(f32[64,384]{1,0:T(8,128)S(1)} %get-tuple-element.80, bf16[64,384]{1,0:T(8,128)(2,1)S(1)} %collective-permute-done.16), kind=kLoop, calls=%fused_computation.6 | loop fusion | flops 49152 | bytes 245760 | tf_op jit(solution)/shard_map/add | solution.py:492
  (7 shorter events, 0.1 us)
Async XLA Ops:
  0.6 7.9 %copy-start.1 = (bf16[256,1024]{1,0:T(8,128)(2,1)S(1)}, bf16[256,1024]{1,0:T(8,128)(2,1)}, u32[]{:S(2)}) copy-start(bf16[256,1024]{1,0:T(8,128)(2,1)} %refs_11_.1) | copy-start | bytes 1572868
  0.6 7.9 %copy-start.3 = (bf16[256,512]{1,0:T(8,128)(2,1)S(1)}, bf16[256,512]{1,0:T(8,128)(2,1)}, u32[]{:S(2)}) copy-start(bf16[256,512]{1,0:T(8,128)(2,1)} %q_ref.7) | copy-start | bytes 786436
  2.2 6.4 %copy-start = (bf16[256,1024]{1,0:T(8,128)(2,1)S(1)}, bf16[256,1024]{1,0:T(8,128)(2,1)}, u32[]{:S(2)}) copy-start(bf16[256,1024]{1,0:T(8,128)(2,1)} %refs_8_.1) | copy-start | bytes 1572868
  2.6 6.0 %copy-start.2 = (bf16[256,512]{1,0:T(8,128)(2,1)S(1)}, bf16[256,512]{1,0:T(8,128)(2,1)}, u32[]{:S(2)}) copy-start(bf16[256,512]{1,0:T(8,128)(2,1)} %refs_10_.1) | copy-start | bytes 786436
  2.6 5.8 %collective-permute-start.2 = (bf16[192,256]{1,0:T(8,128)(2,1)S(1)}, bf16[192,256]{1,0:T(8,128)(2,1)S(1)}, u32[]{:S(2)}, u32[]{:S(2)}) collective-permute-start(bf16[192,256]{1,0:T(8,128)(2,1)S(1)} %get-tuple-element.49), channel_id=1, source_target_pairs={{0,2},{1,3},{2,0},{3,1},{4,6},{5,7},{6,4},{7,5},{8,10},{9,11},{10,... | collective-permute-start | bytes 294920 | tf_op jit(solution)/shard_map/ppermute | solution.py:51
  5.6 6.4 %collective-permute-start = (bf16[512,128]{1,0:T(8,128)(2,1)S(1)}, bf16[512,128]{1,0:T(8,128)(2,1)S(1)}, u32[]{:S(2)}, u32[]{:S(2)}) collective-permute-start(bf16[512,128]{1,0:T(8,128)(2,1)S(1)} %get-tuple-element.44), channel_id=1, source_target_pairs={{0,4},{4,0},{8,12},{12,8},{16,20},{20,16},{24,28},{28,24},{1,5},{5... | collective-permute-start | bytes 393224 | tf_op jit(solution)/shard_map/ppermute | solution.py:51
  8.4 1.3 %collective-permute-start.3 = (bf16[96,256]{1,0:T(8,128)(2,1)S(1)}, bf16[96,256]{1,0:T(8,128)(2,1)S(1)}, u32[]{:S(2)}, u32[]{:S(2)}) collective-permute-start(bf16[96,256]{1,0:T(8,128)(2,1)S(1)} %get-tuple-element.51), channel_id=1, source_target_pairs={{0,1},{1,0},{2,3},{3,2},{4,5},{5,4},{6,7},{7,6},{8,9},{9,8},{10,11... | collective-permute-start | bytes 147464 | tf_op jit(solution)/shard_map/ppermute | solution.py:51
  10.2 4.2 %collective-permute-start.7 = (bf16[96,256]{1,0:T(8,128)(2,1)S(1)}, bf16[96,256]{1,0:T(8,128)(2,1)S(1)}, u32[]{:S(2)}, u32[]{:S(2)}) collective-permute-start(bf16[96,256]{1,0:T(8,128)(2,1)S(1)} %get-tuple-element.64), channel_id=1, source_target_pairs={{0,2},{1,3},{2,0},{3,1},{4,6},{5,7},{6,4},{7,5},{8,10},{9,11},{10,... | collective-permute-start | bytes 147464 | tf_op jit(solution)/shard_map/ppermute | solution.py:51
  12.1 5.3 %collective-permute-start.1 = (bf16[512,128]{1,0:T(8,128)(2,1)S(1)}, bf16[512,128]{1,0:T(8,128)(2,1)S(1)}, u32[]{:S(2)}, u32[]{:S(2)}) collective-permute-start(bf16[512,128]{1,0:T(8,128)(2,1)S(1)} %add_convert_fusion), channel_id=1, source_target_pairs={{0,8},{4,12},{8,0},{12,4},{16,24},{20,28},{24,16},{28,20},{1,9},{5... | collective-permute-start | bytes 393224 | tf_op jit(solution)/shard_map/ppermute | solution.py:51
  14.3 5.8 %collective-permute-start.8 = (bf16[192,256]{1,0:T(8,128)(2,1)S(1)}, bf16[192,256]{1,0:T(8,128)(2,1)S(1)}, u32[]{:S(2)}, u32[]{:S(2)}) collective-permute-start(bf16[192,256]{1,0:T(8,128)(2,1)S(1)} %pad_maximum_fusion.1), channel_id=1, source_target_pairs={{0,1},{1,0},{2,3},{3,2},{4,5},{5,4},{6,7},{7,6},{8,9},{9,8},{10,11... | collective-permute-start | bytes 294920 | tf_op jit(solution)/shard_map/ppermute | solution.py:51
  17.5 8.2 %collective-permute-start.4 = (bf16[512,128]{1,0:T(8,128)(2,1)S(1)}, bf16[512,128]{1,0:T(8,128)(2,1)S(1)}, u32[]{:S(2)}, u32[]{:S(2)}) collective-permute-start(bf16[512,128]{1,0:T(8,128)(2,1)S(1)} %shard_map.123), channel_id=1, source_target_pairs={{0,16},{4,20},{8,24},{12,28},{16,0},{20,4},{24,8},{28,12},{1,17},{... | collective-permute-start | bytes 393224 | tf_op jit(solution)/shard_map/ppermute | solution.py:51
  20.5 10.6 %collective-permute-start.9 = (bf16[256,384]{1,0:T(8,128)(2,1)S(1)}, bf16[256,384]{1,0:T(8,128)(2,1)S(1)}, u32[]{:S(2)}, u32[]{:S(2)}) collective-permute-start(bf16[256,384]{1,0:T(8,128)(2,1)S(1)} %get-tuple-element.67), channel_id=1, source_target_pairs={{0,4},{4,0},{8,12},{12,8},{16,20},{20,16},{24,28},{28,24},{1,5},{5... | collective-permute-start | bytes 589832 | tf_op jit(solution)/shard_map/ppermute | solution.py:51
  25.7 9.1 %collective-permute-start.5 = (bf16[512,128]{1,0:T(8,128)(2,1)S(1)}, bf16[512,128]{1,0:T(8,128)(2,1)S(1)}, u32[]{:S(2)}, u32[]{:S(2)}) collective-permute-start(bf16[512,128]{1,0:T(8,128)(2,1)S(1)} %shard_map.124), channel_id=1, source_target_pairs={{0,8},{4,12},{8,0},{12,4},{16,24},{20,28},{24,16},{28,20},{1,9},{5... | collective-permute-start | bytes 393224 | tf_op jit(solution)/shard_map/ppermute | solution.py:51
  27.2 3.2 %collective-permute-start.12 = (bf16[32,256]{1,0:T(8,128)(2,1)S(1)}, bf16[32,256]{1,0:T(8,128)(2,1)S(1)}, u32[]{:S(2)}, u32[]{:S(2)}) collective-permute-start(bf16[32,256]{1,0:T(8,128)(2,1)S(1)} %shard_map.129.refs_0_), channel_id=1, source_target_pairs={{0,3},{1,2},{2,1},{3,0},{4,7},{5,6},{6,5},{7,4},{8,11},{9,10},{10,... | collective-permute-start | bytes 49160 | tf_op jit(solution)/shard_map/ppermute | solution.py:51
  27.2 3.8 %collective-permute-start.11 = (bf16[32,256]{1,0:T(8,128)(2,1)S(1)}, bf16[32,256]{1,0:T(8,128)(2,1)S(1)}, u32[]{:S(2)}, u32[]{:S(2)}) collective-permute-start(bf16[32,256]{1,0:T(8,128)(2,1)S(1)} %shard_map.129.refs_0_), channel_id=1, source_target_pairs={{0,2},{1,3},{2,0},{3,1},{4,6},{5,7},{6,4},{7,5},{8,10},{9,11},{10,... | collective-permute-start | bytes 49160 | tf_op jit(solution)/shard_map/ppermute | solution.py:51
  28.1 2.9 %collective-permute-start.10 = (bf16[32,256]{1,0:T(8,128)(2,1)S(1)}, bf16[32,256]{1,0:T(8,128)(2,1)S(1)}, u32[]{:S(2)}, u32[]{:S(2)}) collective-permute-start(bf16[32,256]{1,0:T(8,128)(2,1)S(1)} %shard_map.129.refs_0_), channel_id=1, source_target_pairs={{0,1},{1,0},{2,3},{3,2},{4,5},{5,4},{6,7},{7,6},{8,9},{9,8},{10,11... | collective-permute-start | bytes 49160 | tf_op jit(solution)/shard_map/ppermute | solution.py:51
  31.3 6.7 %collective-permute-start.13 = (bf16[128,128]{1,0:T(8,128)(2,1)S(1)}, bf16[128,128]{1,0:T(8,128)(2,1)S(1)}, u32[]{:S(2)}, u32[]{:S(2)}) collective-permute-start(bf16[128,128]{1,0:T(8,128)(2,1)S(1)} %get-tuple-element.77), channel_id=1, source_target_pairs={{0,4},{4,0},{8,12},{12,8},{16,20},{20,16},{24,28},{28,24},{1,5},{5... | collective-permute-start | bytes 98312 | tf_op jit(solution)/shard_map/ppermute | solution.py:51
  32.9 5.2 %collective-permute-start.15 = (bf16[128,128]{1,0:T(8,128)(2,1)S(1)}, bf16[128,128]{1,0:T(8,128)(2,1)S(1)}, u32[]{:S(2)}, u32[]{:S(2)}) collective-permute-start(bf16[128,128]{1,0:T(8,128)(2,1)S(1)} %get-tuple-element.79), channel_id=1, source_target_pairs={{0,12},{4,8},{8,4},{12,0},{16,28},{20,24},{24,20},{28,16},{1,13},{... | collective-permute-start | bytes 98312 | tf_op jit(solution)/shard_map/ppermute | solution.py:51
  34.2 5.0 %collective-permute-start.14 = (bf16[128,512]{1,0:T(8,128)(2,1)S(1)}, bf16[128,512]{1,0:T(8,128)(2,1)S(1)}, u32[]{:S(2)}, u32[]{:S(2)}) collective-permute-start(bf16[128,512]{1,0:T(8,128)(2,1)S(1)} %get-tuple-element.78), channel_id=1, source_target_pairs={{0,8},{4,12},{8,0},{12,4},{16,24},{20,28},{24,16},{28,20},{1,9},{5... | collective-permute-start | bytes 393224 | tf_op jit(solution)/shard_map/ppermute | solution.py:51
  34.9 8.4 %collective-permute-start.6 = (bf16[512,128]{1,0:T(8,128)(2,1)S(1)}, bf16[512,128]{1,0:T(8,128)(2,1)S(1)}, u32[]{:S(2)}, u32[]{:S(2)}) collective-permute-start(bf16[512,128]{1,0:T(8,128)(2,1)S(1)} %shard_map.125), channel_id=1, source_target_pairs={{0,4},{4,0},{8,12},{12,8},{16,20},{20,16},{24,28},{28,24},{1,5},{5... | collective-permute-start | bytes 393224 | tf_op jit(solution)/shard_map/ppermute | solution.py:51
  39.5 3.9 %copy-start.4 = (f32[8,64,128]{2,1,0:T(8,128)S(1)}, f32[8,64,128]{2,1,0:T(8,128)}, u32[]{:S(2)}) copy-start(f32[8,64,128]{2,1,0:T(8,128)} %param.13) | copy-start | bytes 786436
  39.5 6.7 %collective-permute-start.16 = (bf16[64,384]{1,0:T(8,128)(2,1)S(1)}, bf16[64,384]{1,0:T(8,128)(2,1)S(1)}, u32[]{:S(2)}, u32[]{:S(2)}) collective-permute-start(bf16[64,384]{1,0:T(8,128)(2,1)S(1)} %get-tuple-element.81), channel_id=1, source_target_pairs={{0,16},{4,20},{8,24},{12,28},{16,0},{20,4},{24,8},{28,12},{1,17},{... | collective-permute-start | bytes 147464 | tf_op jit(solution)/shard_map/ppermute | solution.py:51

commit v10 on v7

--- a/solution.py
+++ b/solution.py
@@ -255,8 +255,11 @@
     part_ways(nt(xt_ref[...], sorted_ref[...]), (idx_ref[0] & 1) == 1, send_ref, keep_ref, inner)
 
 
-def far_wgrad_kernel(bits, inner, idx_ref, head_ref, xt_ref, gp_ref, keep_ref, one_ref, two_ref, both_ref, sorted_ref):
-    put_in_order(bits, head_ref, gp_ref, sorted_ref)
+def far_wgrad_kernel(inner, idx_ref, head_ref, xt_ref, *refs):
+    gathered, (keep_ref, one_ref, two_ref, both_ref, sorted_ref) = refs[:-5], refs[-5:]
+    for away, gp_ref in enumerate(gathered):
+        own = gp_ref.shape[0]
+        sorted_ref[pl.ds(pl.multiple_of((head_ref[0] ^ away) * own, 16), own), :] = gp_ref[...]
     total = nt(xt_ref[...], sorted_ref[...])
     right, upper = (idx_ref[0] & 1) == 1, ((idx_ref[0] >> 1) & 1) == 1
     for e in range(total.shape[0] // (4 * inner)):
@@ -462,11 +465,11 @@
         [SM] + [VM] * 2, n * cols)(idx, near_w, got)
     near_got = swap(send, "seq", 1)
 
-    far_all = gather_heads(far_rows, head_bits)
+    far_all = [far_rows] + [exchange(far_rows, "head", away) for away in range(1, n_head)]
     far_w, one, two, both, far_all = call(
-        functools.partial(far_wgrad_kernel, head_bits, per),
+        functools.partial(far_wgrad_kernel, per),
         [S((n, far_cols), F32)] + [S((n, far_cols), BF16)] * 3 + [S((far_cols, tokens), BF16)],
-        [SM] * 2 + [VM] * 2, 2 * tokens * width * far_cols)(idx, head_idx, xt, far_all)
+        [SM] * 2 + [VM] * (n_head + 1), 2 * tokens * width * far_cols)(idx, head_idx, xt, *far_all)
     far_gots = [exchange(one, "seq", 1), exchange(two, "seq", 2),
                 exchange(both, "seq", 3)]
 

time: 51.4 us -> 52.4 us (1.019)
  starting transfers between devices: 21.7 us -> 23.2 us
    ppermute x17 -> x18, starting transfers between devices: 21.7 us -> 23.2 us  [exchange(): return lax.ppermute(value, axis, pairs)]
    ppermute x17 -> x18, waiting for transfers between devices: 17.3 us -> 16.8 us  [exchange(): return lax.ppermute(value, axis, pairs)]
  transfers between devices with their start and end apart: 17 -> 18, of which waited for: 9 -> 11; matrix products, arithmetic and copies ran while one was open for 2% -> 2% of each run, Pallas kernels for 12% -> 11%
where the time goes in v10:
time: 52.4 us; the launch traced here: 52.3 us
  starting transfers between devices  23.2 us (44%)
  waiting for transfers between devices  16.8 us (32%)
  Pallas kernels  10.6 us (20%)
  between operations  0.88 us (2%)
  other arithmetic  0.82 us (2%)
    ppermute x18, starting transfers between devices, exchange(): return lax.ppermute(value, axis, pairs)  23.2 us
    ppermute x18, waiting for transfers between devices, exchange(): return lax.ppermute(value, axis, pairs)  16.8 us
    pallas_call x1, Pallas kernels, body(): call(functools.partial(final_kernel, dims, levels, first, seq_bits), [S(s...  2.88 us
    pallas_call x2, Pallas kernels, body(): call(functools.partial(local_kernel, dims, levels, tuple(range(part * hal...  2.81 us
    pallas_call x1, Pallas kernels, body(): call(functools.partial(state_kernel, dims), [S((rows, dv), F32), S((rows,...  1.5 us
  transfers between devices with their start and end apart: 18, of which 11 were waited for; matrix products, arithmetic and copies ran while one was open for 2% of the time, Pallas kernels for 11%

profile of v10, /device:TPU:0, one launch (start us, length us, event | category | flops | bytes accessed | tf_op | source)
XLA Modules:
  0.0 52.3 jit_solution(1977645334884916546)
XLA Ops:
  0.6 0.0 copy-start.1
  0.6 0.0 copy-start.3
  0.7 1.5 %shard_map.118 = (f32[512,128]{1,0:T(8,128)S(1)}, bf16[512,128]{1,0:T(8,128)(2,1)S(1)}, bf16[512,384]{1,0:T(8,128)(2,1)S(1)}, bf16[256,512]{1,0:T(8,128)(2,1)S(1)}) custom-call(s32[1]{0:T(128)} %bitcast.idx_ref, s32[1]{0:T(128)} %bitcast.1.head_ref.idx_ref, bf16[256,512]{1,0:T(8,128)(2,1)} %refs_10_.1, bf16[256,1024]{1,0:T(8,128)(2,1)} %refs_11_.1, ...), custom_call_target="tpu_custom_call" | custom-call | flops 33554432 | bytes 2097152 | tf_op jit(solution)/shard_map/pallas_call | solution.py:404
  2.2 0.0 copy-start
  2.2 0.4 shard_map.119
  2.6 0.0 copy-start.2
  2.6 3.0 %collective-permute-start.2 = (bf16[192,256]{1,0:T(8,128)(2,1)S(1)}, bf16[192,256]{1,0:T(8,128)(2,1)S(1)}, u32[]{:S(2)}, u32[]{:S(2)}) collective-permute-start(bf16[192,256]{1,0:T(8,128)(2,1)S(1)} %get-tuple-element.50), channel_id=1, source_target_pairs={{0,2},{1,3},{2,0},{3,1},{4,6},{5,7},{6,4},{7,5},{8,10},{9,11},{10,... | collective-permute-start | bytes 294920 | tf_op jit(solution)/shard_map/ppermute | solution.py:51
  5.6 1.5 %collective-permute-start = (bf16[512,128]{1,0:T(8,128)(2,1)S(1)}, bf16[512,128]{1,0:T(8,128)(2,1)S(1)}, u32[]{:S(2)}, u32[]{:S(2)}) collective-permute-start(bf16[512,128]{1,0:T(8,128)(2,1)S(1)} %get-tuple-element.45), channel_id=1, source_target_pairs={{0,4},{4,0},{8,12},{12,8},{16,20},{20,16},{24,28},{28,24},{1,5},{5... | collective-permute-start | bytes 393224 | tf_op jit(solution)/shard_map/ppermute | solution.py:51
  7.1 1.3 %collective-permute-done.2.got_ref = bf16[192,256]{1,0:T(8,128)(2,1)S(1)} collective-permute-done((bf16[192,256]{1,0:T(8,128)(2,1)S(1)}, bf16[192,256]{1,0:T(8,128)(2,1)S(1)}, u32[]{:S(2)}, u32[]{:S(2)}) %collective-permute-start.2) | collective-permute-done | bytes 98336 | tf_op jit(solution)/shard_map/ppermute | solution.py:51
  8.4 0.1 collective-permute-start.3
  8.5 0.0 copy-done.1
  8.5 0.0 copy-done.3
  8.5 0.0 copy-done
  8.5 0.0 copy-done.2
  8.6 0.8 %shard_map.121.gl_ref = f32[96,256]{1,0:T(8,128)S(1)} custom-call(bf16[256,512]{1,0:T(8,128)(2,1)S(1)} %copy-done.2, bf16[256,512]{1,0:T(8,128)(2,1)S(1)} %copy-done.3, bf16[256,1024]{1,0:T(8,128)(2,1)S(1)} %copy-done.1, bf16[256,1024]{1,0:T(8,128)(2,1)S(1)} %copy-done), custom_call_target="tpu_custom_call" | custom-call | flops 201326592 | bytes 196608 | tf_op jit(solution)/shard_map/pallas_call | solution.py:433
  9.3 0.4 collective-permute-done.3.got_ref
  9.7 0.4 shard_map.122
  10.2 1.9 %collective-permute-start.7 = (bf16[96,256]{1,0:T(8,128)(2,1)S(1)}, bf16[96,256]{1,0:T(8,128)(2,1)S(1)}, u32[]{:S(2)}, u32[]{:S(2)}) collective-permute-start(bf16[96,256]{1,0:T(8,128)(2,1)S(1)} %get-tuple-element.65), channel_id=1, source_target_pairs={{0,2},{1,3},{2,0},{3,1},{4,6},{5,7},{6,4},{7,5},{8,10},{9,11},{10,... | collective-permute-start | bytes 147464 | tf_op jit(solution)/shard_map/ppermute | solution.py:51
  12.1 0.0 collective-permute-done.refs_0_
  12.1 1.6 %collective-permute-start.1 = (bf16[512,128]{1,0:T(8,128)(2,1)S(1)}, bf16[512,128]{1,0:T(8,128)(2,1)S(1)}, u32[]{:S(2)}, u32[]{:S(2)}) collective-permute-start(bf16[512,128]{1,0:T(8,128)(2,1)S(1)} %add_convert_fusion), channel_id=1, source_target_pairs={{0,8},{4,12},{8,0},{12,4},{16,24},{20,28},{24,16},{28,20},{1,9},{5... | collective-permute-start | bytes 393224 | tf_op jit(solution)/shard_map/ppermute | solution.py:51
  13.7 0.6 %collective-permute-done.7 = bf16[96,256]{1,0:T(8,128)(2,1)S(1)} collective-permute-done((bf16[96,256]{1,0:T(8,128)(2,1)S(1)}, bf16[96,256]{1,0:T(8,128)(2,1)S(1)}, u32[]{:S(2)}, u32[]{:S(2)}) %collective-permute-start.7) | collective-permute-done | bytes 49184 | tf_op jit(solution)/shard_map/ppermute | solution.py:51
  14.3 0.1 collective-permute-start.8
  14.4 3.0 %collective-permute-done.1.refs_1_ = bf16[512,128]{1,0:T(8,128)(2,1)S(1)} collective-permute-done((bf16[512,128]{1,0:T(8,128)(2,1)S(1)}, bf16[512,128]{1,0:T(8,128)(2,1)S(1)}, u32[]{:S(2)}, u32[]{:S(2)}) %collective-permute-start.1) | collective-permute-done | bytes 131104 | tf_op jit(solution)/shard_map/ppermute | solution.py:51
  17.5 2.6 %collective-permute-start.4 = (bf16[512,128]{1,0:T(8,128)(2,1)S(1)}, bf16[512,128]{1,0:T(8,128)(2,1)S(1)}, u32[]{:S(2)}, u32[]{:S(2)}) collective-permute-start(bf16[512,128]{1,0:T(8,128)(2,1)S(1)} %shard_map.123), channel_id=1, source_target_pairs={{0,16},{4,20},{8,24},{12,28},{16,0},{20,4},{24,8},{28,12},{1,17},{... | collective-permute-start | bytes 393224 | tf_op jit(solution)/shard_map/ppermute | solution.py:51
  20.1 0.0 collective-permute-done.8
  20.1 0.3 shard_map.128
  20.5 1.6 %collective-permute-start.12 = (bf16[256,384]{1,0:T(8,128)(2,1)S(1)}, bf16[256,384]{1,0:T(8,128)(2,1)S(1)}, u32[]{:S(2)}, u32[]{:S(2)}) collective-permute-start(bf16[256,384]{1,0:T(8,128)(2,1)S(1)} %get-tuple-element.75), channel_id=1, source_target_pairs={{0,4},{4,0},{8,12},{12,8},{16,20},{20,16},{24,28},{28,24},{1,5},{5... | collective-permute-start | bytes 589832 | tf_op jit(solution)/shard_map/ppermute | solution.py:51
  22.1 3.6 %collective-permute-done.4.refs_0_.refs_2_.refs_3_ = bf16[512,128]{1,0:T(8,128)(2,1)S(1)} collective-permute-done((bf16[512,128]{1,0:T(8,128)(2,1)S(1)}, bf16[512,128]{1,0:T(8,128)(2,1)S(1)}, u32[]{:S(2)}, u32[]{:S(2)}) %collective-permute-start.4) | collective-permute-done | bytes 131104 | tf_op jit(solution)/shard_map/ppermute | solution.py:51
  25.7 0.7 %shard_map.129.refs_0_ = bf16[32,256]{1,0:T(8,128)(2,1)S(1)} custom-call(s32[1]{0:T(128)} %bitcast.idx_ref, bf16[512,128]{1,0:T(8,128)(2,1)S(1)} %collective-permute-done.refs_0_, bf16[512,128]{1,0:T(8,128)(2,1)S(1)} %collective-permute-done.1.refs_1_, bf16[512,128]{1,0:T(8,128)(2,1)S(1)} %collective-permute-done.4.refs_0_.refs_2_.refs_3_, ...), custom_call_target="tpu_custom_call" | custom-call | flops 100663296 | bytes 32768 | tf_op jit(solution)/shard_map/pallas_call | solution.py:446
  26.4 0.1 collective-permute-start.11
  26.5 0.6 %collective-permute-start.10 = (bf16[32,256]{1,0:T(8,128)(2,1)S(1)}, bf16[32,256]{1,0:T(8,128)(2,1)S(1)}, u32[]{:S(2)}, u32[]{:S(2)}) collective-permute-start(bf16[32,256]{1,0:T(8,128)(2,1)S(1)} %shard_map.129.refs_0_), channel_id=1, source_target_pairs={{0,2},{1,3},{2,0},{3,1},{4,6},{5,7},{6,4},{7,5},{8,10},{9,11},{10,... | collective-permute-start | bytes 49160 | tf_op jit(solution)/shard_map/ppermute | solution.py:51
  27.1 1.2 %collective-permute-start.9 = (bf16[32,256]{1,0:T(8,128)(2,1)S(1)}, bf16[32,256]{1,0:T(8,128)(2,1)S(1)}, u32[]{:S(2)}, u32[]{:S(2)}) collective-permute-start(bf16[32,256]{1,0:T(8,128)(2,1)S(1)} %shard_map.129.refs_0_), channel_id=1, source_target_pairs={{0,1},{1,0},{2,3},{3,2},{4,5},{5,4},{6,7},{7,6},{8,9},{9,8},{10,11... | collective-permute-start | bytes 49160 | tf_op jit(solution)/shard_map/ppermute | solution.py:51
  28.3 0.1 shard_map.124
  28.4 0.7 %collective-permute-start.5 = (bf16[512,128]{1,0:T(8,128)(2,1)S(1)}, bf16[512,128]{1,0:T(8,128)(2,1)S(1)}, u32[]{:S(2)}, u32[]{:S(2)}) collective-permute-start(bf16[512,128]{1,0:T(8,128)(2,1)S(1)} %shard_map.124), channel_id=1, source_target_pairs={{0,8},{4,12},{8,0},{12,4},{16,24},{20,28},{24,16},{28,20},{1,9},{5... | collective-permute-start | bytes 393224 | tf_op jit(solution)/shard_map/ppermute | solution.py:51
  29.1 0.5 %collective-permute-done.11.refs_3_ = bf16[32,256]{1,0:T(8,128)(2,1)S(1)} collective-permute-done((bf16[32,256]{1,0:T(8,128)(2,1)S(1)}, bf16[32,256]{1,0:T(8,128)(2,1)S(1)}, u32[]{:S(2)}, u32[]{:S(2)}) %collective-permute-start.11) | collective-permute-done | bytes 16416 | tf_op jit(solution)/shard_map/ppermute | solution.py:51
  29.6 0.7 %collective-permute-done.10.refs_2_ = bf16[32,256]{1,0:T(8,128)(2,1)S(1)} collective-permute-done((bf16[32,256]{1,0:T(8,128)(2,1)S(1)}, bf16[32,256]{1,0:T(8,128)(2,1)S(1)}, u32[]{:S(2)}, u32[]{:S(2)}) %collective-permute-start.10) | collective-permute-done | bytes 16416 | tf_op jit(solution)/shard_map/ppermute | solution.py:51
  30.3 0.0 collective-permute-done.9.refs_1_
  30.3 0.2 shard_map.130
  30.5 1.6 %collective-permute-start.14 = (bf16[128,128]{1,0:T(8,128)(2,1)S(1)}, bf16[128,128]{1,0:T(8,128)(2,1)S(1)}, u32[]{:S(2)}, u32[]{:S(2)}) collective-permute-start(bf16[128,128]{1,0:T(8,128)(2,1)S(1)} %get-tuple-element.79), channel_id=1, source_target_pairs={{0,4},{4,0},{8,12},{12,8},{16,20},{20,16},{24,28},{28,24},{1,5},{5... | collective-permute-start | bytes 98312 | tf_op jit(solution)/shard_map/ppermute | solution.py:51
  32.1 0.6 %collective-permute-start.15 = (bf16[128,128]{1,0:T(8,128)(2,1)S(1)}, bf16[128,128]{1,0:T(8,128)(2,1)S(1)}, u32[]{:S(2)}, u32[]{:S(2)}) collective-permute-start(bf16[128,128]{1,0:T(8,128)(2,1)S(1)} %get-tuple-element.80), channel_id=1, source_target_pairs={{0,8},{4,12},{8,0},{12,4},{16,24},{20,28},{24,16},{28,20},{1,9},{5... | collective-permute-start | bytes 98312 | tf_op jit(solution)/shard_map/ppermute | solution.py:51
  32.7 1.3 %collective-permute-start.16 = (bf16[128,128]{1,0:T(8,128)(2,1)S(1)}, bf16[128,128]{1,0:T(8,128)(2,1)S(1)}, u32[]{:S(2)}, u32[]{:S(2)}) collective-permute-start(bf16[128,128]{1,0:T(8,128)(2,1)S(1)} %get-tuple-element.81), channel_id=1, source_target_pairs={{0,12},{4,8},{8,4},{12,0},{16,28},{20,24},{24,20},{28,16},{1,13},{... | collective-permute-start | bytes 98312 | tf_op jit(solution)/shard_map/ppermute | solution.py:51
  34.1 0.0 collective-permute-done.12.got_ref
  34.1 0.1 shard_map.132
  34.1 0.7 %collective-permute-start.13 = (bf16[128,384]{1,0:T(8,128)(2,1)S(1)}, bf16[128,384]{1,0:T(8,128)(2,1)S(1)}, u32[]{:S(2)}, u32[]{:S(2)}) collective-permute-start(bf16[128,384]{1,0:T(8,128)(2,1)S(1)} %get-tuple-element.77), channel_id=1, source_target_pairs={{0,8},{4,12},{8,0},{12,4},{16,24},{20,28},{24,16},{28,20},{1,9},{5... | collective-permute-start | bytes 294920 | tf_op jit(solution)/shard_map/ppermute | solution.py:51
  34.8 0.1 fusion.1.refs_22_.place_ref
  34.9 0.0 collective-permute-done.14.one_ref
  35.0 1.4 %collective-permute-done.15.two_ref = bf16[128,128]{1,0:T(8,128)(2,1)S(1)} collective-permute-done((bf16[128,128]{1,0:T(8,128)(2,1)S(1)}, bf16[128,128]{1,0:T(8,128)(2,1)S(1)}, u32[]{:S(2)}, u32[]{:S(2)}) %collective-permute-start.15) | collective-permute-done | bytes 32800 | tf_op jit(solution)/shard_map/ppermute | solution.py:51
  36.4 1.4 %collective-permute-done.16.both_ref = bf16[128,128]{1,0:T(8,128)(2,1)S(1)} collective-permute-done((bf16[128,128]{1,0:T(8,128)(2,1)S(1)}, bf16[128,128]{1,0:T(8,128)(2,1)S(1)}, u32[]{:S(2)}, u32[]{:S(2)}) %collective-permute-start.16) | collective-permute-done | bytes 32800 | tf_op jit(solution)/shard_map/ppermute | solution.py:51
  37.8 1.0 %collective-permute-done.13.near_got = bf16[128,384]{1,0:T(8,128)(2,1)S(1)} collective-permute-done((bf16[128,384]{1,0:T(8,128)(2,1)S(1)}, bf16[128,384]{1,0:T(8,128)(2,1)S(1)}, u32[]{:S(2)}, u32[]{:S(2)}) %collective-permute-start.13) | collective-permute-done | bytes 98336 | tf_op jit(solution)/shard_map/ppermute | solution.py:51
  38.8 0.3 shard_map.133
  39.2 2.3 %collective-permute-start.17 = (bf16[64,384]{1,0:T(8,128)(2,1)S(1)}, bf16[64,384]{1,0:T(8,128)(2,1)S(1)}, u32[]{:S(2)}, u32[]{:S(2)}) collective-permute-start(bf16[64,384]{1,0:T(8,128)(2,1)S(1)} %get-tuple-element.83), channel_id=1, source_target_pairs={{0,16},{4,20},{8,24},{12,28},{16,0},{20,4},{24,8},{28,12},{1,17},{... | collective-permute-start | bytes 147464 | tf_op jit(solution)/shard_map/ppermute | solution.py:51
  41.4 1.4 %shard_map.127 = (f32[512,256]{1,0:T(8,128)S(1)}, f32[256,256]{1,0:T(8,128)S(1)}, f32[256,256]{1,0:T(8,128)S(1)}, f32[256,512]{1,0:T(8,128)S(1)}) custom-call(bf16[256,512]{1,0:T(8,128)(2,1)S(1)} %copy-done.2, bf16[256,512]{1,0:T(8,128)(2,1)S(1)} %copy-done.3, bf16[256,1024]{1,0:T(8,128)(2,1)S(1)} %copy-done.1, bf16[256,1024]{1,0:T(8,128)(2,1)S(1)} %copy-done, ...), custom_call_target="tpu_custom_call" | custom-call | flops 301989888 | bytes 3145728 | tf_op jit(solution)/shard_map/pallas_call | solution.py:497
  42.8 1.4 %shard_map.126 = (f32[512,256]{1,0:T(8,128)S(1)}, f32[256,256]{1,0:T(8,128)S(1)}, f32[256,256]{1,0:T(8,128)S(1)}, f32[256,512]{1,0:T(8,128)S(1)}) custom-call(bf16[256,512]{1,0:T(8,128)(2,1)S(1)} %copy-done.2, bf16[256,512]{1,0:T(8,128)(2,1)S(1)} %copy-done.3, bf16[256,1024]{1,0:T(8,128)(2,1)S(1)} %copy-done.1, bf16[256,1024]{1,0:T(8,128)(2,1)S(1)} %copy-done, ...), custom_call_target="tpu_custom_call" | custom-call | flops 301989888 | bytes 3145728 | tf_op jit(solution)/shard_map/pallas_call | solution.py:497
  44.2 0.0 collective-permute-done.5.refs_1_.refs_4_
  44.3 0.1 shard_map.125
  44.3 0.0 copy-start.4
  44.3 1.6 %collective-permute-start.6 = (bf16[512,128]{1,0:T(8,128)(2,1)S(1)}, bf16[512,128]{1,0:T(8,128)(2,1)S(1)}, u32[]{:S(2)}, u32[]{:S(2)}) collective-permute-start(bf16[512,128]{1,0:T(8,128)(2,1)S(1)} %shard_map.125), channel_id=1, source_target_pairs={{0,4},{4,0},{8,12},{12,8},{16,20},{20,16},{24,28},{28,24},{1,5},{5... | collective-permute-start | bytes 393224 | tf_op jit(solution)/shard_map/ppermute | solution.py:51
  45.9 0.0 collective-permute-done.17
  45.9 0.7 %convert_add_fusion = f32[64,384]{1,0:T(8,128)} fusion(f32[64,384]{1,0:T(8,128)S(1)} %get-tuple-element.82, bf16[64,384]{1,0:T(8,128)(2,1)S(1)} %collective-permute-done.17), kind=kLoop, calls=%fused_computation.6 | loop fusion | flops 49152 | bytes 245760 | tf_op jit(solution)/shard_map/add | solution.py:492
  46.6 2.8 %collective-permute-done.6.refs_5_ = bf16[512,128]{1,0:T(8,128)(2,1)S(1)} collective-permute-done((bf16[512,128]{1,0:T(8,128)(2,1)S(1)}, bf16[512,128]{1,0:T(8,128)(2,1)S(1)}, u32[]{:S(2)}, u32[]{:S(2)}) %collective-permute-start.6) | collective-permute-done | bytes 131104 | tf_op jit(solution)/shard_map/ppermute | solution.py:51
  49.4 0.0 copy-done.4
  49.4 2.9 %shard_map.131 = (bf16[256,1024]{1,0:T(8,128)(2,1)}, bf16[256,512]{1,0:T(8,128)(2,1)}, bf16[256,512]{1,0:T(8,128)(2,1)}, bf16[256,512]{1,0:T(8,128)(2,1)}, bf16[256,1024]{1,0:T(8,128)(2,1)}) custom-call(s32[1]{0:T(128)} %bitcast.idx_ref, bf16[512,128]{1,0:T(8,128)(2,1)S(1)} %collective-permute-done.refs_0_, ...), custom_call_target="tpu_custom_call" | custom-call | flops 402653184 | bytes 3670016 | tf_op jit(solution)/shard_map/pallas_call | solution.py:504
  (7 shorter events, 0.1 us)
Async XLA Ops:
  0.6 7.9 %copy-start.1 = (bf16[256,1024]{1,0:T(8,128)(2,1)S(1)}, bf16[256,1024]{1,0:T(8,128)(2,1)}, u32[]{:S(2)}) copy-start(bf16[256,1024]{1,0:T(8,128)(2,1)} %refs_11_.1) | copy-start | bytes 1572868
  0.6 7.9 %copy-start.3 = (bf16[256,512]{1,0:T(8,128)(2,1)S(1)}, bf16[256,512]{1,0:T(8,128)(2,1)}, u32[]{:S(2)}) copy-start(bf16[256,512]{1,0:T(8,128)(2,1)} %q_ref.7) | copy-start | bytes 786436
  2.2 6.4 %copy-start = (bf16[256,1024]{1,0:T(8,128)(2,1)S(1)}, bf16[256,1024]{1,0:T(8,128)(2,1)}, u32[]{:S(2)}) copy-start(bf16[256,1024]{1,0:T(8,128)(2,1)} %refs_8_.1) | copy-start | bytes 1572868
  2.6 6.0 %copy-start.2 = (bf16[256,512]{1,0:T(8,128)(2,1)S(1)}, bf16[256,512]{1,0:T(8,128)(2,1)}, u32[]{:S(2)}) copy-start(bf16[256,512]{1,0:T(8,128)(2,1)} %refs_10_.1) | copy-start | bytes 786436
  2.6 5.8 %collective-permute-start.2 = (bf16[192,256]{1,0:T(8,128)(2,1)S(1)}, bf16[192,256]{1,0:T(8,128)(2,1)S(1)}, u32[]{:S(2)}, u32[]{:S(2)}) collective-permute-start(bf16[192,256]{1,0:T(8,128)(2,1)S(1)} %get-tuple-element.50), channel_id=1, source_target_pairs={{0,2},{1,3},{2,0},{3,1},{4,6},{5,7},{6,4},{7,5},{8,10},{9,11},{10,... | collective-permute-start | bytes 294920 | tf_op jit(solution)/shard_map/ppermute | solution.py:51
  5.6 6.4 %collective-permute-start = (bf16[512,128]{1,0:T(8,128)(2,1)S(1)}, bf16[512,128]{1,0:T(8,128)(2,1)S(1)}, u32[]{:S(2)}, u32[]{:S(2)}) collective-permute-start(bf16[512,128]{1,0:T(8,128)(2,1)S(1)} %get-tuple-element.45), channel_id=1, source_target_pairs={{0,4},{4,0},{8,12},{12,8},{16,20},{20,16},{24,28},{28,24},{1,5},{5... | collective-permute-start | bytes 393224 | tf_op jit(solution)/shard_map/ppermute | solution.py:51
  8.4 1.3 %collective-permute-start.3 = (bf16[96,256]{1,0:T(8,128)(2,1)S(1)}, bf16[96,256]{1,0:T(8,128)(2,1)S(1)}, u32[]{:S(2)}, u32[]{:S(2)}) collective-permute-start(bf16[96,256]{1,0:T(8,128)(2,1)S(1)} %get-tuple-element.52), channel_id=1, source_target_pairs={{0,1},{1,0},{2,3},{3,2},{4,5},{5,4},{6,7},{7,6},{8,9},{9,8},{10,11... | collective-permute-start | bytes 147464 | tf_op jit(solution)/shard_map/ppermute | solution.py:51
  10.2 4.2 %collective-permute-start.7 = (bf16[96,256]{1,0:T(8,128)(2,1)S(1)}, bf16[96,256]{1,0:T(8,128)(2,1)S(1)}, u32[]{:S(2)}, u32[]{:S(2)}) collective-permute-start(bf16[96,256]{1,0:T(8,128)(2,1)S(1)} %get-tuple-element.65), channel_id=1, source_target_pairs={{0,2},{1,3},{2,0},{3,1},{4,6},{5,7},{6,4},{7,5},{8,10},{9,11},{10,... | collective-permute-start | bytes 147464 | tf_op jit(solution)/shard_map/ppermute | solution.py:51
  12.1 5.3 %collective-permute-start.1 = (bf16[512,128]{1,0:T(8,128)(2,1)S(1)}, bf16[512,128]{1,0:T(8,128)(2,1)S(1)}, u32[]{:S(2)}, u32[]{:S(2)}) collective-permute-start(bf16[512,128]{1,0:T(8,128)(2,1)S(1)} %add_convert_fusion), channel_id=1, source_target_pairs={{0,8},{4,12},{8,0},{12,4},{16,24},{20,28},{24,16},{28,20},{1,9},{5... | collective-permute-start | bytes 393224 | tf_op jit(solution)/shard_map/ppermute | solution.py:51
  14.3 5.8 %collective-permute-start.8 = (bf16[192,256]{1,0:T(8,128)(2,1)S(1)}, bf16[192,256]{1,0:T(8,128)(2,1)S(1)}, u32[]{:S(2)}, u32[]{:S(2)}) collective-permute-start(bf16[192,256]{1,0:T(8,128)(2,1)S(1)} %pad_maximum_fusion.1), channel_id=1, source_target_pairs={{0,1},{1,0},{2,3},{3,2},{4,5},{5,4},{6,7},{7,6},{8,9},{9,8},{10,11... | collective-permute-start | bytes 294920 | tf_op jit(solution)/shard_map/ppermute | solution.py:51
  17.5 8.2 %collective-permute-start.4 = (bf16[512,128]{1,0:T(8,128)(2,1)S(1)}, bf16[512,128]{1,0:T(8,128)(2,1)S(1)}, u32[]{:S(2)}, u32[]{:S(2)}) collective-permute-start(bf16[512,128]{1,0:T(8,128)(2,1)S(1)} %shard_map.123), channel_id=1, source_target_pairs={{0,16},{4,20},{8,24},{12,28},{16,0},{20,4},{24,8},{28,12},{1,17},{... | collective-permute-start | bytes 393224 | tf_op jit(solution)/shard_map/ppermute | solution.py:51
  20.5 13.6 %collective-permute-start.12 = (bf16[256,384]{1,0:T(8,128)(2,1)S(1)}, bf16[256,384]{1,0:T(8,128)(2,1)S(1)}, u32[]{:S(2)}, u32[]{:S(2)}) collective-permute-start(bf16[256,384]{1,0:T(8,128)(2,1)S(1)} %get-tuple-element.75), channel_id=1, source_target_pairs={{0,4},{4,0},{8,12},{12,8},{16,20},{20,16},{24,28},{28,24},{1,5},{5... | collective-permute-start | bytes 589832 | tf_op jit(solution)/shard_map/ppermute | solution.py:51
  26.4 3.2 %collective-permute-start.11 = (bf16[32,256]{1,0:T(8,128)(2,1)S(1)}, bf16[32,256]{1,0:T(8,128)(2,1)S(1)}, u32[]{:S(2)}, u32[]{:S(2)}) collective-permute-start(bf16[32,256]{1,0:T(8,128)(2,1)S(1)} %shard_map.129.refs_0_), channel_id=1, source_target_pairs={{0,3},{1,2},{2,1},{3,0},{4,7},{5,6},{6,5},{7,4},{8,11},{9,10},{10,... | collective-permute-start | bytes 49160 | tf_op jit(solution)/shard_map/ppermute | solution.py:51
  26.5 3.8 %collective-permute-start.10 = (bf16[32,256]{1,0:T(8,128)(2,1)S(1)}, bf16[32,256]{1,0:T(8,128)(2,1)S(1)}, u32[]{:S(2)}, u32[]{:S(2)}) collective-permute-start(bf16[32,256]{1,0:T(8,128)(2,1)S(1)} %shard_map.129.refs_0_), channel_id=1, source_target_pairs={{0,2},{1,3},{2,0},{3,1},{4,6},{5,7},{6,4},{7,5},{8,10},{9,11},{10,... | collective-permute-start | bytes 49160 | tf_op jit(solution)/shard_map/ppermute | solution.py:51
  27.1 3.2 %collective-permute-start.9 = (bf16[32,256]{1,0:T(8,128)(2,1)S(1)}, bf16[32,256]{1,0:T(8,128)(2,1)S(1)}, u32[]{:S(2)}, u32[]{:S(2)}) collective-permute-start(bf16[32,256]{1,0:T(8,128)(2,1)S(1)} %shard_map.129.refs_0_), channel_id=1, source_target_pairs={{0,1},{1,0},{2,3},{3,2},{4,5},{5,4},{6,7},{7,6},{8,9},{9,8},{10,11... | collective-permute-start | bytes 49160 | tf_op jit(solution)/shard_map/ppermute | solution.py:51
  28.4 15.9 %collective-permute-start.5 = (bf16[512,128]{1,0:T(8,128)(2,1)S(1)}, bf16[512,128]{1,0:T(8,128)(2,1)S(1)}, u32[]{:S(2)}, u32[]{:S(2)}) collective-permute-start(bf16[512,128]{1,0:T(8,128)(2,1)S(1)} %shard_map.124), channel_id=1, source_target_pairs={{0,8},{4,12},{8,0},{12,4},{16,24},{20,28},{24,16},{28,20},{1,9},{5... | collective-permute-start | bytes 393224 | tf_op jit(solution)/shard_map/ppermute | solution.py:51
  30.5 4.4 %collective-permute-start.14 = (bf16[128,128]{1,0:T(8,128)(2,1)S(1)}, bf16[128,128]{1,0:T(8,128)(2,1)S(1)}, u32[]{:S(2)}, u32[]{:S(2)}) collective-permute-start(bf16[128,128]{1,0:T(8,128)(2,1)S(1)} %get-tuple-element.79), channel_id=1, source_target_pairs={{0,4},{4,0},{8,12},{12,8},{16,20},{20,16},{24,28},{28,24},{1,5},{5... | collective-permute-start | bytes 98312 | tf_op jit(solution)/shard_map/ppermute | solution.py:51
  32.1 4.3 %collective-permute-start.15 = (bf16[128,128]{1,0:T(8,128)(2,1)S(1)}, bf16[128,128]{1,0:T(8,128)(2,1)S(1)}, u32[]{:S(2)}, u32[]{:S(2)}) collective-permute-start(bf16[128,128]{1,0:T(8,128)(2,1)S(1)} %get-tuple-element.80), channel_id=1, source_target_pairs={{0,8},{4,12},{8,0},{12,4},{16,24},{20,28},{24,16},{28,20},{1,9},{5... | collective-permute-start | bytes 98312 | tf_op jit(solution)/shard_map/ppermute | solution.py:51
  32.7 5.0 %collective-permute-start.16 = (bf16[128,128]{1,0:T(8,128)(2,1)S(1)}, bf16[128,128]{1,0:T(8,128)(2,1)S(1)}, u32[]{:S(2)}, u32[]{:S(2)}) collective-permute-start(bf16[128,128]{1,0:T(8,128)(2,1)S(1)} %get-tuple-element.81), channel_id=1, source_target_pairs={{0,12},{4,8},{8,4},{12,0},{16,28},{20,24},{24,20},{28,16},{1,13},{... | collective-permute-start | bytes 98312 | tf_op jit(solution)/shard_map/ppermute | solution.py:51
  34.1 4.7 %collective-permute-start.13 = (bf16[128,384]{1,0:T(8,128)(2,1)S(1)}, bf16[128,384]{1,0:T(8,128)(2,1)S(1)}, u32[]{:S(2)}, u32[]{:S(2)}) collective-permute-start(bf16[128,384]{1,0:T(8,128)(2,1)S(1)} %get-tuple-element.77), channel_id=1, source_target_pairs={{0,8},{4,12},{8,0},{12,4},{16,24},{20,28},{24,16},{28,20},{1,9},{5... | collective-permute-start | bytes 294920 | tf_op jit(solution)/shard_map/ppermute | solution.py:51
  39.2 6.8 %collective-permute-start.17 = (bf16[64,384]{1,0:T(8,128)(2,1)S(1)}, bf16[64,384]{1,0:T(8,128)(2,1)S(1)}, u32[]{:S(2)}, u32[]{:S(2)}) collective-permute-start(bf16[64,384]{1,0:T(8,128)(2,1)S(1)} %get-tuple-element.83), channel_id=1, source_target_pairs={{0,16},{4,20},{8,24},{12,28},{16,0},{20,4},{24,8},{28,12},{1,17},{... | collective-permute-start | bytes 147464 | tf_op jit(solution)/shard_map/ppermute | solution.py:51
  44.3 5.0 %copy-start.4 = (f32[8,64,128]{2,1,0:T(8,128)S(1)}, f32[8,64,128]{2,1,0:T(8,128)}, u32[]{:S(2)}) copy-start(f32[8,64,128]{2,1,0:T(8,128)} %param.13) | copy-start | bytes 786436
  44.3 5.0 %collective-permute-start.6 = (bf16[512,128]{1,0:T(8,128)(2,1)S(1)}, bf16[512,128]{1,0:T(8,128)(2,1)S(1)}, u32[]{:S(2)}, u32[]{:S(2)}) collective-permute-start(bf16[512,128]{1,0:T(8,128)(2,1)S(1)} %shard_map.125), channel_id=1, source_target_pairs={{0,4},{4,0},{8,12},{12,8},{16,20},{20,16},{24,28},{28,24},{1,5},{5... | collective-permute-start | bytes 393224 | tf_op jit(solution)/shard_map/ppermute | solution.py:51

commit v11 on v7

--- a/solution.py
+++ b/solution.py
@@ -91,9 +91,13 @@
     part_ways(tn(w_ref[...], xt), upper, send_ref, keep_ref, keep_ref.shape[0])
 
 
-def fold_kernel(bit, inner, idx_ref, keep_in, got_ref, send_ref, keep_ref):
+def fold_kernel(bit, inner, idx_ref, keep_in, *refs):
+    gots, (send_ref, keep_ref) = refs[:-2], refs[-2:]
     upper = ((idx_ref[0] >> bit) & 1) == 1
-    part_ways(keep_in[...] + got_ref[...].astype(F32), upper, send_ref, keep_ref, inner)
+    total = keep_in[...]
+    for got in gots:
+        total = total + got[...].astype(F32)
+    part_ways(total, upper, send_ref, keep_ref, inner)
 
 
 def weight_kernel(dims, levels, first, count, keep_ref, got_ref, gl_ref, q_ref, g_ref,
@@ -241,23 +245,18 @@
         far_ref[m * nh:(m + 1) * nh, :] = jnp.concatenate(found, axis=0).astype(BF16)
 
 
-def put_in_order(bits, head_ref, gp_ref, sorted_ref):
-    count = 1 << bits
-    own = gp_ref.shape[0] // count
-    for n in range(count):
+def wgrad_kernel(bits, inner, idx_ref, head_ref, xt_ref, place_ref, near_ref, *refs):
+    gathered, (keep_ref, one_ref, two_ref, both_ref, gp_ref, far_ref) = refs[:-6], refs[-6:]
+    own = near_ref.shape[0] >> bits
+    for n, rows_ref in enumerate(gathered):
         away = sum(((n >> k) & 1) << (bits - 1 - k) for k in range(bits))
         at = pl.multiple_of((head_ref[0] ^ away) * own, 16)
-        sorted_ref[pl.ds(at, own), :] = gp_ref[n * own:(n + 1) * own, :]
-
-
-def near_wgrad_kernel(bits, inner, idx_ref, head_ref, xt_ref, gp_ref, send_ref, keep_ref, sorted_ref):
-    put_in_order(bits, head_ref, gp_ref, sorted_ref)
-    part_ways(nt(xt_ref[...], sorted_ref[...]), (idx_ref[0] & 1) == 1, send_ref, keep_ref, inner)
-
-
-def far_wgrad_kernel(bits, inner, idx_ref, head_ref, xt_ref, gp_ref, keep_ref, one_ref, two_ref, both_ref, sorted_ref):
-    put_in_order(bits, head_ref, gp_ref, sorted_ref)
-    total = nt(xt_ref[...], sorted_ref[...])
+        gp_ref[pl.ds(at, own), :] = near_ref[n * own:(n + 1) * own, :]
+        some = rows_ref.shape[0]
+        far_ref[pl.ds(pl.multiple_of((head_ref[0] ^ n) * some, 16), some), :] = rows_ref[...]
+    gp = (gp_ref[...].astype(F32) + tn(place_ref[...], far_ref[...])).astype(BF16)
+    gp_ref[...] = gp
+    total = nt(xt_ref[...], gp)
     right, upper = (idx_ref[0] & 1) == 1, ((idx_ref[0] >> 1) & 1) == 1
     for e in range(total.shape[0] // (4 * inner)):
         parts = [total[(4 * e + n) * inner:(4 * e + n + 1) * inner] for n in range(4)]
@@ -270,14 +269,6 @@
         both_ref[at, :] = jnp.where(upper, sent, sent_up).astype(BF16)
 
 
-def merge_kernel(bit, inner, idx_ref, near_ref, near_got, far_ref, one_ref, two_ref, both_ref, place_ref,
-                 send_ref, keep_ref):
-    far = far_ref[...] + one_ref[...].astype(F32) + two_ref[...].astype(F32) + both_ref[...].astype(F32)
-    total = near_ref[...] + near_got[...].astype(F32) + lax.dot_general(
-        far, place_ref[...], (((1,), (0,)), ((), ())), preferred_element_type=F32, precision=lax.Precision.HIGHEST)
-    part_ways(total, ((idx_ref[0] >> bit) & 1) == 1, send_ref, keep_ref, inner)
-
-
 def join_kernel(top, count, idx_ref, kv_ref, *refs):
     ups = refs[:count]
     gu_ref, send_ref = refs[count:]
@@ -309,7 +300,7 @@
     top = count - 1
     ups, gots = refs[:count], refs[count:2 * count]
     (qt_ref, lw_ref, g_ref, ds_ref, k_ref, v_ref, low_o, low_q, low_k, low_v, high_o, high_q, high_k, high_v,
-     near_ref, far_ref, place_ref, w_ref, out_hbm, dq_hbm, dx_hbm, dk_hbm, dv_hbm,
+     gp_ref, w_ref, out_hbm, dq_hbm, dx_hbm, dk_hbm, dv_hbm,
      out_ref, dq_ref, dx_ref, dk_ref, dv_ref, sems) = refs[2 * count:]
     index = idx_ref[0]
     copies = []
@@ -342,9 +333,8 @@
         cols = slice(pair * 2 * dk, (pair + 1) * 2 * dk)
         dq_ref[:, cols] = jnp.concatenate(halves, axis=0).astype(BF16).T
         send(dq_ref, dq_hbm, cols)
-    gp = (near_ref[...].astype(F32) + tn(place_ref[...].astype(BF16), far_ref[...])).astype(BF16)
     dx_ref[...] = lax.dot_general(
-        gp, w_ref[...], (((0,), (1,)), ((), ())), preferred_element_type=F32).astype(BF16)
+        gp_ref[...], w_ref[...], (((0,), (1,)), ((), ())), preferred_element_type=F32).astype(BF16)
     send(dx_ref, dx_hbm, slice(0, dx_ref.shape[1]))
     upper = ((index >> top) & 1) == 1
     zero = jnp.zeros((dk, dv), BF16)
@@ -450,43 +440,27 @@
         gots.append(swap(down, "seq", bit))
 
     near_all = gather_heads(near, head_bits)
-    n = width // 2
-    send, near_w, near_all = call(
-        functools.partial(near_wgrad_kernel, head_bits, per),
-        [S((n, cols), BF16), S((n, cols), F32), S((cols, tokens), BF16)],
-        [SM] * 2 + [VM] * 2, 2 * tokens * width * cols)(idx, head_idx, xt, near_all)
-    got = swap(send, "seq", 0)
-    n = n // 2
-    send, near_w = call(
-        functools.partial(fold_kernel, 1, per), [S((n, cols), BF16), S((n, cols), F32)],
-        [SM] + [VM] * 2, n * cols)(idx, near_w, got)
-    near_got = swap(send, "seq", 1)
-
-    far_all = gather_heads(far_rows, head_bits)
-    far_w, one, two, both, far_all = call(
-        functools.partial(far_wgrad_kernel, head_bits, per),
-        [S((n, far_cols), F32)] + [S((n, far_cols), BF16)] * 3 + [S((far_cols, tokens), BF16)],
-        [SM] * 2 + [VM] * 2, 2 * tokens * width * far_cols)(idx, head_idx, xt, far_all)
-    far_gots = [exchange(one, "seq", 1), exchange(two, "seq", 2),
-                exchange(both, "seq", 3)]
-
+    far_all = [far_rows] + [exchange(far_rows, "head", away) for away in range(1, n_head)]
     col = jnp.arange(cols, dtype=jnp.int32)[None, :]
     row = jnp.arange(far_cols, dtype=jnp.int32)[:, None]
     within = row % far_own
     at = (row // far_own * nh + within % nh) * levels + first + within // nh
-    place = ((at == col) & (within < far)).astype(F32)
-    n = n // 2
-    send, keep = call(
-        functools.partial(merge_kernel, 2, per), [S((n, cols), BF16), S((n, cols), F32)], [SM] + [VM] * 7,
-        4 * n * far_cols * cols)(idx, near_w, near_got, far_w, *far_gots, place)
-    got = swap(send, "seq", 2)
-    for bit in range(3, seq_bits):
+    place = ((at == col) & (within < far)).astype(BF16)
+
+    n = width // 4
+    keep, one, two, both, gp = call(
+        functools.partial(wgrad_kernel, head_bits, per),
+        [S((n, cols), F32)] + [S((n, cols), BF16)] * 3 + [S((cols, tokens), BF16)],
+        [SM] * 2 + [VM] * (n_head + 3), 2 * tokens * width * cols,
+        scratch_shapes=[pltpu.VMEM((far_cols, tokens), BF16)])(idx, head_idx, xt, place, near_all, *far_all)
+    got = [exchange(one, "seq", 1), exchange(two, "seq", 2), exchange(both, "seq", 3)]
+    for bit in range(2, seq_bits):
         n = n // 2
         send, keep = call(
             functools.partial(fold_kernel, bit, per), [S((n, cols), BF16), S((n, cols), F32)],
-            [SM] + [VM] * 2, n * cols)(idx, keep, got)
-        got = swap(send, "seq", bit)
-    d_w = keep + got.astype(F32)
+            [SM] + [VM] * (1 + len(got)), n * cols)(idx, keep, *got)
+        got = [swap(send, "seq", bit)]
+    d_w = keep + got[0].astype(F32)
 
     half = nh // 4
     local = []
@@ -500,10 +474,10 @@
     shapes = [(tokens, nh * dv), (tokens, rows), (tokens, width), (tokens, rows), (tokens, nh * dv)]
     out, d_queries, d_hidden, d_keys, d_values = call(
         functools.partial(final_kernel, dims, levels, first, seq_bits), [S(shape, BF16) for shape in shapes],
-        [SM] + [VM] * (2 * seq_bits + 18), 8 * tokens * rows * dv * seq_bits, out_specs=[hbm] * len(shapes),
+        [SM] + [VM] * (2 * seq_bits + 16), 8 * tokens * rows * dv * seq_bits, out_specs=[hbm] * len(shapes),
         scratch_shapes=[pltpu.VMEM(shape, BF16) for shape in shapes] + [pltpu.SemaphoreType.DMA((2 * nh + 1,))])(
             idx, *ups, *gots, qt, lw, d_out, d_state.reshape(rows, dv), keys, values, *local[0], *local[1],
-            near_all, far_all, place, w_near)
+            gp, w_near)
     return (out, d_queries, d_keys, d_values, d_hidden, d_w)
 
 

time: 51.4 us -> 54.1 us (1.053)
  waiting for transfers between devices: 17.3 us -> 22.8 us
  starting transfers between devices: 21.7 us -> 19.4 us
    ppermute x17 -> x16, waiting for transfers between devices: 17.3 us -> 22.8 us  [exchange(): return lax.ppermute(value, axis, pairs)]
    ppermute x17 -> x16, starting transfers between devices: 21.7 us -> 19.4 us  [exchange(): return lax.ppermute(value, axis, pairs)]
  transfers between devices with their start and end apart: 17 -> 16, of which waited for: 9 -> 9; matrix products, arithmetic and copies ran while one was open for 2% -> 2% of each run, Pallas kernels for 12% -> 10%
where the time goes in v11:
time: 54.1 us; the launch traced here: 54 us
  waiting for transfers between devices  22.8 us (42%)
  starting transfers between devices  19.4 us (36%)
  Pallas kernels  10.1 us (19%)
  between operations  0.84 us (2%)
  other arithmetic  0.82 us (2%)
    ppermute x16, waiting for transfers between devices, exchange(): return lax.ppermute(value, axis, pairs)  22.8 us
    ppermute x16, starting transfers between devices, exchange(): return lax.ppermute(value, axis, pairs)  19.4 us
    pallas_call x2, Pallas kernels, body(): call(functools.partial(local_kernel, dims, levels, tuple(range(part * hal...  2.81 us
    pallas_call x1, Pallas kernels, body(): call(functools.partial(final_kernel, dims, levels, first, seq_bits), [S(s...  2.72 us
    pallas_call x1, Pallas kernels, body(): call(functools.partial(state_kernel, dims), [S((rows, dv), F32), S((rows,...  1.51 us
  transfers between devices with their start and end apart: 16, of which 9 were waited for; matrix products, arithmetic and copies ran while one was open for 2% of the time, Pallas kernels for 10%

profile of v11, /device:TPU:0, one launch (start us, length us, event | category | flops | bytes accessed | tf_op | source)
XLA Modules:
  0.0 54.0 jit_solution(10310144912055889636)
XLA Ops:
  0.6 0.0 copy-start.1
  0.6 0.0 copy-start.2
  0.7 0.0 copy-start.3
  0.7 1.5 %shard_map.118 = (f32[512,128]{1,0:T(8,128)S(1)}, bf16[512,128]{1,0:T(8,128)(2,1)S(1)}, bf16[512,384]{1,0:T(8,128)(2,1)S(1)}, bf16[256,512]{1,0:T(8,128)(2,1)S(1)}) custom-call(s32[1]{0:T(128)} %bitcast.idx_ref, s32[1]{0:T(128)} %bitcast.1.head_ref.idx_ref, bf16[256,512]{1,0:T(8,128)(2,1)} %refs_10_.1, bf16[256,1024]{1,0:T(8,128)(2,1)} %refs_11_.1, ...), custom_call_target="tpu_custom_call" | custom-call | flops 33554432 | bytes 2097152 | tf_op jit(solution)/shard_map/pallas_call | solution.py:391
  2.2 0.0 copy-start
  2.2 3.1 %collective-permute-start = (bf16[512,128]{1,0:T(8,128)(2,1)S(1)}, bf16[512,128]{1,0:T(8,128)(2,1)S(1)}, u32[]{:S(2)}, u32[]{:S(2)}) collective-permute-start(bf16[512,128]{1,0:T(8,128)(2,1)S(1)} %get-tuple-element.40), channel_id=1, source_target_pairs={{0,4},{4,0},{8,12},{12,8},{16,20},{20,16},{24,28},{28,24},{1,5},{5... | collective-permute-start | bytes 393224 | tf_op jit(solution)/shard_map/ppermute | solution.py:51
  5.3 0.4 shard_map.119
  5.6 1.6 %collective-permute-start.2 = (bf16[192,256]{1,0:T(8,128)(2,1)S(1)}, bf16[192,256]{1,0:T(8,128)(2,1)S(1)}, u32[]{:S(2)}, u32[]{:S(2)}) collective-permute-start(bf16[192,256]{1,0:T(8,128)(2,1)S(1)} %get-tuple-element.45), channel_id=1, source_target_pairs={{0,2},{1,3},{2,0},{3,1},{4,6},{5,7},{6,4},{7,5},{8,10},{9,11},{10,... | collective-permute-start | bytes 294920 | tf_op jit(solution)/shard_map/ppermute | solution.py:51
  7.2 0.0 copy-done.1
  7.2 0.0 copy-done.2
  7.2 0.0 copy-done.3
  7.2 0.0 copy-done
  7.2 0.8 %shard_map.121.gl_ref = f32[96,256]{1,0:T(8,128)S(1)} custom-call(bf16[256,512]{1,0:T(8,128)(2,1)S(1)} %copy-done.2, bf16[256,512]{1,0:T(8,128)(2,1)S(1)} %copy-done.3, bf16[256,1024]{1,0:T(8,128)(2,1)S(1)} %copy-done.1, bf16[256,1024]{1,0:T(8,128)(2,1)S(1)} %copy-done), custom_call_target="tpu_custom_call" | custom-call | flops 201326592 | bytes 196608 | tf_op jit(solution)/shard_map/pallas_call | solution.py:420
  8.0 2.3 %collective-permute-done.2.refs_0_ = bf16[192,256]{1,0:T(8,128)(2,1)S(1)} collective-permute-done((bf16[192,256]{1,0:T(8,128)(2,1)S(1)}, bf16[192,256]{1,0:T(8,128)(2,1)S(1)}, u32[]{:S(2)}, u32[]{:S(2)}) %collective-permute-start.2) | collective-permute-done | bytes 98336 | tf_op jit(solution)/shard_map/ppermute | solution.py:51
  10.4 0.1 collective-permute-start.3
  10.4 0.0 collective-permute-done.refs_0_
  10.5 1.6 %collective-permute-start.1 = (bf16[512,128]{1,0:T(8,128)(2,1)S(1)}, bf16[512,128]{1,0:T(8,128)(2,1)S(1)}, u32[]{:S(2)}, u32[]{:S(2)}) collective-permute-start(bf16[512,128]{1,0:T(8,128)(2,1)S(1)} %add_convert_fusion), channel_id=1, source_target_pairs={{0,8},{4,12},{8,0},{12,4},{16,24},{20,28},{24,16},{28,20},{1,9},{5... | collective-permute-start | bytes 393224 | tf_op jit(solution)/shard_map/ppermute | solution.py:51
  12.1 0.0 collective-permute-done.3.got_ref
  12.1 0.4 shard_map.122
  12.6 1.6 %collective-permute-start.7 = (bf16[96,256]{1,0:T(8,128)(2,1)S(1)}, bf16[96,256]{1,0:T(8,128)(2,1)S(1)}, u32[]{:S(2)}, u32[]{:S(2)}) collective-permute-start(bf16[96,256]{1,0:T(8,128)(2,1)S(1)} %get-tuple-element.60), channel_id=1, source_target_pairs={{0,2},{1,3},{2,0},{3,1},{4,6},{5,7},{6,4},{7,5},{8,10},{9,11},{10,... | collective-permute-start | bytes 147464 | tf_op jit(solution)/shard_map/ppermute | solution.py:51
  14.1 2.6 %collective-permute-done.7 = bf16[96,256]{1,0:T(8,128)(2,1)S(1)} collective-permute-done((bf16[96,256]{1,0:T(8,128)(2,1)S(1)}, bf16[96,256]{1,0:T(8,128)(2,1)S(1)}, u32[]{:S(2)}, u32[]{:S(2)}) %collective-permute-start.7) | collective-permute-done | bytes 49184 | tf_op jit(solution)/shard_map/ppermute | solution.py:51
  16.7 0.1 collective-permute-start.8
  16.8 0.0 collective-permute-done.1.refs_1_
  16.8 0.1 shard_map.123
  16.9 2.6 %collective-permute-start.4 = (bf16[512,128]{1,0:T(8,128)(2,1)S(1)}, bf16[512,128]{1,0:T(8,128)(2,1)S(1)}, u32[]{:S(2)}, u32[]{:S(2)}) collective-permute-start(bf16[512,128]{1,0:T(8,128)(2,1)S(1)} %shard_map.123), channel_id=1, source_target_pairs={{0,16},{4,20},{8,24},{12,28},{16,0},{20,4},{24,8},{28,12},{1,17},{... | collective-permute-start | bytes 393224 | tf_op jit(solution)/shard_map/ppermute | solution.py:51
  19.5 0.1 fusion.1.place_ref
  19.6 6.9 %collective-permute-done.4.refs_0_.refs_2_.refs_3_ = bf16[512,128]{1,0:T(8,128)(2,1)S(1)} collective-permute-done((bf16[512,128]{1,0:T(8,128)(2,1)S(1)}, bf16[512,128]{1,0:T(8,128)(2,1)S(1)}, u32[]{:S(2)}, u32[]{:S(2)}) %collective-permute-start.4) | collective-permute-done | bytes 131104 | tf_op jit(solution)/shard_map/ppermute | solution.py:51
  26.5 0.7 %shard_map.128.refs_0_ = bf16[32,256]{1,0:T(8,128)(2,1)S(1)} custom-call(s32[1]{0:T(128)} %bitcast.idx_ref, bf16[512,128]{1,0:T(8,128)(2,1)S(1)} %collective-permute-done.refs_0_, bf16[512,128]{1,0:T(8,128)(2,1)S(1)} %collective-permute-done.1.refs_1_, bf16[512,128]{1,0:T(8,128)(2,1)S(1)} %collective-permute-done.4.refs_0_.refs_2_.refs_3_, ...), custom_call_target="tpu_custom_call" | custom-call | flops 100663296 | bytes 32768 | tf_op jit(solution)/shard_map/pallas_call | solution.py:433
  27.2 0.8 %collective-permute-start.11 = (bf16[32,256]{1,0:T(8,128)(2,1)S(1)}, bf16[32,256]{1,0:T(8,128)(2,1)S(1)}, u32[]{:S(2)}, u32[]{:S(2)}) collective-permute-start(bf16[32,256]{1,0:T(8,128)(2,1)S(1)} %shard_map.128.refs_0_), channel_id=1, source_target_pairs={{0,3},{1,2},{2,1},{3,0},{4,7},{5,6},{6,5},{7,4},{8,11},{9,10},{10,... | collective-permute-start | bytes 49160 | tf_op jit(solution)/shard_map/ppermute | solution.py:51
  28.0 0.8 %collective-permute-start.10 = (bf16[32,256]{1,0:T(8,128)(2,1)S(1)}, bf16[32,256]{1,0:T(8,128)(2,1)S(1)}, u32[]{:S(2)}, u32[]{:S(2)}) collective-permute-start(bf16[32,256]{1,0:T(8,128)(2,1)S(1)} %shard_map.128.refs_0_), channel_id=1, source_target_pairs={{0,2},{1,3},{2,0},{3,1},{4,6},{5,7},{6,4},{7,5},{8,10},{9,11},{10,... | collective-permute-start | bytes 49160 | tf_op jit(solution)/shard_map/ppermute | solution.py:51
  28.9 0.3 collective-permute-start.9
  29.1 0.0 collective-permute-done.8
  29.2 1.4 %collective-permute-done.11.refs_3_ = bf16[32,256]{1,0:T(8,128)(2,1)S(1)} collective-permute-done((bf16[32,256]{1,0:T(8,128)(2,1)S(1)}, bf16[32,256]{1,0:T(8,128)(2,1)S(1)}, u32[]{:S(2)}, u32[]{:S(2)}) %collective-permute-start.11) | collective-permute-done | bytes 16416 | tf_op jit(solution)/shard_map/ppermute | solution.py:51
  30.6 1.3 %collective-permute-done.10.refs_2_ = bf16[32,256]{1,0:T(8,128)(2,1)S(1)} collective-permute-done((bf16[32,256]{1,0:T(8,128)(2,1)S(1)}, bf16[32,256]{1,0:T(8,128)(2,1)S(1)}, u32[]{:S(2)}, u32[]{:S(2)}) %collective-permute-start.10) | collective-permute-done | bytes 16416 | tf_op jit(solution)/shard_map/ppermute | solution.py:51
  31.8 0.0 collective-permute-done.9.refs_1_
  31.8 0.5 shard_map.129
  32.4 0.6 %collective-permute-start.12 = (bf16[128,384]{1,0:T(8,128)(2,1)S(1)}, bf16[128,384]{1,0:T(8,128)(2,1)S(1)}, u32[]{:S(2)}, u32[]{:S(2)}) collective-permute-start(bf16[128,384]{1,0:T(8,128)(2,1)S(1)} %get-tuple-element.69), channel_id=1, source_target_pairs={{0,4},{4,0},{8,12},{12,8},{16,20},{20,16},{24,28},{28,24},{1,5},{5... | collective-permute-start | bytes 294920 | tf_op jit(solution)/shard_map/ppermute | solution.py:51
  32.9 0.3 collective-permute-start.13
  33.2 2.7 %collective-permute-start.14 = (bf16[128,384]{1,0:T(8,128)(2,1)S(1)}, bf16[128,384]{1,0:T(8,128)(2,1)S(1)}, u32[]{:S(2)}, u32[]{:S(2)}) collective-permute-start(bf16[128,384]{1,0:T(8,128)(2,1)S(1)} %get-tuple-element.71), channel_id=1, source_target_pairs={{0,12},{4,8},{8,4},{12,0},{16,28},{20,24},{24,20},{28,16},{1,13},{... | collective-permute-start | bytes 294920 | tf_op jit(solution)/shard_map/ppermute | solution.py:51
  35.9 0.1 shard_map.124
  36.0 0.3 collective-permute-start.5
  36.3 0.8 %collective-permute-done.12.refs_0_ = bf16[128,384]{1,0:T(8,128)(2,1)S(1)} collective-permute-done((bf16[128,384]{1,0:T(8,128)(2,1)S(1)}, bf16[128,384]{1,0:T(8,128)(2,1)S(1)}, u32[]{:S(2)}, u32[]{:S(2)}) %collective-permute-start.12) | collective-permute-done | bytes 98336 | tf_op jit(solution)/shard_map/ppermute | solution.py:51
  37.2 1.5 %collective-permute-done.13.refs_1_ = bf16[128,384]{1,0:T(8,128)(2,1)S(1)} collective-permute-done((bf16[128,384]{1,0:T(8,128)(2,1)S(1)}, bf16[128,384]{1,0:T(8,128)(2,1)S(1)}, u32[]{:S(2)}, u32[]{:S(2)}) %collective-permute-start.13) | collective-permute-done | bytes 98336 | tf_op jit(solution)/shard_map/ppermute | solution.py:51
  38.6 3.1 %collective-permute-done.14.refs_2_ = bf16[128,384]{1,0:T(8,128)(2,1)S(1)} collective-permute-done((bf16[128,384]{1,0:T(8,128)(2,1)S(1)}, bf16[128,384]{1,0:T(8,128)(2,1)S(1)}, u32[]{:S(2)}, u32[]{:S(2)}) %collective-permute-start.14) | collective-permute-done | bytes 98336 | tf_op jit(solution)/shard_map/ppermute | solution.py:51
  41.7 0.1 shard_map.131
  41.7 1.6 %collective-permute-start.15 = (bf16[64,384]{1,0:T(8,128)(2,1)S(1)}, bf16[64,384]{1,0:T(8,128)(2,1)S(1)}, u32[]{:S(2)}, u32[]{:S(2)}) collective-permute-start(bf16[64,384]{1,0:T(8,128)(2,1)S(1)} %get-tuple-element.73), channel_id=1, source_target_pairs={{0,16},{4,20},{8,24},{12,28},{16,0},{20,4},{24,8},{28,12},{1,17},{... | collective-permute-start | bytes 147464 | tf_op jit(solution)/shard_map/ppermute | solution.py:51
  43.3 1.4 %shard_map.127 = (f32[512,256]{1,0:T(8,128)S(1)}, f32[256,256]{1,0:T(8,128)S(1)}, f32[256,256]{1,0:T(8,128)S(1)}, f32[256,512]{1,0:T(8,128)S(1)}) custom-call(bf16[256,512]{1,0:T(8,128)(2,1)S(1)} %copy-done.2, bf16[256,512]{1,0:T(8,128)(2,1)S(1)} %copy-done.3, bf16[256,1024]{1,0:T(8,128)(2,1)S(1)} %copy-done.1, bf16[256,1024]{1,0:T(8,128)(2,1)S(1)} %copy-done, ...), custom_call_target="tpu_custom_call" | custom-call | flops 301989888 | bytes 3145728 | tf_op jit(solution)/shard_map/pallas_call | solution.py:468
  44.7 1.4 %shard_map.126 = (f32[512,256]{1,0:T(8,128)S(1)}, f32[256,256]{1,0:T(8,128)S(1)}, f32[256,256]{1,0:T(8,128)S(1)}, f32[256,512]{1,0:T(8,128)S(1)}) custom-call(bf16[256,512]{1,0:T(8,128)(2,1)S(1)} %copy-done.2, bf16[256,512]{1,0:T(8,128)(2,1)S(1)} %copy-done.3, bf16[256,1024]{1,0:T(8,128)(2,1)S(1)} %copy-done.1, bf16[256,1024]{1,0:T(8,128)(2,1)S(1)} %copy-done, ...), custom_call_target="tpu_custom_call" | custom-call | flops 301989888 | bytes 3145728 | tf_op jit(solution)/shard_map/pallas_call | solution.py:468
  46.1 0.0 collective-permute-done.5.refs_1_.refs_4_
  46.1 0.1 shard_map.125
  46.2 0.0 copy-start.4
  46.2 1.4 %collective-permute-start.6 = (bf16[512,128]{1,0:T(8,128)(2,1)S(1)}, bf16[512,128]{1,0:T(8,128)(2,1)S(1)}, u32[]{:S(2)}, u32[]{:S(2)}) collective-permute-start(bf16[512,128]{1,0:T(8,128)(2,1)S(1)} %shard_map.125), channel_id=1, source_target_pairs={{0,4},{4,0},{8,12},{12,8},{16,20},{20,16},{24,28},{28,24},{1,5},{5... | collective-permute-start | bytes 393224 | tf_op jit(solution)/shard_map/ppermute | solution.py:51
  47.7 0.0 collective-permute-done.15
  47.7 0.7 %convert_add_fusion = f32[64,384]{1,0:T(8,128)} fusion(f32[64,384]{1,0:T(8,128)S(1)} %get-tuple-element.72, bf16[64,384]{1,0:T(8,128)(2,1)S(1)} %collective-permute-done.15), kind=kLoop, calls=%fused_computation.6 | loop fusion | flops 49152 | bytes 245760 | tf_op jit(solution)/shard_map/add | solution.py:463
  48.3 2.9 %collective-permute-done.6.refs_5_ = bf16[512,128]{1,0:T(8,128)(2,1)S(1)} collective-permute-done((bf16[512,128]{1,0:T(8,128)(2,1)S(1)}, bf16[512,128]{1,0:T(8,128)(2,1)S(1)}, u32[]{:S(2)}, u32[]{:S(2)}) %collective-permute-start.6) | collective-permute-done | bytes 131104 | tf_op jit(solution)/shard_map/ppermute | solution.py:51
  51.3 0.0 copy-done.4
  51.3 2.7 %shard_map.130 = (bf16[256,1024]{1,0:T(8,128)(2,1)}, bf16[256,512]{1,0:T(8,128)(2,1)}, bf16[256,512]{1,0:T(8,128)(2,1)}, bf16[256,512]{1,0:T(8,128)(2,1)}, bf16[256,1024]{1,0:T(8,128)(2,1)}) custom-call(s32[1]{0:T(128)} %bitcast.idx_ref, bf16[512,128]{1,0:T(8,128)(2,1)S(1)} %collective-permute-done.refs_0_, ...), custom_call_target="tpu_custom_call" | custom-call | flops 402653184 | bytes 3670016 | tf_op jit(solution)/shard_map/pallas_call | solution.py:475
  (6 shorter events, 0.1 us)
Async XLA Ops:
  0.6 6.6 %copy-start.1 = (bf16[256,1024]{1,0:T(8,128)(2,1)S(1)}, bf16[256,1024]{1,0:T(8,128)(2,1)}, u32[]{:S(2)}) copy-start(bf16[256,1024]{1,0:T(8,128)(2,1)} %refs_11_.1) | copy-start | bytes 1572868
  0.6 6.6 %copy-start.2 = (bf16[256,512]{1,0:T(8,128)(2,1)S(1)}, bf16[256,512]{1,0:T(8,128)(2,1)}, u32[]{:S(2)}) copy-start(bf16[256,512]{1,0:T(8,128)(2,1)} %refs_10_.1) | copy-start | bytes 786436
  0.7 6.6 %copy-start.3 = (bf16[256,512]{1,0:T(8,128)(2,1)S(1)}, bf16[256,512]{1,0:T(8,128)(2,1)}, u32[]{:S(2)}) copy-start(bf16[256,512]{1,0:T(8,128)(2,1)} %q_ref.7) | copy-start | bytes 786436
  2.2 5.0 %copy-start = (bf16[256,1024]{1,0:T(8,128)(2,1)S(1)}, bf16[256,1024]{1,0:T(8,128)(2,1)}, u32[]{:S(2)}) copy-start(bf16[256,1024]{1,0:T(8,128)(2,1)} %refs_8_.1) | copy-start | bytes 1572868
  2.2 8.2 %collective-permute-start = (bf16[512,128]{1,0:T(8,128)(2,1)S(1)}, bf16[512,128]{1,0:T(8,128)(2,1)S(1)}, u32[]{:S(2)}, u32[]{:S(2)}) collective-permute-start(bf16[512,128]{1,0:T(8,128)(2,1)S(1)} %get-tuple-element.40), channel_id=1, source_target_pairs={{0,4},{4,0},{8,12},{12,8},{16,20},{20,16},{24,28},{28,24},{1,5},{5... | collective-permute-start | bytes 393224 | tf_op jit(solution)/shard_map/ppermute | solution.py:51
  5.6 4.7 %collective-permute-start.2 = (bf16[192,256]{1,0:T(8,128)(2,1)S(1)}, bf16[192,256]{1,0:T(8,128)(2,1)S(1)}, u32[]{:S(2)}, u32[]{:S(2)}) collective-permute-start(bf16[192,256]{1,0:T(8,128)(2,1)S(1)} %get-tuple-element.45), channel_id=1, source_target_pairs={{0,2},{1,3},{2,0},{3,1},{4,6},{5,7},{6,4},{7,5},{8,10},{9,11},{10,... | collective-permute-start | bytes 294920 | tf_op jit(solution)/shard_map/ppermute | solution.py:51
  10.4 1.8 %collective-permute-start.3 = (bf16[96,256]{1,0:T(8,128)(2,1)S(1)}, bf16[96,256]{1,0:T(8,128)(2,1)S(1)}, u32[]{:S(2)}, u32[]{:S(2)}) collective-permute-start(bf16[96,256]{1,0:T(8,128)(2,1)S(1)} %get-tuple-element.47), channel_id=1, source_target_pairs={{0,1},{1,0},{2,3},{3,2},{4,5},{5,4},{6,7},{7,6},{8,9},{9,8},{10,11... | collective-permute-start | bytes 147464 | tf_op jit(solution)/shard_map/ppermute | solution.py:51
  10.5 6.3 %collective-permute-start.1 = (bf16[512,128]{1,0:T(8,128)(2,1)S(1)}, bf16[512,128]{1,0:T(8,128)(2,1)S(1)}, u32[]{:S(2)}, u32[]{:S(2)}) collective-permute-start(bf16[512,128]{1,0:T(8,128)(2,1)S(1)} %add_convert_fusion), channel_id=1, source_target_pairs={{0,8},{4,12},{8,0},{12,4},{16,24},{20,28},{24,16},{28,20},{1,9},{5... | collective-permute-start | bytes 393224 | tf_op jit(solution)/shard_map/ppermute | solution.py:51
  12.6 4.2 %collective-permute-start.7 = (bf16[96,256]{1,0:T(8,128)(2,1)S(1)}, bf16[96,256]{1,0:T(8,128)(2,1)S(1)}, u32[]{:S(2)}, u32[]{:S(2)}) collective-permute-start(bf16[96,256]{1,0:T(8,128)(2,1)S(1)} %get-tuple-element.60), channel_id=1, source_target_pairs={{0,2},{1,3},{2,0},{3,1},{4,6},{5,7},{6,4},{7,5},{8,10},{9,11},{10,... | collective-permute-start | bytes 147464 | tf_op jit(solution)/shard_map/ppermute | solution.py:51
  16.7 12.4 %collective-permute-start.8 = (bf16[192,256]{1,0:T(8,128)(2,1)S(1)}, bf16[192,256]{1,0:T(8,128)(2,1)S(1)}, u32[]{:S(2)}, u32[]{:S(2)}) collective-permute-start(bf16[192,256]{1,0:T(8,128)(2,1)S(1)} %pad_maximum_fusion.1), channel_id=1, source_target_pairs={{0,1},{1,0},{2,3},{3,2},{4,5},{5,4},{6,7},{7,6},{8,9},{9,8},{10,11... | collective-permute-start | bytes 294920 | tf_op jit(solution)/shard_map/ppermute | solution.py:51
  16.9 9.7 %collective-permute-start.4 = (bf16[512,128]{1,0:T(8,128)(2,1)S(1)}, bf16[512,128]{1,0:T(8,128)(2,1)S(1)}, u32[]{:S(2)}, u32[]{:S(2)}) collective-permute-start(bf16[512,128]{1,0:T(8,128)(2,1)S(1)} %shard_map.123), channel_id=1, source_target_pairs={{0,16},{4,20},{8,24},{12,28},{16,0},{20,4},{24,8},{28,12},{1,17},{... | collective-permute-start | bytes 393224 | tf_op jit(solution)/shard_map/ppermute | solution.py:51
  27.2 3.4 %collective-permute-start.11 = (bf16[32,256]{1,0:T(8,128)(2,1)S(1)}, bf16[32,256]{1,0:T(8,128)(2,1)S(1)}, u32[]{:S(2)}, u32[]{:S(2)}) collective-permute-start(bf16[32,256]{1,0:T(8,128)(2,1)S(1)} %shard_map.128.refs_0_), channel_id=1, source_target_pairs={{0,3},{1,2},{2,1},{3,0},{4,7},{5,6},{6,5},{7,4},{8,11},{9,10},{10,... | collective-permute-start | bytes 49160 | tf_op jit(solution)/shard_map/ppermute | solution.py:51
  28.0 3.8 %collective-permute-start.10 = (bf16[32,256]{1,0:T(8,128)(2,1)S(1)}, bf16[32,256]{1,0:T(8,128)(2,1)S(1)}, u32[]{:S(2)}, u32[]{:S(2)}) collective-permute-start(bf16[32,256]{1,0:T(8,128)(2,1)S(1)} %shard_map.128.refs_0_), channel_id=1, source_target_pairs={{0,2},{1,3},{2,0},{3,1},{4,6},{5,7},{6,4},{7,5},{8,10},{9,11},{10,... | collective-permute-start | bytes 49160 | tf_op jit(solution)/shard_map/ppermute | solution.py:51
  28.9 3.0 %collective-permute-start.9 = (bf16[32,256]{1,0:T(8,128)(2,1)S(1)}, bf16[32,256]{1,0:T(8,128)(2,1)S(1)}, u32[]{:S(2)}, u32[]{:S(2)}) collective-permute-start(bf16[32,256]{1,0:T(8,128)(2,1)S(1)} %shard_map.128.refs_0_), channel_id=1, source_target_pairs={{0,1},{1,0},{2,3},{3,2},{4,5},{5,4},{6,7},{7,6},{8,9},{9,8},{10,11... | collective-permute-start | bytes 49160 | tf_op jit(solution)/shard_map/ppermute | solution.py:51
  32.4 4.8 %collective-permute-start.12 = (bf16[128,384]{1,0:T(8,128)(2,1)S(1)}, bf16[128,384]{1,0:T(8,128)(2,1)S(1)}, u32[]{:S(2)}, u32[]{:S(2)}) collective-permute-start(bf16[128,384]{1,0:T(8,128)(2,1)S(1)} %get-tuple-element.69), channel_id=1, source_target_pairs={{0,4},{4,0},{8,12},{12,8},{16,20},{20,16},{24,28},{28,24},{1,5},{5... | collective-permute-start | bytes 294920 | tf_op jit(solution)/shard_map/ppermute | solution.py:51
  32.9 5.7 %collective-permute-start.13 = (bf16[128,384]{1,0:T(8,128)(2,1)S(1)}, bf16[128,384]{1,0:T(8,128)(2,1)S(1)}, u32[]{:S(2)}, u32[]{:S(2)}) collective-permute-start(bf16[128,384]{1,0:T(8,128)(2,1)S(1)} %get-tuple-element.70), channel_id=1, source_target_pairs={{0,8},{4,12},{8,0},{12,4},{16,24},{20,28},{24,16},{28,20},{1,9},{5... | collective-permute-start | bytes 294920 | tf_op jit(solution)/shard_map/ppermute | solution.py:51
  33.2 8.4 %collective-permute-start.14 = (bf16[128,384]{1,0:T(8,128)(2,1)S(1)}, bf16[128,384]{1,0:T(8,128)(2,1)S(1)}, u32[]{:S(2)}, u32[]{:S(2)}) collective-permute-start(bf16[128,384]{1,0:T(8,128)(2,1)S(1)} %get-tuple-element.71), channel_id=1, source_target_pairs={{0,12},{4,8},{8,4},{12,0},{16,28},{20,24},{24,20},{28,16},{1,13},{... | collective-permute-start | bytes 294920 | tf_op jit(solution)/shard_map/ppermute | solution.py:51
  36.0 10.2 %collective-permute-start.5 = (bf16[512,128]{1,0:T(8,128)(2,1)S(1)}, bf16[512,128]{1,0:T(8,128)(2,1)S(1)}, u32[]{:S(2)}, u32[]{:S(2)}) collective-permute-start(bf16[512,128]{1,0:T(8,128)(2,1)S(1)} %shard_map.124), channel_id=1, source_target_pairs={{0,8},{4,12},{8,0},{12,4},{16,24},{20,28},{24,16},{28,20},{1,9},{5... | collective-permute-start | bytes 393224 | tf_op jit(solution)/shard_map/ppermute | solution.py:51
  41.7 6.0 %collective-permute-start.15 = (bf16[64,384]{1,0:T(8,128)(2,1)S(1)}, bf16[64,384]{1,0:T(8,128)(2,1)S(1)}, u32[]{:S(2)}, u32[]{:S(2)}) collective-permute-start(bf16[64,384]{1,0:T(8,128)(2,1)S(1)} %get-tuple-element.73), channel_id=1, source_target_pairs={{0,16},{4,20},{8,24},{12,28},{16,0},{20,4},{24,8},{28,12},{1,17},{... | collective-permute-start | bytes 147464 | tf_op jit(solution)/shard_map/ppermute | solution.py:51
  46.2 5.0 %copy-start.4 = (f32[8,64,128]{2,1,0:T(8,128)S(1)}, f32[8,64,128]{2,1,0:T(8,128)}, u32[]{:S(2)}) copy-start(f32[8,64,128]{2,1,0:T(8,128)} %param.13) | copy-start | bytes 786436
  46.2 5.0 %collective-permute-start.6 = (bf16[512,128]{1,0:T(8,128)(2,1)S(1)}, bf16[512,128]{1,0:T(8,128)(2,1)S(1)}, u32[]{:S(2)}, u32[]{:S(2)}) collective-permute-start(bf16[512,128]{1,0:T(8,128)(2,1)S(1)} %shard_map.125), channel_id=1, source_target_pairs={{0,4},{4,0},{8,12},{12,8},{16,20},{20,16},{24,28},{28,24},{1,5},{5... | collective-permute-start | bytes 393224 | tf_op jit(solution)/shard_map/ppermute | solution.py:51

commit v12 on v11

--- a/solution.py
+++ b/solution.py
@@ -46,8 +46,9 @@
     return copy
 
 
-def exchange(value, axis, mask):
-    pairs = [(source, source ^ mask) for source in range(lax.axis_size(axis))]
+def exchange(value, axis, mask, only=None):
+    pairs = [(source, source ^ mask) for source in range(lax.axis_size(axis))
+             if only is None or bool(source & mask) == only]
     return lax.ppermute(value, axis, pairs)
 
 
@@ -101,7 +102,7 @@
 
 
 def weight_kernel(dims, levels, first, count, keep_ref, got_ref, gl_ref, q_ref, g_ref,
-                  sig_ref, lw_ref, near_ref, qt_ref, gu_ref):
+                  sig_ref, lw_ref, near_ref, qt_ref, gu_ref, gu_top_ref):
     nh, dk, dv = dims
     proj = keep_ref[...] + got_ref[...].astype(F32)
     sig = jax.nn.sigmoid(proj)
@@ -118,8 +119,9 @@
                 [wide[j * dk:(j + 1) * dk] * lw_ref[h * levels + first + m:h * levels + first + m + 1, :]
                  for m in range(count)], axis=0)
             grad = nn(scaled.astype(BF16), g_ref[:, h * dv:(h + 1) * dv])
-            for m in range(count):
+            for m in range(count - 1):
                 gu_ref[m, h * dk:(h + 1) * dk, :] = grad[m * dk:(m + 1) * dk].astype(BF16)
+            gu_top_ref[h * dk:(h + 1) * dk, :] = grad[(count - 1) * dk:].astype(BF16)
 
 
 def spread_half(rows, lane, low, t_low):
@@ -269,21 +271,12 @@
         both_ref[at, :] = jnp.where(upper, sent, sent_up).astype(BF16)
 
 
-def join_kernel(top, count, idx_ref, kv_ref, *refs):
-    ups = refs[:count]
-    gu_ref, send_ref = refs[count:]
-    upper = ((idx_ref[0] >> top) & 1) == 1
-
-    @pl.when(upper)
-    def _():
-        send_ref[...] = gu_ref[top]
-
-    @pl.when(jnp.logical_not(upper))
-    def _():
-        total = kv_ref[...]
-        for up in ups:
-            total = total + up[...].astype(F32)
-        send_ref[...] = total.astype(BF16)
+def quad_kernel(kv_ref, one_ref, two_ref, both_ref, upper_ref, sum_ref, send_ref):
+    upper = two_ref[...].astype(F32) + both_ref[...].astype(F32)
+    upper_ref[...] = upper.astype(BF16)
+    total = kv_ref[...] + one_ref[...].astype(F32) + upper
+    sum_ref[...] = total
+    send_ref[...] = total.astype(BF16)
 
 
 def pend_kernel(bit, top, idx_ref, *refs):
@@ -400,14 +393,7 @@
         [S((cols // 2, tokens), BF16), S((cols // 2, tokens), F32), S((width, tokens), BF16)], [SM] + [VM] * 2,
         2 * tokens * width * cols)(head_idx, w_near, x_near)
 
-    total, up = kv, kvb
-    ups = []
-    for bit in range(top):
-        partner = swap(up, "seq", bit)
-        ups.append(partner)
-        if bit < top - 1:
-            total = total + partner.astype(F32)
-            up = total.astype(BF16)
+    quad = [exchange(kvb, "seq", 1), exchange(kvb, "seq", 2), exchange(kvb, "seq", 3)]
 
     got = swap(send, "head", head_bits - 1)
     for bit in reversed(range(head_bits - 1)):
@@ -420,20 +406,25 @@
     gl = call(
         functools.partial(level_kernel, dims, levels), [S((own, tokens), F32)], [VM] * 4,
         2 * tokens * tokens * nh * (dk + dv))(keys, queries, values, d_out)[0]
-    sig, lw, near, qt, gu = call(
+    sig, lw, near, qt, gu, gu_top = call(
         functools.partial(weight_kernel, dims, levels, first, seq_bits),
         [S((own, tokens), F32), S((own, tokens), F32), S((own, tokens), BF16), S((rows, tokens), BF16),
-         S((seq_bits, rows, dv), BF16)],
+         S((top, rows, dv), BF16), S((rows, dv), BF16)],
         [VM] * 5, 2 * tokens * rows * dv * seq_bits)(keep, got, gl, queries, d_out)
 
-    up = call(functools.partial(join_kernel, top, top), [S((rows, dv), BF16)], [SM] + [VM] * (top + 2),
-              rows * dv)(idx, kv, *ups, gu)[0]
-    partner = swap(up, "seq", top)
-    ups.append(partner)
+    second, total, up = call(
+        quad_kernel, [S((rows, dv), BF16), S((rows, dv), F32), S((rows, dv), BF16)], [VM] * 4, 4 * rows * dv)(
+            kv, *quad)
+    ups = [quad[0], second]
+    for bit in range(2, top):
+        ups.append(swap(up, "seq", bit))
+        total = total + ups[-1].astype(F32)
+        up = total.astype(BF16)
+    ups.append(exchange(up, "seq", 1 << top, only=False))
     far_rows = call(
         functools.partial(carry_kernel, dims, levels, first, seq_bits), [S((far_own, tokens), BF16)],
         [SM] + [VM] * (seq_bits + 3), 2 * tokens * rows * dv * seq_bits)(idx, *ups, d_out, qt, sig)[0]
-    gots = [partner]
+    gots = [exchange(gu_top, "seq", 1 << top, only=True)]
     for bit in reversed(range(top)):
         down = call(functools.partial(pend_kernel, bit, top), [S((rows, dv), BF16)], [SM] + [VM] * (len(gots) + 1),
                     rows * dv)(idx, *gots, gu)[0]

time: 54.1 us -> 53.3 us (0.985)
  waiting for transfers between devices: 22.8 us -> 12.8 us
  starting transfers between devices: 19.4 us -> 27.8 us
  Pallas kernels: 10.1 us -> 10.8 us
    ppermute x16 -> x18, waiting for transfers between devices: 22.8 us -> 12.8 us  [exchange(): return lax.ppermute(value, axis, pairs)]
    ppermute x16 -> x18, starting transfers between devices: 19.4 us -> 27.8 us  [exchange(): return lax.ppermute(value, axis, pairs)]
    pallas_call x1, Pallas kernels: 0.06 us -> 0.77 us  [body(): call(quad_kernel, [S((rows, dv), BF16), S((rows, dv), F32), S((rows, dv),...]
  transfers between devices with their start and end apart: 16 -> 18, of which waited for: 9 -> 9; matrix products, arithmetic and copies ran while one was open for 2% -> 1% of each run, Pallas kernels for 10% -> 12%
where the time goes in v12:
time: 53.3 us; the launch traced here: 53.1 us
  starting transfers between devices  27.8 us (52%)
  waiting for transfers between devices  12.8 us (24%)
  Pallas kernels  10.8 us (20%)
  between operations  0.88 us (2%)
  other arithmetic  0.79 us (1%)
    ppermute x18, starting transfers between devices, exchange(): return lax.ppermute(value, axis, pairs)  27.8 us
    ppermute x18, waiting for transfers between devices, exchange(): return lax.ppermute(value, axis, pairs)  12.8 us
    pallas_call x2, Pallas kernels, body(): call(functools.partial(local_kernel, dims, levels, tuple(range(part * hal...  2.81 us
    pallas_call x1, Pallas kernels, body(): call(functools.partial(final_kernel, dims, levels, first, seq_bits), [S(s...  2.72 us
    pallas_call x1, Pallas kernels, body(): call(functools.partial(state_kernel, dims), [S((rows, dv), F32), S((rows,...  1.5 us
  transfers between devices with their start and end apart: 18, of which 9 were waited for; matrix products, arithmetic and copies ran while one was open for 1% of the time, Pallas kernels for 12%

profile of v12, /device:TPU:0, one launch (start us, length us, event | category | flops | bytes accessed | tf_op | source)
XLA Modules:
  0.0 53.1 jit_solution(16993745504132032012)
XLA Ops:
  0.6 0.0 copy-start.1
  0.6 0.0 copy-start.3
  0.7 1.5 %shard_map.118 = (f32[512,128]{1,0:T(8,128)S(1)}, bf16[512,128]{1,0:T(8,128)(2,1)S(1)}, bf16[512,384]{1,0:T(8,128)(2,1)S(1)}, bf16[256,512]{1,0:T(8,128)(2,1)S(1)}) custom-call(s32[1]{0:T(128)} %bitcast.idx_ref, s32[1]{0:T(128)} %bitcast.1.head_ref.idx_ref, bf16[256,512]{1,0:T(8,128)(2,1)} %refs_10_.1, bf16[256,1024]{1,0:T(8,128)(2,1)} %refs_11_.1, ...), custom_call_target="tpu_custom_call" | custom-call | flops 33554432 | bytes 2097152 | tf_op jit(solution)/shard_map/pallas_call | solution.py:384
  2.2 0.0 copy-start
  2.2 0.4 shard_map.120
  2.6 0.0 copy-start.2
  2.6 3.0 %collective-permute-start.4 = (bf16[192,256]{1,0:T(8,128)(2,1)S(1)}, bf16[192,256]{1,0:T(8,128)(2,1)S(1)}, u32[]{:S(2)}, u32[]{:S(2)}) collective-permute-start(bf16[192,256]{1,0:T(8,128)(2,1)S(1)} %get-tuple-element.50), channel_id=1, source_target_pairs={{0,2},{1,3},{2,0},{3,1},{4,6},{5,7},{6,4},{7,5},{8,10},{9,11},{10,... | collective-permute-start | bytes 294920 | tf_op jit(solution)/shard_map/ppermute | solution.py:52
  5.6 2.5 %collective-permute-start.2 = (bf16[512,128]{1,0:T(8,128)(2,1)S(1)}, bf16[512,128]{1,0:T(8,128)(2,1)S(1)}, u32[]{:S(2)}, u32[]{:S(2)}) collective-permute-start(bf16[512,128]{1,0:T(8,128)(2,1)S(1)} %get-tuple-element.43), channel_id=1, source_target_pairs={{0,12},{4,8},{8,4},{12,0},{16,28},{20,24},{24,20},{28,16},{1,13},{... | collective-permute-start | bytes 393224 | tf_op jit(solution)/shard_map/ppermute | solution.py:52
  8.1 0.4 collective-permute-start.1
  8.6 0.5 collective-permute-start
  9.1 0.0 collective-permute-done.4.refs_0_
  9.1 0.1 collective-permute-start.5
  9.2 0.0 copy-done.1
  9.2 0.0 copy-done.3
  9.2 0.0 copy-done
  9.3 0.0 copy-done.2
  9.3 0.8 %shard_map.122.gl_ref = f32[96,256]{1,0:T(8,128)S(1)} custom-call(bf16[256,512]{1,0:T(8,128)(2,1)S(1)} %copy-done.2, bf16[256,512]{1,0:T(8,128)(2,1)S(1)} %copy-done.3, bf16[256,1024]{1,0:T(8,128)(2,1)S(1)} %copy-done.1, bf16[256,1024]{1,0:T(8,128)(2,1)S(1)} %copy-done), custom_call_target="tpu_custom_call" | custom-call | flops 201326592 | bytes 196608 | tf_op jit(solution)/shard_map/pallas_call | solution.py:406
  10.0 0.4 collective-permute-done.5.got_ref
  10.4 0.4 shard_map.123
  10.9 1.2 %collective-permute-start.9 = (bf16[96,256]{1,0:T(8,128)(2,1)S(1)}, bf16[96,256]{1,0:T(8,128)(2,1)S(1)}, u32[]{:S(2)}, u32[]{:S(2)}) collective-permute-start(bf16[96,256]{1,0:T(8,128)(2,1)S(1)} %get-tuple-element.66), channel_id=1, source_target_pairs={{0,2},{1,3},{2,0},{3,1},{4,6},{5,7},{6,4},{7,5},{8,10},{9,11},{10,... | collective-permute-start | bytes 147464 | tf_op jit(solution)/shard_map/ppermute | solution.py:52
  12.1 0.8 %collective-permute-done.2.both_ref = bf16[512,128]{1,0:T(8,128)(2,1)S(1)} collective-permute-done((bf16[512,128]{1,0:T(8,128)(2,1)S(1)}, bf16[512,128]{1,0:T(8,128)(2,1)S(1)}, u32[]{:S(2)}, u32[]{:S(2)}) %collective-permute-start.2) | collective-permute-done | bytes 131104 | tf_op jit(solution)/shard_map/ppermute | solution.py:52
  12.9 1.5 %collective-permute-done.1.two_ref = bf16[512,128]{1,0:T(8,128)(2,1)S(1)} collective-permute-done((bf16[512,128]{1,0:T(8,128)(2,1)S(1)}, bf16[512,128]{1,0:T(8,128)(2,1)S(1)}, u32[]{:S(2)}, u32[]{:S(2)}) %collective-permute-start.1) | collective-permute-done | bytes 131104 | tf_op jit(solution)/shard_map/ppermute | solution.py:52
  14.3 0.0 collective-permute-done.one_ref.refs_0_
  14.3 0.8 %shard_map.119 = (bf16[512,128]{1,0:T(8,128)(2,1)S(1)}, f32[512,128]{1,0:T(8,128)}, bf16[512,128]{1,0:T(8,128)(2,1)S(1)}) custom-call(f32[512,128]{1,0:T(8,128)S(1)} %get-tuple-element.44.kv_ref, bf16[512,128]{1,0:T(8,128)(2,1)S(1)} %collective-permute-done.one_ref.refs_0_, bf16[512,128]{1,0:T(8,128)(2,1)S(1)} %collective-permute-done.1.two_ref, ...), custom_call_target="tpu_custom_call" | custom-call | flops 262144 | bytes 1048576 | tf_op jit(solution)/shard_map/pallas_call | solution.py:415
  15.1 4.5 %collective-permute-start.3 = (bf16[512,128]{1,0:T(8,128)(2,1)S(1)}, bf16[512,128]{1,0:T(8,128)(2,1)S(1)}, u32[]{:S(2)}, u32[]{:S(2)}) collective-permute-start(bf16[512,128]{1,0:T(8,128)(2,1)S(1)} %get-tuple-element.46), channel_id=1, source_target_pairs={{0,16},{4,20},{8,24},{12,28},{1,17},{5,21},{9,25},{13,29},{2,18},{... | collective-permute-start | bytes 393224 | tf_op jit(solution)/shard_map/ppermute | solution.py:52
  19.6 0.0 collective-permute-done.9
  19.6 0.1 collective-permute-start.10
  19.7 0.1 fusion.1.place_ref
  19.8 1.3 %collective-permute-start.6 = (bf16[512,128]{1,0:T(8,128)(2,1)S(1)}, bf16[512,128]{1,0:T(8,128)(2,1)S(1)}, u32[]{:S(2)}, u32[]{:S(2)}) collective-permute-start(bf16[512,128]{1,0:T(8,128)(2,1)S(1)} %get-tuple-element.53), channel_id=1, source_target_pairs={{16,0},{20,4},{24,8},{28,12},{17,1},{21,5},{25,9},{29,13},{18,2},{... | collective-permute-start | bytes 393224 | tf_op jit(solution)/shard_map/ppermute | solution.py:52
  21.1 1.0 %collective-permute-done.3.refs_2_ = bf16[512,128]{1,0:T(8,128)(2,1)S(1)} collective-permute-done((bf16[512,128]{1,0:T(8,128)(2,1)S(1)}, bf16[512,128]{1,0:T(8,128)(2,1)S(1)}, u32[]{:S(2)}, u32[]{:S(2)}) %collective-permute-start.3) | collective-permute-done | bytes 131104 | tf_op jit(solution)/shard_map/ppermute | solution.py:52
  22.1 0.7 %shard_map.128.refs_0_ = bf16[32,256]{1,0:T(8,128)(2,1)S(1)} custom-call(s32[1]{0:T(128)} %bitcast.idx_ref, bf16[512,128]{1,0:T(8,128)(2,1)S(1)} %collective-permute-done.one_ref.refs_0_, bf16[512,128]{1,0:T(8,128)(2,1)S(1)} %get-tuple-element.45.refs_1_, bf16[512,128]{1,0:T(8,128)(2,1)S(1)} %collective-permute-done.3.refs_2_, ...), custom_call_target="tpu_custom_call" | custom-call | flops 100663296 | bytes 32768 | tf_op jit(solution)/shard_map/pallas_call | solution.py:424
  22.8 0.1 collective-permute-start.13
  22.9 1.2 %collective-permute-start.12 = (bf16[32,256]{1,0:T(8,128)(2,1)S(1)}, bf16[32,256]{1,0:T(8,128)(2,1)S(1)}, u32[]{:S(2)}, u32[]{:S(2)}) collective-permute-start(bf16[32,256]{1,0:T(8,128)(2,1)S(1)} %shard_map.128.refs_0_), channel_id=1, source_target_pairs={{0,2},{1,3},{2,0},{3,1},{4,6},{5,7},{6,4},{7,5},{8,10},{9,11},{10,... | collective-permute-start | bytes 49160 | tf_op jit(solution)/shard_map/ppermute | solution.py:52
  24.0 0.7 %collective-permute-start.11 = (bf16[32,256]{1,0:T(8,128)(2,1)S(1)}, bf16[32,256]{1,0:T(8,128)(2,1)S(1)}, u32[]{:S(2)}, u32[]{:S(2)}) collective-permute-start(bf16[32,256]{1,0:T(8,128)(2,1)S(1)} %shard_map.128.refs_0_), channel_id=1, source_target_pairs={{0,1},{1,0},{2,3},{3,2},{4,5},{5,4},{6,7},{7,6},{8,9},{9,8},{10,11... | collective-permute-start | bytes 49160 | tf_op jit(solution)/shard_map/ppermute | solution.py:52
  24.7 0.0 collective-permute-done.10
  24.7 1.3 %collective-permute-done.13.refs_3_ = bf16[32,256]{1,0:T(8,128)(2,1)S(1)} collective-permute-done((bf16[32,256]{1,0:T(8,128)(2,1)S(1)}, bf16[32,256]{1,0:T(8,128)(2,1)S(1)}, u32[]{:S(2)}, u32[]{:S(2)}) %collective-permute-start.13) | collective-permute-done | bytes 16416 | tf_op jit(solution)/shard_map/ppermute | solution.py:52
  26.0 0.7 %collective-permute-done.12.refs_2_ = bf16[32,256]{1,0:T(8,128)(2,1)S(1)} collective-permute-done((bf16[32,256]{1,0:T(8,128)(2,1)S(1)}, bf16[32,256]{1,0:T(8,128)(2,1)S(1)}, u32[]{:S(2)}, u32[]{:S(2)}) %collective-permute-start.12) | collective-permute-done | bytes 16416 | tf_op jit(solution)/shard_map/ppermute | solution.py:52
  26.7 0.0 collective-permute-done.11.refs_1_
  26.7 0.5 shard_map.129
  27.2 1.5 %collective-permute-start.14 = (bf16[128,384]{1,0:T(8,128)(2,1)S(1)}, bf16[128,384]{1,0:T(8,128)(2,1)S(1)}, u32[]{:S(2)}, u32[]{:S(2)}) collective-permute-start(bf16[128,384]{1,0:T(8,128)(2,1)S(1)} %get-tuple-element.75), channel_id=1, source_target_pairs={{0,4},{4,0},{8,12},{12,8},{16,20},{20,16},{24,28},{28,24},{1,5},{5... | collective-permute-start | bytes 294920 | tf_op jit(solution)/shard_map/ppermute | solution.py:52
  28.7 4.3 %collective-permute-start.15 = (bf16[128,384]{1,0:T(8,128)(2,1)S(1)}, bf16[128,384]{1,0:T(8,128)(2,1)S(1)}, u32[]{:S(2)}, u32[]{:S(2)}) collective-permute-start(bf16[128,384]{1,0:T(8,128)(2,1)S(1)} %get-tuple-element.76), channel_id=1, source_target_pairs={{0,8},{4,12},{8,0},{12,4},{16,24},{20,28},{24,16},{28,20},{1,9},{5... | collective-permute-start | bytes 294920 | tf_op jit(solution)/shard_map/ppermute | solution.py:52
  33.0 0.0 collective-permute-start.16
  33.0 0.0 collective-permute-done.6.refs_0_.refs_3_
  33.0 0.1 shard_map.124
  33.1 1.6 %collective-permute-start.7 = (bf16[512,128]{1,0:T(8,128)(2,1)S(1)}, bf16[512,128]{1,0:T(8,128)(2,1)S(1)}, u32[]{:S(2)}, u32[]{:S(2)}) collective-permute-start(bf16[512,128]{1,0:T(8,128)(2,1)S(1)} %shard_map.124), channel_id=1, source_target_pairs={{0,8},{4,12},{8,0},{12,4},{16,24},{20,28},{24,16},{28,20},{1,9},{5... | collective-permute-start | bytes 393224 | tf_op jit(solution)/shard_map/ppermute | solution.py:52
  34.7 0.0 collective-permute-done.14.refs_0_
  34.7 2.0 %collective-permute-done.15.refs_1_ = bf16[128,384]{1,0:T(8,128)(2,1)S(1)} collective-permute-done((bf16[128,384]{1,0:T(8,128)(2,1)S(1)}, bf16[128,384]{1,0:T(8,128)(2,1)S(1)}, u32[]{:S(2)}, u32[]{:S(2)}) %collective-permute-start.15) | collective-permute-done | bytes 98336 | tf_op jit(solution)/shard_map/ppermute | solution.py:52
  36.7 2.3 %collective-permute-done.16.refs_2_ = bf16[128,384]{1,0:T(8,128)(2,1)S(1)} collective-permute-done((bf16[128,384]{1,0:T(8,128)(2,1)S(1)}, bf16[128,384]{1,0:T(8,128)(2,1)S(1)}, u32[]{:S(2)}, u32[]{:S(2)}) %collective-permute-start.16) | collective-permute-done | bytes 98336 | tf_op jit(solution)/shard_map/ppermute | solution.py:52
  39.0 0.1 shard_map.131
  39.0 3.4 %collective-permute-start.17 = (bf16[64,384]{1,0:T(8,128)(2,1)S(1)}, bf16[64,384]{1,0:T(8,128)(2,1)S(1)}, u32[]{:S(2)}, u32[]{:S(2)}) collective-permute-start(bf16[64,384]{1,0:T(8,128)(2,1)S(1)} %get-tuple-element.79), channel_id=1, source_target_pairs={{0,16},{4,20},{8,24},{12,28},{16,0},{20,4},{24,8},{28,12},{1,17},{... | collective-permute-start | bytes 147464 | tf_op jit(solution)/shard_map/ppermute | solution.py:52
  42.5 1.4 %shard_map.127 = (f32[512,256]{1,0:T(8,128)S(1)}, f32[256,256]{1,0:T(8,128)S(1)}, f32[256,256]{1,0:T(8,128)S(1)}, f32[256,512]{1,0:T(8,128)S(1)}) custom-call(bf16[256,512]{1,0:T(8,128)(2,1)S(1)} %copy-done.2, bf16[256,512]{1,0:T(8,128)(2,1)S(1)} %copy-done.3, bf16[256,1024]{1,0:T(8,128)(2,1)S(1)} %copy-done.1, bf16[256,1024]{1,0:T(8,128)(2,1)S(1)} %copy-done, ...), custom_call_target="tpu_custom_call" | custom-call | flops 301989888 | bytes 3145728 | tf_op jit(solution)/shard_map/pallas_call | solution.py:459
  43.9 1.4 %shard_map.126 = (f32[512,256]{1,0:T(8,128)S(1)}, f32[256,256]{1,0:T(8,128)S(1)}, f32[256,256]{1,0:T(8,128)S(1)}, f32[256,512]{1,0:T(8,128)S(1)}) custom-call(bf16[256,512]{1,0:T(8,128)(2,1)S(1)} %copy-done.2, bf16[256,512]{1,0:T(8,128)(2,1)S(1)} %copy-done.3, bf16[256,1024]{1,0:T(8,128)(2,1)S(1)} %copy-done.1, bf16[256,1024]{1,0:T(8,128)(2,1)S(1)} %copy-done, ...), custom_call_target="tpu_custom_call" | custom-call | flops 301989888 | bytes 3145728 | tf_op jit(solution)/shard_map/pallas_call | solution.py:459
  45.3 0.0 collective-permute-done.7.refs_1_.refs_4_
  45.3 0.1 shard_map.125
  45.4 0.0 copy-start.4
  45.4 1.4 %collective-permute-start.8 = (bf16[512,128]{1,0:T(8,128)(2,1)S(1)}, bf16[512,128]{1,0:T(8,128)(2,1)S(1)}, u32[]{:S(2)}, u32[]{:S(2)}) collective-permute-start(bf16[512,128]{1,0:T(8,128)(2,1)S(1)} %shard_map.125), channel_id=1, source_target_pairs={{0,4},{4,0},{8,12},{12,8},{16,20},{20,16},{24,28},{28,24},{1,5},{5... | collective-permute-start | bytes 393224 | tf_op jit(solution)/shard_map/ppermute | solution.py:52
  46.8 0.0 collective-permute-done.17
  46.8 0.7 %convert_add_fusion = f32[64,384]{1,0:T(8,128)} fusion(f32[64,384]{1,0:T(8,128)S(1)} %get-tuple-element.78, bf16[64,384]{1,0:T(8,128)(2,1)S(1)} %collective-permute-done.17), kind=kLoop, calls=%fused_computation.5 | loop fusion | flops 49152 | bytes 245760 | tf_op jit(solution)/shard_map/add | solution.py:454
  47.4 3.0 %collective-permute-done.8.refs_5_ = bf16[512,128]{1,0:T(8,128)(2,1)S(1)} collective-permute-done((bf16[512,128]{1,0:T(8,128)(2,1)S(1)}, bf16[512,128]{1,0:T(8,128)(2,1)S(1)}, u32[]{:S(2)}, u32[]{:S(2)}) %collective-permute-start.8) | collective-permute-done | bytes 131104 | tf_op jit(solution)/shard_map/ppermute | solution.py:52
  50.4 0.0 copy-done.4
  50.4 2.7 %shard_map.130 = (bf16[256,1024]{1,0:T(8,128)(2,1)}, bf16[256,512]{1,0:T(8,128)(2,1)}, bf16[256,512]{1,0:T(8,128)(2,1)}, bf16[256,512]{1,0:T(8,128)(2,1)}, bf16[256,1024]{1,0:T(8,128)(2,1)}) custom-call(s32[1]{0:T(128)} %bitcast.idx_ref, bf16[512,128]{1,0:T(8,128)(2,1)S(1)} %collective-permute-done.one_ref.refs_0_, ...), custom_call_target="tpu_custom_call" | custom-call | flops 402653184 | bytes 3670016 | tf_op jit(solution)/shard_map/pallas_call | solution.py:466
  (5 shorter events, 0.1 us)
Async XLA Ops:
  0.6 8.6 %copy-start.1 = (bf16[256,1024]{1,0:T(8,128)(2,1)S(1)}, bf16[256,1024]{1,0:T(8,128)(2,1)}, u32[]{:S(2)}) copy-start(bf16[256,1024]{1,0:T(8,128)(2,1)} %refs_11_.1) | copy-start | bytes 1572868
  0.6 8.6 %copy-start.3 = (bf16[256,512]{1,0:T(8,128)(2,1)S(1)}, bf16[256,512]{1,0:T(8,128)(2,1)}, u32[]{:S(2)}) copy-start(bf16[256,512]{1,0:T(8,128)(2,1)} %q_ref.7) | copy-start | bytes 786436
  2.2 7.1 %copy-start = (bf16[256,1024]{1,0:T(8,128)(2,1)S(1)}, bf16[256,1024]{1,0:T(8,128)(2,1)}, u32[]{:S(2)}) copy-start(bf16[256,1024]{1,0:T(8,128)(2,1)} %refs_8_.1) | copy-start | bytes 1572868
  2.6 6.7 %copy-start.2 = (bf16[256,512]{1,0:T(8,128)(2,1)S(1)}, bf16[256,512]{1,0:T(8,128)(2,1)}, u32[]{:S(2)}) copy-start(bf16[256,512]{1,0:T(8,128)(2,1)} %refs_10_.1) | copy-start | bytes 786436
  2.6 6.5 %collective-permute-start.4 = (bf16[192,256]{1,0:T(8,128)(2,1)S(1)}, bf16[192,256]{1,0:T(8,128)(2,1)S(1)}, u32[]{:S(2)}, u32[]{:S(2)}) collective-permute-start(bf16[192,256]{1,0:T(8,128)(2,1)S(1)} %get-tuple-element.50), channel_id=1, source_target_pairs={{0,2},{1,3},{2,0},{3,1},{4,6},{5,7},{6,4},{7,5},{8,10},{9,11},{10,... | collective-permute-start | bytes 294920 | tf_op jit(solution)/shard_map/ppermute | solution.py:52
  5.6 7.3 %collective-permute-start.2 = (bf16[512,128]{1,0:T(8,128)(2,1)S(1)}, bf16[512,128]{1,0:T(8,128)(2,1)S(1)}, u32[]{:S(2)}, u32[]{:S(2)}) collective-permute-start(bf16[512,128]{1,0:T(8,128)(2,1)S(1)} %get-tuple-element.43), channel_id=1, source_target_pairs={{0,12},{4,8},{8,4},{12,0},{16,28},{20,24},{24,20},{28,16},{1,13},{... | collective-permute-start | bytes 393224 | tf_op jit(solution)/shard_map/ppermute | solution.py:52
  8.1 6.2 %collective-permute-start.1 = (bf16[512,128]{1,0:T(8,128)(2,1)S(1)}, bf16[512,128]{1,0:T(8,128)(2,1)S(1)}, u32[]{:S(2)}, u32[]{:S(2)}) collective-permute-start(bf16[512,128]{1,0:T(8,128)(2,1)S(1)} %get-tuple-element.43), channel_id=1, source_target_pairs={{0,8},{4,12},{8,0},{12,4},{16,24},{20,28},{24,16},{28,20},{1,9},{5... | collective-permute-start | bytes 393224 | tf_op jit(solution)/shard_map/ppermute | solution.py:52
  8.6 5.7 %collective-permute-start = (bf16[512,128]{1,0:T(8,128)(2,1)S(1)}, bf16[512,128]{1,0:T(8,128)(2,1)S(1)}, u32[]{:S(2)}, u32[]{:S(2)}) collective-permute-start(bf16[512,128]{1,0:T(8,128)(2,1)S(1)} %get-tuple-element.43), channel_id=1, source_target_pairs={{0,4},{4,0},{8,12},{12,8},{16,20},{20,16},{24,28},{28,24},{1,5},{5... | collective-permute-start | bytes 393224 | tf_op jit(solution)/shard_map/ppermute | solution.py:52
  9.1 1.3 %collective-permute-start.5 = (bf16[96,256]{1,0:T(8,128)(2,1)S(1)}, bf16[96,256]{1,0:T(8,128)(2,1)S(1)}, u32[]{:S(2)}, u32[]{:S(2)}) collective-permute-start(bf16[96,256]{1,0:T(8,128)(2,1)S(1)} %get-tuple-element.52), channel_id=1, source_target_pairs={{0,1},{1,0},{2,3},{3,2},{4,5},{5,4},{6,7},{7,6},{8,9},{9,8},{10,11... | collective-permute-start | bytes 147464 | tf_op jit(solution)/shard_map/ppermute | solution.py:52
  10.9 8.7 %collective-permute-start.9 = (bf16[96,256]{1,0:T(8,128)(2,1)S(1)}, bf16[96,256]{1,0:T(8,128)(2,1)S(1)}, u32[]{:S(2)}, u32[]{:S(2)}) collective-permute-start(bf16[96,256]{1,0:T(8,128)(2,1)S(1)} %get-tuple-element.66), channel_id=1, source_target_pairs={{0,2},{1,3},{2,0},{3,1},{4,6},{5,7},{6,4},{7,5},{8,10},{9,11},{10,... | collective-permute-start | bytes 147464 | tf_op jit(solution)/shard_map/ppermute | solution.py:52
  15.1 7.0 %collective-permute-start.3 = (bf16[512,128]{1,0:T(8,128)(2,1)S(1)}, bf16[512,128]{1,0:T(8,128)(2,1)S(1)}, u32[]{:S(2)}, u32[]{:S(2)}) collective-permute-start(bf16[512,128]{1,0:T(8,128)(2,1)S(1)} %get-tuple-element.46), channel_id=1, source_target_pairs={{0,16},{4,20},{8,24},{12,28},{1,17},{5,21},{9,25},{13,29},{2,18},{... | collective-permute-start | bytes 393224 | tf_op jit(solution)/shard_map/ppermute | solution.py:52
  19.6 5.1 %collective-permute-start.10 = (bf16[192,256]{1,0:T(8,128)(2,1)S(1)}, bf16[192,256]{1,0:T(8,128)(2,1)S(1)}, u32[]{:S(2)}, u32[]{:S(2)}) collective-permute-start(bf16[192,256]{1,0:T(8,128)(2,1)S(1)} %pad_maximum_fusion.1), channel_id=1, source_target_pairs={{0,1},{1,0},{2,3},{3,2},{4,5},{5,4},{6,7},{7,6},{8,9},{9,8},{10,11... | collective-permute-start | bytes 294920 | tf_op jit(solution)/shard_map/ppermute | solution.py:52
  19.8 13.2 %collective-permute-start.6 = (bf16[512,128]{1,0:T(8,128)(2,1)S(1)}, bf16[512,128]{1,0:T(8,128)(2,1)S(1)}, u32[]{:S(2)}, u32[]{:S(2)}) collective-permute-start(bf16[512,128]{1,0:T(8,128)(2,1)S(1)} %get-tuple-element.53), channel_id=1, source_target_pairs={{16,0},{20,4},{24,8},{28,12},{17,1},{21,5},{25,9},{29,13},{18,2},{... | collective-permute-start | bytes 393224 | tf_op jit(solution)/shard_map/ppermute | solution.py:52
  22.8 3.2 %collective-permute-start.13 = (bf16[32,256]{1,0:T(8,128)(2,1)S(1)}, bf16[32,256]{1,0:T(8,128)(2,1)S(1)}, u32[]{:S(2)}, u32[]{:S(2)}) collective-permute-start(bf16[32,256]{1,0:T(8,128)(2,1)S(1)} %shard_map.128.refs_0_), channel_id=1, source_target_pairs={{0,3},{1,2},{2,1},{3,0},{4,7},{5,6},{6,5},{7,4},{8,11},{9,10},{10,... | collective-permute-start | bytes 49160 | tf_op jit(solution)/shard_map/ppermute | solution.py:52
  22.9 3.8 %collective-permute-start.12 = (bf16[32,256]{1,0:T(8,128)(2,1)S(1)}, bf16[32,256]{1,0:T(8,128)(2,1)S(1)}, u32[]{:S(2)}, u32[]{:S(2)}) collective-permute-start(bf16[32,256]{1,0:T(8,128)(2,1)S(1)} %shard_map.128.refs_0_), channel_id=1, source_target_pairs={{0,2},{1,3},{2,0},{3,1},{4,6},{5,7},{6,4},{7,5},{8,10},{9,11},{10,... | collective-permute-start | bytes 49160 | tf_op jit(solution)/shard_map/ppermute | solution.py:52
  24.0 2.7 %collective-permute-start.11 = (bf16[32,256]{1,0:T(8,128)(2,1)S(1)}, bf16[32,256]{1,0:T(8,128)(2,1)S(1)}, u32[]{:S(2)}, u32[]{:S(2)}) collective-permute-start(bf16[32,256]{1,0:T(8,128)(2,1)S(1)} %shard_map.128.refs_0_), channel_id=1, source_target_pairs={{0,1},{1,0},{2,3},{3,2},{4,5},{5,4},{6,7},{7,6},{8,9},{9,8},{10,11... | collective-permute-start | bytes 49160 | tf_op jit(solution)/shard_map/ppermute | solution.py:52
  27.2 7.5 %collective-permute-start.14 = (bf16[128,384]{1,0:T(8,128)(2,1)S(1)}, bf16[128,384]{1,0:T(8,128)(2,1)S(1)}, u32[]{:S(2)}, u32[]{:S(2)}) collective-permute-start(bf16[128,384]{1,0:T(8,128)(2,1)S(1)} %get-tuple-element.75), channel_id=1, source_target_pairs={{0,4},{4,0},{8,12},{12,8},{16,20},{20,16},{24,28},{28,24},{1,5},{5... | collective-permute-start | bytes 294920 | tf_op jit(solution)/shard_map/ppermute | solution.py:52
  28.7 8.0 %collective-permute-start.15 = (bf16[128,384]{1,0:T(8,128)(2,1)S(1)}, bf16[128,384]{1,0:T(8,128)(2,1)S(1)}, u32[]{:S(2)}, u32[]{:S(2)}) collective-permute-start(bf16[128,384]{1,0:T(8,128)(2,1)S(1)} %get-tuple-element.76), channel_id=1, source_target_pairs={{0,8},{4,12},{8,0},{12,4},{16,24},{20,28},{24,16},{28,20},{1,9},{5... | collective-permute-start | bytes 294920 | tf_op jit(solution)/shard_map/ppermute | solution.py:52
  33.0 5.9 %collective-permute-start.16 = (bf16[128,384]{1,0:T(8,128)(2,1)S(1)}, bf16[128,384]{1,0:T(8,128)(2,1)S(1)}, u32[]{:S(2)}, u32[]{:S(2)}) collective-permute-start(bf16[128,384]{1,0:T(8,128)(2,1)S(1)} %get-tuple-element.77), channel_id=1, source_target_pairs={{0,12},{4,8},{8,4},{12,0},{16,28},{20,24},{24,20},{28,16},{1,13},{... | collective-permute-start | bytes 294920 | tf_op jit(solution)/shard_map/ppermute | solution.py:52
  33.1 12.2 %collective-permute-start.7 = (bf16[512,128]{1,0:T(8,128)(2,1)S(1)}, bf16[512,128]{1,0:T(8,128)(2,1)S(1)}, u32[]{:S(2)}, u32[]{:S(2)}) collective-permute-start(bf16[512,128]{1,0:T(8,128)(2,1)S(1)} %shard_map.124), channel_id=1, source_target_pairs={{0,8},{4,12},{8,0},{12,4},{16,24},{20,28},{24,16},{28,20},{1,9},{5... | collective-permute-start | bytes 393224 | tf_op jit(solution)/shard_map/ppermute | solution.py:52
  39.0 7.7 %collective-permute-start.17 = (bf16[64,384]{1,0:T(8,128)(2,1)S(1)}, bf16[64,384]{1,0:T(8,128)(2,1)S(1)}, u32[]{:S(2)}, u32[]{:S(2)}) collective-permute-start(bf16[64,384]{1,0:T(8,128)(2,1)S(1)} %get-tuple-element.79), channel_id=1, source_target_pairs={{0,16},{4,20},{8,24},{12,28},{16,0},{20,4},{24,8},{28,12},{1,17},{... | collective-permute-start | bytes 147464 | tf_op jit(solution)/shard_map/ppermute | solution.py:52
  45.4 5.0 %copy-start.4 = (f32[8,64,128]{2,1,0:T(8,128)S(1)}, f32[8,64,128]{2,1,0:T(8,128)}, u32[]{:S(2)}) copy-start(f32[8,64,128]{2,1,0:T(8,128)} %param.13) | copy-start | bytes 786436
  45.4 5.0 %collective-permute-start.8 = (bf16[512,128]{1,0:T(8,128)(2,1)S(1)}, bf16[512,128]{1,0:T(8,128)(2,1)S(1)}, u32[]{:S(2)}, u32[]{:S(2)}) collective-permute-start(bf16[512,128]{1,0:T(8,128)(2,1)S(1)} %shard_map.125), channel_id=1, source_target_pairs={{0,4},{4,0},{8,12},{12,8},{16,20},{20,16},{24,28},{28,24},{1,5},{5... | collective-permute-start | bytes 393224 | tf_op jit(solution)/shard_map/ppermute | solution.py:52

commit v13 on v10

--- a/solution.py
+++ b/solution.py
@@ -223,19 +223,21 @@
         dk_ref[:, n * 2 * dk:(n + 1) * 2 * dk] = dk_sum
 
 
-def carry_kernel(dims, levels, first, count, idx_ref, *refs):
+def carry_kernel(dims, levels, first, some, idx_ref, *refs):
     nh, dk, dv = dims
+    count = len(some)
     ups = refs[:count]
-    g_ref, qt_ref, sig_ref, far_ref = refs[count:]
+    g_ref, qt_ref, sig_ref = refs[count:count + 3]
+    far_ref = refs[-1]
+    far_ref[...] = refs[count + 3][...] if len(refs) > count + 4 else jnp.zeros_like(far_ref)
     index = idx_ref[0]
-    far_ref[...] = jnp.zeros_like(far_ref)
-    for m in range(count):
+    for m, up_ref in zip(some, ups):
         up = ((index >> m) & 1).astype(F32)
         found = []
         for h in range(nh):
             rows = slice(h * dk, (h + 1) * dk)
             r = h * levels + first + m
-            x = nt(ups[m][rows, :], g_ref[:, h * dv:(h + 1) * dv])
+            x = nt(up_ref[rows, :], g_ref[:, h * dv:(h + 1) * dv])
             row = jnp.sum(x * qt_ref[rows, :].astype(F32), axis=0, keepdims=True)
             found.append(row * (sig_ref[r:r + 1, :] * up))
         far_ref[m * nh:(m + 1) * nh, :] = jnp.concatenate(found, axis=0).astype(BF16)
@@ -307,18 +309,24 @@
     send_ref[...] = (total + jnp.where(((index >> bit) & 1) == 1, gu_ref[bit].astype(F32), 0.0)).astype(BF16)
 
 
-def final_kernel(dims, levels, first, count, idx_ref, *refs):
+def final_kernel(dims, levels, first, count, cuts, idx_ref, *refs):
     nh, dk, dv = dims
     top = count - 1
     ups, gots = refs[:count], refs[count:2 * count]
-    (qt_ref, lw_ref, g_ref, ds_ref, k_ref, v_ref, low_o, low_q, low_k, low_v, high_o, high_q, high_k, high_v,
-     near_ref, far_ref, place_ref, w_ref, out_hbm, dq_hbm, dx_hbm, dk_hbm, dv_hbm,
-     out_ref, dq_ref, dx_ref, dk_ref, dv_ref, sems) = refs[2 * count:]
+    qt_ref, lw_ref, g_ref, ds_ref, k_ref, v_ref = refs[2 * count:2 * count + 6]
+    at = 2 * count + 6 + 4 * (len(cuts) - 1)
+    local = refs[2 * count + 6:at]
+    (near_ref, far_ref, place_ref, w_ref, out_hbm, dq_hbm, dx_hbm, dk_hbm, dv_hbm,
+     out_ref, dq_ref, dx_ref, dk_ref, dv_ref, sems) = refs[at:]
     index = idx_ref[0]
     copies = []
 
     def send(buf_ref, hbm_ref, cols):
         copies.append(leave(buf_ref, hbm_ref, sems.at[len(copies)], cols))
+
+    def piece(kind, pair):
+        part = sum(pair >= cut for cut in cuts) - 1
+        return local[4 * part + kind], pair - cuts[part]
 
     def weights(h, m):
         r = h * levels + first + m
@@ -326,7 +334,8 @@
 
     for h in range(nh):
         rows = slice(h * dk, (h + 1) * dk)
-        local_ref, n = (low_o, h) if h < nh // 2 else (high_o, h - nh // 2)
+        local_ref, n = piece(0, h // 2)
+        n = 2 * n + h % 2
         total = local_ref[n * dv:(n + 1) * dv, :]
         for m in range(count):
             total = total + tn(ups[m][rows, :], qt_ref[rows, :]) * weights(h, m)
@@ -337,7 +346,8 @@
         halves = []
         for j in range(2):
             h = 2 * pair + j
-            local_ref, n = (low_q, h) if h < nh // 2 else (high_q, h - nh // 2)
+            local_ref, n = piece(1, pair)
+            n = 2 * n + j
             total = local_ref[n * dk:(n + 1) * dk, :]
             for m in range(count):
                 total = total + nt(ups[m][h * dk:(h + 1) * dk, :], g_ref[:, h * dv:(h + 1) * dv]) * weights(h, m)
@@ -358,7 +368,8 @@
             total = total + got[pair_rows, :].astype(F32)
         adj = [total[:dk].astype(BF16), total[dk:].astype(BF16)]
         kp = k_ref[:, pair * 2 * dk:(pair + 1) * 2 * dk]
-        dkl_ref, dvl_ref, p = (low_k, low_v, pair) if pair < nh // 4 else (high_k, high_v, pair - nh // 4)
+        dkl_ref, p = piece(2, pair)
+        dvl_ref, p = piece(3, pair)
         total = dkl_ref[:, p * 2 * dk:(p + 1) * 2 * dk]
         for j in range(2):
             h = 2 * pair + j
@@ -443,9 +454,13 @@
               rows * dv)(idx, kv, *ups, gu)[0]
     partner = swap(up, "seq", top)
     ups.append(partner)
-    far_rows = call(
-        functools.partial(carry_kernel, dims, levels, first, seq_bits), [S((far_own, tokens), BF16)],
-        [SM] + [VM] * (seq_bits + 3), 2 * tokens * rows * dv * seq_bits)(idx, *ups, d_out, qt, sig)[0]
+    far_rows = []
+    for some in (tuple(range(top)), (top,)):
+        far_rows = call(
+            functools.partial(carry_kernel, dims, levels, first, some), [S((far_own, tokens), BF16)],
+            [SM] + [VM] * (len(some) + 3 + len(far_rows)), 2 * tokens * rows * dv * len(some))(
+                idx, *[ups[m] for m in some], d_out, qt, sig, *far_rows)
+    far_rows = far_rows[0]
     gots = [partner]
     for bit in reversed(range(top)):
         down = call(functools.partial(pend_kernel, bit, top), [S((rows, dv), BF16)], [SM] + [VM] * (len(gots) + 1),
@@ -491,21 +506,23 @@
         got = swap(send, "seq", bit)
     d_w = keep + got.astype(F32)
 
-    half = nh // 4
     local = []
-    for part in range(2):
-        local.append(call(
-            functools.partial(local_kernel, dims, levels, tuple(range(part * half, (part + 1) * half))),
-            [S((nh * dv // 2, tokens), F32), S((rows // 2, tokens), F32), S((tokens, rows // 2), F32),
-             S((tokens, nh * dv // 2), F32)],
-            [VM] * 5, tokens * tokens * nh * (3 * dk + 3 * dv),
-        )(keys, queries, values, d_out, lw))
+    cuts = (0, nh // 8, nh // 4, nh // 2)
+    for part in range(3):
+        pairs = tuple(range(cuts[part], cuts[part + 1]))
+        heads = 2 * len(pairs)
+        local += call(
+            functools.partial(local_kernel, dims, levels, pairs),
+            [S((heads * dv, tokens), F32), S((heads * dk, tokens), F32), S((tokens, heads * dk), F32),
+             S((tokens, heads * dv), F32)],
+            [VM] * 5, 2 * tokens * tokens * heads * (3 * dk + 3 * dv),
+        )(keys, queries, values, d_out, lw)
     shapes = [(tokens, nh * dv), (tokens, rows), (tokens, width), (tokens, rows), (tokens, nh * dv)]
     out, d_queries, d_hidden, d_keys, d_values = call(
-        functools.partial(final_kernel, dims, levels, first, seq_bits), [S(shape, BF16) for shape in shapes],
-        [SM] + [VM] * (2 * seq_bits + 18), 8 * tokens * rows * dv * seq_bits, out_specs=[hbm] * len(shapes),
+        functools.partial(final_kernel, dims, levels, first, seq_bits, cuts), [S(shape, BF16) for shape in shapes],
+        [SM] + [VM] * (2 * seq_bits + 10 + len(local)), 8 * tokens * rows * dv * seq_bits, out_specs=[hbm] * len(shapes),
         scratch_shapes=[pltpu.VMEM(shape, BF16) for shape in shapes] + [pltpu.SemaphoreType.DMA((2 * nh + 1,))])(
-            idx, *ups, *gots, qt, lw, d_out, d_state.reshape(rows, dv), keys, values, *local[0], *local[1],
+            idx, *ups, *gots, qt, lw, d_out, d_state.reshape(rows, dv), keys, values, *local,
             near_all, far_all, place, w_near)
     return (out, d_queries, d_keys, d_values, d_hidden, d_w)
 

time: 52.4 us -> 52.3 us (level)
    pallas_call x4 -> x6, Pallas kernels: 6.36 us -> 6.68 us  [the longest x3 2.98 us: body(): call(functools.partial(local_kernel, dims, levels, pairs), [S((heads * dv...]
  transfers between devices with their start and end apart: 18 -> 18, of which waited for: 11 -> 11; matrix products, arithmetic and copies ran while one was open for 2% -> 2% of each run, Pallas kernels for 11% -> 12%
where the time goes in v13:
time: 52.3 us; the launch traced here: 52.1 us
  starting transfers between devices  23.1 us (44%)
  waiting for transfers between devices  16.3 us (31%)
  Pallas kernels  10.9 us (21%)
  between operations  0.89 us (2%)
  other arithmetic  0.82 us (2%)
    ppermute x18, starting transfers between devices, exchange(): return lax.ppermute(value, axis, pairs)  23.1 us
    ppermute x18, waiting for transfers between devices, exchange(): return lax.ppermute(value, axis, pairs)  16.3 us
    pallas_call x3, Pallas kernels, body(): call(functools.partial(local_kernel, dims, levels, pairs), [S((heads * dv...  2.98 us
    pallas_call x1, Pallas kernels, body(): call(functools.partial(final_kernel, dims, levels, first, seq_bits, cuts)...  2.9 us
    pallas_call x1, Pallas kernels, body(): call(functools.partial(state_kernel, dims), [S((rows, dv), F32), S((rows,...  1.5 us
  transfers between devices with their start and end apart: 18, of which 11 were waited for; matrix products, arithmetic and copies ran while one was open for 2% of the time, Pallas kernels for 12%

profile of v13, /device:TPU:0, one launch (start us, length us, event | category | flops | bytes accessed | tf_op | source)
XLA Modules:
  0.0 52.1 jit_solution(9959789110411063014)
XLA Ops:
  0.6 0.0 copy-start.1
  0.6 0.0 copy-start.3
  0.7 1.5 %shard_map.118 = (f32[512,128]{1,0:T(8,128)S(1)}, bf16[512,128]{1,0:T(8,128)(2,1)S(1)}, bf16[512,384]{1,0:T(8,128)(2,1)S(1)}, bf16[256,512]{1,0:T(8,128)(2,1)S(1)}) custom-call(s32[1]{0:T(128)} %bitcast.idx_ref, s32[1]{0:T(128)} %bitcast.1.head_ref.idx_ref, bf16[256,512]{1,0:T(8,128)(2,1)} %refs_10_.1, bf16[256,1024]{1,0:T(8,128)(2,1)} %refs_11_.1, ...), custom_call_target="tpu_custom_call" | custom-call | flops 33554432 | bytes 2097152 | tf_op jit(solution)/shard_map/pallas_call | solution.py:415
  2.2 0.0 copy-start
  2.2 0.4 shard_map.119
  2.6 0.0 copy-start.2
  2.6 3.0 %collective-permute-start.2 = (bf16[192,256]{1,0:T(8,128)(2,1)S(1)}, bf16[192,256]{1,0:T(8,128)(2,1)S(1)}, u32[]{:S(2)}, u32[]{:S(2)}) collective-permute-start(bf16[192,256]{1,0:T(8,128)(2,1)S(1)} %get-tuple-element.54), channel_id=1, source_target_pairs={{0,2},{1,3},{2,0},{3,1},{4,6},{5,7},{6,4},{7,5},{8,10},{9,11},{10,... | collective-permute-start | bytes 294920 | tf_op jit(solution)/shard_map/ppermute | solution.py:51
  5.6 1.5 %collective-permute-start = (bf16[512,128]{1,0:T(8,128)(2,1)S(1)}, bf16[512,128]{1,0:T(8,128)(2,1)S(1)}, u32[]{:S(2)}, u32[]{:S(2)}) collective-permute-start(bf16[512,128]{1,0:T(8,128)(2,1)S(1)} %get-tuple-element.49), channel_id=1, source_target_pairs={{0,4},{4,0},{8,12},{12,8},{16,20},{20,16},{24,28},{28,24},{1,5},{5... | collective-permute-start | bytes 393224 | tf_op jit(solution)/shard_map/ppermute | solution.py:51
  7.1 1.3 %collective-permute-done.2.got_ref = bf16[192,256]{1,0:T(8,128)(2,1)S(1)} collective-permute-done((bf16[192,256]{1,0:T(8,128)(2,1)S(1)}, bf16[192,256]{1,0:T(8,128)(2,1)S(1)}, u32[]{:S(2)}, u32[]{:S(2)}) %collective-permute-start.2) | collective-permute-done | bytes 98336 | tf_op jit(solution)/shard_map/ppermute | solution.py:51
  8.4 0.1 collective-permute-start.3
  8.5 0.0 copy-done.1
  8.5 0.0 copy-done.3
  8.5 0.0 copy-done
  8.5 0.0 copy-done.2
  8.6 0.8 %shard_map.121.gl_ref = f32[96,256]{1,0:T(8,128)S(1)} custom-call(bf16[256,512]{1,0:T(8,128)(2,1)S(1)} %copy-done.2, bf16[256,512]{1,0:T(8,128)(2,1)S(1)} %copy-done.3, bf16[256,1024]{1,0:T(8,128)(2,1)S(1)} %copy-done.1, bf16[256,1024]{1,0:T(8,128)(2,1)S(1)} %copy-done), custom_call_target="tpu_custom_call" | custom-call | flops 201326592 | bytes 196608 | tf_op jit(solution)/shard_map/pallas_call | solution.py:444
  9.3 0.4 collective-permute-done.3.got_ref
  9.7 0.4 shard_map.122
  10.2 1.9 %collective-permute-start.7 = (bf16[96,256]{1,0:T(8,128)(2,1)S(1)}, bf16[96,256]{1,0:T(8,128)(2,1)S(1)}, u32[]{:S(2)}, u32[]{:S(2)}) collective-permute-start(bf16[96,256]{1,0:T(8,128)(2,1)S(1)} %get-tuple-element.73), channel_id=1, source_target_pairs={{0,2},{1,3},{2,0},{3,1},{4,6},{5,7},{6,4},{7,5},{8,10},{9,11},{10,... | collective-permute-start | bytes 147464 | tf_op jit(solution)/shard_map/ppermute | solution.py:51
  12.1 0.0 collective-permute-done.refs_0_
  12.1 1.6 %collective-permute-start.1 = (bf16[512,128]{1,0:T(8,128)(2,1)S(1)}, bf16[512,128]{1,0:T(8,128)(2,1)S(1)}, u32[]{:S(2)}, u32[]{:S(2)}) collective-permute-start(bf16[512,128]{1,0:T(8,128)(2,1)S(1)} %add_convert_fusion), channel_id=1, source_target_pairs={{0,8},{4,12},{8,0},{12,4},{16,24},{20,28},{24,16},{28,20},{1,9},{5... | collective-permute-start | bytes 393224 | tf_op jit(solution)/shard_map/ppermute | solution.py:51
  13.7 0.6 %collective-permute-done.7 = bf16[96,256]{1,0:T(8,128)(2,1)S(1)} collective-permute-done((bf16[96,256]{1,0:T(8,128)(2,1)S(1)}, bf16[96,256]{1,0:T(8,128)(2,1)S(1)}, u32[]{:S(2)}, u32[]{:S(2)}) %collective-permute-start.7) | collective-permute-done | bytes 49184 | tf_op jit(solution)/shard_map/ppermute | solution.py:51
  14.3 0.1 collective-permute-start.8
  14.4 3.0 %collective-permute-done.1.refs_1_ = bf16[512,128]{1,0:T(8,128)(2,1)S(1)} collective-permute-done((bf16[512,128]{1,0:T(8,128)(2,1)S(1)}, bf16[512,128]{1,0:T(8,128)(2,1)S(1)}, u32[]{:S(2)}, u32[]{:S(2)}) %collective-permute-start.1) | collective-permute-done | bytes 131104 | tf_op jit(solution)/shard_map/ppermute | solution.py:51
  17.4 0.1 shard_map.123
  17.5 2.6 %collective-permute-start.4 = (bf16[512,128]{1,0:T(8,128)(2,1)S(1)}, bf16[512,128]{1,0:T(8,128)(2,1)S(1)}, u32[]{:S(2)}, u32[]{:S(2)}) collective-permute-start(bf16[512,128]{1,0:T(8,128)(2,1)S(1)} %shard_map.123), channel_id=1, source_target_pairs={{0,16},{4,20},{8,24},{12,28},{16,0},{20,4},{24,8},{28,12},{1,17},{... | collective-permute-start | bytes 393224 | tf_op jit(solution)/shard_map/ppermute | solution.py:51
  20.1 0.0 collective-permute-done.8
  20.1 0.3 shard_map.129
  20.5 1.6 %collective-permute-start.12 = (bf16[256,384]{1,0:T(8,128)(2,1)S(1)}, bf16[256,384]{1,0:T(8,128)(2,1)S(1)}, u32[]{:S(2)}, u32[]{:S(2)}) collective-permute-start(bf16[256,384]{1,0:T(8,128)(2,1)S(1)} %get-tuple-element.83), channel_id=1, source_target_pairs={{0,4},{4,0},{8,12},{12,8},{16,20},{20,16},{24,28},{28,24},{1,5},{5... | collective-permute-start | bytes 589832 | tf_op jit(solution)/shard_map/ppermute | solution.py:51
  22.1 0.5 shard_map.130.refs_4_
  22.6 3.1 %collective-permute-done.4.refs_0_.refs_2_.refs_3_ = bf16[512,128]{1,0:T(8,128)(2,1)S(1)} collective-permute-done((bf16[512,128]{1,0:T(8,128)(2,1)S(1)}, bf16[512,128]{1,0:T(8,128)(2,1)S(1)}, u32[]{:S(2)}, u32[]{:S(2)}) %collective-permute-start.4) | collective-permute-done | bytes 131104 | tf_op jit(solution)/shard_map/ppermute | solution.py:51
  25.7 0.3 shard_map.131.refs_0_
  26.0 0.1 collective-permute-start.11
  26.1 0.6 %collective-permute-start.10 = (bf16[32,256]{1,0:T(8,128)(2,1)S(1)}, bf16[32,256]{1,0:T(8,128)(2,1)S(1)}, u32[]{:S(2)}, u32[]{:S(2)}) collective-permute-start(bf16[32,256]{1,0:T(8,128)(2,1)S(1)} %shard_map.131.refs_0_), channel_id=1, source_target_pairs={{0,2},{1,3},{2,0},{3,1},{4,6},{5,7},{6,4},{7,5},{8,10},{9,11},{10,... | collective-permute-start | bytes 49160 | tf_op jit(solution)/shard_map/ppermute | solution.py:51
  26.7 1.2 %collective-permute-start.9 = (bf16[32,256]{1,0:T(8,128)(2,1)S(1)}, bf16[32,256]{1,0:T(8,128)(2,1)S(1)}, u32[]{:S(2)}, u32[]{:S(2)}) collective-permute-start(bf16[32,256]{1,0:T(8,128)(2,1)S(1)} %shard_map.131.refs_0_), channel_id=1, source_target_pairs={{0,1},{1,0},{2,3},{3,2},{4,5},{5,4},{6,7},{7,6},{8,9},{9,8},{10,11... | collective-permute-start | bytes 49160 | tf_op jit(solution)/shard_map/ppermute | solution.py:51
  28.0 0.1 shard_map.124
  28.0 0.7 %collective-permute-start.5 = (bf16[512,128]{1,0:T(8,128)(2,1)S(1)}, bf16[512,128]{1,0:T(8,128)(2,1)S(1)}, u32[]{:S(2)}, u32[]{:S(2)}) collective-permute-start(bf16[512,128]{1,0:T(8,128)(2,1)S(1)} %shard_map.124), channel_id=1, source_target_pairs={{0,8},{4,12},{8,0},{12,4},{16,24},{20,28},{24,16},{28,20},{1,9},{5... | collective-permute-start | bytes 393224 | tf_op jit(solution)/shard_map/ppermute | solution.py:51
  28.7 0.5 %collective-permute-done.11.refs_3_ = bf16[32,256]{1,0:T(8,128)(2,1)S(1)} collective-permute-done((bf16[32,256]{1,0:T(8,128)(2,1)S(1)}, bf16[32,256]{1,0:T(8,128)(2,1)S(1)}, u32[]{:S(2)}, u32[]{:S(2)}) %collective-permute-start.11) | collective-permute-done | bytes 16416 | tf_op jit(solution)/shard_map/ppermute | solution.py:51
  29.3 0.7 %collective-permute-done.10.refs_2_ = bf16[32,256]{1,0:T(8,128)(2,1)S(1)} collective-permute-done((bf16[32,256]{1,0:T(8,128)(2,1)S(1)}, bf16[32,256]{1,0:T(8,128)(2,1)S(1)}, u32[]{:S(2)}, u32[]{:S(2)}) %collective-permute-start.10) | collective-permute-done | bytes 16416 | tf_op jit(solution)/shard_map/ppermute | solution.py:51
  29.9 0.0 collective-permute-done.9.refs_1_
  29.9 0.2 shard_map.132
  30.2 1.6 %collective-permute-start.14 = (bf16[128,128]{1,0:T(8,128)(2,1)S(1)}, bf16[128,128]{1,0:T(8,128)(2,1)S(1)}, u32[]{:S(2)}, u32[]{:S(2)}) collective-permute-start(bf16[128,128]{1,0:T(8,128)(2,1)S(1)} %get-tuple-element.87), channel_id=1, source_target_pairs={{0,4},{4,0},{8,12},{12,8},{16,20},{20,16},{24,28},{28,24},{1,5},{5... | collective-permute-start | bytes 98312 | tf_op jit(solution)/shard_map/ppermute | solution.py:51
  31.7 0.6 %collective-permute-start.15 = (bf16[128,128]{1,0:T(8,128)(2,1)S(1)}, bf16[128,128]{1,0:T(8,128)(2,1)S(1)}, u32[]{:S(2)}, u32[]{:S(2)}) collective-permute-start(bf16[128,128]{1,0:T(8,128)(2,1)S(1)} %get-tuple-element.88), channel_id=1, source_target_pairs={{0,8},{4,12},{8,0},{12,4},{16,24},{20,28},{24,16},{28,20},{1,9},{5... | collective-permute-start | bytes 98312 | tf_op jit(solution)/shard_map/ppermute | solution.py:51
  32.4 1.3 %collective-permute-start.16 = (bf16[128,128]{1,0:T(8,128)(2,1)S(1)}, bf16[128,128]{1,0:T(8,128)(2,1)S(1)}, u32[]{:S(2)}, u32[]{:S(2)}) collective-permute-start(bf16[128,128]{1,0:T(8,128)(2,1)S(1)} %get-tuple-element.89), channel_id=1, source_target_pairs={{0,12},{4,8},{8,4},{12,0},{16,28},{20,24},{24,20},{28,16},{1,13},{... | collective-permute-start | bytes 98312 | tf_op jit(solution)/shard_map/ppermute | solution.py:51
  33.7 0.0 collective-permute-done.12.got_ref
  33.7 0.1 shard_map.134
  33.8 0.7 %collective-permute-start.13 = (bf16[128,384]{1,0:T(8,128)(2,1)S(1)}, bf16[128,384]{1,0:T(8,128)(2,1)S(1)}, u32[]{:S(2)}, u32[]{:S(2)}) collective-permute-start(bf16[128,384]{1,0:T(8,128)(2,1)S(1)} %get-tuple-element.85), channel_id=1, source_target_pairs={{0,8},{4,12},{8,0},{12,4},{16,24},{20,28},{24,16},{28,20},{1,9},{5... | collective-permute-start | bytes 294920 | tf_op jit(solution)/shard_map/ppermute | solution.py:51
  34.5 0.1 fusion.1.refs_26_.place_ref
  34.6 0.0 collective-permute-done.14.one_ref
  34.6 1.4 %collective-permute-done.15.two_ref = bf16[128,128]{1,0:T(8,128)(2,1)S(1)} collective-permute-done((bf16[128,128]{1,0:T(8,128)(2,1)S(1)}, bf16[128,128]{1,0:T(8,128)(2,1)S(1)}, u32[]{:S(2)}, u32[]{:S(2)}) %collective-permute-start.15) | collective-permute-done | bytes 32800 | tf_op jit(solution)/shard_map/ppermute | solution.py:51
  36.0 1.4 %collective-permute-done.16.both_ref = bf16[128,128]{1,0:T(8,128)(2,1)S(1)} collective-permute-done((bf16[128,128]{1,0:T(8,128)(2,1)S(1)}, bf16[128,128]{1,0:T(8,128)(2,1)S(1)}, u32[]{:S(2)}, u32[]{:S(2)}) %collective-permute-start.16) | collective-permute-done | bytes 32800 | tf_op jit(solution)/shard_map/ppermute | solution.py:51
  37.4 1.0 %collective-permute-done.13.near_got = bf16[128,384]{1,0:T(8,128)(2,1)S(1)} collective-permute-done((bf16[128,384]{1,0:T(8,128)(2,1)S(1)}, bf16[128,384]{1,0:T(8,128)(2,1)S(1)}, u32[]{:S(2)}, u32[]{:S(2)}) %collective-permute-start.13) | collective-permute-done | bytes 98336 | tf_op jit(solution)/shard_map/ppermute | solution.py:51
  38.5 0.3 shard_map.135
  38.8 2.3 %collective-permute-start.17 = (bf16[64,384]{1,0:T(8,128)(2,1)S(1)}, bf16[64,384]{1,0:T(8,128)(2,1)S(1)}, u32[]{:S(2)}, u32[]{:S(2)}) collective-permute-start(bf16[64,384]{1,0:T(8,128)(2,1)S(1)} %get-tuple-element.91), channel_id=1, source_target_pairs={{0,16},{4,20},{8,24},{12,28},{16,0},{20,4},{24,8},{28,12},{1,17},{... | collective-permute-start | bytes 147464 | tf_op jit(solution)/shard_map/ppermute | solution.py:51
  41.1 0.8 %shard_map.127 = (f32[256,256]{1,0:T(8,128)S(1)}, f32[128,256]{1,0:T(8,128)S(1)}, f32[256,128]{1,0:T(8,128)S(1)}, f32[256,256]{1,0:T(8,128)S(1)}) custom-call(bf16[256,512]{1,0:T(8,128)(2,1)S(1)} %copy-done.2, bf16[256,512]{1,0:T(8,128)(2,1)S(1)} %copy-done.3, bf16[256,1024]{1,0:T(8,128)(2,1)S(1)} %copy-done.1, bf16[256,1024]{1,0:T(8,128)(2,1)S(1)} %copy-done, ...), custom_call_target="tpu_custom_call" | custom-call | flops 150994944 | bytes 1572864 | tf_op jit(solution)/shard_map/pallas_call | solution.py:514
  41.9 0.8 %shard_map.126 = (f32[256,256]{1,0:T(8,128)S(1)}, f32[128,256]{1,0:T(8,128)S(1)}, f32[256,128]{1,0:T(8,128)S(1)}, f32[256,256]{1,0:T(8,128)S(1)}) custom-call(bf16[256,512]{1,0:T(8,128)(2,1)S(1)} %copy-done.2, bf16[256,512]{1,0:T(8,128)(2,1)S(1)} %copy-done.3, bf16[256,1024]{1,0:T(8,128)(2,1)S(1)} %copy-done.1, bf16[256,1024]{1,0:T(8,128)(2,1)S(1)} %copy-done, ...), custom_call_target="tpu_custom_call" | custom-call | flops 150994944 | bytes 1572864 | tf_op jit(solution)/shard_map/pallas_call | solution.py:514
  42.7 1.4 %shard_map.128 = (f32[512,256]{1,0:T(8,128)S(1)}, f32[256,256]{1,0:T(8,128)S(1)}, f32[256,256]{1,0:T(8,128)S(1)}, f32[256,512]{1,0:T(8,128)S(1)}) custom-call(bf16[256,512]{1,0:T(8,128)(2,1)S(1)} %copy-done.2, bf16[256,512]{1,0:T(8,128)(2,1)S(1)} %copy-done.3, bf16[256,1024]{1,0:T(8,128)(2,1)S(1)} %copy-done.1, bf16[256,1024]{1,0:T(8,128)(2,1)S(1)} %copy-done, ...), custom_call_target="tpu_custom_call" | custom-call | flops 301989888 | bytes 3145728 | tf_op jit(solution)/shard_map/pallas_call | solution.py:514
  44.1 0.0 collective-permute-done.5.refs_1_.refs_4_
  44.1 0.1 shard_map.125
  44.2 0.0 copy-start.4
  44.2 1.6 %collective-permute-start.6 = (bf16[512,128]{1,0:T(8,128)(2,1)S(1)}, bf16[512,128]{1,0:T(8,128)(2,1)S(1)}, u32[]{:S(2)}, u32[]{:S(2)}) collective-permute-start(bf16[512,128]{1,0:T(8,128)(2,1)S(1)} %shard_map.125), channel_id=1, source_target_pairs={{0,4},{4,0},{8,12},{12,8},{16,20},{20,16},{24,28},{28,24},{1,5},{5... | collective-permute-start | bytes 393224 | tf_op jit(solution)/shard_map/ppermute | solution.py:51
  45.7 0.0 collective-permute-done.17
  45.7 0.7 %convert_add_fusion = f32[64,384]{1,0:T(8,128)} fusion(f32[64,384]{1,0:T(8,128)S(1)} %get-tuple-element.90, bf16[64,384]{1,0:T(8,128)(2,1)S(1)} %collective-permute-done.17), kind=kLoop, calls=%fused_computation.6 | loop fusion | flops 49152 | bytes 245760 | tf_op jit(solution)/shard_map/add | solution.py:507
  46.4 2.8 %collective-permute-done.6.refs_5_ = bf16[512,128]{1,0:T(8,128)(2,1)S(1)} collective-permute-done((bf16[512,128]{1,0:T(8,128)(2,1)S(1)}, bf16[512,128]{1,0:T(8,128)(2,1)S(1)}, u32[]{:S(2)}, u32[]{:S(2)}) %collective-permute-start.6) | collective-permute-done | bytes 131104 | tf_op jit(solution)/shard_map/ppermute | solution.py:51
  49.2 2.9 %shard_map.133 = (bf16[256,1024]{1,0:T(8,128)(2,1)}, bf16[256,512]{1,0:T(8,128)(2,1)}, bf16[256,512]{1,0:T(8,128)(2,1)}, bf16[256,512]{1,0:T(8,128)(2,1)}, bf16[256,1024]{1,0:T(8,128)(2,1)}) custom-call(s32[1]{0:T(128)} %bitcast.idx_ref, bf16[512,128]{1,0:T(8,128)(2,1)S(1)} %collective-permute-done.refs_0_, ...), custom_call_target="tpu_custom_call" | custom-call | flops 402653184 | bytes 3670016 | tf_op jit(solution)/shard_map/pallas_call | solution.py:521
  (7 shorter events, 0.1 us)
Async XLA Ops:
  0.6 7.9 %copy-start.1 = (bf16[256,1024]{1,0:T(8,128)(2,1)S(1)}, bf16[256,1024]{1,0:T(8,128)(2,1)}, u32[]{:S(2)}) copy-start(bf16[256,1024]{1,0:T(8,128)(2,1)} %refs_11_.1) | copy-start | bytes 1572868
  0.6 7.9 %copy-start.3 = (bf16[256,512]{1,0:T(8,128)(2,1)S(1)}, bf16[256,512]{1,0:T(8,128)(2,1)}, u32[]{:S(2)}) copy-start(bf16[256,512]{1,0:T(8,128)(2,1)} %q_ref.9) | copy-start | bytes 786436
  2.2 6.4 %copy-start = (bf16[256,1024]{1,0:T(8,128)(2,1)S(1)}, bf16[256,1024]{1,0:T(8,128)(2,1)}, u32[]{:S(2)}) copy-start(bf16[256,1024]{1,0:T(8,128)(2,1)} %refs_8_.1) | copy-start | bytes 1572868
  2.6 6.0 %copy-start.2 = (bf16[256,512]{1,0:T(8,128)(2,1)S(1)}, bf16[256,512]{1,0:T(8,128)(2,1)}, u32[]{:S(2)}) copy-start(bf16[256,512]{1,0:T(8,128)(2,1)} %refs_10_.1) | copy-start | bytes 786436
  2.6 5.8 %collective-permute-start.2 = (bf16[192,256]{1,0:T(8,128)(2,1)S(1)}, bf16[192,256]{1,0:T(8,128)(2,1)S(1)}, u32[]{:S(2)}, u32[]{:S(2)}) collective-permute-start(bf16[192,256]{1,0:T(8,128)(2,1)S(1)} %get-tuple-element.54), channel_id=1, source_target_pairs={{0,2},{1,3},{2,0},{3,1},{4,6},{5,7},{6,4},{7,5},{8,10},{9,11},{10,... | collective-permute-start | bytes 294920 | tf_op jit(solution)/shard_map/ppermute | solution.py:51
  5.6 6.5 %collective-permute-start = (bf16[512,128]{1,0:T(8,128)(2,1)S(1)}, bf16[512,128]{1,0:T(8,128)(2,1)S(1)}, u32[]{:S(2)}, u32[]{:S(2)}) collective-permute-start(bf16[512,128]{1,0:T(8,128)(2,1)S(1)} %get-tuple-element.49), channel_id=1, source_target_pairs={{0,4},{4,0},{8,12},{12,8},{16,20},{20,16},{24,28},{28,24},{1,5},{5... | collective-permute-start | bytes 393224 | tf_op jit(solution)/shard_map/ppermute | solution.py:51
  8.4 1.3 %collective-permute-start.3 = (bf16[96,256]{1,0:T(8,128)(2,1)S(1)}, bf16[96,256]{1,0:T(8,128)(2,1)S(1)}, u32[]{:S(2)}, u32[]{:S(2)}) collective-permute-start(bf16[96,256]{1,0:T(8,128)(2,1)S(1)} %get-tuple-element.56), channel_id=1, source_target_pairs={{0,1},{1,0},{2,3},{3,2},{4,5},{5,4},{6,7},{7,6},{8,9},{9,8},{10,11... | collective-permute-start | bytes 147464 | tf_op jit(solution)/shard_map/ppermute | solution.py:51
  10.2 4.2 %collective-permute-start.7 = (bf16[96,256]{1,0:T(8,128)(2,1)S(1)}, bf16[96,256]{1,0:T(8,128)(2,1)S(1)}, u32[]{:S(2)}, u32[]{:S(2)}) collective-permute-start(bf16[96,256]{1,0:T(8,128)(2,1)S(1)} %get-tuple-element.73), channel_id=1, source_target_pairs={{0,2},{1,3},{2,0},{3,1},{4,6},{5,7},{6,4},{7,5},{8,10},{9,11},{10,... | collective-permute-start | bytes 147464 | tf_op jit(solution)/shard_map/ppermute | solution.py:51
  12.1 5.3 %collective-permute-start.1 = (bf16[512,128]{1,0:T(8,128)(2,1)S(1)}, bf16[512,128]{1,0:T(8,128)(2,1)S(1)}, u32[]{:S(2)}, u32[]{:S(2)}) collective-permute-start(bf16[512,128]{1,0:T(8,128)(2,1)S(1)} %add_convert_fusion), channel_id=1, source_target_pairs={{0,8},{4,12},{8,0},{12,4},{16,24},{20,28},{24,16},{28,20},{1,9},{5... | collective-permute-start | bytes 393224 | tf_op jit(solution)/shard_map/ppermute | solution.py:51
  14.3 5.8 %collective-permute-start.8 = (bf16[192,256]{1,0:T(8,128)(2,1)S(1)}, bf16[192,256]{1,0:T(8,128)(2,1)S(1)}, u32[]{:S(2)}, u32[]{:S(2)}) collective-permute-start(bf16[192,256]{1,0:T(8,128)(2,1)S(1)} %pad_maximum_fusion.1), channel_id=1, source_target_pairs={{0,1},{1,0},{2,3},{3,2},{4,5},{5,4},{6,7},{7,6},{8,9},{9,8},{10,11... | collective-permute-start | bytes 294920 | tf_op jit(solution)/shard_map/ppermute | solution.py:51
  17.5 8.2 %collective-permute-start.4 = (bf16[512,128]{1,0:T(8,128)(2,1)S(1)}, bf16[512,128]{1,0:T(8,128)(2,1)S(1)}, u32[]{:S(2)}, u32[]{:S(2)}) collective-permute-start(bf16[512,128]{1,0:T(8,128)(2,1)S(1)} %shard_map.123), channel_id=1, source_target_pairs={{0,16},{4,20},{8,24},{12,28},{16,0},{20,4},{24,8},{28,12},{1,17},{... | collective-permute-start | bytes 393224 | tf_op jit(solution)/shard_map/ppermute | solution.py:51
  20.5 13.2 %collective-permute-start.12 = (bf16[256,384]{1,0:T(8,128)(2,1)S(1)}, bf16[256,384]{1,0:T(8,128)(2,1)S(1)}, u32[]{:S(2)}, u32[]{:S(2)}) collective-permute-start(bf16[256,384]{1,0:T(8,128)(2,1)S(1)} %get-tuple-element.83), channel_id=1, source_target_pairs={{0,4},{4,0},{8,12},{12,8},{16,20},{20,16},{24,28},{28,24},{1,5},{5... | collective-permute-start | bytes 589832 | tf_op jit(solution)/shard_map/ppermute | solution.py:51
  26.0 3.2 %collective-permute-start.11 = (bf16[32,256]{1,0:T(8,128)(2,1)S(1)}, bf16[32,256]{1,0:T(8,128)(2,1)S(1)}, u32[]{:S(2)}, u32[]{:S(2)}) collective-permute-start(bf16[32,256]{1,0:T(8,128)(2,1)S(1)} %shard_map.131.refs_0_), channel_id=1, source_target_pairs={{0,3},{1,2},{2,1},{3,0},{4,7},{5,6},{6,5},{7,4},{8,11},{9,10},{10,... | collective-permute-start | bytes 49160 | tf_op jit(solution)/shard_map/ppermute | solution.py:51
  26.1 3.8 %collective-permute-start.10 = (bf16[32,256]{1,0:T(8,128)(2,1)S(1)}, bf16[32,256]{1,0:T(8,128)(2,1)S(1)}, u32[]{:S(2)}, u32[]{:S(2)}) collective-permute-start(bf16[32,256]{1,0:T(8,128)(2,1)S(1)} %shard_map.131.refs_0_), channel_id=1, source_target_pairs={{0,2},{1,3},{2,0},{3,1},{4,6},{5,7},{6,4},{7,5},{8,10},{9,11},{10,... | collective-permute-start | bytes 49160 | tf_op jit(solution)/shard_map/ppermute | solution.py:51
  26.7 3.2 %collective-permute-start.9 = (bf16[32,256]{1,0:T(8,128)(2,1)S(1)}, bf16[32,256]{1,0:T(8,128)(2,1)S(1)}, u32[]{:S(2)}, u32[]{:S(2)}) collective-permute-start(bf16[32,256]{1,0:T(8,128)(2,1)S(1)} %shard_map.131.refs_0_), channel_id=1, source_target_pairs={{0,1},{1,0},{2,3},{3,2},{4,5},{5,4},{6,7},{7,6},{8,9},{9,8},{10,11... | collective-permute-start | bytes 49160 | tf_op jit(solution)/shard_map/ppermute | solution.py:51
  28.0 16.1 %collective-permute-start.5 = (bf16[512,128]{1,0:T(8,128)(2,1)S(1)}, bf16[512,128]{1,0:T(8,128)(2,1)S(1)}, u32[]{:S(2)}, u32[]{:S(2)}) collective-permute-start(bf16[512,128]{1,0:T(8,128)(2,1)S(1)} %shard_map.124), channel_id=1, source_target_pairs={{0,8},{4,12},{8,0},{12,4},{16,24},{20,28},{24,16},{28,20},{1,9},{5... | collective-permute-start | bytes 393224 | tf_op jit(solution)/shard_map/ppermute | solution.py:51
  30.2 4.4 %collective-permute-start.14 = (bf16[128,128]{1,0:T(8,128)(2,1)S(1)}, bf16[128,128]{1,0:T(8,128)(2,1)S(1)}, u32[]{:S(2)}, u32[]{:S(2)}) collective-permute-start(bf16[128,128]{1,0:T(8,128)(2,1)S(1)} %get-tuple-element.87), channel_id=1, source_target_pairs={{0,4},{4,0},{8,12},{12,8},{16,20},{20,16},{24,28},{28,24},{1,5},{5... | collective-permute-start | bytes 98312 | tf_op jit(solution)/shard_map/ppermute | solution.py:51
  31.7 4.3 %collective-permute-start.15 = (bf16[128,128]{1,0:T(8,128)(2,1)S(1)}, bf16[128,128]{1,0:T(8,128)(2,1)S(1)}, u32[]{:S(2)}, u32[]{:S(2)}) collective-permute-start(bf16[128,128]{1,0:T(8,128)(2,1)S(1)} %get-tuple-element.88), channel_id=1, source_target_pairs={{0,8},{4,12},{8,0},{12,4},{16,24},{20,28},{24,16},{28,20},{1,9},{5... | collective-permute-start | bytes 98312 | tf_op jit(solution)/shard_map/ppermute | solution.py:51
  32.4 5.0 %collective-permute-start.16 = (bf16[128,128]{1,0:T(8,128)(2,1)S(1)}, bf16[128,128]{1,0:T(8,128)(2,1)S(1)}, u32[]{:S(2)}, u32[]{:S(2)}) collective-permute-start(bf16[128,128]{1,0:T(8,128)(2,1)S(1)} %get-tuple-element.89), channel_id=1, source_target_pairs={{0,12},{4,8},{8,4},{12,0},{16,28},{20,24},{24,20},{28,16},{1,13},{... | collective-permute-start | bytes 98312 | tf_op jit(solution)/shard_map/ppermute | solution.py:51
  33.8 4.7 %collective-permute-start.13 = (bf16[128,384]{1,0:T(8,128)(2,1)S(1)}, bf16[128,384]{1,0:T(8,128)(2,1)S(1)}, u32[]{:S(2)}, u32[]{:S(2)}) collective-permute-start(bf16[128,384]{1,0:T(8,128)(2,1)S(1)} %get-tuple-element.85), channel_id=1, source_target_pairs={{0,8},{4,12},{8,0},{12,4},{16,24},{20,28},{24,16},{28,20},{1,9},{5... | collective-permute-start | bytes 294920 | tf_op jit(solution)/shard_map/ppermute | solution.py:51
  38.8 7.0 %collective-permute-start.17 = (bf16[64,384]{1,0:T(8,128)(2,1)S(1)}, bf16[64,384]{1,0:T(8,128)(2,1)S(1)}, u32[]{:S(2)}, u32[]{:S(2)}) collective-permute-start(bf16[64,384]{1,0:T(8,128)(2,1)S(1)} %get-tuple-element.91), channel_id=1, source_target_pairs={{0,16},{4,20},{8,24},{12,28},{16,0},{20,4},{24,8},{28,12},{1,17},{... | collective-permute-start | bytes 147464 | tf_op jit(solution)/shard_map/ppermute | solution.py:51
  44.2 5.0 %copy-start.4 = (f32[8,64,128]{2,1,0:T(8,128)S(1)}, f32[8,64,128]{2,1,0:T(8,128)}, u32[]{:S(2)}) copy-start(f32[8,64,128]{2,1,0:T(8,128)} %param.13) | copy-start | bytes 786436
  44.2 5.0 %collective-permute-start.6 = (bf16[512,128]{1,0:T(8,128)(2,1)S(1)}, bf16[512,128]{1,0:T(8,128)(2,1)S(1)}, u32[]{:S(2)}, u32[]{:S(2)}) collective-permute-start(bf16[512,128]{1,0:T(8,128)(2,1)S(1)} %shard_map.125), channel_id=1, source_target_pairs={{0,4},{4,0},{8,12},{12,8},{16,20},{20,16},{24,28},{28,24},{1,5},{5... | collective-permute-start | bytes 393224 | tf_op jit(solution)/shard_map/ppermute | solution.py:51

commit v14 on v13

--- a/solution.py
+++ b/solution.py
@@ -254,7 +254,7 @@
 
 def near_wgrad_kernel(bits, inner, idx_ref, head_ref, xt_ref, gp_ref, send_ref, keep_ref, sorted_ref):
     put_in_order(bits, head_ref, gp_ref, sorted_ref)
-    part_ways(nt(xt_ref[...], sorted_ref[...]), (idx_ref[0] & 1) == 1, send_ref, keep_ref, inner)
+    part_ways(nt(xt_ref[...], sorted_ref[...]), (idx_ref[0] & 2) == 2, send_ref, keep_ref, inner)
 
 
 def far_wgrad_kernel(inner, idx_ref, head_ref, xt_ref, *refs):
@@ -470,15 +470,15 @@
     near_all = gather_heads(near, head_bits)
     n = width // 2
     send, near_w, near_all = call(
-        functools.partial(near_wgrad_kernel, head_bits, per),
+        functools.partial(near_wgrad_kernel, head_bits, 2 * per),
         [S((n, cols), BF16), S((n, cols), F32), S((cols, tokens), BF16)],
         [SM] * 2 + [VM] * 2, 2 * tokens * width * cols)(idx, head_idx, xt, near_all)
-    got = swap(send, "seq", 0)
+    got = swap(send, "seq", 1)
     n = n // 2
     send, near_w = call(
-        functools.partial(fold_kernel, 1, per), [S((n, cols), BF16), S((n, cols), F32)],
+        functools.partial(fold_kernel, 0, per), [S((n, cols), BF16), S((n, cols), F32)],
         [SM] + [VM] * 2, n * cols)(idx, near_w, got)
-    near_got = swap(send, "seq", 1)
+    near_got = swap(send, "seq", 0)
 
     far_all = [far_rows] + [exchange(far_rows, "head", away) for away in range(1, n_head)]
     far_w, one, two, both, far_all = call(

time: 52.3 us -> 52.6 us (level)
  starting transfers between devices: 23.1 us -> 24.4 us
  waiting for transfers between devices: 16.3 us -> 15.4 us
    ppermute x18, starting transfers between devices: 23.1 us -> 24.4 us  [exchange(): return lax.ppermute(value, axis, pairs)]
    ppermute x18, waiting for transfers between devices: 16.3 us -> 15.4 us  [exchange(): return lax.ppermute(value, axis, pairs)]
where the time goes in v14:
time: 52.6 us; the launch traced here: 52.5 us
  starting transfers between devices  24.4 us (46%)
  waiting for transfers between devices  15.4 us (29%)
  Pallas kernels  10.9 us (21%)
  between operations  0.89 us (2%)
  other arithmetic  0.82 us (2%)
    ppermute x18, starting transfers between devices, exchange(): return lax.ppermute(value, axis, pairs)  24.4 us
    ppermute x18, waiting for transfers between devices, exchange(): return lax.ppermute(value, axis, pairs)  15.4 us
    pallas_call x3, Pallas kernels, body(): call(functools.partial(local_kernel, dims, levels, pairs), [S((heads * dv...  2.98 us
    pallas_call x1, Pallas kernels, body(): call(functools.partial(final_kernel, dims, levels, first, seq_bits, cuts)...  2.9 us
    pallas_call x1, Pallas kernels, body(): call(functools.partial(state_kernel, dims), [S((rows, dv), F32), S((rows,...  1.5 us
  transfers between devices with their start and end apart: 18, of which 11 were waited for; matrix products, arithmetic and copies ran while one was open for 2% of the time, Pallas kernels for 12%

profile of v14, /device:TPU:0, one launch (start us, length us, event | category | flops | bytes accessed | tf_op | source)
XLA Modules:
  0.0 52.5 jit_solution(10632817519521901067)
XLA Ops:
  0.6 0.0 copy-start.1
  0.6 0.0 copy-start.3
  0.7 1.5 %shard_map.118 = (f32[512,128]{1,0:T(8,128)S(1)}, bf16[512,128]{1,0:T(8,128)(2,1)S(1)}, bf16[512,384]{1,0:T(8,128)(2,1)S(1)}, bf16[256,512]{1,0:T(8,128)(2,1)S(1)}) custom-call(s32[1]{0:T(128)} %bitcast.idx_ref, s32[1]{0:T(128)} %bitcast.1.head_ref.idx_ref, bf16[256,512]{1,0:T(8,128)(2,1)} %refs_10_.1, bf16[256,1024]{1,0:T(8,128)(2,1)} %refs_11_.1, ...), custom_call_target="tpu_custom_call" | custom-call | flops 33554432 | bytes 2097152 | tf_op jit(solution)/shard_map/pallas_call | solution.py:415
  2.2 0.0 copy-start
  2.2 0.4 shard_map.119
  2.6 0.0 copy-start.2
  2.6 3.0 %collective-permute-start.2 = (bf16[192,256]{1,0:T(8,128)(2,1)S(1)}, bf16[192,256]{1,0:T(8,128)(2,1)S(1)}, u32[]{:S(2)}, u32[]{:S(2)}) collective-permute-start(bf16[192,256]{1,0:T(8,128)(2,1)S(1)} %get-tuple-element.54), channel_id=1, source_target_pairs={{0,2},{1,3},{2,0},{3,1},{4,6},{5,7},{6,4},{7,5},{8,10},{9,11},{10,... | collective-permute-start | bytes 294920 | tf_op jit(solution)/shard_map/ppermute | solution.py:51
  5.6 1.5 %collective-permute-start = (bf16[512,128]{1,0:T(8,128)(2,1)S(1)}, bf16[512,128]{1,0:T(8,128)(2,1)S(1)}, u32[]{:S(2)}, u32[]{:S(2)}) collective-permute-start(bf16[512,128]{1,0:T(8,128)(2,1)S(1)} %get-tuple-element.49), channel_id=1, source_target_pairs={{0,4},{4,0},{8,12},{12,8},{16,20},{20,16},{24,28},{28,24},{1,5},{5... | collective-permute-start | bytes 393224 | tf_op jit(solution)/shard_map/ppermute | solution.py:51
  7.1 1.3 %collective-permute-done.2.got_ref = bf16[192,256]{1,0:T(8,128)(2,1)S(1)} collective-permute-done((bf16[192,256]{1,0:T(8,128)(2,1)S(1)}, bf16[192,256]{1,0:T(8,128)(2,1)S(1)}, u32[]{:S(2)}, u32[]{:S(2)}) %collective-permute-start.2) | collective-permute-done | bytes 98336 | tf_op jit(solution)/shard_map/ppermute | solution.py:51
  8.4 0.1 collective-permute-start.3
  8.5 0.0 copy-done.1
  8.5 0.0 copy-done.3
  8.5 0.0 copy-done
  8.5 0.0 copy-done.2
  8.6 0.8 %shard_map.121.gl_ref = f32[96,256]{1,0:T(8,128)S(1)} custom-call(bf16[256,512]{1,0:T(8,128)(2,1)S(1)} %copy-done.2, bf16[256,512]{1,0:T(8,128)(2,1)S(1)} %copy-done.3, bf16[256,1024]{1,0:T(8,128)(2,1)S(1)} %copy-done.1, bf16[256,1024]{1,0:T(8,128)(2,1)S(1)} %copy-done), custom_call_target="tpu_custom_call" | custom-call | flops 201326592 | bytes 196608 | tf_op jit(solution)/shard_map/pallas_call | solution.py:444
  9.3 0.4 collective-permute-done.3.got_ref
  9.7 0.4 shard_map.122
  10.2 1.9 %collective-permute-start.7 = (bf16[96,256]{1,0:T(8,128)(2,1)S(1)}, bf16[96,256]{1,0:T(8,128)(2,1)S(1)}, u32[]{:S(2)}, u32[]{:S(2)}) collective-permute-start(bf16[96,256]{1,0:T(8,128)(2,1)S(1)} %get-tuple-element.73), channel_id=1, source_target_pairs={{0,2},{1,3},{2,0},{3,1},{4,6},{5,7},{6,4},{7,5},{8,10},{9,11},{10,... | collective-permute-start | bytes 147464 | tf_op jit(solution)/shard_map/ppermute | solution.py:51
  12.1 0.0 collective-permute-done.refs_0_
  12.1 1.6 %collective-permute-start.1 = (bf16[512,128]{1,0:T(8,128)(2,1)S(1)}, bf16[512,128]{1,0:T(8,128)(2,1)S(1)}, u32[]{:S(2)}, u32[]{:S(2)}) collective-permute-start(bf16[512,128]{1,0:T(8,128)(2,1)S(1)} %add_convert_fusion), channel_id=1, source_target_pairs={{0,8},{4,12},{8,0},{12,4},{16,24},{20,28},{24,16},{28,20},{1,9},{5... | collective-permute-start | bytes 393224 | tf_op jit(solution)/shard_map/ppermute | solution.py:51
  13.7 0.6 %collective-permute-done.7 = bf16[96,256]{1,0:T(8,128)(2,1)S(1)} collective-permute-done((bf16[96,256]{1,0:T(8,128)(2,1)S(1)}, bf16[96,256]{1,0:T(8,128)(2,1)S(1)}, u32[]{:S(2)}, u32[]{:S(2)}) %collective-permute-start.7) | collective-permute-done | bytes 49184 | tf_op jit(solution)/shard_map/ppermute | solution.py:51
  14.3 0.1 collective-permute-start.8
  14.4 3.0 %collective-permute-done.1.refs_1_ = bf16[512,128]{1,0:T(8,128)(2,1)S(1)} collective-permute-done((bf16[512,128]{1,0:T(8,128)(2,1)S(1)}, bf16[512,128]{1,0:T(8,128)(2,1)S(1)}, u32[]{:S(2)}, u32[]{:S(2)}) %collective-permute-start.1) | collective-permute-done | bytes 131104 | tf_op jit(solution)/shard_map/ppermute | solution.py:51
  17.4 0.1 shard_map.123
  17.5 2.6 %collective-permute-start.4 = (bf16[512,128]{1,0:T(8,128)(2,1)S(1)}, bf16[512,128]{1,0:T(8,128)(2,1)S(1)}, u32[]{:S(2)}, u32[]{:S(2)}) collective-permute-start(bf16[512,128]{1,0:T(8,128)(2,1)S(1)} %shard_map.123), channel_id=1, source_target_pairs={{0,16},{4,20},{8,24},{12,28},{16,0},{20,4},{24,8},{28,12},{1,17},{... | collective-permute-start | bytes 393224 | tf_op jit(solution)/shard_map/ppermute | solution.py:51
  20.1 0.0 collective-permute-done.8
  20.1 0.3 shard_map.129
  20.5 1.6 %collective-permute-start.12 = (bf16[256,384]{1,0:T(8,128)(2,1)S(1)}, bf16[256,384]{1,0:T(8,128)(2,1)S(1)}, u32[]{:S(2)}, u32[]{:S(2)}) collective-permute-start(bf16[256,384]{1,0:T(8,128)(2,1)S(1)} %get-tuple-element.83), channel_id=1, source_target_pairs={{0,8},{4,12},{8,0},{12,4},{16,24},{20,28},{24,16},{28,20},{1,9},{5... | collective-permute-start | bytes 589832 | tf_op jit(solution)/shard_map/ppermute | solution.py:51
  22.1 0.5 shard_map.130.refs_4_
  22.6 2.9 %collective-permute-done.4.refs_0_.refs_2_.refs_3_ = bf16[512,128]{1,0:T(8,128)(2,1)S(1)} collective-permute-done((bf16[512,128]{1,0:T(8,128)(2,1)S(1)}, bf16[512,128]{1,0:T(8,128)(2,1)S(1)}, u32[]{:S(2)}, u32[]{:S(2)}) %collective-permute-start.4) | collective-permute-done | bytes 131104 | tf_op jit(solution)/shard_map/ppermute | solution.py:51
  25.6 0.3 shard_map.131.refs_0_
  25.9 0.1 collective-permute-start.11
  26.0 0.6 %collective-permute-start.10 = (bf16[32,256]{1,0:T(8,128)(2,1)S(1)}, bf16[32,256]{1,0:T(8,128)(2,1)S(1)}, u32[]{:S(2)}, u32[]{:S(2)}) collective-permute-start(bf16[32,256]{1,0:T(8,128)(2,1)S(1)} %shard_map.131.refs_0_), channel_id=1, source_target_pairs={{0,2},{1,3},{2,0},{3,1},{4,6},{5,7},{6,4},{7,5},{8,10},{9,11},{10,... | collective-permute-start | bytes 49160 | tf_op jit(solution)/shard_map/ppermute | solution.py:51
  26.5 1.3 %collective-permute-start.9 = (bf16[32,256]{1,0:T(8,128)(2,1)S(1)}, bf16[32,256]{1,0:T(8,128)(2,1)S(1)}, u32[]{:S(2)}, u32[]{:S(2)}) collective-permute-start(bf16[32,256]{1,0:T(8,128)(2,1)S(1)} %shard_map.131.refs_0_), channel_id=1, source_target_pairs={{0,1},{1,0},{2,3},{3,2},{4,5},{5,4},{6,7},{7,6},{8,9},{9,8},{10,11... | collective-permute-start | bytes 49160 | tf_op jit(solution)/shard_map/ppermute | solution.py:51
  27.8 0.1 shard_map.124
  27.9 0.9 %collective-permute-start.5 = (bf16[512,128]{1,0:T(8,128)(2,1)S(1)}, bf16[512,128]{1,0:T(8,128)(2,1)S(1)}, u32[]{:S(2)}, u32[]{:S(2)}) collective-permute-start(bf16[512,128]{1,0:T(8,128)(2,1)S(1)} %shard_map.124), channel_id=1, source_target_pairs={{0,8},{4,12},{8,0},{12,4},{16,24},{20,28},{24,16},{28,20},{1,9},{5... | collective-permute-start | bytes 393224 | tf_op jit(solution)/shard_map/ppermute | solution.py:51
  28.8 0.3 collective-permute-done.11.refs_3_
  29.1 0.7 %collective-permute-done.10.refs_2_ = bf16[32,256]{1,0:T(8,128)(2,1)S(1)} collective-permute-done((bf16[32,256]{1,0:T(8,128)(2,1)S(1)}, bf16[32,256]{1,0:T(8,128)(2,1)S(1)}, u32[]{:S(2)}, u32[]{:S(2)}) %collective-permute-start.10) | collective-permute-done | bytes 16416 | tf_op jit(solution)/shard_map/ppermute | solution.py:51
  29.8 0.0 collective-permute-done.9.refs_1_
  29.8 0.2 shard_map.132
  30.0 1.6 %collective-permute-start.14 = (bf16[128,128]{1,0:T(8,128)(2,1)S(1)}, bf16[128,128]{1,0:T(8,128)(2,1)S(1)}, u32[]{:S(2)}, u32[]{:S(2)}) collective-permute-start(bf16[128,128]{1,0:T(8,128)(2,1)S(1)} %get-tuple-element.87), channel_id=1, source_target_pairs={{0,4},{4,0},{8,12},{12,8},{16,20},{20,16},{24,28},{28,24},{1,5},{5... | collective-permute-start | bytes 98312 | tf_op jit(solution)/shard_map/ppermute | solution.py:51
  31.6 0.9 %collective-permute-start.15 = (bf16[128,128]{1,0:T(8,128)(2,1)S(1)}, bf16[128,128]{1,0:T(8,128)(2,1)S(1)}, u32[]{:S(2)}, u32[]{:S(2)}) collective-permute-start(bf16[128,128]{1,0:T(8,128)(2,1)S(1)} %get-tuple-element.88), channel_id=1, source_target_pairs={{0,8},{4,12},{8,0},{12,4},{16,24},{20,28},{24,16},{28,20},{1,9},{5... | collective-permute-start | bytes 98312 | tf_op jit(solution)/shard_map/ppermute | solution.py:51
  32.4 1.1 %collective-permute-start.16 = (bf16[128,128]{1,0:T(8,128)(2,1)S(1)}, bf16[128,128]{1,0:T(8,128)(2,1)S(1)}, u32[]{:S(2)}, u32[]{:S(2)}) collective-permute-start(bf16[128,128]{1,0:T(8,128)(2,1)S(1)} %get-tuple-element.89), channel_id=1, source_target_pairs={{0,12},{4,8},{8,4},{12,0},{16,28},{20,24},{24,20},{28,16},{1,13},{... | collective-permute-start | bytes 98312 | tf_op jit(solution)/shard_map/ppermute | solution.py:51
  33.6 0.0 collective-permute-done.12.got_ref
  33.6 0.1 shard_map.134
  33.6 1.6 %collective-permute-start.13 = (bf16[128,384]{1,0:T(8,128)(2,1)S(1)}, bf16[128,384]{1,0:T(8,128)(2,1)S(1)}, u32[]{:S(2)}, u32[]{:S(2)}) collective-permute-start(bf16[128,384]{1,0:T(8,128)(2,1)S(1)} %get-tuple-element.85), channel_id=1, source_target_pairs={{0,4},{4,0},{8,12},{12,8},{16,20},{20,16},{24,28},{28,24},{1,5},{5... | collective-permute-start | bytes 294920 | tf_op jit(solution)/shard_map/ppermute | solution.py:51
  35.2 0.1 fusion.1.refs_26_.place_ref
  35.3 0.0 collective-permute-done.14.one_ref
  35.3 0.2 collective-permute-done.15.two_ref
  35.5 1.8 %collective-permute-done.16.both_ref = bf16[128,128]{1,0:T(8,128)(2,1)S(1)} collective-permute-done((bf16[128,128]{1,0:T(8,128)(2,1)S(1)}, bf16[128,128]{1,0:T(8,128)(2,1)S(1)}, u32[]{:S(2)}, u32[]{:S(2)}) %collective-permute-start.16) | collective-permute-done | bytes 32800 | tf_op jit(solution)/shard_map/ppermute | solution.py:51
  37.3 1.1 %collective-permute-done.13.near_got = bf16[128,384]{1,0:T(8,128)(2,1)S(1)} collective-permute-done((bf16[128,384]{1,0:T(8,128)(2,1)S(1)}, bf16[128,384]{1,0:T(8,128)(2,1)S(1)}, u32[]{:S(2)}, u32[]{:S(2)}) %collective-permute-start.13) | collective-permute-done | bytes 98336 | tf_op jit(solution)/shard_map/ppermute | solution.py:51
  38.3 0.3 shard_map.135
  38.6 2.8 %collective-permute-start.17 = (bf16[64,384]{1,0:T(8,128)(2,1)S(1)}, bf16[64,384]{1,0:T(8,128)(2,1)S(1)}, u32[]{:S(2)}, u32[]{:S(2)}) collective-permute-start(bf16[64,384]{1,0:T(8,128)(2,1)S(1)} %get-tuple-element.91), channel_id=1, source_target_pairs={{0,16},{4,20},{8,24},{12,28},{16,0},{20,4},{24,8},{28,12},{1,17},{... | collective-permute-start | bytes 147464 | tf_op jit(solution)/shard_map/ppermute | solution.py:51
  41.4 0.8 %shard_map.127 = (f32[256,256]{1,0:T(8,128)S(1)}, f32[128,256]{1,0:T(8,128)S(1)}, f32[256,128]{1,0:T(8,128)S(1)}, f32[256,256]{1,0:T(8,128)S(1)}) custom-call(bf16[256,512]{1,0:T(8,128)(2,1)S(1)} %copy-done.2, bf16[256,512]{1,0:T(8,128)(2,1)S(1)} %copy-done.3, bf16[256,1024]{1,0:T(8,128)(2,1)S(1)} %copy-done.1, bf16[256,1024]{1,0:T(8,128)(2,1)S(1)} %copy-done, ...), custom_call_target="tpu_custom_call" | custom-call | flops 150994944 | bytes 1572864 | tf_op jit(solution)/shard_map/pallas_call | solution.py:514
  42.2 0.8 %shard_map.126 = (f32[256,256]{1,0:T(8,128)S(1)}, f32[128,256]{1,0:T(8,128)S(1)}, f32[256,128]{1,0:T(8,128)S(1)}, f32[256,256]{1,0:T(8,128)S(1)}) custom-call(bf16[256,512]{1,0:T(8,128)(2,1)S(1)} %copy-done.2, bf16[256,512]{1,0:T(8,128)(2,1)S(1)} %copy-done.3, bf16[256,1024]{1,0:T(8,128)(2,1)S(1)} %copy-done.1, bf16[256,1024]{1,0:T(8,128)(2,1)S(1)} %copy-done, ...), custom_call_target="tpu_custom_call" | custom-call | flops 150994944 | bytes 1572864 | tf_op jit(solution)/shard_map/pallas_call | solution.py:514
  43.0 1.4 %shard_map.128 = (f32[512,256]{1,0:T(8,128)S(1)}, f32[256,256]{1,0:T(8,128)S(1)}, f32[256,256]{1,0:T(8,128)S(1)}, f32[256,512]{1,0:T(8,128)S(1)}) custom-call(bf16[256,512]{1,0:T(8,128)(2,1)S(1)} %copy-done.2, bf16[256,512]{1,0:T(8,128)(2,1)S(1)} %copy-done.3, bf16[256,1024]{1,0:T(8,128)(2,1)S(1)} %copy-done.1, bf16[256,1024]{1,0:T(8,128)(2,1)S(1)} %copy-done, ...), custom_call_target="tpu_custom_call" | custom-call | flops 301989888 | bytes 3145728 | tf_op jit(solution)/shard_map/pallas_call | solution.py:514
  44.4 0.0 collective-permute-done.5.refs_1_.refs_4_
  44.4 0.1 shard_map.125
  44.5 0.0 copy-start.4
  44.5 1.2 %collective-permute-start.6 = (bf16[512,128]{1,0:T(8,128)(2,1)S(1)}, bf16[512,128]{1,0:T(8,128)(2,1)S(1)}, u32[]{:S(2)}, u32[]{:S(2)}) collective-permute-start(bf16[512,128]{1,0:T(8,128)(2,1)S(1)} %shard_map.125), channel_id=1, source_target_pairs={{0,4},{4,0},{8,12},{12,8},{16,20},{20,16},{24,28},{28,24},{1,5},{5... | collective-permute-start | bytes 393224 | tf_op jit(solution)/shard_map/ppermute | solution.py:51
  45.7 0.0 collective-permute-done.17
  45.7 0.7 %convert_add_fusion = f32[64,384]{1,0:T(8,128)} fusion(f32[64,384]{1,0:T(8,128)S(1)} %get-tuple-element.90, bf16[64,384]{1,0:T(8,128)(2,1)S(1)} %collective-permute-done.17), kind=kLoop, calls=%fused_computation.6 | loop fusion | flops 49152 | bytes 245760 | tf_op jit(solution)/shard_map/add | solution.py:507
  46.4 3.2 %collective-permute-done.6.refs_5_ = bf16[512,128]{1,0:T(8,128)(2,1)S(1)} collective-permute-done((bf16[512,128]{1,0:T(8,128)(2,1)S(1)}, bf16[512,128]{1,0:T(8,128)(2,1)S(1)}, u32[]{:S(2)}, u32[]{:S(2)}) %collective-permute-start.6) | collective-permute-done | bytes 131104 | tf_op jit(solution)/shard_map/ppermute | solution.py:51
  49.6 2.9 %shard_map.133 = (bf16[256,1024]{1,0:T(8,128)(2,1)}, bf16[256,512]{1,0:T(8,128)(2,1)}, bf16[256,512]{1,0:T(8,128)(2,1)}, bf16[256,512]{1,0:T(8,128)(2,1)}, bf16[256,1024]{1,0:T(8,128)(2,1)}) custom-call(s32[1]{0:T(128)} %bitcast.idx_ref, bf16[512,128]{1,0:T(8,128)(2,1)S(1)} %collective-permute-done.refs_0_, ...), custom_call_target="tpu_custom_call" | custom-call | flops 402653184 | bytes 3670016 | tf_op jit(solution)/shard_map/pallas_call | solution.py:521
  (7 shorter events, 0.1 us)
Async XLA Ops:
  0.6 7.9 %copy-start.1 = (bf16[256,1024]{1,0:T(8,128)(2,1)S(1)}, bf16[256,1024]{1,0:T(8,128)(2,1)}, u32[]{:S(2)}) copy-start(bf16[256,1024]{1,0:T(8,128)(2,1)} %refs_11_.1) | copy-start | bytes 1572868
  0.6 7.9 %copy-start.3 = (bf16[256,512]{1,0:T(8,128)(2,1)S(1)}, bf16[256,512]{1,0:T(8,128)(2,1)}, u32[]{:S(2)}) copy-start(bf16[256,512]{1,0:T(8,128)(2,1)} %q_ref.9) | copy-start | bytes 786436
  2.2 6.4 %copy-start = (bf16[256,1024]{1,0:T(8,128)(2,1)S(1)}, bf16[256,1024]{1,0:T(8,128)(2,1)}, u32[]{:S(2)}) copy-start(bf16[256,1024]{1,0:T(8,128)(2,1)} %refs_8_.1) | copy-start | bytes 1572868
  2.6 6.0 %copy-start.2 = (bf16[256,512]{1,0:T(8,128)(2,1)S(1)}, bf16[256,512]{1,0:T(8,128)(2,1)}, u32[]{:S(2)}) copy-start(bf16[256,512]{1,0:T(8,128)(2,1)} %refs_10_.1) | copy-start | bytes 786436
  2.6 5.8 %collective-permute-start.2 = (bf16[192,256]{1,0:T(8,128)(2,1)S(1)}, bf16[192,256]{1,0:T(8,128)(2,1)S(1)}, u32[]{:S(2)}, u32[]{:S(2)}) collective-permute-start(bf16[192,256]{1,0:T(8,128)(2,1)S(1)} %get-tuple-element.54), channel_id=1, source_target_pairs={{0,2},{1,3},{2,0},{3,1},{4,6},{5,7},{6,4},{7,5},{8,10},{9,11},{10,... | collective-permute-start | bytes 294920 | tf_op jit(solution)/shard_map/ppermute | solution.py:51
  5.6 6.5 %collective-permute-start = (bf16[512,128]{1,0:T(8,128)(2,1)S(1)}, bf16[512,128]{1,0:T(8,128)(2,1)S(1)}, u32[]{:S(2)}, u32[]{:S(2)}) collective-permute-start(bf16[512,128]{1,0:T(8,128)(2,1)S(1)} %get-tuple-element.49), channel_id=1, source_target_pairs={{0,4},{4,0},{8,12},{12,8},{16,20},{20,16},{24,28},{28,24},{1,5},{5... | collective-permute-start | bytes 393224 | tf_op jit(solution)/shard_map/ppermute | solution.py:51
  8.4 1.3 %collective-permute-start.3 = (bf16[96,256]{1,0:T(8,128)(2,1)S(1)}, bf16[96,256]{1,0:T(8,128)(2,1)S(1)}, u32[]{:S(2)}, u32[]{:S(2)}) collective-permute-start(bf16[96,256]{1,0:T(8,128)(2,1)S(1)} %get-tuple-element.56), channel_id=1, source_target_pairs={{0,1},{1,0},{2,3},{3,2},{4,5},{5,4},{6,7},{7,6},{8,9},{9,8},{10,11... | collective-permute-start | bytes 147464 | tf_op jit(solution)/shard_map/ppermute | solution.py:51
  10.2 4.2 %collective-permute-start.7 = (bf16[96,256]{1,0:T(8,128)(2,1)S(1)}, bf16[96,256]{1,0:T(8,128)(2,1)S(1)}, u32[]{:S(2)}, u32[]{:S(2)}) collective-permute-start(bf16[96,256]{1,0:T(8,128)(2,1)S(1)} %get-tuple-element.73), channel_id=1, source_target_pairs={{0,2},{1,3},{2,0},{3,1},{4,6},{5,7},{6,4},{7,5},{8,10},{9,11},{10,... | collective-permute-start | bytes 147464 | tf_op jit(solution)/shard_map/ppermute | solution.py:51
  12.1 5.3 %collective-permute-start.1 = (bf16[512,128]{1,0:T(8,128)(2,1)S(1)}, bf16[512,128]{1,0:T(8,128)(2,1)S(1)}, u32[]{:S(2)}, u32[]{:S(2)}) collective-permute-start(bf16[512,128]{1,0:T(8,128)(2,1)S(1)} %add_convert_fusion), channel_id=1, source_target_pairs={{0,8},{4,12},{8,0},{12,4},{16,24},{20,28},{24,16},{28,20},{1,9},{5... | collective-permute-start | bytes 393224 | tf_op jit(solution)/shard_map/ppermute | solution.py:51
  14.3 5.8 %collective-permute-start.8 = (bf16[192,256]{1,0:T(8,128)(2,1)S(1)}, bf16[192,256]{1,0:T(8,128)(2,1)S(1)}, u32[]{:S(2)}, u32[]{:S(2)}) collective-permute-start(bf16[192,256]{1,0:T(8,128)(2,1)S(1)} %pad_maximum_fusion.1), channel_id=1, source_target_pairs={{0,1},{1,0},{2,3},{3,2},{4,5},{5,4},{6,7},{7,6},{8,9},{9,8},{10,11... | collective-permute-start | bytes 294920 | tf_op jit(solution)/shard_map/ppermute | solution.py:51
  17.5 8.0 %collective-permute-start.4 = (bf16[512,128]{1,0:T(8,128)(2,1)S(1)}, bf16[512,128]{1,0:T(8,128)(2,1)S(1)}, u32[]{:S(2)}, u32[]{:S(2)}) collective-permute-start(bf16[512,128]{1,0:T(8,128)(2,1)S(1)} %shard_map.123), channel_id=1, source_target_pairs={{0,16},{4,20},{8,24},{12,28},{16,0},{20,4},{24,8},{28,12},{1,17},{... | collective-permute-start | bytes 393224 | tf_op jit(solution)/shard_map/ppermute | solution.py:51
  20.5 13.1 %collective-permute-start.12 = (bf16[256,384]{1,0:T(8,128)(2,1)S(1)}, bf16[256,384]{1,0:T(8,128)(2,1)S(1)}, u32[]{:S(2)}, u32[]{:S(2)}) collective-permute-start(bf16[256,384]{1,0:T(8,128)(2,1)S(1)} %get-tuple-element.83), channel_id=1, source_target_pairs={{0,8},{4,12},{8,0},{12,4},{16,24},{20,28},{24,16},{28,20},{1,9},{5... | collective-permute-start | bytes 589832 | tf_op jit(solution)/shard_map/ppermute | solution.py:51
  25.9 3.2 %collective-permute-start.11 = (bf16[32,256]{1,0:T(8,128)(2,1)S(1)}, bf16[32,256]{1,0:T(8,128)(2,1)S(1)}, u32[]{:S(2)}, u32[]{:S(2)}) collective-permute-start(bf16[32,256]{1,0:T(8,128)(2,1)S(1)} %shard_map.131.refs_0_), channel_id=1, source_target_pairs={{0,3},{1,2},{2,1},{3,0},{4,7},{5,6},{6,5},{7,4},{8,11},{9,10},{10,... | collective-permute-start | bytes 49160 | tf_op jit(solution)/shard_map/ppermute | solution.py:51
  26.0 3.8 %collective-permute-start.10 = (bf16[32,256]{1,0:T(8,128)(2,1)S(1)}, bf16[32,256]{1,0:T(8,128)(2,1)S(1)}, u32[]{:S(2)}, u32[]{:S(2)}) collective-permute-start(bf16[32,256]{1,0:T(8,128)(2,1)S(1)} %shard_map.131.refs_0_), channel_id=1, source_target_pairs={{0,2},{1,3},{2,0},{3,1},{4,6},{5,7},{6,4},{7,5},{8,10},{9,11},{10,... | collective-permute-start | bytes 49160 | tf_op jit(solution)/shard_map/ppermute | solution.py:51
  26.5 3.2 %collective-permute-start.9 = (bf16[32,256]{1,0:T(8,128)(2,1)S(1)}, bf16[32,256]{1,0:T(8,128)(2,1)S(1)}, u32[]{:S(2)}, u32[]{:S(2)}) collective-permute-start(bf16[32,256]{1,0:T(8,128)(2,1)S(1)} %shard_map.131.refs_0_), channel_id=1, source_target_pairs={{0,1},{1,0},{2,3},{3,2},{4,5},{5,4},{6,7},{7,6},{8,9},{9,8},{10,11... | collective-permute-start | bytes 49160 | tf_op jit(solution)/shard_map/ppermute | solution.py:51
  27.9 16.5 %collective-permute-start.5 = (bf16[512,128]{1,0:T(8,128)(2,1)S(1)}, bf16[512,128]{1,0:T(8,128)(2,1)S(1)}, u32[]{:S(2)}, u32[]{:S(2)}) collective-permute-start(bf16[512,128]{1,0:T(8,128)(2,1)S(1)} %shard_map.124), channel_id=1, source_target_pairs={{0,8},{4,12},{8,0},{12,4},{16,24},{20,28},{24,16},{28,20},{1,9},{5... | collective-permute-start | bytes 393224 | tf_op jit(solution)/shard_map/ppermute | solution.py:51
  30.0 5.3 %collective-permute-start.14 = (bf16[128,128]{1,0:T(8,128)(2,1)S(1)}, bf16[128,128]{1,0:T(8,128)(2,1)S(1)}, u32[]{:S(2)}, u32[]{:S(2)}) collective-permute-start(bf16[128,128]{1,0:T(8,128)(2,1)S(1)} %get-tuple-element.87), channel_id=1, source_target_pairs={{0,4},{4,0},{8,12},{12,8},{16,20},{20,16},{24,28},{28,24},{1,5},{5... | collective-permute-start | bytes 98312 | tf_op jit(solution)/shard_map/ppermute | solution.py:51
  31.6 3.9 %collective-permute-start.15 = (bf16[128,128]{1,0:T(8,128)(2,1)S(1)}, bf16[128,128]{1,0:T(8,128)(2,1)S(1)}, u32[]{:S(2)}, u32[]{:S(2)}) collective-permute-start(bf16[128,128]{1,0:T(8,128)(2,1)S(1)} %get-tuple-element.88), channel_id=1, source_target_pairs={{0,8},{4,12},{8,0},{12,4},{16,24},{20,28},{24,16},{28,20},{1,9},{5... | collective-permute-start | bytes 98312 | tf_op jit(solution)/shard_map/ppermute | solution.py:51
  32.4 4.8 %collective-permute-start.16 = (bf16[128,128]{1,0:T(8,128)(2,1)S(1)}, bf16[128,128]{1,0:T(8,128)(2,1)S(1)}, u32[]{:S(2)}, u32[]{:S(2)}) collective-permute-start(bf16[128,128]{1,0:T(8,128)(2,1)S(1)} %get-tuple-element.89), channel_id=1, source_target_pairs={{0,12},{4,8},{8,4},{12,0},{16,28},{20,24},{24,20},{28,16},{1,13},{... | collective-permute-start | bytes 98312 | tf_op jit(solution)/shard_map/ppermute | solution.py:51
  33.6 4.7 %collective-permute-start.13 = (bf16[128,384]{1,0:T(8,128)(2,1)S(1)}, bf16[128,384]{1,0:T(8,128)(2,1)S(1)}, u32[]{:S(2)}, u32[]{:S(2)}) collective-permute-start(bf16[128,384]{1,0:T(8,128)(2,1)S(1)} %get-tuple-element.85), channel_id=1, source_target_pairs={{0,4},{4,0},{8,12},{12,8},{16,20},{20,16},{24,28},{28,24},{1,5},{5... | collective-permute-start | bytes 294920 | tf_op jit(solution)/shard_map/ppermute | solution.py:51
  38.6 7.1 %collective-permute-start.17 = (bf16[64,384]{1,0:T(8,128)(2,1)S(1)}, bf16[64,384]{1,0:T(8,128)(2,1)S(1)}, u32[]{:S(2)}, u32[]{:S(2)}) collective-permute-start(bf16[64,384]{1,0:T(8,128)(2,1)S(1)} %get-tuple-element.91), channel_id=1, source_target_pairs={{0,16},{4,20},{8,24},{12,28},{16,0},{20,4},{24,8},{28,12},{1,17},{... | collective-permute-start | bytes 147464 | tf_op jit(solution)/shard_map/ppermute | solution.py:51
  44.5 5.0 %copy-start.4 = (f32[8,64,128]{2,1,0:T(8,128)S(1)}, f32[8,64,128]{2,1,0:T(8,128)}, u32[]{:S(2)}) copy-start(f32[8,64,128]{2,1,0:T(8,128)} %param.13) | copy-start | bytes 786436
  44.5 5.0 %collective-permute-start.6 = (bf16[512,128]{1,0:T(8,128)(2,1)S(1)}, bf16[512,128]{1,0:T(8,128)(2,1)S(1)}, u32[]{:S(2)}, u32[]{:S(2)}) collective-permute-start(bf16[512,128]{1,0:T(8,128)(2,1)S(1)} %shard_map.125), channel_id=1, source_target_pairs={{0,4},{4,0},{8,12},{12,8},{16,20},{20,16},{24,28},{28,24},{1,5},{5... | collective-permute-start | bytes 393224 | tf_op jit(solution)/shard_map/ppermute | solution.py:51

commit v15 on v14

--- a/solution.py
+++ b/solution.py
@@ -257,28 +257,30 @@
     part_ways(nt(xt_ref[...], sorted_ref[...]), (idx_ref[0] & 2) == 2, send_ref, keep_ref, inner)
 
 
-def far_wgrad_kernel(inner, idx_ref, head_ref, xt_ref, *refs):
-    gathered, (keep_ref, one_ref, two_ref, both_ref, sorted_ref) = refs[:-5], refs[-5:]
+def far_wgrad_kernel(inner, idx_ref, head_ref, xt_ref, near_in, near_got, *refs):
+    gathered, (keep_ref, one_ref, two_ref, both_ref, near_ref, sorted_ref) = refs[:-6], refs[-6:]
     for away, gp_ref in enumerate(gathered):
         own = gp_ref.shape[0]
         sorted_ref[pl.ds(pl.multiple_of((head_ref[0] ^ away) * own, 16), own), :] = gp_ref[...]
     total = nt(xt_ref[...], sorted_ref[...])
     right, upper = (idx_ref[0] & 1) == 1, ((idx_ref[0] >> 1) & 1) == 1
+    cols = near_ref.shape[1]
+    part_ways(near_in[...] + near_got[...].astype(F32), right, one_ref.at[:, :cols], near_ref, inner)
     for e in range(total.shape[0] // (4 * inner)):
         parts = [total[(4 * e + n) * inner:(4 * e + n + 1) * inner] for n in range(4)]
         kept, sent = jnp.where(right, parts[1], parts[0]), jnp.where(right, parts[0], parts[1])
         kept_up, sent_up = jnp.where(right, parts[3], parts[2]), jnp.where(right, parts[2], parts[3])
         at = slice(e * inner, (e + 1) * inner)
         keep_ref[at, :] = jnp.where(upper, kept_up, kept)
-        one_ref[at, :] = jnp.where(upper, sent_up, sent).astype(BF16)
+        one_ref[at, cols:] = jnp.where(upper, sent_up, sent).astype(BF16)
         two_ref[at, :] = jnp.where(upper, kept, kept_up).astype(BF16)
         both_ref[at, :] = jnp.where(upper, sent, sent_up).astype(BF16)
 
 
-def merge_kernel(bit, inner, idx_ref, near_ref, near_got, far_ref, one_ref, two_ref, both_ref, place_ref,
-                 send_ref, keep_ref):
-    far = far_ref[...] + one_ref[...].astype(F32) + two_ref[...].astype(F32) + both_ref[...].astype(F32)
-    total = near_ref[...] + near_got[...].astype(F32) + lax.dot_general(
+def merge_kernel(bit, inner, idx_ref, near_ref, far_ref, one_ref, two_ref, both_ref, place_ref, send_ref, keep_ref):
+    cols = near_ref.shape[1]
+    far = far_ref[...] + one_ref[:, cols:].astype(F32) + two_ref[...].astype(F32) + both_ref[...].astype(F32)
+    total = near_ref[...] + one_ref[:, :cols].astype(F32) + lax.dot_general(
         far, place_ref[...], (((1,), (0,)), ((), ())), preferred_element_type=F32, precision=lax.Precision.HIGHEST)
     part_ways(total, ((idx_ref[0] >> bit) & 1) == 1, send_ref, keep_ref, inner)
 
@@ -473,18 +475,16 @@
         functools.partial(near_wgrad_kernel, head_bits, 2 * per),
         [S((n, cols), BF16), S((n, cols), F32), S((cols, tokens), BF16)],
         [SM] * 2 + [VM] * 2, 2 * tokens * width * cols)(idx, head_idx, xt, near_all)
-    got = swap(send, "seq", 1)
+    near_got = swap(send, "seq", 1)
+
+    far_all = [far_rows] + [exchange(far_rows, "head", away) for away in range(1, n_head)]
     n = n // 2
-    send, near_w = call(
-        functools.partial(fold_kernel, 0, per), [S((n, cols), BF16), S((n, cols), F32)],
-        [SM] + [VM] * 2, n * cols)(idx, near_w, got)
-    near_got = swap(send, "seq", 0)
-
-    far_all = [far_rows] + [exchange(far_rows, "head", away) for away in range(1, n_head)]
-    far_w, one, two, both, far_all = call(
+    part, joined = S((n, far_cols), BF16), S((n, cols + far_cols), BF16)
+    far_w, one, two, both, near_w, far_all = call(
         functools.partial(far_wgrad_kernel, per),
-        [S((n, far_cols), F32)] + [S((n, far_cols), BF16)] * 3 + [S((far_cols, tokens), BF16)],
-        [SM] * 2 + [VM] * (n_head + 1), 2 * tokens * width * far_cols)(idx, head_idx, xt, *far_all)
+        [S((n, far_cols), F32), joined, part, part, S((n, cols), F32), S((far_cols, tokens), BF16)],
+        [SM] * 2 + [VM] * (n_head + 3), 2 * tokens * width * far_cols)(
+            idx, head_idx, xt, near_w, near_got, *far_all)
     far_gots = [exchange(one, "seq", 1), exchange(two, "seq", 2),
                 exchange(both, "seq", 3)]
 
@@ -495,8 +495,8 @@
     place = ((at == col) & (within < far)).astype(F32)
     n = n // 2
     send, keep = call(
-        functools.partial(merge_kernel, 2, per), [S((n, cols), BF16), S((n, cols), F32)], [SM] + [VM] * 7,
-        4 * n * far_cols * cols)(idx, near_w, near_got, far_w, *far_gots, place)
+        functools.partial(merge_kernel, 2, per), [S((n, cols), BF16), S((n, cols), F32)], [SM] + [VM] * 6,
+        4 * n * far_cols * cols)(idx, near_w, far_w, *far_gots, place)
     got = swap(send, "seq", 2)
     for bit in range(3, seq_bits):
         n = n // 2

time: 52.6 us -> 47.5 us (0.903)
  waiting for transfers between devices: 15.4 us -> 11.6 us
  starting transfers between devices: 24.4 us -> 23.1 us
    ppermute x18 -> x17, waiting for transfers between devices: 15.4 us -> 11.6 us  [exchange(): return lax.ppermute(value, axis, pairs)]
    ppermute x18 -> x17, starting transfers between devices: 24.4 us -> 23.1 us  [exchange(): return lax.ppermute(value, axis, pairs)]
  transfers between devices with their start and end apart: 18 -> 17, of which waited for: 11 -> 8; matrix products, arithmetic and copies ran while one was open for 2% -> 0% of each run, Pallas kernels for 12% -> 19%
where the time goes in v15:
time: 47.5 us; the launch traced here: 47.4 us
  starting transfers between devices  23.1 us (49%)
  waiting for transfers between devices  11.6 us (24%)
  Pallas kernels  10.9 us (23%)
  between operations  0.9 us (2%)
  other arithmetic  0.82 us (2%)
    ppermute x17, starting transfers between devices, exchange(): return lax.ppermute(value, axis, pairs)  23.1 us
    ppermute x17, waiting for transfers between devices, exchange(): return lax.ppermute(value, axis, pairs)  11.6 us
    pallas_call x3, Pallas kernels, body(): call(functools.partial(local_kernel, dims, levels, pairs), [S((heads * dv...  2.98 us
    pallas_call x1, Pallas kernels, body(): call(functools.partial(final_kernel, dims, levels, first, seq_bits, cuts)...  2.91 us
    pallas_call x1, Pallas kernels, body(): call(functools.partial(state_kernel, dims), [S((rows, dv), F32), S((rows,...  1.5 us
  transfers between devices with their start and end apart: 17, of which 8 were waited for; matrix products, arithmetic and copies ran while one was open for 0% of the time, Pallas kernels for 19%

profile of v15, /device:TPU:0, one launch (start us, length us, event | category | flops | bytes accessed | tf_op | source)
XLA Modules:
  0.0 47.4 jit_solution(13172021892607446995)
XLA Ops:
  0.6 0.0 copy-start.1
  0.6 0.0 copy-start.3
  0.7 1.5 %shard_map.118 = (f32[512,128]{1,0:T(8,128)S(1)}, bf16[512,128]{1,0:T(8,128)(2,1)S(1)}, bf16[512,384]{1,0:T(8,128)(2,1)S(1)}, bf16[256,512]{1,0:T(8,128)(2,1)S(1)}) custom-call(s32[1]{0:T(128)} %bitcast.idx_ref, s32[1]{0:T(128)} %bitcast.1.head_ref.idx_ref, bf16[256,512]{1,0:T(8,128)(2,1)} %refs_10_.1, bf16[256,1024]{1,0:T(8,128)(2,1)} %refs_11_.1, ...), custom_call_target="tpu_custom_call" | custom-call | flops 33554432 | bytes 2097152 | tf_op jit(solution)/shard_map/pallas_call | solution.py:417
  2.2 0.0 copy-start
  2.2 0.4 shard_map.119
  2.6 0.0 copy-start.2
  2.6 3.0 %collective-permute-start.2 = (bf16[192,256]{1,0:T(8,128)(2,1)S(1)}, bf16[192,256]{1,0:T(8,128)(2,1)S(1)}, u32[]{:S(2)}, u32[]{:S(2)}) collective-permute-start(bf16[192,256]{1,0:T(8,128)(2,1)S(1)} %get-tuple-element.53), channel_id=1, source_target_pairs={{0,2},{1,3},{2,0},{3,1},{4,6},{5,7},{6,4},{7,5},{8,10},{9,11},{10,... | collective-permute-start | bytes 294920 | tf_op jit(solution)/shard_map/ppermute | solution.py:51
  5.6 1.5 %collective-permute-start = (bf16[512,128]{1,0:T(8,128)(2,1)S(1)}, bf16[512,128]{1,0:T(8,128)(2,1)S(1)}, u32[]{:S(2)}, u32[]{:S(2)}) collective-permute-start(bf16[512,128]{1,0:T(8,128)(2,1)S(1)} %get-tuple-element.48), channel_id=1, source_target_pairs={{0,4},{4,0},{8,12},{12,8},{16,20},{20,16},{24,28},{28,24},{1,5},{5... | collective-permute-start | bytes 393224 | tf_op jit(solution)/shard_map/ppermute | solution.py:51
  7.1 1.3 %collective-permute-done.2.got_ref = bf16[192,256]{1,0:T(8,128)(2,1)S(1)} collective-permute-done((bf16[192,256]{1,0:T(8,128)(2,1)S(1)}, bf16[192,256]{1,0:T(8,128)(2,1)S(1)}, u32[]{:S(2)}, u32[]{:S(2)}) %collective-permute-start.2) | collective-permute-done | bytes 98336 | tf_op jit(solution)/shard_map/ppermute | solution.py:51
  8.4 0.1 collective-permute-start.3
  8.5 0.0 copy-done.1
  8.5 0.0 copy-done.3
  8.5 0.0 copy-done
  8.5 0.0 copy-done.2
  8.6 0.8 %shard_map.121.gl_ref = f32[96,256]{1,0:T(8,128)S(1)} custom-call(bf16[256,512]{1,0:T(8,128)(2,1)S(1)} %copy-done.2, bf16[256,512]{1,0:T(8,128)(2,1)S(1)} %copy-done.3, bf16[256,1024]{1,0:T(8,128)(2,1)S(1)} %copy-done.1, bf16[256,1024]{1,0:T(8,128)(2,1)S(1)} %copy-done), custom_call_target="tpu_custom_call" | custom-call | flops 201326592 | bytes 196608 | tf_op jit(solution)/shard_map/pallas_call | solution.py:446
  9.3 0.4 collective-permute-done.3.got_ref
  9.7 0.4 shard_map.122
  10.2 1.9 %collective-permute-start.7 = (bf16[96,256]{1,0:T(8,128)(2,1)S(1)}, bf16[96,256]{1,0:T(8,128)(2,1)S(1)}, u32[]{:S(2)}, u32[]{:S(2)}) collective-permute-start(bf16[96,256]{1,0:T(8,128)(2,1)S(1)} %get-tuple-element.72), channel_id=1, source_target_pairs={{0,2},{1,3},{2,0},{3,1},{4,6},{5,7},{6,4},{7,5},{8,10},{9,11},{10,... | collective-permute-start | bytes 147464 | tf_op jit(solution)/shard_map/ppermute | solution.py:51
  12.1 0.0 collective-permute-done.refs_0_
  12.1 1.6 %collective-permute-start.1 = (bf16[512,128]{1,0:T(8,128)(2,1)S(1)}, bf16[512,128]{1,0:T(8,128)(2,1)S(1)}, u32[]{:S(2)}, u32[]{:S(2)}) collective-permute-start(bf16[512,128]{1,0:T(8,128)(2,1)S(1)} %add_convert_fusion), channel_id=1, source_target_pairs={{0,8},{4,12},{8,0},{12,4},{16,24},{20,28},{24,16},{28,20},{1,9},{5... | collective-permute-start | bytes 393224 | tf_op jit(solution)/shard_map/ppermute | solution.py:51
  13.7 0.6 %collective-permute-done.7 = bf16[96,256]{1,0:T(8,128)(2,1)S(1)} collective-permute-done((bf16[96,256]{1,0:T(8,128)(2,1)S(1)}, bf16[96,256]{1,0:T(8,128)(2,1)S(1)}, u32[]{:S(2)}, u32[]{:S(2)}) %collective-permute-start.7) | collective-permute-done | bytes 49184 | tf_op jit(solution)/shard_map/ppermute | solution.py:51
  14.3 0.1 collective-permute-start.8
  14.4 3.0 %collective-permute-done.1.refs_1_ = bf16[512,128]{1,0:T(8,128)(2,1)S(1)} collective-permute-done((bf16[512,128]{1,0:T(8,128)(2,1)S(1)}, bf16[512,128]{1,0:T(8,128)(2,1)S(1)}, u32[]{:S(2)}, u32[]{:S(2)}) %collective-permute-start.1) | collective-permute-done | bytes 131104 | tf_op jit(solution)/shard_map/ppermute | solution.py:51
  17.5 2.6 %collective-permute-start.4 = (bf16[512,128]{1,0:T(8,128)(2,1)S(1)}, bf16[512,128]{1,0:T(8,128)(2,1)S(1)}, u32[]{:S(2)}, u32[]{:S(2)}) collective-permute-start(bf16[512,128]{1,0:T(8,128)(2,1)S(1)} %shard_map.123), channel_id=1, source_target_pairs={{0,16},{4,20},{8,24},{12,28},{16,0},{20,4},{24,8},{28,12},{1,17},{... | collective-permute-start | bytes 393224 | tf_op jit(solution)/shard_map/ppermute | solution.py:51
  20.1 0.0 collective-permute-done.8
  20.1 0.3 shard_map.129
  20.5 1.6 %collective-permute-start.9 = (bf16[256,384]{1,0:T(8,128)(2,1)S(1)}, bf16[256,384]{1,0:T(8,128)(2,1)S(1)}, u32[]{:S(2)}, u32[]{:S(2)}) collective-permute-start(bf16[256,384]{1,0:T(8,128)(2,1)S(1)} %get-tuple-element.75), channel_id=1, source_target_pairs={{0,8},{4,12},{8,0},{12,4},{16,24},{20,28},{24,16},{28,20},{1,9},{5... | collective-permute-start | bytes 589832 | tf_op jit(solution)/shard_map/ppermute | solution.py:51
  22.1 3.4 %collective-permute-done.4.refs_0_.refs_2_.refs_3_ = bf16[512,128]{1,0:T(8,128)(2,1)S(1)} collective-permute-done((bf16[512,128]{1,0:T(8,128)(2,1)S(1)}, bf16[512,128]{1,0:T(8,128)(2,1)S(1)}, u32[]{:S(2)}, u32[]{:S(2)}) %collective-permute-start.4) | collective-permute-done | bytes 131104 | tf_op jit(solution)/shard_map/ppermute | solution.py:51
  25.5 0.1 shard_map.124
  25.6 0.9 %collective-permute-start.5 = (bf16[512,128]{1,0:T(8,128)(2,1)S(1)}, bf16[512,128]{1,0:T(8,128)(2,1)S(1)}, u32[]{:S(2)}, u32[]{:S(2)}) collective-permute-start(bf16[512,128]{1,0:T(8,128)(2,1)S(1)} %shard_map.124), channel_id=1, source_target_pairs={{0,8},{4,12},{8,0},{12,4},{16,24},{20,28},{24,16},{28,20},{1,9},{5... | collective-permute-start | bytes 393224 | tf_op jit(solution)/shard_map/ppermute | solution.py:51
  26.5 0.5 %shard_map.130.refs_4_ = bf16[32,256]{1,0:T(8,128)(2,1)S(1)} custom-call(s32[1]{0:T(128)} %bitcast.idx_ref, bf16[512,128]{1,0:T(8,128)(2,1)S(1)} %collective-permute-done.refs_0_, bf16[512,128]{1,0:T(8,128)(2,1)S(1)} %collective-permute-done.1.refs_1_, bf16[256,1024]{1,0:T(8,128)(2,1)S(1)} %copy-done, ...), custom_call_target="tpu_custom_call" | custom-call | flops 67108864 | bytes 32768 | tf_op jit(solution)/shard_map/pallas_call | solution.py:461
  27.0 0.3 shard_map.131.refs_0_
  27.3 0.1 collective-permute-start.12
  27.4 0.6 %collective-permute-start.11 = (bf16[32,256]{1,0:T(8,128)(2,1)S(1)}, bf16[32,256]{1,0:T(8,128)(2,1)S(1)}, u32[]{:S(2)}, u32[]{:S(2)}) collective-permute-start(bf16[32,256]{1,0:T(8,128)(2,1)S(1)} %shard_map.131.refs_0_), channel_id=1, source_target_pairs={{0,2},{1,3},{2,0},{3,1},{4,6},{5,7},{6,4},{7,5},{8,10},{9,11},{10,... | collective-permute-start | bytes 49160 | tf_op jit(solution)/shard_map/ppermute | solution.py:51
  28.0 1.2 %collective-permute-start.10 = (bf16[32,256]{1,0:T(8,128)(2,1)S(1)}, bf16[32,256]{1,0:T(8,128)(2,1)S(1)}, u32[]{:S(2)}, u32[]{:S(2)}) collective-permute-start(bf16[32,256]{1,0:T(8,128)(2,1)S(1)} %shard_map.131.refs_0_), channel_id=1, source_target_pairs={{0,1},{1,0},{2,3},{3,2},{4,5},{5,4},{6,7},{7,6},{8,9},{9,8},{10,11... | collective-permute-start | bytes 49160 | tf_op jit(solution)/shard_map/ppermute | solution.py:51
  29.3 1.3 %collective-permute-done.12.refs_3_ = bf16[32,256]{1,0:T(8,128)(2,1)S(1)} collective-permute-done((bf16[32,256]{1,0:T(8,128)(2,1)S(1)}, bf16[32,256]{1,0:T(8,128)(2,1)S(1)}, u32[]{:S(2)}, u32[]{:S(2)}) %collective-permute-start.12) | collective-permute-done | bytes 16416 | tf_op jit(solution)/shard_map/ppermute | solution.py:51
  30.6 0.7 %collective-permute-done.11.refs_2_ = bf16[32,256]{1,0:T(8,128)(2,1)S(1)} collective-permute-done((bf16[32,256]{1,0:T(8,128)(2,1)S(1)}, bf16[32,256]{1,0:T(8,128)(2,1)S(1)}, u32[]{:S(2)}, u32[]{:S(2)}) %collective-permute-start.11) | collective-permute-done | bytes 16416 | tf_op jit(solution)/shard_map/ppermute | solution.py:51
  31.2 0.0 collective-permute-done.10.refs_1_
  31.2 0.0 collective-permute-done.9.near_got
  31.2 0.3 shard_map.132
  31.5 1.6 %collective-permute-start.13 = (bf16[128,512]{1,0:T(8,128)(2,1)S(1)}, bf16[128,512]{1,0:T(8,128)(2,1)S(1)}, u32[]{:S(2)}, u32[]{:S(2)}) collective-permute-start(bf16[128,512]{1,0:T(8,128)(2,1)S(1)} %get-tuple-element.85), channel_id=1, source_target_pairs={{0,4},{4,0},{8,12},{12,8},{16,20},{20,16},{24,28},{28,24},{1,5},{5... | collective-permute-start | bytes 393224 | tf_op jit(solution)/shard_map/ppermute | solution.py:51
  33.1 0.0 collective-permute-done.5.refs_1_.refs_4_
  33.1 0.1 shard_map.125
  33.2 0.6 %collective-permute-start.6 = (bf16[512,128]{1,0:T(8,128)(2,1)S(1)}, bf16[512,128]{1,0:T(8,128)(2,1)S(1)}, u32[]{:S(2)}, u32[]{:S(2)}) collective-permute-start(bf16[512,128]{1,0:T(8,128)(2,1)S(1)} %shard_map.125), channel_id=1, source_target_pairs={{0,4},{4,0},{8,12},{12,8},{16,20},{20,16},{24,28},{28,24},{1,5},{5... | collective-permute-start | bytes 393224 | tf_op jit(solution)/shard_map/ppermute | solution.py:51
  33.7 0.1 fusion.1.refs_26_.place_ref
  33.8 1.2 %collective-permute-start.14 = (bf16[128,128]{1,0:T(8,128)(2,1)S(1)}, bf16[128,128]{1,0:T(8,128)(2,1)S(1)}, u32[]{:S(2)}, u32[]{:S(2)}) collective-permute-start(bf16[128,128]{1,0:T(8,128)(2,1)S(1)} %get-tuple-element.86), channel_id=1, source_target_pairs={{0,8},{4,12},{8,0},{12,4},{16,24},{20,28},{24,16},{28,20},{1,9},{5... | collective-permute-start | bytes 98312 | tf_op jit(solution)/shard_map/ppermute | solution.py:51
  35.1 1.8 %collective-permute-start.15 = (bf16[128,128]{1,0:T(8,128)(2,1)S(1)}, bf16[128,128]{1,0:T(8,128)(2,1)S(1)}, u32[]{:S(2)}, u32[]{:S(2)}) collective-permute-start(bf16[128,128]{1,0:T(8,128)(2,1)S(1)} %get-tuple-element.87), channel_id=1, source_target_pairs={{0,12},{4,8},{8,4},{12,0},{16,28},{20,24},{24,20},{28,16},{1,13},{... | collective-permute-start | bytes 98312 | tf_op jit(solution)/shard_map/ppermute | solution.py:51
  36.9 0.8 %shard_map.127 = (f32[256,256]{1,0:T(8,128)S(1)}, f32[128,256]{1,0:T(8,128)S(1)}, f32[256,128]{1,0:T(8,128)S(1)}, f32[256,256]{1,0:T(8,128)S(1)}) custom-call(bf16[256,512]{1,0:T(8,128)(2,1)S(1)} %copy-done.2, bf16[256,512]{1,0:T(8,128)(2,1)S(1)} %copy-done.3, bf16[256,1024]{1,0:T(8,128)(2,1)S(1)} %copy-done.1, bf16[256,1024]{1,0:T(8,128)(2,1)S(1)} %copy-done, ...), custom_call_target="tpu_custom_call" | custom-call | flops 150994944 | bytes 1572864 | tf_op jit(solution)/shard_map/pallas_call | solution.py:514
  37.7 1.4 %shard_map.128 = (f32[512,256]{1,0:T(8,128)S(1)}, f32[256,256]{1,0:T(8,128)S(1)}, f32[256,256]{1,0:T(8,128)S(1)}, f32[256,512]{1,0:T(8,128)S(1)}) custom-call(bf16[256,512]{1,0:T(8,128)(2,1)S(1)} %copy-done.2, bf16[256,512]{1,0:T(8,128)(2,1)S(1)} %copy-done.3, bf16[256,1024]{1,0:T(8,128)(2,1)S(1)} %copy-done.1, bf16[256,1024]{1,0:T(8,128)(2,1)S(1)} %copy-done, ...), custom_call_target="tpu_custom_call" | custom-call | flops 301989888 | bytes 3145728 | tf_op jit(solution)/shard_map/pallas_call | solution.py:514
  39.1 0.0 collective-permute-done.14.two_ref
  39.1 0.9 %collective-permute-done.15.both_ref = bf16[128,128]{1,0:T(8,128)(2,1)S(1)} collective-permute-done((bf16[128,128]{1,0:T(8,128)(2,1)S(1)}, bf16[128,128]{1,0:T(8,128)(2,1)S(1)}, u32[]{:S(2)}, u32[]{:S(2)}) %collective-permute-start.15) | collective-permute-done | bytes 32800 | tf_op jit(solution)/shard_map/ppermute | solution.py:51
  40.0 0.0 collective-permute-done.13.one_ref
  40.0 0.3 shard_map.134
  40.3 0.0 copy-start.4
  40.3 2.6 %collective-permute-start.16 = (bf16[64,384]{1,0:T(8,128)(2,1)S(1)}, bf16[64,384]{1,0:T(8,128)(2,1)S(1)}, u32[]{:S(2)}, u32[]{:S(2)}) collective-permute-start(bf16[64,384]{1,0:T(8,128)(2,1)S(1)} %get-tuple-element.89), channel_id=1, source_target_pairs={{0,16},{4,20},{8,24},{12,28},{16,0},{20,4},{24,8},{28,12},{1,17},{... | collective-permute-start | bytes 147464 | tf_op jit(solution)/shard_map/ppermute | solution.py:51
  43.0 0.8 %shard_map.126 = (f32[256,256]{1,0:T(8,128)S(1)}, f32[128,256]{1,0:T(8,128)S(1)}, f32[256,128]{1,0:T(8,128)S(1)}, f32[256,256]{1,0:T(8,128)S(1)}) custom-call(bf16[256,512]{1,0:T(8,128)(2,1)S(1)} %copy-done.2, bf16[256,512]{1,0:T(8,128)(2,1)S(1)} %copy-done.3, bf16[256,1024]{1,0:T(8,128)(2,1)S(1)} %copy-done.1, bf16[256,1024]{1,0:T(8,128)(2,1)S(1)} %copy-done, ...), custom_call_target="tpu_custom_call" | custom-call | flops 150994944 | bytes 1572864 | tf_op jit(solution)/shard_map/pallas_call | solution.py:514
  43.8 0.0 collective-permute-done.6.refs_5_
  43.8 0.0 copy-done.4
  43.8 2.9 %shard_map.133 = (bf16[256,1024]{1,0:T(8,128)(2,1)}, bf16[256,512]{1,0:T(8,128)(2,1)}, bf16[256,512]{1,0:T(8,128)(2,1)}, bf16[256,512]{1,0:T(8,128)(2,1)}, bf16[256,1024]{1,0:T(8,128)(2,1)}) custom-call(s32[1]{0:T(128)} %bitcast.idx_ref, bf16[512,128]{1,0:T(8,128)(2,1)S(1)} %collective-permute-done.refs_0_, ...), custom_call_target="tpu_custom_call" | custom-call | flops 402653184 | bytes 3670016 | tf_op jit(solution)/shard_map/pallas_call | solution.py:521
  46.7 0.0 collective-permute-done.16
  46.7 0.7 %convert_add_fusion = f32[64,384]{1,0:T(8,128)} fusion(f32[64,384]{1,0:T(8,128)S(1)} %get-tuple-element.88, bf16[64,384]{1,0:T(8,128)(2,1)S(1)} %collective-permute-done.16), kind=kLoop, calls=%fused_computation.6 | loop fusion | flops 49152 | bytes 245760 | tf_op jit(solution)/shard_map/add | solution.py:507
  (7 shorter events, 0.1 us)
Async XLA Ops:
  0.6 7.9 %copy-start.1 = (bf16[256,1024]{1,0:T(8,128)(2,1)S(1)}, bf16[256,1024]{1,0:T(8,128)(2,1)}, u32[]{:S(2)}) copy-start(bf16[256,1024]{1,0:T(8,128)(2,1)} %refs_11_.1) | copy-start | bytes 1572868
  0.6 7.9 %copy-start.3 = (bf16[256,512]{1,0:T(8,128)(2,1)S(1)}, bf16[256,512]{1,0:T(8,128)(2,1)}, u32[]{:S(2)}) copy-start(bf16[256,512]{1,0:T(8,128)(2,1)} %q_ref.9) | copy-start | bytes 786436
  2.2 6.4 %copy-start = (bf16[256,1024]{1,0:T(8,128)(2,1)S(1)}, bf16[256,1024]{1,0:T(8,128)(2,1)}, u32[]{:S(2)}) copy-start(bf16[256,1024]{1,0:T(8,128)(2,1)} %refs_8_.1) | copy-start | bytes 1572868
  2.6 6.0 %copy-start.2 = (bf16[256,512]{1,0:T(8,128)(2,1)S(1)}, bf16[256,512]{1,0:T(8,128)(2,1)}, u32[]{:S(2)}) copy-start(bf16[256,512]{1,0:T(8,128)(2,1)} %refs_10_.1) | copy-start | bytes 786436
  2.6 5.8 %collective-permute-start.2 = (bf16[192,256]{1,0:T(8,128)(2,1)S(1)}, bf16[192,256]{1,0:T(8,128)(2,1)S(1)}, u32[]{:S(2)}, u32[]{:S(2)}) collective-permute-start(bf16[192,256]{1,0:T(8,128)(2,1)S(1)} %get-tuple-element.53), channel_id=1, source_target_pairs={{0,2},{1,3},{2,0},{3,1},{4,6},{5,7},{6,4},{7,5},{8,10},{9,11},{10,... | collective-permute-start | bytes 294920 | tf_op jit(solution)/shard_map/ppermute | solution.py:51
  5.6 6.5 %collective-permute-start = (bf16[512,128]{1,0:T(8,128)(2,1)S(1)}, bf16[512,128]{1,0:T(8,128)(2,1)S(1)}, u32[]{:S(2)}, u32[]{:S(2)}) collective-permute-start(bf16[512,128]{1,0:T(8,128)(2,1)S(1)} %get-tuple-element.48), channel_id=1, source_target_pairs={{0,4},{4,0},{8,12},{12,8},{16,20},{20,16},{24,28},{28,24},{1,5},{5... | collective-permute-start | bytes 393224 | tf_op jit(solution)/shard_map/ppermute | solution.py:51
  8.4 1.3 %collective-permute-start.3 = (bf16[96,256]{1,0:T(8,128)(2,1)S(1)}, bf16[96,256]{1,0:T(8,128)(2,1)S(1)}, u32[]{:S(2)}, u32[]{:S(2)}) collective-permute-start(bf16[96,256]{1,0:T(8,128)(2,1)S(1)} %get-tuple-element.55), channel_id=1, source_target_pairs={{0,1},{1,0},{2,3},{3,2},{4,5},{5,4},{6,7},{7,6},{8,9},{9,8},{10,11... | collective-permute-start | bytes 147464 | tf_op jit(solution)/shard_map/ppermute | solution.py:51
  10.2 4.2 %collective-permute-start.7 = (bf16[96,256]{1,0:T(8,128)(2,1)S(1)}, bf16[96,256]{1,0:T(8,128)(2,1)S(1)}, u32[]{:S(2)}, u32[]{:S(2)}) collective-permute-start(bf16[96,256]{1,0:T(8,128)(2,1)S(1)} %get-tuple-element.72), channel_id=1, source_target_pairs={{0,2},{1,3},{2,0},{3,1},{4,6},{5,7},{6,4},{7,5},{8,10},{9,11},{10,... | collective-permute-start | bytes 147464 | tf_op jit(solution)/shard_map/ppermute | solution.py:51
  12.1 5.3 %collective-permute-start.1 = (bf16[512,128]{1,0:T(8,128)(2,1)S(1)}, bf16[512,128]{1,0:T(8,128)(2,1)S(1)}, u32[]{:S(2)}, u32[]{:S(2)}) collective-permute-start(bf16[512,128]{1,0:T(8,128)(2,1)S(1)} %add_convert_fusion), channel_id=1, source_target_pairs={{0,8},{4,12},{8,0},{12,4},{16,24},{20,28},{24,16},{28,20},{1,9},{5... | collective-permute-start | bytes 393224 | tf_op jit(solution)/shard_map/ppermute | solution.py:51
  14.3 5.8 %collective-permute-start.8 = (bf16[192,256]{1,0:T(8,128)(2,1)S(1)}, bf16[192,256]{1,0:T(8,128)(2,1)S(1)}, u32[]{:S(2)}, u32[]{:S(2)}) collective-permute-start(bf16[192,256]{1,0:T(8,128)(2,1)S(1)} %pad_maximum_fusion.1), channel_id=1, source_target_pairs={{0,1},{1,0},{2,3},{3,2},{4,5},{5,4},{6,7},{7,6},{8,9},{9,8},{10,11... | collective-permute-start | bytes 294920 | tf_op jit(solution)/shard_map/ppermute | solution.py:51
  17.5 8.1 %collective-permute-start.4 = (bf16[512,128]{1,0:T(8,128)(2,1)S(1)}, bf16[512,128]{1,0:T(8,128)(2,1)S(1)}, u32[]{:S(2)}, u32[]{:S(2)}) collective-permute-start(bf16[512,128]{1,0:T(8,128)(2,1)S(1)} %shard_map.123), channel_id=1, source_target_pairs={{0,16},{4,20},{8,24},{12,28},{16,0},{20,4},{24,8},{28,12},{1,17},{... | collective-permute-start | bytes 393224 | tf_op jit(solution)/shard_map/ppermute | solution.py:51
  20.5 10.8 %collective-permute-start.9 = (bf16[256,384]{1,0:T(8,128)(2,1)S(1)}, bf16[256,384]{1,0:T(8,128)(2,1)S(1)}, u32[]{:S(2)}, u32[]{:S(2)}) collective-permute-start(bf16[256,384]{1,0:T(8,128)(2,1)S(1)} %get-tuple-element.75), channel_id=1, source_target_pairs={{0,8},{4,12},{8,0},{12,4},{16,24},{20,28},{24,16},{28,20},{1,9},{5... | collective-permute-start | bytes 589832 | tf_op jit(solution)/shard_map/ppermute | solution.py:51
  25.6 7.5 %collective-permute-start.5 = (bf16[512,128]{1,0:T(8,128)(2,1)S(1)}, bf16[512,128]{1,0:T(8,128)(2,1)S(1)}, u32[]{:S(2)}, u32[]{:S(2)}) collective-permute-start(bf16[512,128]{1,0:T(8,128)(2,1)S(1)} %shard_map.124), channel_id=1, source_target_pairs={{0,8},{4,12},{8,0},{12,4},{16,24},{20,28},{24,16},{28,20},{1,9},{5... | collective-permute-start | bytes 393224 | tf_op jit(solution)/shard_map/ppermute | solution.py:51
  27.3 3.2 %collective-permute-start.12 = (bf16[32,256]{1,0:T(8,128)(2,1)S(1)}, bf16[32,256]{1,0:T(8,128)(2,1)S(1)}, u32[]{:S(2)}, u32[]{:S(2)}) collective-permute-start(bf16[32,256]{1,0:T(8,128)(2,1)S(1)} %shard_map.131.refs_0_), channel_id=1, source_target_pairs={{0,3},{1,2},{2,1},{3,0},{4,7},{5,6},{6,5},{7,4},{8,11},{9,10},{10,... | collective-permute-start | bytes 49160 | tf_op jit(solution)/shard_map/ppermute | solution.py:51
  27.4 3.8 %collective-permute-start.11 = (bf16[32,256]{1,0:T(8,128)(2,1)S(1)}, bf16[32,256]{1,0:T(8,128)(2,1)S(1)}, u32[]{:S(2)}, u32[]{:S(2)}) collective-permute-start(bf16[32,256]{1,0:T(8,128)(2,1)S(1)} %shard_map.131.refs_0_), channel_id=1, source_target_pairs={{0,2},{1,3},{2,0},{3,1},{4,6},{5,7},{6,4},{7,5},{8,10},{9,11},{10,... | collective-permute-start | bytes 49160 | tf_op jit(solution)/shard_map/ppermute | solution.py:51
  28.0 3.2 %collective-permute-start.10 = (bf16[32,256]{1,0:T(8,128)(2,1)S(1)}, bf16[32,256]{1,0:T(8,128)(2,1)S(1)}, u32[]{:S(2)}, u32[]{:S(2)}) collective-permute-start(bf16[32,256]{1,0:T(8,128)(2,1)S(1)} %shard_map.131.refs_0_), channel_id=1, source_target_pairs={{0,1},{1,0},{2,3},{3,2},{4,5},{5,4},{6,7},{7,6},{8,9},{9,8},{10,11... | collective-permute-start | bytes 49160 | tf_op jit(solution)/shard_map/ppermute | solution.py:51
  31.5 8.5 %collective-permute-start.13 = (bf16[128,512]{1,0:T(8,128)(2,1)S(1)}, bf16[128,512]{1,0:T(8,128)(2,1)S(1)}, u32[]{:S(2)}, u32[]{:S(2)}) collective-permute-start(bf16[128,512]{1,0:T(8,128)(2,1)S(1)} %get-tuple-element.85), channel_id=1, source_target_pairs={{0,4},{4,0},{8,12},{12,8},{16,20},{20,16},{24,28},{28,24},{1,5},{5... | collective-permute-start | bytes 393224 | tf_op jit(solution)/shard_map/ppermute | solution.py:51
  33.2 10.6 %collective-permute-start.6 = (bf16[512,128]{1,0:T(8,128)(2,1)S(1)}, bf16[512,128]{1,0:T(8,128)(2,1)S(1)}, u32[]{:S(2)}, u32[]{:S(2)}) collective-permute-start(bf16[512,128]{1,0:T(8,128)(2,1)S(1)} %shard_map.125), channel_id=1, source_target_pairs={{0,4},{4,0},{8,12},{12,8},{16,20},{20,16},{24,28},{28,24},{1,5},{5... | collective-permute-start | bytes 393224 | tf_op jit(solution)/shard_map/ppermute | solution.py:51
  33.8 5.2 %collective-permute-start.14 = (bf16[128,128]{1,0:T(8,128)(2,1)S(1)}, bf16[128,128]{1,0:T(8,128)(2,1)S(1)}, u32[]{:S(2)}, u32[]{:S(2)}) collective-permute-start(bf16[128,128]{1,0:T(8,128)(2,1)S(1)} %get-tuple-element.86), channel_id=1, source_target_pairs={{0,8},{4,12},{8,0},{12,4},{16,24},{20,28},{24,16},{28,20},{1,9},{5... | collective-permute-start | bytes 98312 | tf_op jit(solution)/shard_map/ppermute | solution.py:51
  35.1 4.9 %collective-permute-start.15 = (bf16[128,128]{1,0:T(8,128)(2,1)S(1)}, bf16[128,128]{1,0:T(8,128)(2,1)S(1)}, u32[]{:S(2)}, u32[]{:S(2)}) collective-permute-start(bf16[128,128]{1,0:T(8,128)(2,1)S(1)} %get-tuple-element.87), channel_id=1, source_target_pairs={{0,12},{4,8},{8,4},{12,0},{16,28},{20,24},{24,20},{28,16},{1,13},{... | collective-permute-start | bytes 98312 | tf_op jit(solution)/shard_map/ppermute | solution.py:51
  40.3 3.4 %copy-start.4 = (f32[8,64,128]{2,1,0:T(8,128)S(1)}, f32[8,64,128]{2,1,0:T(8,128)}, u32[]{:S(2)}) copy-start(f32[8,64,128]{2,1,0:T(8,128)} %param.13) | copy-start | bytes 786436
  40.3 6.4 %collective-permute-start.16 = (bf16[64,384]{1,0:T(8,128)(2,1)S(1)}, bf16[64,384]{1,0:T(8,128)(2,1)S(1)}, u32[]{:S(2)}, u32[]{:S(2)}) collective-permute-start(bf16[64,384]{1,0:T(8,128)(2,1)S(1)} %get-tuple-element.89), channel_id=1, source_target_pairs={{0,16},{4,20},{8,24},{12,28},{16,0},{20,4},{24,8},{28,12},{1,17},{... | collective-permute-start | bytes 147464 | tf_op jit(solution)/shard_map/ppermute | solution.py:51

commit v16 on v15

--- a/solution.py
+++ b/solution.py
@@ -280,8 +280,9 @@
 def merge_kernel(bit, inner, idx_ref, near_ref, far_ref, one_ref, two_ref, both_ref, place_ref, send_ref, keep_ref):
     cols = near_ref.shape[1]
     far = far_ref[...] + one_ref[:, cols:].astype(F32) + two_ref[...].astype(F32) + both_ref[...].astype(F32)
-    total = near_ref[...] + one_ref[:, :cols].astype(F32) + lax.dot_general(
-        far, place_ref[...], (((1,), (0,)), ((), ())), preferred_element_type=F32, precision=lax.Precision.HIGHEST)
+    place = place_ref[...].astype(BF16)
+    high = far.astype(BF16)
+    total = near_ref[...] + one_ref[:, :cols].astype(F32) + nn(high, place) + nn((far - high.astype(F32)).astype(BF16), place)
     part_ways(total, ((idx_ref[0] >> bit) & 1) == 1, send_ref, keep_ref, inner)
 
 

time: 47.5 us -> 47.4 us (level)
  no operation moved by 1% of the time
where the time goes in v16:
time: 47.4 us; the launch traced here: 47.2 us
  starting transfers between devices  23.1 us (49%)
  waiting for transfers between devices  11.6 us (24%)
  Pallas kernels  10.8 us (23%)
  between operations  0.9 us (2%)
  other arithmetic  0.82 us (2%)
    ppermute x17, starting transfers between devices, exchange(): return lax.ppermute(value, axis, pairs)  23.1 us
    ppermute x17, waiting for transfers between devices, exchange(): return lax.ppermute(value, axis, pairs)  11.6 us
    pallas_call x3, Pallas kernels, body(): call(functools.partial(local_kernel, dims, levels, pairs), [S((heads * dv...  2.98 us
    pallas_call x1, Pallas kernels, body(): call(functools.partial(final_kernel, dims, levels, first, seq_bits, cuts)...  2.91 us
    pallas_call x1, Pallas kernels, body(): call(functools.partial(state_kernel, dims), [S((rows, dv), F32), S((rows,...  1.5 us
  transfers between devices with their start and end apart: 17, of which 8 were waited for; matrix products, arithmetic and copies ran while one was open for 0% of the time, Pallas kernels for 19%

profile of v16, /device:TPU:0, one launch (start us, length us, event | category | flops | bytes accessed | tf_op | source)
XLA Modules:
  0.0 47.2 jit_solution(16013730022427907439)
XLA Ops:
  0.6 0.0 copy-start.1
  0.6 0.0 copy-start.3
  0.7 1.5 %shard_map.118 = (f32[512,128]{1,0:T(8,128)S(1)}, bf16[512,128]{1,0:T(8,128)(2,1)S(1)}, bf16[512,384]{1,0:T(8,128)(2,1)S(1)}, bf16[256,512]{1,0:T(8,128)(2,1)S(1)}) custom-call(s32[1]{0:T(128)} %bitcast.idx_ref, s32[1]{0:T(128)} %bitcast.1.head_ref.idx_ref, bf16[256,512]{1,0:T(8,128)(2,1)} %refs_10_.1, bf16[256,1024]{1,0:T(8,128)(2,1)} %refs_11_.1, ...), custom_call_target="tpu_custom_call" | custom-call | flops 33554432 | bytes 2097152 | tf_op jit(solution)/shard_map/pallas_call | solution.py:418
  2.2 0.0 copy-start
  2.2 0.4 shard_map.119
  2.6 0.0 copy-start.2
  2.6 3.0 %collective-permute-start.2 = (bf16[192,256]{1,0:T(8,128)(2,1)S(1)}, bf16[192,256]{1,0:T(8,128)(2,1)S(1)}, u32[]{:S(2)}, u32[]{:S(2)}) collective-permute-start(bf16[192,256]{1,0:T(8,128)(2,1)S(1)} %get-tuple-element.53), channel_id=1, source_target_pairs={{0,2},{1,3},{2,0},{3,1},{4,6},{5,7},{6,4},{7,5},{8,10},{9,11},{10,... | collective-permute-start | bytes 294920 | tf_op jit(solution)/shard_map/ppermute | solution.py:51
  5.6 1.5 %collective-permute-start = (bf16[512,128]{1,0:T(8,128)(2,1)S(1)}, bf16[512,128]{1,0:T(8,128)(2,1)S(1)}, u32[]{:S(2)}, u32[]{:S(2)}) collective-permute-start(bf16[512,128]{1,0:T(8,128)(2,1)S(1)} %get-tuple-element.48), channel_id=1, source_target_pairs={{0,4},{4,0},{8,12},{12,8},{16,20},{20,16},{24,28},{28,24},{1,5},{5... | collective-permute-start | bytes 393224 | tf_op jit(solution)/shard_map/ppermute | solution.py:51
  7.1 1.3 %collective-permute-done.2.got_ref = bf16[192,256]{1,0:T(8,128)(2,1)S(1)} collective-permute-done((bf16[192,256]{1,0:T(8,128)(2,1)S(1)}, bf16[192,256]{1,0:T(8,128)(2,1)S(1)}, u32[]{:S(2)}, u32[]{:S(2)}) %collective-permute-start.2) | collective-permute-done | bytes 98336 | tf_op jit(solution)/shard_map/ppermute | solution.py:51
  8.4 0.1 collective-permute-start.3
  8.5 0.0 copy-done.1
  8.5 0.0 copy-done.3
  8.5 0.0 copy-done
  8.5 0.0 copy-done.2
  8.6 0.8 %shard_map.121.gl_ref = f32[96,256]{1,0:T(8,128)S(1)} custom-call(bf16[256,512]{1,0:T(8,128)(2,1)S(1)} %copy-done.2, bf16[256,512]{1,0:T(8,128)(2,1)S(1)} %copy-done.3, bf16[256,1024]{1,0:T(8,128)(2,1)S(1)} %copy-done.1, bf16[256,1024]{1,0:T(8,128)(2,1)S(1)} %copy-done), custom_call_target="tpu_custom_call" | custom-call | flops 201326592 | bytes 196608 | tf_op jit(solution)/shard_map/pallas_call | solution.py:447
  9.3 0.4 collective-permute-done.3.got_ref
  9.7 0.4 shard_map.122
  10.2 1.9 %collective-permute-start.7 = (bf16[96,256]{1,0:T(8,128)(2,1)S(1)}, bf16[96,256]{1,0:T(8,128)(2,1)S(1)}, u32[]{:S(2)}, u32[]{:S(2)}) collective-permute-start(bf16[96,256]{1,0:T(8,128)(2,1)S(1)} %get-tuple-element.72), channel_id=1, source_target_pairs={{0,2},{1,3},{2,0},{3,1},{4,6},{5,7},{6,4},{7,5},{8,10},{9,11},{10,... | collective-permute-start | bytes 147464 | tf_op jit(solution)/shard_map/ppermute | solution.py:51
  12.1 0.0 collective-permute-done.refs_0_
  12.1 1.6 %collective-permute-start.1 = (bf16[512,128]{1,0:T(8,128)(2,1)S(1)}, bf16[512,128]{1,0:T(8,128)(2,1)S(1)}, u32[]{:S(2)}, u32[]{:S(2)}) collective-permute-start(bf16[512,128]{1,0:T(8,128)(2,1)S(1)} %add_convert_fusion), channel_id=1, source_target_pairs={{0,8},{4,12},{8,0},{12,4},{16,24},{20,28},{24,16},{28,20},{1,9},{5... | collective-permute-start | bytes 393224 | tf_op jit(solution)/shard_map/ppermute | solution.py:51
  13.7 0.6 %collective-permute-done.7 = bf16[96,256]{1,0:T(8,128)(2,1)S(1)} collective-permute-done((bf16[96,256]{1,0:T(8,128)(2,1)S(1)}, bf16[96,256]{1,0:T(8,128)(2,1)S(1)}, u32[]{:S(2)}, u32[]{:S(2)}) %collective-permute-start.7) | collective-permute-done | bytes 49184 | tf_op jit(solution)/shard_map/ppermute | solution.py:51
  14.3 0.1 collective-permute-start.8
  14.4 3.0 %collective-permute-done.1.refs_1_ = bf16[512,128]{1,0:T(8,128)(2,1)S(1)} collective-permute-done((bf16[512,128]{1,0:T(8,128)(2,1)S(1)}, bf16[512,128]{1,0:T(8,128)(2,1)S(1)}, u32[]{:S(2)}, u32[]{:S(2)}) %collective-permute-start.1) | collective-permute-done | bytes 131104 | tf_op jit(solution)/shard_map/ppermute | solution.py:51
  17.5 2.6 %collective-permute-start.4 = (bf16[512,128]{1,0:T(8,128)(2,1)S(1)}, bf16[512,128]{1,0:T(8,128)(2,1)S(1)}, u32[]{:S(2)}, u32[]{:S(2)}) collective-permute-start(bf16[512,128]{1,0:T(8,128)(2,1)S(1)} %shard_map.123), channel_id=1, source_target_pairs={{0,16},{4,20},{8,24},{12,28},{16,0},{20,4},{24,8},{28,12},{1,17},{... | collective-permute-start | bytes 393224 | tf_op jit(solution)/shard_map/ppermute | solution.py:51
  20.1 0.0 collective-permute-done.8
  20.1 0.3 shard_map.129
  20.5 1.6 %collective-permute-start.9 = (bf16[256,384]{1,0:T(8,128)(2,1)S(1)}, bf16[256,384]{1,0:T(8,128)(2,1)S(1)}, u32[]{:S(2)}, u32[]{:S(2)}) collective-permute-start(bf16[256,384]{1,0:T(8,128)(2,1)S(1)} %get-tuple-element.75), channel_id=1, source_target_pairs={{0,8},{4,12},{8,0},{12,4},{16,24},{20,28},{24,16},{28,20},{1,9},{5... | collective-permute-start | bytes 589832 | tf_op jit(solution)/shard_map/ppermute | solution.py:51
  22.1 3.4 %collective-permute-done.4.refs_0_.refs_2_.refs_3_ = bf16[512,128]{1,0:T(8,128)(2,1)S(1)} collective-permute-done((bf16[512,128]{1,0:T(8,128)(2,1)S(1)}, bf16[512,128]{1,0:T(8,128)(2,1)S(1)}, u32[]{:S(2)}, u32[]{:S(2)}) %collective-permute-start.4) | collective-permute-done | bytes 131104 | tf_op jit(solution)/shard_map/ppermute | solution.py:51
  25.5 0.1 shard_map.124
  25.6 0.9 %collective-permute-start.5 = (bf16[512,128]{1,0:T(8,128)(2,1)S(1)}, bf16[512,128]{1,0:T(8,128)(2,1)S(1)}, u32[]{:S(2)}, u32[]{:S(2)}) collective-permute-start(bf16[512,128]{1,0:T(8,128)(2,1)S(1)} %shard_map.124), channel_id=1, source_target_pairs={{0,8},{4,12},{8,0},{12,4},{16,24},{20,28},{24,16},{28,20},{1,9},{5... | collective-permute-start | bytes 393224 | tf_op jit(solution)/shard_map/ppermute | solution.py:51
  26.5 0.5 %shard_map.130.refs_4_ = bf16[32,256]{1,0:T(8,128)(2,1)S(1)} custom-call(s32[1]{0:T(128)} %bitcast.idx_ref, bf16[512,128]{1,0:T(8,128)(2,1)S(1)} %collective-permute-done.refs_0_, bf16[512,128]{1,0:T(8,128)(2,1)S(1)} %collective-permute-done.1.refs_1_, bf16[256,1024]{1,0:T(8,128)(2,1)S(1)} %copy-done, ...), custom_call_target="tpu_custom_call" | custom-call | flops 67108864 | bytes 32768 | tf_op jit(solution)/shard_map/pallas_call | solution.py:462
  27.0 0.3 shard_map.131.refs_0_
  27.3 0.1 collective-permute-start.12
  27.4 0.6 %collective-permute-start.11 = (bf16[32,256]{1,0:T(8,128)(2,1)S(1)}, bf16[32,256]{1,0:T(8,128)(2,1)S(1)}, u32[]{:S(2)}, u32[]{:S(2)}) collective-permute-start(bf16[32,256]{1,0:T(8,128)(2,1)S(1)} %shard_map.131.refs_0_), channel_id=1, source_target_pairs={{0,2},{1,3},{2,0},{3,1},{4,6},{5,7},{6,4},{7,5},{8,10},{9,11},{10,... | collective-permute-start | bytes 49160 | tf_op jit(solution)/shard_map/ppermute | solution.py:51
  28.0 1.2 %collective-permute-start.10 = (bf16[32,256]{1,0:T(8,128)(2,1)S(1)}, bf16[32,256]{1,0:T(8,128)(2,1)S(1)}, u32[]{:S(2)}, u32[]{:S(2)}) collective-permute-start(bf16[32,256]{1,0:T(8,128)(2,1)S(1)} %shard_map.131.refs_0_), channel_id=1, source_target_pairs={{0,1},{1,0},{2,3},{3,2},{4,5},{5,4},{6,7},{7,6},{8,9},{9,8},{10,11... | collective-permute-start | bytes 49160 | tf_op jit(solution)/shard_map/ppermute | solution.py:51
  29.3 1.3 %collective-permute-done.12.refs_3_ = bf16[32,256]{1,0:T(8,128)(2,1)S(1)} collective-permute-done((bf16[32,256]{1,0:T(8,128)(2,1)S(1)}, bf16[32,256]{1,0:T(8,128)(2,1)S(1)}, u32[]{:S(2)}, u32[]{:S(2)}) %collective-permute-start.12) | collective-permute-done | bytes 16416 | tf_op jit(solution)/shard_map/ppermute | solution.py:51
  30.6 0.7 %collective-permute-done.11.refs_2_ = bf16[32,256]{1,0:T(8,128)(2,1)S(1)} collective-permute-done((bf16[32,256]{1,0:T(8,128)(2,1)S(1)}, bf16[32,256]{1,0:T(8,128)(2,1)S(1)}, u32[]{:S(2)}, u32[]{:S(2)}) %collective-permute-start.11) | collective-permute-done | bytes 16416 | tf_op jit(solution)/shard_map/ppermute | solution.py:51
  31.2 0.0 collective-permute-done.10.refs_1_
  31.2 0.0 collective-permute-done.9.near_got
  31.2 0.3 shard_map.132
  31.5 1.6 %collective-permute-start.13 = (bf16[128,512]{1,0:T(8,128)(2,1)S(1)}, bf16[128,512]{1,0:T(8,128)(2,1)S(1)}, u32[]{:S(2)}, u32[]{:S(2)}) collective-permute-start(bf16[128,512]{1,0:T(8,128)(2,1)S(1)} %get-tuple-element.85), channel_id=1, source_target_pairs={{0,4},{4,0},{8,12},{12,8},{16,20},{20,16},{24,28},{28,24},{1,5},{5... | collective-permute-start | bytes 393224 | tf_op jit(solution)/shard_map/ppermute | solution.py:51
  33.1 0.0 collective-permute-done.5.refs_1_.refs_4_
  33.1 0.1 shard_map.125
  33.2 0.6 %collective-permute-start.6 = (bf16[512,128]{1,0:T(8,128)(2,1)S(1)}, bf16[512,128]{1,0:T(8,128)(2,1)S(1)}, u32[]{:S(2)}, u32[]{:S(2)}) collective-permute-start(bf16[512,128]{1,0:T(8,128)(2,1)S(1)} %shard_map.125), channel_id=1, source_target_pairs={{0,4},{4,0},{8,12},{12,8},{16,20},{20,16},{24,28},{28,24},{1,5},{5... | collective-permute-start | bytes 393224 | tf_op jit(solution)/shard_map/ppermute | solution.py:51
  33.7 0.1 fusion.1.refs_26_.place_ref
  33.8 1.2 %collective-permute-start.14 = (bf16[128,128]{1,0:T(8,128)(2,1)S(1)}, bf16[128,128]{1,0:T(8,128)(2,1)S(1)}, u32[]{:S(2)}, u32[]{:S(2)}) collective-permute-start(bf16[128,128]{1,0:T(8,128)(2,1)S(1)} %get-tuple-element.86), channel_id=1, source_target_pairs={{0,8},{4,12},{8,0},{12,4},{16,24},{20,28},{24,16},{28,20},{1,9},{5... | collective-permute-start | bytes 98312 | tf_op jit(solution)/shard_map/ppermute | solution.py:51
  35.1 1.8 %collective-permute-start.15 = (bf16[128,128]{1,0:T(8,128)(2,1)S(1)}, bf16[128,128]{1,0:T(8,128)(2,1)S(1)}, u32[]{:S(2)}, u32[]{:S(2)}) collective-permute-start(bf16[128,128]{1,0:T(8,128)(2,1)S(1)} %get-tuple-element.87), channel_id=1, source_target_pairs={{0,12},{4,8},{8,4},{12,0},{16,28},{20,24},{24,20},{28,16},{1,13},{... | collective-permute-start | bytes 98312 | tf_op jit(solution)/shard_map/ppermute | solution.py:51
  36.9 0.8 %shard_map.127 = (f32[256,256]{1,0:T(8,128)S(1)}, f32[128,256]{1,0:T(8,128)S(1)}, f32[256,128]{1,0:T(8,128)S(1)}, f32[256,256]{1,0:T(8,128)S(1)}) custom-call(bf16[256,512]{1,0:T(8,128)(2,1)S(1)} %copy-done.2, bf16[256,512]{1,0:T(8,128)(2,1)S(1)} %copy-done.3, bf16[256,1024]{1,0:T(8,128)(2,1)S(1)} %copy-done.1, bf16[256,1024]{1,0:T(8,128)(2,1)S(1)} %copy-done, ...), custom_call_target="tpu_custom_call" | custom-call | flops 150994944 | bytes 1572864 | tf_op jit(solution)/shard_map/pallas_call | solution.py:515
  37.7 1.4 %shard_map.128 = (f32[512,256]{1,0:T(8,128)S(1)}, f32[256,256]{1,0:T(8,128)S(1)}, f32[256,256]{1,0:T(8,128)S(1)}, f32[256,512]{1,0:T(8,128)S(1)}) custom-call(bf16[256,512]{1,0:T(8,128)(2,1)S(1)} %copy-done.2, bf16[256,512]{1,0:T(8,128)(2,1)S(1)} %copy-done.3, bf16[256,1024]{1,0:T(8,128)(2,1)S(1)} %copy-done.1, bf16[256,1024]{1,0:T(8,128)(2,1)S(1)} %copy-done, ...), custom_call_target="tpu_custom_call" | custom-call | flops 301989888 | bytes 3145728 | tf_op jit(solution)/shard_map/pallas_call | solution.py:515
  39.1 0.0 collective-permute-done.14.two_ref
  39.1 0.9 %collective-permute-done.15.both_ref = bf16[128,128]{1,0:T(8,128)(2,1)S(1)} collective-permute-done((bf16[128,128]{1,0:T(8,128)(2,1)S(1)}, bf16[128,128]{1,0:T(8,128)(2,1)S(1)}, u32[]{:S(2)}, u32[]{:S(2)}) %collective-permute-start.15) | collective-permute-done | bytes 32800 | tf_op jit(solution)/shard_map/ppermute | solution.py:51
  40.0 0.0 collective-permute-done.13.one_ref
  40.0 0.2 shard_map.134
  40.2 0.0 copy-start.4
  40.2 2.6 %collective-permute-start.16 = (bf16[64,384]{1,0:T(8,128)(2,1)S(1)}, bf16[64,384]{1,0:T(8,128)(2,1)S(1)}, u32[]{:S(2)}, u32[]{:S(2)}) collective-permute-start(bf16[64,384]{1,0:T(8,128)(2,1)S(1)} %get-tuple-element.89), channel_id=1, source_target_pairs={{0,16},{4,20},{8,24},{12,28},{16,0},{20,4},{24,8},{28,12},{1,17},{... | collective-permute-start | bytes 147464 | tf_op jit(solution)/shard_map/ppermute | solution.py:51
  42.8 0.8 %shard_map.126 = (f32[256,256]{1,0:T(8,128)S(1)}, f32[128,256]{1,0:T(8,128)S(1)}, f32[256,128]{1,0:T(8,128)S(1)}, f32[256,256]{1,0:T(8,128)S(1)}) custom-call(bf16[256,512]{1,0:T(8,128)(2,1)S(1)} %copy-done.2, bf16[256,512]{1,0:T(8,128)(2,1)S(1)} %copy-done.3, bf16[256,1024]{1,0:T(8,128)(2,1)S(1)} %copy-done.1, bf16[256,1024]{1,0:T(8,128)(2,1)S(1)} %copy-done, ...), custom_call_target="tpu_custom_call" | custom-call | flops 150994944 | bytes 1572864 | tf_op jit(solution)/shard_map/pallas_call | solution.py:515
  43.6 0.0 collective-permute-done.6.refs_5_
  43.7 0.0 copy-done.4
  43.7 2.9 %shard_map.133 = (bf16[256,1024]{1,0:T(8,128)(2,1)}, bf16[256,512]{1,0:T(8,128)(2,1)}, bf16[256,512]{1,0:T(8,128)(2,1)}, bf16[256,512]{1,0:T(8,128)(2,1)}, bf16[256,1024]{1,0:T(8,128)(2,1)}) custom-call(s32[1]{0:T(128)} %bitcast.idx_ref, bf16[512,128]{1,0:T(8,128)(2,1)S(1)} %collective-permute-done.refs_0_, ...), custom_call_target="tpu_custom_call" | custom-call | flops 402653184 | bytes 3670016 | tf_op jit(solution)/shard_map/pallas_call | solution.py:522
  46.6 0.0 collective-permute-done.16
  46.6 0.7 %convert_add_fusion = f32[64,384]{1,0:T(8,128)} fusion(f32[64,384]{1,0:T(8,128)S(1)} %get-tuple-element.88, bf16[64,384]{1,0:T(8,128)(2,1)S(1)} %collective-permute-done.16), kind=kLoop, calls=%fused_computation.6 | loop fusion | flops 49152 | bytes 245760 | tf_op jit(solution)/shard_map/add | solution.py:508
  (7 shorter events, 0.1 us)
Async XLA Ops:
  0.6 7.9 %copy-start.1 = (bf16[256,1024]{1,0:T(8,128)(2,1)S(1)}, bf16[256,1024]{1,0:T(8,128)(2,1)}, u32[]{:S(2)}) copy-start(bf16[256,1024]{1,0:T(8,128)(2,1)} %refs_11_.1) | copy-start | bytes 1572868
  0.6 7.9 %copy-start.3 = (bf16[256,512]{1,0:T(8,128)(2,1)S(1)}, bf16[256,512]{1,0:T(8,128)(2,1)}, u32[]{:S(2)}) copy-start(bf16[256,512]{1,0:T(8,128)(2,1)} %q_ref.9) | copy-start | bytes 786436
  2.2 6.4 %copy-start = (bf16[256,1024]{1,0:T(8,128)(2,1)S(1)}, bf16[256,1024]{1,0:T(8,128)(2,1)}, u32[]{:S(2)}) copy-start(bf16[256,1024]{1,0:T(8,128)(2,1)} %refs_8_.1) | copy-start | bytes 1572868
  2.6 6.0 %copy-start.2 = (bf16[256,512]{1,0:T(8,128)(2,1)S(1)}, bf16[256,512]{1,0:T(8,128)(2,1)}, u32[]{:S(2)}) copy-start(bf16[256,512]{1,0:T(8,128)(2,1)} %refs_10_.1) | copy-start | bytes 786436
  2.6 5.8 %collective-permute-start.2 = (bf16[192,256]{1,0:T(8,128)(2,1)S(1)}, bf16[192,256]{1,0:T(8,128)(2,1)S(1)}, u32[]{:S(2)}, u32[]{:S(2)}) collective-permute-start(bf16[192,256]{1,0:T(8,128)(2,1)S(1)} %get-tuple-element.53), channel_id=1, source_target_pairs={{0,2},{1,3},{2,0},{3,1},{4,6},{5,7},{6,4},{7,5},{8,10},{9,11},{10,... | collective-permute-start | bytes 294920 | tf_op jit(solution)/shard_map/ppermute | solution.py:51
  5.6 6.5 %collective-permute-start = (bf16[512,128]{1,0:T(8,128)(2,1)S(1)}, bf16[512,128]{1,0:T(8,128)(2,1)S(1)}, u32[]{:S(2)}, u32[]{:S(2)}) collective-permute-start(bf16[512,128]{1,0:T(8,128)(2,1)S(1)} %get-tuple-element.48), channel_id=1, source_target_pairs={{0,4},{4,0},{8,12},{12,8},{16,20},{20,16},{24,28},{28,24},{1,5},{5... | collective-permute-start | bytes 393224 | tf_op jit(solution)/shard_map/ppermute | solution.py:51
  8.4 1.3 %collective-permute-start.3 = (bf16[96,256]{1,0:T(8,128)(2,1)S(1)}, bf16[96,256]{1,0:T(8,128)(2,1)S(1)}, u32[]{:S(2)}, u32[]{:S(2)}) collective-permute-start(bf16[96,256]{1,0:T(8,128)(2,1)S(1)} %get-tuple-element.55), channel_id=1, source_target_pairs={{0,1},{1,0},{2,3},{3,2},{4,5},{5,4},{6,7},{7,6},{8,9},{9,8},{10,11... | collective-permute-start | bytes 147464 | tf_op jit(solution)/shard_map/ppermute | solution.py:51
  10.2 4.2 %collective-permute-start.7 = (bf16[96,256]{1,0:T(8,128)(2,1)S(1)}, bf16[96,256]{1,0:T(8,128)(2,1)S(1)}, u32[]{:S(2)}, u32[]{:S(2)}) collective-permute-start(bf16[96,256]{1,0:T(8,128)(2,1)S(1)} %get-tuple-element.72), channel_id=1, source_target_pairs={{0,2},{1,3},{2,0},{3,1},{4,6},{5,7},{6,4},{7,5},{8,10},{9,11},{10,... | collective-permute-start | bytes 147464 | tf_op jit(solution)/shard_map/ppermute | solution.py:51
  12.1 5.3 %collective-permute-start.1 = (bf16[512,128]{1,0:T(8,128)(2,1)S(1)}, bf16[512,128]{1,0:T(8,128)(2,1)S(1)}, u32[]{:S(2)}, u32[]{:S(2)}) collective-permute-start(bf16[512,128]{1,0:T(8,128)(2,1)S(1)} %add_convert_fusion), channel_id=1, source_target_pairs={{0,8},{4,12},{8,0},{12,4},{16,24},{20,28},{24,16},{28,20},{1,9},{5... | collective-permute-start | bytes 393224 | tf_op jit(solution)/shard_map/ppermute | solution.py:51
  14.3 5.8 %collective-permute-start.8 = (bf16[192,256]{1,0:T(8,128)(2,1)S(1)}, bf16[192,256]{1,0:T(8,128)(2,1)S(1)}, u32[]{:S(2)}, u32[]{:S(2)}) collective-permute-start(bf16[192,256]{1,0:T(8,128)(2,1)S(1)} %pad_maximum_fusion.1), channel_id=1, source_target_pairs={{0,1},{1,0},{2,3},{3,2},{4,5},{5,4},{6,7},{7,6},{8,9},{9,8},{10,11... | collective-permute-start | bytes 294920 | tf_op jit(solution)/shard_map/ppermute | solution.py:51
  17.5 8.1 %collective-permute-start.4 = (bf16[512,128]{1,0:T(8,128)(2,1)S(1)}, bf16[512,128]{1,0:T(8,128)(2,1)S(1)}, u32[]{:S(2)}, u32[]{:S(2)}) collective-permute-start(bf16[512,128]{1,0:T(8,128)(2,1)S(1)} %shard_map.123), channel_id=1, source_target_pairs={{0,16},{4,20},{8,24},{12,28},{16,0},{20,4},{24,8},{28,12},{1,17},{... | collective-permute-start | bytes 393224 | tf_op jit(solution)/shard_map/ppermute | solution.py:51
  20.5 10.8 %collective-permute-start.9 = (bf16[256,384]{1,0:T(8,128)(2,1)S(1)}, bf16[256,384]{1,0:T(8,128)(2,1)S(1)}, u32[]{:S(2)}, u32[]{:S(2)}) collective-permute-start(bf16[256,384]{1,0:T(8,128)(2,1)S(1)} %get-tuple-element.75), channel_id=1, source_target_pairs={{0,8},{4,12},{8,0},{12,4},{16,24},{20,28},{24,16},{28,20},{1,9},{5... | collective-permute-start | bytes 589832 | tf_op jit(solution)/shard_map/ppermute | solution.py:51
  25.6 7.5 %collective-permute-start.5 = (bf16[512,128]{1,0:T(8,128)(2,1)S(1)}, bf16[512,128]{1,0:T(8,128)(2,1)S(1)}, u32[]{:S(2)}, u32[]{:S(2)}) collective-permute-start(bf16[512,128]{1,0:T(8,128)(2,1)S(1)} %shard_map.124), channel_id=1, source_target_pairs={{0,8},{4,12},{8,0},{12,4},{16,24},{20,28},{24,16},{28,20},{1,9},{5... | collective-permute-start | bytes 393224 | tf_op jit(solution)/shard_map/ppermute | solution.py:51
  27.3 3.2 %collective-permute-start.12 = (bf16[32,256]{1,0:T(8,128)(2,1)S(1)}, bf16[32,256]{1,0:T(8,128)(2,1)S(1)}, u32[]{:S(2)}, u32[]{:S(2)}) collective-permute-start(bf16[32,256]{1,0:T(8,128)(2,1)S(1)} %shard_map.131.refs_0_), channel_id=1, source_target_pairs={{0,3},{1,2},{2,1},{3,0},{4,7},{5,6},{6,5},{7,4},{8,11},{9,10},{10,... | collective-permute-start | bytes 49160 | tf_op jit(solution)/shard_map/ppermute | solution.py:51
  27.4 3.8 %collective-permute-start.11 = (bf16[32,256]{1,0:T(8,128)(2,1)S(1)}, bf16[32,256]{1,0:T(8,128)(2,1)S(1)}, u32[]{:S(2)}, u32[]{:S(2)}) collective-permute-start(bf16[32,256]{1,0:T(8,128)(2,1)S(1)} %shard_map.131.refs_0_), channel_id=1, source_target_pairs={{0,2},{1,3},{2,0},{3,1},{4,6},{5,7},{6,4},{7,5},{8,10},{9,11},{10,... | collective-permute-start | bytes 49160 | tf_op jit(solution)/shard_map/ppermute | solution.py:51
  28.0 3.2 %collective-permute-start.10 = (bf16[32,256]{1,0:T(8,128)(2,1)S(1)}, bf16[32,256]{1,0:T(8,128)(2,1)S(1)}, u32[]{:S(2)}, u32[]{:S(2)}) collective-permute-start(bf16[32,256]{1,0:T(8,128)(2,1)S(1)} %shard_map.131.refs_0_), channel_id=1, source_target_pairs={{0,1},{1,0},{2,3},{3,2},{4,5},{5,4},{6,7},{7,6},{8,9},{9,8},{10,11... | collective-permute-start | bytes 49160 | tf_op jit(solution)/shard_map/ppermute | solution.py:51
  31.5 8.5 %collective-permute-start.13 = (bf16[128,512]{1,0:T(8,128)(2,1)S(1)}, bf16[128,512]{1,0:T(8,128)(2,1)S(1)}, u32[]{:S(2)}, u32[]{:S(2)}) collective-permute-start(bf16[128,512]{1,0:T(8,128)(2,1)S(1)} %get-tuple-element.85), channel_id=1, source_target_pairs={{0,4},{4,0},{8,12},{12,8},{16,20},{20,16},{24,28},{28,24},{1,5},{5... | collective-permute-start | bytes 393224 | tf_op jit(solution)/shard_map/ppermute | solution.py:51
  33.2 10.5 %collective-permute-start.6 = (bf16[512,128]{1,0:T(8,128)(2,1)S(1)}, bf16[512,128]{1,0:T(8,128)(2,1)S(1)}, u32[]{:S(2)}, u32[]{:S(2)}) collective-permute-start(bf16[512,128]{1,0:T(8,128)(2,1)S(1)} %shard_map.125), channel_id=1, source_target_pairs={{0,4},{4,0},{8,12},{12,8},{16,20},{20,16},{24,28},{28,24},{1,5},{5... | collective-permute-start | bytes 393224 | tf_op jit(solution)/shard_map/ppermute | solution.py:51
  33.8 5.2 %collective-permute-start.14 = (bf16[128,128]{1,0:T(8,128)(2,1)S(1)}, bf16[128,128]{1,0:T(8,128)(2,1)S(1)}, u32[]{:S(2)}, u32[]{:S(2)}) collective-permute-start(bf16[128,128]{1,0:T(8,128)(2,1)S(1)} %get-tuple-element.86), channel_id=1, source_target_pairs={{0,8},{4,12},{8,0},{12,4},{16,24},{20,28},{24,16},{28,20},{1,9},{5... | collective-permute-start | bytes 98312 | tf_op jit(solution)/shard_map/ppermute | solution.py:51
  35.1 4.9 %collective-permute-start.15 = (bf16[128,128]{1,0:T(8,128)(2,1)S(1)}, bf16[128,128]{1,0:T(8,128)(2,1)S(1)}, u32[]{:S(2)}, u32[]{:S(2)}) collective-permute-start(bf16[128,128]{1,0:T(8,128)(2,1)S(1)} %get-tuple-element.87), channel_id=1, source_target_pairs={{0,12},{4,8},{8,4},{12,0},{16,28},{20,24},{24,20},{28,16},{1,13},{... | collective-permute-start | bytes 98312 | tf_op jit(solution)/shard_map/ppermute | solution.py:51
  40.2 3.4 %copy-start.4 = (f32[8,64,128]{2,1,0:T(8,128)S(1)}, f32[8,64,128]{2,1,0:T(8,128)}, u32[]{:S(2)}) copy-start(f32[8,64,128]{2,1,0:T(8,128)} %param.13) | copy-start | bytes 786436
  40.2 6.4 %collective-permute-start.16 = (bf16[64,384]{1,0:T(8,128)(2,1)S(1)}, bf16[64,384]{1,0:T(8,128)(2,1)S(1)}, u32[]{:S(2)}, u32[]{:S(2)}) collective-permute-start(bf16[64,384]{1,0:T(8,128)(2,1)S(1)} %get-tuple-element.89), channel_id=1, source_target_pairs={{0,16},{4,20},{8,24},{12,28},{16,0},{20,4},{24,8},{28,12},{1,17},{... | collective-permute-start | bytes 147464 | tf_op jit(solution)/shard_map/ppermute | solution.py:51

commit v17 on v16

--- a/solution.py
+++ b/solution.py
@@ -113,7 +113,9 @@
             scaled = jnp.concatenate(
                 [wide[j * dk:(j + 1) * dk] * lw_ref[h * levels + first + m:h * levels + first + m + 1, :]
                  for m in range(count)], axis=0)
-            grad = nn(scaled.astype(BF16), g_ref[:, h * dv:(h + 1) * dv])
+            high = scaled.astype(BF16)
+            gh = g_ref[:, h * dv:(h + 1) * dv]
+            grad = nn(high, gh) + nn((scaled - high.astype(F32)).astype(BF16), gh)
             for m in range(count):
                 gu_ref[m, h * dk:(h + 1) * dk, :] = grad[m * dk:(m + 1) * dk].astype(BF16)
 
@@ -369,18 +371,20 @@
         total = ds_ref[pair_rows, :] + jnp.where(upper, 0.0, gots[0][pair_rows, :].astype(F32))
         for got in gots[1:]:
             total = total + got[pair_rows, :].astype(F32)
-        adj = [total[:dk].astype(BF16), total[dk:].astype(BF16)]
+        high = total.astype(BF16)
+        low = (total - high.astype(F32)).astype(BF16)
         kp = k_ref[:, pair * 2 * dk:(pair + 1) * 2 * dk]
         dkl_ref, p = piece(2, pair)
         dvl_ref, p = piece(3, pair)
         total = dkl_ref[:, p * 2 * dk:(p + 1) * 2 * dk]
         for j in range(2):
             h = 2 * pair + j
-            padded = jnp.concatenate([adj[j], zero] if j == 0 else [zero, adj[j]], axis=0)
+            padded, rest = [jnp.concatenate([adj[:dk], zero] if j == 0 else [zero, adj[dk:]], axis=0)
+                            for adj in (high, low)]
             cols = slice(h * dv, (h + 1) * dv)
-            total = total + nt(v_ref[:, cols], padded)
+            total = total + nt(v_ref[:, cols], padded) + nt(v_ref[:, cols], rest)
             near = dvl_ref[:, (2 * p + j) * dv:(2 * p + j + 1) * dv]
-            dv_ref[:, cols] = (near + nn(kp, padded)).astype(BF16)
+            dv_ref[:, cols] = (near + nn(kp, padded) + nn(kp, rest)).astype(BF16)
         dk_ref[:, pair * 2 * dk:(pair + 1) * 2 * dk] = total.astype(BF16)
         send(dv_ref, dv_hbm, slice(2 * pair * dv, (2 * pair + 2) * dv))
         send(dk_ref, dk_hbm, slice(pair * 2 * dk, (pair + 1) * 2 * dk))

time: 47.4 us -> 47.6 us (level)
  no operation moved by 1% of the time
where the time goes in v17:
time: 47.6 us; the launch traced here: 47.5 us
  starting transfers between devices  23.1 us (49%)
  waiting for transfers between devices  11.6 us (24%)
  Pallas kernels  11 us (23%)
  between operations  0.9 us (2%)
  other arithmetic  0.82 us (2%)
    ppermute x17, starting transfers between devices, exchange(): return lax.ppermute(value, axis, pairs)  23.1 us
    ppermute x17, waiting for transfers between devices, exchange(): return lax.ppermute(value, axis, pairs)  11.6 us
    pallas_call x3, Pallas kernels, body(): call(functools.partial(local_kernel, dims, levels, pairs), [S((heads * dv...  2.97 us
    pallas_call x1, Pallas kernels, body(): call(functools.partial(final_kernel, dims, levels, first, seq_bits, cuts)...  2.93 us
    pallas_call x1, Pallas kernels, body(): call(functools.partial(state_kernel, dims), [S((rows, dv), F32), S((rows,...  1.5 us
  transfers between devices with their start and end apart: 17, of which 8 were waited for; matrix products, arithmetic and copies ran while one was open for 0% of the time, Pallas kernels for 19%

profile of v17, /device:TPU:0, one launch (start us, length us, event | category | flops | bytes accessed | tf_op | source)
XLA Modules:
  0.0 47.5 jit_solution(5088379502266539324)
XLA Ops:
  0.6 0.0 copy-start.1
  0.6 0.0 copy-start.3
  0.7 1.5 %shard_map.118 = (f32[512,128]{1,0:T(8,128)S(1)}, bf16[512,128]{1,0:T(8,128)(2,1)S(1)}, bf16[512,384]{1,0:T(8,128)(2,1)S(1)}, bf16[256,512]{1,0:T(8,128)(2,1)S(1)}) custom-call(s32[1]{0:T(128)} %bitcast.idx_ref, s32[1]{0:T(128)} %bitcast.1.head_ref.idx_ref, bf16[256,512]{1,0:T(8,128)(2,1)} %refs_10_.1, bf16[256,1024]{1,0:T(8,128)(2,1)} %refs_11_.1, ...), custom_call_target="tpu_custom_call" | custom-call | flops 33554432 | bytes 2097152 | tf_op jit(solution)/shard_map/pallas_call | solution.py:422
  2.2 0.0 copy-start
  2.2 0.4 shard_map.119
  2.6 0.0 copy-start.2
  2.6 3.0 %collective-permute-start.2 = (bf16[192,256]{1,0:T(8,128)(2,1)S(1)}, bf16[192,256]{1,0:T(8,128)(2,1)S(1)}, u32[]{:S(2)}, u32[]{:S(2)}) collective-permute-start(bf16[192,256]{1,0:T(8,128)(2,1)S(1)} %get-tuple-element.53), channel_id=1, source_target_pairs={{0,2},{1,3},{2,0},{3,1},{4,6},{5,7},{6,4},{7,5},{8,10},{9,11},{10,... | collective-permute-start | bytes 294920 | tf_op jit(solution)/shard_map/ppermute | solution.py:51
  5.6 1.5 %collective-permute-start = (bf16[512,128]{1,0:T(8,128)(2,1)S(1)}, bf16[512,128]{1,0:T(8,128)(2,1)S(1)}, u32[]{:S(2)}, u32[]{:S(2)}) collective-permute-start(bf16[512,128]{1,0:T(8,128)(2,1)S(1)} %get-tuple-element.48), channel_id=1, source_target_pairs={{0,4},{4,0},{8,12},{12,8},{16,20},{20,16},{24,28},{28,24},{1,5},{5... | collective-permute-start | bytes 393224 | tf_op jit(solution)/shard_map/ppermute | solution.py:51
  7.1 1.3 %collective-permute-done.2.got_ref = bf16[192,256]{1,0:T(8,128)(2,1)S(1)} collective-permute-done((bf16[192,256]{1,0:T(8,128)(2,1)S(1)}, bf16[192,256]{1,0:T(8,128)(2,1)S(1)}, u32[]{:S(2)}, u32[]{:S(2)}) %collective-permute-start.2) | collective-permute-done | bytes 98336 | tf_op jit(solution)/shard_map/ppermute | solution.py:51
  8.4 0.1 collective-permute-start.3
  8.5 0.0 copy-done.1
  8.5 0.0 copy-done.3
  8.5 0.0 copy-done
  8.5 0.0 copy-done.2
  8.6 0.8 %shard_map.121.gl_ref = f32[96,256]{1,0:T(8,128)S(1)} custom-call(bf16[256,512]{1,0:T(8,128)(2,1)S(1)} %copy-done.2, bf16[256,512]{1,0:T(8,128)(2,1)S(1)} %copy-done.3, bf16[256,1024]{1,0:T(8,128)(2,1)S(1)} %copy-done.1, bf16[256,1024]{1,0:T(8,128)(2,1)S(1)} %copy-done), custom_call_target="tpu_custom_call" | custom-call | flops 201326592 | bytes 196608 | tf_op jit(solution)/shard_map/pallas_call | solution.py:451
  9.3 0.4 collective-permute-done.3.got_ref
  9.7 0.6 %shard_map.122 = (f32[96,256]{1,0:T(8,128)S(1)}, f32[96,256]{1,0:T(8,128)S(1)}, bf16[96,256]{1,0:T(8,128)(2,1)S(1)}, bf16[512,256]{1,0:T(8,128)(2,1)S(1)}, bf16[3,512,128]{2,1,0:T(8,128)(2,1)S(1)}) custom-call(f32[96,256]{1,0:T(8,128)S(1)} %get-tuple-element.54.keep_ref, bf16[96,256]{1,0:T(8,128)(2,1)S(1)} %collective-permute-done.3.got_ref, ...), custom_call_target="tpu_custom_call" | custom-call | flops 100663296 | bytes 1802240 | tf_op jit(solution)/shard_map/pallas_call | solution.py:454
  10.4 1.9 %collective-permute-start.7 = (bf16[96,256]{1,0:T(8,128)(2,1)S(1)}, bf16[96,256]{1,0:T(8,128)(2,1)S(1)}, u32[]{:S(2)}, u32[]{:S(2)}) collective-permute-start(bf16[96,256]{1,0:T(8,128)(2,1)S(1)} %get-tuple-element.72), channel_id=1, source_target_pairs={{0,2},{1,3},{2,0},{3,1},{4,6},{5,7},{6,4},{7,5},{8,10},{9,11},{10,... | collective-permute-start | bytes 147464 | tf_op jit(solution)/shard_map/ppermute | solution.py:51
  12.3 0.0 collective-permute-done.refs_0_
  12.3 1.6 %collective-permute-start.1 = (bf16[512,128]{1,0:T(8,128)(2,1)S(1)}, bf16[512,128]{1,0:T(8,128)(2,1)S(1)}, u32[]{:S(2)}, u32[]{:S(2)}) collective-permute-start(bf16[512,128]{1,0:T(8,128)(2,1)S(1)} %add_convert_fusion), channel_id=1, source_target_pairs={{0,8},{4,12},{8,0},{12,4},{16,24},{20,28},{24,16},{28,20},{1,9},{5... | collective-permute-start | bytes 393224 | tf_op jit(solution)/shard_map/ppermute | solution.py:51
  14.0 0.6 %collective-permute-done.7 = bf16[96,256]{1,0:T(8,128)(2,1)S(1)} collective-permute-done((bf16[96,256]{1,0:T(8,128)(2,1)S(1)}, bf16[96,256]{1,0:T(8,128)(2,1)S(1)}, u32[]{:S(2)}, u32[]{:S(2)}) %collective-permute-start.7) | collective-permute-done | bytes 49184 | tf_op jit(solution)/shard_map/ppermute | solution.py:51
  14.5 0.1 collective-permute-start.8
  14.6 3.0 %collective-permute-done.1.refs_1_ = bf16[512,128]{1,0:T(8,128)(2,1)S(1)} collective-permute-done((bf16[512,128]{1,0:T(8,128)(2,1)S(1)}, bf16[512,128]{1,0:T(8,128)(2,1)S(1)}, u32[]{:S(2)}, u32[]{:S(2)}) %collective-permute-start.1) | collective-permute-done | bytes 131104 | tf_op jit(solution)/shard_map/ppermute | solution.py:51
  17.7 2.6 %collective-permute-start.4 = (bf16[512,128]{1,0:T(8,128)(2,1)S(1)}, bf16[512,128]{1,0:T(8,128)(2,1)S(1)}, u32[]{:S(2)}, u32[]{:S(2)}) collective-permute-start(bf16[512,128]{1,0:T(8,128)(2,1)S(1)} %shard_map.123), channel_id=1, source_target_pairs={{0,16},{4,20},{8,24},{12,28},{16,0},{20,4},{24,8},{28,12},{1,17},{... | collective-permute-start | bytes 393224 | tf_op jit(solution)/shard_map/ppermute | solution.py:51
  20.3 0.0 collective-permute-done.8
  20.3 0.3 shard_map.129
  20.7 1.6 %collective-permute-start.9 = (bf16[256,384]{1,0:T(8,128)(2,1)S(1)}, bf16[256,384]{1,0:T(8,128)(2,1)S(1)}, u32[]{:S(2)}, u32[]{:S(2)}) collective-permute-start(bf16[256,384]{1,0:T(8,128)(2,1)S(1)} %get-tuple-element.75), channel_id=1, source_target_pairs={{0,8},{4,12},{8,0},{12,4},{16,24},{20,28},{24,16},{28,20},{1,9},{5... | collective-permute-start | bytes 589832 | tf_op jit(solution)/shard_map/ppermute | solution.py:51
  22.3 3.4 %collective-permute-done.4.refs_0_.refs_2_.refs_3_ = bf16[512,128]{1,0:T(8,128)(2,1)S(1)} collective-permute-done((bf16[512,128]{1,0:T(8,128)(2,1)S(1)}, bf16[512,128]{1,0:T(8,128)(2,1)S(1)}, u32[]{:S(2)}, u32[]{:S(2)}) %collective-permute-start.4) | collective-permute-done | bytes 131104 | tf_op jit(solution)/shard_map/ppermute | solution.py:51
  25.8 0.1 shard_map.124
  25.8 0.9 %collective-permute-start.5 = (bf16[512,128]{1,0:T(8,128)(2,1)S(1)}, bf16[512,128]{1,0:T(8,128)(2,1)S(1)}, u32[]{:S(2)}, u32[]{:S(2)}) collective-permute-start(bf16[512,128]{1,0:T(8,128)(2,1)S(1)} %shard_map.124), channel_id=1, source_target_pairs={{0,8},{4,12},{8,0},{12,4},{16,24},{20,28},{24,16},{28,20},{1,9},{5... | collective-permute-start | bytes 393224 | tf_op jit(solution)/shard_map/ppermute | solution.py:51
  26.7 0.5 %shard_map.130.refs_4_ = bf16[32,256]{1,0:T(8,128)(2,1)S(1)} custom-call(s32[1]{0:T(128)} %bitcast.idx_ref, bf16[512,128]{1,0:T(8,128)(2,1)S(1)} %collective-permute-done.refs_0_, bf16[512,128]{1,0:T(8,128)(2,1)S(1)} %collective-permute-done.1.refs_1_, bf16[256,1024]{1,0:T(8,128)(2,1)S(1)} %copy-done, ...), custom_call_target="tpu_custom_call" | custom-call | flops 67108864 | bytes 32768 | tf_op jit(solution)/shard_map/pallas_call | solution.py:466
  27.3 0.3 shard_map.131.refs_0_
  27.6 0.1 collective-permute-start.12
  27.6 0.6 %collective-permute-start.11 = (bf16[32,256]{1,0:T(8,128)(2,1)S(1)}, bf16[32,256]{1,0:T(8,128)(2,1)S(1)}, u32[]{:S(2)}, u32[]{:S(2)}) collective-permute-start(bf16[32,256]{1,0:T(8,128)(2,1)S(1)} %shard_map.131.refs_0_), channel_id=1, source_target_pairs={{0,2},{1,3},{2,0},{3,1},{4,6},{5,7},{6,4},{7,5},{8,10},{9,11},{10,... | collective-permute-start | bytes 49160 | tf_op jit(solution)/shard_map/ppermute | solution.py:51
  28.2 1.3 %collective-permute-start.10 = (bf16[32,256]{1,0:T(8,128)(2,1)S(1)}, bf16[32,256]{1,0:T(8,128)(2,1)S(1)}, u32[]{:S(2)}, u32[]{:S(2)}) collective-permute-start(bf16[32,256]{1,0:T(8,128)(2,1)S(1)} %shard_map.131.refs_0_), channel_id=1, source_target_pairs={{0,1},{1,0},{2,3},{3,2},{4,5},{5,4},{6,7},{7,6},{8,9},{9,8},{10,11... | collective-permute-start | bytes 49160 | tf_op jit(solution)/shard_map/ppermute | solution.py:51
  29.5 1.3 %collective-permute-done.12.refs_3_ = bf16[32,256]{1,0:T(8,128)(2,1)S(1)} collective-permute-done((bf16[32,256]{1,0:T(8,128)(2,1)S(1)}, bf16[32,256]{1,0:T(8,128)(2,1)S(1)}, u32[]{:S(2)}, u32[]{:S(2)}) %collective-permute-start.12) | collective-permute-done | bytes 16416 | tf_op jit(solution)/shard_map/ppermute | solution.py:51
  30.8 0.7 %collective-permute-done.11.refs_2_ = bf16[32,256]{1,0:T(8,128)(2,1)S(1)} collective-permute-done((bf16[32,256]{1,0:T(8,128)(2,1)S(1)}, bf16[32,256]{1,0:T(8,128)(2,1)S(1)}, u32[]{:S(2)}, u32[]{:S(2)}) %collective-permute-start.11) | collective-permute-done | bytes 16416 | tf_op jit(solution)/shard_map/ppermute | solution.py:51
  31.5 0.0 collective-permute-done.10.refs_1_
  31.5 0.0 collective-permute-done.9.near_got
  31.5 0.3 shard_map.132
  31.7 1.6 %collective-permute-start.13 = (bf16[128,512]{1,0:T(8,128)(2,1)S(1)}, bf16[128,512]{1,0:T(8,128)(2,1)S(1)}, u32[]{:S(2)}, u32[]{:S(2)}) collective-permute-start(bf16[128,512]{1,0:T(8,128)(2,1)S(1)} %get-tuple-element.85), channel_id=1, source_target_pairs={{0,4},{4,0},{8,12},{12,8},{16,20},{20,16},{24,28},{28,24},{1,5},{5... | collective-permute-start | bytes 393224 | tf_op jit(solution)/shard_map/ppermute | solution.py:51
  33.3 0.0 collective-permute-done.5.refs_1_.refs_4_
  33.3 0.1 shard_map.125
  33.4 0.6 %collective-permute-start.6 = (bf16[512,128]{1,0:T(8,128)(2,1)S(1)}, bf16[512,128]{1,0:T(8,128)(2,1)S(1)}, u32[]{:S(2)}, u32[]{:S(2)}) collective-permute-start(bf16[512,128]{1,0:T(8,128)(2,1)S(1)} %shard_map.125), channel_id=1, source_target_pairs={{0,4},{4,0},{8,12},{12,8},{16,20},{20,16},{24,28},{28,24},{1,5},{5... | collective-permute-start | bytes 393224 | tf_op jit(solution)/shard_map/ppermute | solution.py:51
  34.0 0.1 fusion.1.refs_26_.place_ref
  34.1 1.2 %collective-permute-start.14 = (bf16[128,128]{1,0:T(8,128)(2,1)S(1)}, bf16[128,128]{1,0:T(8,128)(2,1)S(1)}, u32[]{:S(2)}, u32[]{:S(2)}) collective-permute-start(bf16[128,128]{1,0:T(8,128)(2,1)S(1)} %get-tuple-element.86), channel_id=1, source_target_pairs={{0,8},{4,12},{8,0},{12,4},{16,24},{20,28},{24,16},{28,20},{1,9},{5... | collective-permute-start | bytes 98312 | tf_op jit(solution)/shard_map/ppermute | solution.py:51
  35.3 1.8 %collective-permute-start.15 = (bf16[128,128]{1,0:T(8,128)(2,1)S(1)}, bf16[128,128]{1,0:T(8,128)(2,1)S(1)}, u32[]{:S(2)}, u32[]{:S(2)}) collective-permute-start(bf16[128,128]{1,0:T(8,128)(2,1)S(1)} %get-tuple-element.87), channel_id=1, source_target_pairs={{0,12},{4,8},{8,4},{12,0},{16,28},{20,24},{24,20},{28,16},{1,13},{... | collective-permute-start | bytes 98312 | tf_op jit(solution)/shard_map/ppermute | solution.py:51
  37.1 0.8 %shard_map.127 = (f32[256,256]{1,0:T(8,128)S(1)}, f32[128,256]{1,0:T(8,128)S(1)}, f32[256,128]{1,0:T(8,128)S(1)}, f32[256,256]{1,0:T(8,128)S(1)}) custom-call(bf16[256,512]{1,0:T(8,128)(2,1)S(1)} %copy-done.2, bf16[256,512]{1,0:T(8,128)(2,1)S(1)} %copy-done.3, bf16[256,1024]{1,0:T(8,128)(2,1)S(1)} %copy-done.1, bf16[256,1024]{1,0:T(8,128)(2,1)S(1)} %copy-done, ...), custom_call_target="tpu_custom_call" | custom-call | flops 150994944 | bytes 1572864 | tf_op jit(solution)/shard_map/pallas_call | solution.py:519
  37.9 1.4 %shard_map.128 = (f32[512,256]{1,0:T(8,128)S(1)}, f32[256,256]{1,0:T(8,128)S(1)}, f32[256,256]{1,0:T(8,128)S(1)}, f32[256,512]{1,0:T(8,128)S(1)}) custom-call(bf16[256,512]{1,0:T(8,128)(2,1)S(1)} %copy-done.2, bf16[256,512]{1,0:T(8,128)(2,1)S(1)} %copy-done.3, bf16[256,1024]{1,0:T(8,128)(2,1)S(1)} %copy-done.1, bf16[256,1024]{1,0:T(8,128)(2,1)S(1)} %copy-done, ...), custom_call_target="tpu_custom_call" | custom-call | flops 301989888 | bytes 3145728 | tf_op jit(solution)/shard_map/pallas_call | solution.py:519
  39.3 0.0 collective-permute-done.14.two_ref
  39.3 0.9 %collective-permute-done.15.both_ref = bf16[128,128]{1,0:T(8,128)(2,1)S(1)} collective-permute-done((bf16[128,128]{1,0:T(8,128)(2,1)S(1)}, bf16[128,128]{1,0:T(8,128)(2,1)S(1)}, u32[]{:S(2)}, u32[]{:S(2)}) %collective-permute-start.15) | collective-permute-done | bytes 32800 | tf_op jit(solution)/shard_map/ppermute | solution.py:51
  40.2 0.0 collective-permute-done.13.one_ref
  40.2 0.2 shard_map.134
  40.4 0.0 copy-start.4
  40.4 2.6 %collective-permute-start.16 = (bf16[64,384]{1,0:T(8,128)(2,1)S(1)}, bf16[64,384]{1,0:T(8,128)(2,1)S(1)}, u32[]{:S(2)}, u32[]{:S(2)}) collective-permute-start(bf16[64,384]{1,0:T(8,128)(2,1)S(1)} %get-tuple-element.89), channel_id=1, source_target_pairs={{0,16},{4,20},{8,24},{12,28},{16,0},{20,4},{24,8},{28,12},{1,17},{... | collective-permute-start | bytes 147464 | tf_op jit(solution)/shard_map/ppermute | solution.py:51
  43.1 0.8 %shard_map.126 = (f32[256,256]{1,0:T(8,128)S(1)}, f32[128,256]{1,0:T(8,128)S(1)}, f32[256,128]{1,0:T(8,128)S(1)}, f32[256,256]{1,0:T(8,128)S(1)}) custom-call(bf16[256,512]{1,0:T(8,128)(2,1)S(1)} %copy-done.2, bf16[256,512]{1,0:T(8,128)(2,1)S(1)} %copy-done.3, bf16[256,1024]{1,0:T(8,128)(2,1)S(1)} %copy-done.1, bf16[256,1024]{1,0:T(8,128)(2,1)S(1)} %copy-done, ...), custom_call_target="tpu_custom_call" | custom-call | flops 150994944 | bytes 1572864 | tf_op jit(solution)/shard_map/pallas_call | solution.py:519
  43.9 0.0 collective-permute-done.6.refs_5_
  43.9 0.0 copy-done.4
  43.9 2.9 %shard_map.133 = (bf16[256,1024]{1,0:T(8,128)(2,1)}, bf16[256,512]{1,0:T(8,128)(2,1)}, bf16[256,512]{1,0:T(8,128)(2,1)}, bf16[256,512]{1,0:T(8,128)(2,1)}, bf16[256,1024]{1,0:T(8,128)(2,1)}) custom-call(s32[1]{0:T(128)} %bitcast.idx_ref, bf16[512,128]{1,0:T(8,128)(2,1)S(1)} %collective-permute-done.refs_0_, ...), custom_call_target="tpu_custom_call" | custom-call | flops 402653184 | bytes 3670016 | tf_op jit(solution)/shard_map/pallas_call | solution.py:526
  46.8 0.0 collective-permute-done.16
  46.8 0.7 %convert_add_fusion = f32[64,384]{1,0:T(8,128)} fusion(f32[64,384]{1,0:T(8,128)S(1)} %get-tuple-element.88, bf16[64,384]{1,0:T(8,128)(2,1)S(1)} %collective-permute-done.16), kind=kLoop, calls=%fused_computation.6 | loop fusion | flops 49152 | bytes 245760 | tf_op jit(solution)/shard_map/add | solution.py:512
  (7 shorter events, 0.1 us)
Async XLA Ops:
  0.6 7.9 %copy-start.1 = (bf16[256,1024]{1,0:T(8,128)(2,1)S(1)}, bf16[256,1024]{1,0:T(8,128)(2,1)}, u32[]{:S(2)}) copy-start(bf16[256,1024]{1,0:T(8,128)(2,1)} %refs_11_.1) | copy-start | bytes 1572868
  0.6 7.9 %copy-start.3 = (bf16[256,512]{1,0:T(8,128)(2,1)S(1)}, bf16[256,512]{1,0:T(8,128)(2,1)}, u32[]{:S(2)}) copy-start(bf16[256,512]{1,0:T(8,128)(2,1)} %q_ref.9) | copy-start | bytes 786436
  2.2 6.4 %copy-start = (bf16[256,1024]{1,0:T(8,128)(2,1)S(1)}, bf16[256,1024]{1,0:T(8,128)(2,1)}, u32[]{:S(2)}) copy-start(bf16[256,1024]{1,0:T(8,128)(2,1)} %refs_8_.1) | copy-start | bytes 1572868
  2.6 6.0 %copy-start.2 = (bf16[256,512]{1,0:T(8,128)(2,1)S(1)}, bf16[256,512]{1,0:T(8,128)(2,1)}, u32[]{:S(2)}) copy-start(bf16[256,512]{1,0:T(8,128)(2,1)} %refs_10_.1) | copy-start | bytes 786436
  2.6 5.8 %collective-permute-start.2 = (bf16[192,256]{1,0:T(8,128)(2,1)S(1)}, bf16[192,256]{1,0:T(8,128)(2,1)S(1)}, u32[]{:S(2)}, u32[]{:S(2)}) collective-permute-start(bf16[192,256]{1,0:T(8,128)(2,1)S(1)} %get-tuple-element.53), channel_id=1, source_target_pairs={{0,2},{1,3},{2,0},{3,1},{4,6},{5,7},{6,4},{7,5},{8,10},{9,11},{10,... | collective-permute-start | bytes 294920 | tf_op jit(solution)/shard_map/ppermute | solution.py:51
  5.6 6.7 %collective-permute-start = (bf16[512,128]{1,0:T(8,128)(2,1)S(1)}, bf16[512,128]{1,0:T(8,128)(2,1)S(1)}, u32[]{:S(2)}, u32[]{:S(2)}) collective-permute-start(bf16[512,128]{1,0:T(8,128)(2,1)S(1)} %get-tuple-element.48), channel_id=1, source_target_pairs={{0,4},{4,0},{8,12},{12,8},{16,20},{20,16},{24,28},{28,24},{1,5},{5... | collective-permute-start | bytes 393224 | tf_op jit(solution)/shard_map/ppermute | solution.py:51
  8.4 1.3 %collective-permute-start.3 = (bf16[96,256]{1,0:T(8,128)(2,1)S(1)}, bf16[96,256]{1,0:T(8,128)(2,1)S(1)}, u32[]{:S(2)}, u32[]{:S(2)}) collective-permute-start(bf16[96,256]{1,0:T(8,128)(2,1)S(1)} %get-tuple-element.55), channel_id=1, source_target_pairs={{0,1},{1,0},{2,3},{3,2},{4,5},{5,4},{6,7},{7,6},{8,9},{9,8},{10,11... | collective-permute-start | bytes 147464 | tf_op jit(solution)/shard_map/ppermute | solution.py:51
  10.4 4.2 %collective-permute-start.7 = (bf16[96,256]{1,0:T(8,128)(2,1)S(1)}, bf16[96,256]{1,0:T(8,128)(2,1)S(1)}, u32[]{:S(2)}, u32[]{:S(2)}) collective-permute-start(bf16[96,256]{1,0:T(8,128)(2,1)S(1)} %get-tuple-element.72), channel_id=1, source_target_pairs={{0,2},{1,3},{2,0},{3,1},{4,6},{5,7},{6,4},{7,5},{8,10},{9,11},{10,... | collective-permute-start | bytes 147464 | tf_op jit(solution)/shard_map/ppermute | solution.py:51
  12.3 5.3 %collective-permute-start.1 = (bf16[512,128]{1,0:T(8,128)(2,1)S(1)}, bf16[512,128]{1,0:T(8,128)(2,1)S(1)}, u32[]{:S(2)}, u32[]{:S(2)}) collective-permute-start(bf16[512,128]{1,0:T(8,128)(2,1)S(1)} %add_convert_fusion), channel_id=1, source_target_pairs={{0,8},{4,12},{8,0},{12,4},{16,24},{20,28},{24,16},{28,20},{1,9},{5... | collective-permute-start | bytes 393224 | tf_op jit(solution)/shard_map/ppermute | solution.py:51
  14.5 5.8 %collective-permute-start.8 = (bf16[192,256]{1,0:T(8,128)(2,1)S(1)}, bf16[192,256]{1,0:T(8,128)(2,1)S(1)}, u32[]{:S(2)}, u32[]{:S(2)}) collective-permute-start(bf16[192,256]{1,0:T(8,128)(2,1)S(1)} %pad_maximum_fusion.1), channel_id=1, source_target_pairs={{0,1},{1,0},{2,3},{3,2},{4,5},{5,4},{6,7},{7,6},{8,9},{9,8},{10,11... | collective-permute-start | bytes 294920 | tf_op jit(solution)/shard_map/ppermute | solution.py:51
  17.7 8.1 %collective-permute-start.4 = (bf16[512,128]{1,0:T(8,128)(2,1)S(1)}, bf16[512,128]{1,0:T(8,128)(2,1)S(1)}, u32[]{:S(2)}, u32[]{:S(2)}) collective-permute-start(bf16[512,128]{1,0:T(8,128)(2,1)S(1)} %shard_map.123), channel_id=1, source_target_pairs={{0,16},{4,20},{8,24},{12,28},{16,0},{20,4},{24,8},{28,12},{1,17},{... | collective-permute-start | bytes 393224 | tf_op jit(solution)/shard_map/ppermute | solution.py:51
  20.7 10.8 %collective-permute-start.9 = (bf16[256,384]{1,0:T(8,128)(2,1)S(1)}, bf16[256,384]{1,0:T(8,128)(2,1)S(1)}, u32[]{:S(2)}, u32[]{:S(2)}) collective-permute-start(bf16[256,384]{1,0:T(8,128)(2,1)S(1)} %get-tuple-element.75), channel_id=1, source_target_pairs={{0,8},{4,12},{8,0},{12,4},{16,24},{20,28},{24,16},{28,20},{1,9},{5... | collective-permute-start | bytes 589832 | tf_op jit(solution)/shard_map/ppermute | solution.py:51
  25.8 7.5 %collective-permute-start.5 = (bf16[512,128]{1,0:T(8,128)(2,1)S(1)}, bf16[512,128]{1,0:T(8,128)(2,1)S(1)}, u32[]{:S(2)}, u32[]{:S(2)}) collective-permute-start(bf16[512,128]{1,0:T(8,128)(2,1)S(1)} %shard_map.124), channel_id=1, source_target_pairs={{0,8},{4,12},{8,0},{12,4},{16,24},{20,28},{24,16},{28,20},{1,9},{5... | collective-permute-start | bytes 393224 | tf_op jit(solution)/shard_map/ppermute | solution.py:51
  27.6 3.2 %collective-permute-start.12 = (bf16[32,256]{1,0:T(8,128)(2,1)S(1)}, bf16[32,256]{1,0:T(8,128)(2,1)S(1)}, u32[]{:S(2)}, u32[]{:S(2)}) collective-permute-start(bf16[32,256]{1,0:T(8,128)(2,1)S(1)} %shard_map.131.refs_0_), channel_id=1, source_target_pairs={{0,3},{1,2},{2,1},{3,0},{4,7},{5,6},{6,5},{7,4},{8,11},{9,10},{10,... | collective-permute-start | bytes 49160 | tf_op jit(solution)/shard_map/ppermute | solution.py:51
  27.6 3.8 %collective-permute-start.11 = (bf16[32,256]{1,0:T(8,128)(2,1)S(1)}, bf16[32,256]{1,0:T(8,128)(2,1)S(1)}, u32[]{:S(2)}, u32[]{:S(2)}) collective-permute-start(bf16[32,256]{1,0:T(8,128)(2,1)S(1)} %shard_map.131.refs_0_), channel_id=1, source_target_pairs={{0,2},{1,3},{2,0},{3,1},{4,6},{5,7},{6,4},{7,5},{8,10},{9,11},{10,... | collective-permute-start | bytes 49160 | tf_op jit(solution)/shard_map/ppermute | solution.py:51
  28.2 3.2 %collective-permute-start.10 = (bf16[32,256]{1,0:T(8,128)(2,1)S(1)}, bf16[32,256]{1,0:T(8,128)(2,1)S(1)}, u32[]{:S(2)}, u32[]{:S(2)}) collective-permute-start(bf16[32,256]{1,0:T(8,128)(2,1)S(1)} %shard_map.131.refs_0_), channel_id=1, source_target_pairs={{0,1},{1,0},{2,3},{3,2},{4,5},{5,4},{6,7},{7,6},{8,9},{9,8},{10,11... | collective-permute-start | bytes 49160 | tf_op jit(solution)/shard_map/ppermute | solution.py:51
  31.7 8.5 %collective-permute-start.13 = (bf16[128,512]{1,0:T(8,128)(2,1)S(1)}, bf16[128,512]{1,0:T(8,128)(2,1)S(1)}, u32[]{:S(2)}, u32[]{:S(2)}) collective-permute-start(bf16[128,512]{1,0:T(8,128)(2,1)S(1)} %get-tuple-element.85), channel_id=1, source_target_pairs={{0,4},{4,0},{8,12},{12,8},{16,20},{20,16},{24,28},{28,24},{1,5},{5... | collective-permute-start | bytes 393224 | tf_op jit(solution)/shard_map/ppermute | solution.py:51
  33.4 10.5 %collective-permute-start.6 = (bf16[512,128]{1,0:T(8,128)(2,1)S(1)}, bf16[512,128]{1,0:T(8,128)(2,1)S(1)}, u32[]{:S(2)}, u32[]{:S(2)}) collective-permute-start(bf16[512,128]{1,0:T(8,128)(2,1)S(1)} %shard_map.125), channel_id=1, source_target_pairs={{0,4},{4,0},{8,12},{12,8},{16,20},{20,16},{24,28},{28,24},{1,5},{5... | collective-permute-start | bytes 393224 | tf_op jit(solution)/shard_map/ppermute | solution.py:51
  34.1 5.2 %collective-permute-start.14 = (bf16[128,128]{1,0:T(8,128)(2,1)S(1)}, bf16[128,128]{1,0:T(8,128)(2,1)S(1)}, u32[]{:S(2)}, u32[]{:S(2)}) collective-permute-start(bf16[128,128]{1,0:T(8,128)(2,1)S(1)} %get-tuple-element.86), channel_id=1, source_target_pairs={{0,8},{4,12},{8,0},{12,4},{16,24},{20,28},{24,16},{28,20},{1,9},{5... | collective-permute-start | bytes 98312 | tf_op jit(solution)/shard_map/ppermute | solution.py:51
  35.3 4.9 %collective-permute-start.15 = (bf16[128,128]{1,0:T(8,128)(2,1)S(1)}, bf16[128,128]{1,0:T(8,128)(2,1)S(1)}, u32[]{:S(2)}, u32[]{:S(2)}) collective-permute-start(bf16[128,128]{1,0:T(8,128)(2,1)S(1)} %get-tuple-element.87), channel_id=1, source_target_pairs={{0,12},{4,8},{8,4},{12,0},{16,28},{20,24},{24,20},{28,16},{1,13},{... | collective-permute-start | bytes 98312 | tf_op jit(solution)/shard_map/ppermute | solution.py:51
  40.4 3.4 %copy-start.4 = (f32[8,64,128]{2,1,0:T(8,128)S(1)}, f32[8,64,128]{2,1,0:T(8,128)}, u32[]{:S(2)}) copy-start(f32[8,64,128]{2,1,0:T(8,128)} %param.13) | copy-start | bytes 786436
  40.4 6.4 %collective-permute-start.16 = (bf16[64,384]{1,0:T(8,128)(2,1)S(1)}, bf16[64,384]{1,0:T(8,128)(2,1)S(1)}, u32[]{:S(2)}, u32[]{:S(2)}) collective-permute-start(bf16[64,384]{1,0:T(8,128)(2,1)S(1)} %get-tuple-element.89), channel_id=1, source_target_pairs={{0,16},{4,20},{8,24},{12,28},{16,0},{20,4},{24,8},{28,12},{1,17},{... | collective-permute-start | bytes 147464 | tf_op jit(solution)/shard_map/ppermute | solution.py:51
